TPU v7x, 128 devices: a whole 4x4x4 slice. The times are simulated.
128 devices in a mesh: mode: 2 (over x_hi), scan: 64 (over y, z, x_lo, core).
Axes of the slice: x: 4 (x_hi: 2, x_lo: 2; x = x_hi * 2 + x_lo), y: 4, z: 4, core: 2. Of those that a mesh axis runs over, the one named last changes fastest.
Arguments:
- object_field: float32 [2, 32768, 1024], P(None, 'scan'), may hold values from -4.2 to 4.2
- probe: bfloat16 [2, 12, 512, 512], P(None, 'mode'), may hold values from -1.796875 to 1.796875
- patterns: float32 [64, 512, 512], P('scan'), may hold values from 0.2 to 6
- row_shift: int32 [64], P('scan'), may hold values from 0 to 1
- col_start: int32 [64], P('scan'), may hold values from 0 to 2
- mixing: int32 [12, 12], replicated, may hold values from -5 to 20, as said below
Outputs:
- object_new: float32 [2, 32768, 1024], P(None, 'scan')
- probe_new: bfloat16 [2, 12, 512, 512], P(None, 'mode', 'scan')
Inputs may be any that keep to these rules, and one draw needn't show every extreme that they name: `mixing`: diagonal entries are 12 to 20, the others -5 to 5.
All inputs are finite; a program needn't handle non-finite values.
Results may differ from a plain program's by a relative error of at most 0.0095.
The roundings to bfloat16 on the way count: a program that leaves them out, or rounds other values in their place, can miss the bound.
Values sent between devices are 32-bit elements; how exact they have to be, the bound alone decides.
No kernel may reach another device: no remote copies, remote signals or barrier semaphores. Data moves between devices by JAX's collectives and lax.ppermute only.
A program may use at most 128 MiB of HBM per device.

v0:
```python
import math

import jax
import jax.numpy as jnp
from jax import lax
from jax.sharding import Mesh
from jax.sharding import PartitionSpec as P

SCAN = ("scan_0", "scan_1", "scan_2", "scan_3")


def passed_along(value, axis, steps):
    count = lax.axis_size(axis)
    leading, last = (max(0, -steps), min(count, count - steps))
    return lax.ppermute(value, axis, [(source, source + steps) for source in range(leading, last)])


def copy_for_each(shard, axis):
    peers = lax.axis_size(axis)
    return lax.all_to_all(
        jnp.broadcast_to(shard[None], (peers, *shard.shape)), axis, 0, 0, tiled=True
    )


def over_copies(shard, axis):
    everything = copy_for_each(shard, axis)
    return jnp.sum(everything, axis=0)


def in_one(arrays, axis):
    ends = [0]
    for a in arrays:
        ends.append(ends[-1] + a.size)
    so_far = over_copies(jnp.concatenate([a.ravel() for a in arrays]), axis)
    return tuple((so_far[b:e].reshape(a.shape) for a, b, e in zip(arrays, ends, ends[1:])))


def in_blocks(shard, dim, peers):
    dims = shard.shape
    pieces = shard.reshape(*dims[:dim], peers, dims[dim] // peers, *dims[dim + 1 :])
    return jnp.moveaxis(pieces, dim, 0)


def scatter_pairs(shard, chips, core, dim):
    sizes = (lax.axis_size(chips), lax.axis_size(core))
    pieces = in_blocks(shard, dim, sizes[0] * sizes[1])
    inside = pieces.shape[1:]
    pieces = pieces.reshape(*sizes, *inside).swapaxes(0, 1).reshape(-1, *inside)
    pieces = lax.psum_scatter(pieces, core, scatter_dimension=0, tiled=True)
    return lax.psum_scatter(pieces, chips, scatter_dimension=0, tiled=True)[0]


def in_order(pieces, dim):
    dims = list(pieces.shape[1:])
    dims[dim] *= pieces.shape[0]
    return jnp.moveaxis(pieces, 0, dim).reshape(dims)


def gather_directly(shard, axis, dim):
    return in_order(copy_for_each(shard, axis), dim)


def tables(tile_size):
    indices = jnp.arange(tile_size, dtype=jnp.int32)
    products = indices[:, None] * indices[None, :] % tile_size
    angles = products.astype(jnp.float32) * (2.0 * math.pi / tile_size)
    factor = 1.0 / math.sqrt(tile_size)
    return (
        (jnp.cos(angles) * factor).astype(jnp.bfloat16),
        (jnp.sin(angles) * factor).astype(jnp.bfloat16),
    )


def right_mult(first, second):
    return jnp.einsum("...ij,jk->...ik", first, second, preferred_element_type=jnp.float32)


def left_mult(first, second):
    return jnp.einsum("ij,...jk->...ik", first, second, preferred_element_type=jnp.float32)


def transform(real_part, imag_part, cosine, sine_table, direction):
    half_real = right_mult(real_part, cosine) - direction * right_mult(imag_part, sine_table)
    half_imag = right_mult(imag_part, cosine) + direction * right_mult(real_part, sine_table)
    half_real = half_real.astype(jnp.bfloat16)
    half_imag = half_imag.astype(jnp.bfloat16)
    out_real = left_mult(cosine, half_real) - direction * left_mult(sine_table, half_imag)
    out_imag = left_mult(cosine, half_imag) + direction * left_mult(sine_table, half_real)
    return (out_real, out_imag)


def per_device(object_field, probe, patterns, row_shift, col_start, mixing):
    tile_size = probe.shape[2]
    half_rows = tile_size // 2
    local_modes = probe.shape[1]
    positions = patterns.shape[0]
    scan_devices = lax.axis_size(SCAN)
    cosine, sine_table = tables(tile_size)
    lower_rim = passed_along(object_field[:, :half_rows, :], SCAN, -1)
    extended = jnp.concatenate([object_field, lower_rim], axis=1)
    zero_index = jnp.zeros((), jnp.int32)
    slot = 0
    row_first = row_shift[slot] * half_rows
    col_first = col_start[slot] * half_rows
    corners = [(row_first, col_first)]
    gathered = [
        lax.dynamic_slice(extended, (zero_index, row_first, col_first), (2, tile_size, tile_size))
    ]
    patches = jnp.stack(gathered, axis=1)
    obj_real = patches[0][:, None]
    obj_imag = patches[1][:, None]
    probe_real = probe[0].astype(jnp.float32)[None]
    probe_imag = probe[1].astype(jnp.float32)[None]
    exit_real = (probe_real * obj_real - probe_imag * obj_imag).astype(jnp.bfloat16)
    exit_imag = (probe_real * obj_imag + probe_imag * obj_real).astype(jnp.bfloat16)
    wave_real, wave_imag = transform(exit_real, exit_imag, cosine, sine_table, -1.0)
    partial_sum = jnp.sum(wave_real * wave_real + wave_imag * wave_imag, axis=1)
    summed = over_copies(partial_sum, "mode")
    scaling = (jnp.sqrt(patterns) / jnp.sqrt(jnp.maximum(summed, 1.0)))[:, None]
    fixed_real = (wave_real * scaling).astype(jnp.bfloat16)
    fixed_imag = (wave_imag * scaling).astype(jnp.bfloat16)
    back_real, back_imag = transform(fixed_real, fixed_imag, cosine, sine_table, 1.0)
    resid_real = back_real - exit_real.astype(jnp.float32)
    resid_imag = back_imag - exit_imag.astype(jnp.float32)
    grad_real = jnp.sum(probe_real * resid_real + probe_imag * resid_imag, axis=1)
    grad_imag = jnp.sum(probe_real * resid_imag - probe_imag * resid_real, axis=1)
    own_light = jnp.sum(probe_real[0] * probe_real[0] + probe_imag[0] * probe_imag[0], axis=0)
    grad_real, grad_imag, illumination = in_one((grad_real, grad_imag, own_light), "mode")
    accum = jnp.zeros((2, tile_size + half_rows, object_field.shape[2]), jnp.float32)
    slot = 0
    row_first, col_first = corners[slot]
    region = jnp.stack([grad_real[slot], grad_imag[slot]])
    accum = lax.dynamic_update_slice(accum, region, (zero_index, row_first, col_first))
    overflow = passed_along(accum[:, tile_size:, :], SCAN, 1)
    own_rows = accum[:, :tile_size, :]
    own_rows = own_rows.at[:, :half_rows, :].add(overflow)
    object_new = object_field + own_rows / jnp.max(illumination)
    step_real = jnp.sum(obj_real * resid_real + obj_imag * resid_imag, axis=0)
    step_imag = jnp.sum(obj_real * resid_imag - obj_imag * resid_real, axis=0)
    probe_grad = jnp.stack([step_real, step_imag])
    share_rows = tile_size // scan_devices
    row_start = lax.axis_index(SCAN) * share_rows
    my_rows = scatter_pairs(probe_grad, ("scan_0", "scan_1", "scan_2"), "scan_3", 2)
    probe_rows = lax.dynamic_slice_in_dim(probe, row_start, share_rows, 2).astype(jnp.float32)
    updated = probe_rows + my_rows / math.sqrt(positions * scan_devices)
    everyone = gather_directly(updated, "mode", 1)
    weights = mixing.astype(jnp.float32) / 16.0
    my_weights = lax.dynamic_slice_in_dim(
        weights, lax.axis_index("mode") * local_modes, local_modes, 0
    )
    probe_new = jnp.einsum("kj,cjrt->ckrt", my_weights, everyone, precision=lax.Precision.HIGHEST)
    return (object_new, probe_new.astype(jnp.bfloat16))


def solution(mesh):
    split = Mesh(
        mesh.devices.reshape(mesh.shape["mode"], 4, 4, 2, 2),
        ("mode", "scan_0", "scan_1", "scan_2", "scan_3"),
    )
    return jax.shard_map(
        per_device,
        mesh=split,
        in_specs=(
            P(None, SCAN, None),
            P(None, "mode", None, None),
            P(SCAN, None, None),
            P(SCAN),
            P(SCAN),
            P(),
        ),
        out_specs=(P(None, SCAN, None), P(None, "mode", SCAN, None)),
        check_vma=False,
    )
```

profile of v0, /device:TPU:1, one launch (start us, length us, event | category | flops | bytes accessed | tf_op | source)
XLA Modules:
  0.0 549.6 jit_solution(9926847268434274811)
XLA Ops:
  7.2 0.0 reduce-scatter.3.cloned.1.call-start
  7.2 3.2 slice.80
  10.4 3.3 collective-permute-start
  15.0 23.8 %collective-permute-done = f32[2,256,1024]{2,1,0:T(8,128)S(1)} collective-permute-done((f32[2,256,1024]{2,1,0:T(8,128)}, f32[2,256,1024]{2,1,0:T(8,128)S(1)}, u32[]{:S(2)}, u32[]{:S(2)}) %collective-permute-start) | collective-permute-done | bytes 2097184 | tf_op jit(solution)/shard_map/ppermute | solution.py:15
  38.8 1.8 fusion.28
  40.6 0.2 slice_bitcast_fusion.1
  40.8 4.7 fusion.3
  45.5 0.0 copy-start.7
  45.5 9.0 %fusion.16 = f32[6,512,512]{2,1,0:T(8,128)S(1)} fusion(bf16[1,6,512,512]{3,2,1,0:T(8,128)(2,1)S(1)} %get-tuple-element.32), kind=kOutput, calls=%fused_computation.45 | convolution fusion | flops 1614807040 | bytes 9437184 | tf_op jit(solution)/shard_map/...ij,jk->...ik/dot_general | solution.py:75
  54.5 9.0 %fusion.18 = f32[6,512,512]{2,1,0:T(8,128)S(1)} fusion(bf16[1,6,512,512]{3,2,1,0:T(8,128)(2,1)S(1)} %get-tuple-element.32), kind=kOutput, calls=%fused_computation.47 | convolution fusion | flops 1614807040 | bytes 9437184 | tf_op jit(solution)/shard_map/...ij,jk->...ik/dot_general | solution.py:75
  63.5 7.8 %add_convert_fusion.1 = bf16[6,512,512]{2,1,0:T(8,128)(2,1)S(1)} fusion(f32[6,512,512]{2,1,0:T(8,128)S(1)} %fusion.16, bf16[1,6,512,512]{3,2,1,0:T(8,128)(2,1)S(1)} %get-tuple-element.33), kind=kOutput, calls=%fused_computation.39 | convolution fusion | flops 1619525632 | bytes 12582912 | tf_op jit(solution)/shard_map/...ij,jk->...ik/dot_general | solution.py:75
  71.2 7.9 %subtract_convert_fusion.1 = bf16[6,512,512]{2,1,0:T(8,128)(2,1)S(1)} fusion(f32[6,512,512]{2,1,0:T(8,128)S(1)} %fusion.18, bf16[1,6,512,512]{3,2,1,0:T(8,128)(2,1)S(1)} %get-tuple-element.33), kind=kOutput, calls=%fused_computation.40 | convolution fusion | flops 1619525632 | bytes 12582912 | tf_op jit(solution)/shard_map/...ij,jk->...ik/dot_general | solution.py:75
  79.1 10.6 %fusion.64 = f32[6,512,512]{2,1,0:T(8,128)S(1)} fusion(bf16[6,512,512]{2,1,0:T(8,128)(2,1)S(1)} %subtract_convert_fusion.1), kind=kOutput, calls=%fused_computation.83 | convolution fusion | flops 1614807040 | bytes 9437184 | tf_op jit(solution)/shard_map/ij,...jk->...ik/dot_general | solution.py:79
  89.7 10.4 %fusion.61 = f32[6,512,512]{2,1,0:T(8,128)S(1)} fusion(bf16[6,512,512]{2,1,0:T(8,128)(2,1)S(1)} %add_convert_fusion.1), kind=kOutput, calls=%fused_computation.82 | convolution fusion | flops 1614807040 | bytes 9437184 | tf_op jit(solution)/shard_map/ij,...jk->...ik/dot_general | solution.py:79
  100.1 13.2 %multiply_subtract_fusion = f32[6,512,512]{2,1,0:T(8,128)S(1)} fusion(f32[6,512,512]{2,1,0:T(8,128)S(1)} %fusion.64, bf16[6,512,512]{2,1,0:T(8,128)(2,1)S(1)} %add_convert_fusion.1), kind=kOutput, calls=%fused_computation.38 | convolution fusion | flops 1617952768 | bytes 15728640 | tf_op jit(solution)/shard_map/ij,...jk->...ik/dot_general | solution.py:79
  113.3 10.8 %fusion.11 = (f32[512,512]{0,1:T(8,128)}, f32[6,512,512]{2,1,0:T(8,128)}) fusion(f32[6,512,512]{2,1,0:T(8,128)S(1)} %multiply_subtract_fusion, f32[6,512,512]{2,1,0:T(8,128)S(1)} %fusion.61, bf16[6,512,512]{2,1,0:T(8,128)(2,1)S(1)} %subtract_convert_fusion.1), kind=kOutput, calls=%fused_computation.28 | convolution fusion | flops 1623982080 | bytes 23068672 | tf_op jit(solution)/shard_map/ij,...jk->...ik/dot_general | solution.py:79
  124.1 2.5 copy.64
  126.7 1.5 broadcast_in_dim.9
  128.2 19.2 %all_to_all.16 = f32[2,1,512,512]{3,2,1,0:T(8,128)} all-to-all(f32[2,1,512,512]{3,2,1,0:T(8,128)S(1)} %broadcast_in_dim.9), channel_id=1, replica_groups=mesh['mode'=2,'scan_0'=4,'scan_1'=4,'scan_2'=2,'scan_3'=2] {'mode'}, dimensions={0} | all-to-all | bytes 4194304 | tf_op jit(solution)/shard_map/all_to_all | solution.py:20
  147.4 2.9 reduce_sum.55
  150.3 2.9 fusion.34
  153.2 2.5 copy.65
  155.7 12.0 %fusion.42 = f32[6,512,512]{2,1,0:T(8,128)} fusion(f32[6,512,512]{2,1,0:T(8,128)} %copy-done, f32[512,512]{0,1:T(8,128)} %copy.65), kind=kOutput, calls=%fused_computation.76 | convolution fusion | flops 1617952768 | bytes 13631488 | tf_op jit(solution)/shard_map/...ij,jk->...ik/dot_general | solution.py:75
  167.7 8.3 %fusion.38 = f32[6,512,512]{2,1,0:T(8,128)S(1)} fusion(f32[6,512,512]{2,1,0:T(8,128)} %get-tuple-element.40, f32[512,512]{0,1:T(8,128)S(1)} %copy-done.2), kind=kOutput, calls=%fused_computation.75 | convolution fusion | flops 1617952768 | bytes 13631488 | tf_op jit(solution)/shard_map/...ij,jk->...ik/dot_general | solution.py:75
  176.1 0.0 slice-start.1
  176.1 9.9 %subtract_convert_fusion = bf16[6,512,512]{2,1,0:T(8,128)(2,1)S(1)} fusion(f32[6,512,512]{2,1,0:T(8,128)} %fusion.42, f32[6,512,512]{2,1,0:T(8,128)S(1)} %bitcast.135, f32[512,512]{0,1:T(8,128)S(1)} %copy-done.2), kind=kOutput, calls=%fused_computation.36 | convolution fusion | flops 1621098496 | bytes 16777216 | tf_op jit(solution)/shard_map/...ij,jk->...ik/dot_general | solution.py:75
  186.0 7.6 %add_convert_fusion = bf16[6,512,512]{2,1,0:T(8,128)(2,1)S(1)} fusion(f32[6,512,512]{2,1,0:T(8,128)S(1)} %fusion.38, f32[6,512,512]{2,1,0:T(8,128)S(1)} %bitcast.133, f32[512,512]{0,1:T(8,128)S(1)} %copy-done.2), kind=kOutput, calls=%fused_computation.35 | convolution fusion | flops 1621098496 | bytes 16777216 | tf_op jit(solution)/shard_map/...ij,jk->...ik/dot_general | solution.py:75
  193.7 5.4 fusion.58
  199.1 0.0 slice-start.4
  199.1 5.4 fusion.55
  204.5 0.0 slice-start.5
  204.5 7.2 %bitcast_subtract_fusion = f32[1,6,512,512]{3,2,1,0:T(8,128)} fusion(bf16[1,6,512,512]{3,2,1,0:T(8,128)(2,1)S(1)} %get-tuple-element.32, f32[6,512,512]{1,2,0:T(8,128)S(1)} %fusion.58, bf16[6,512,512]{2,1,0:T(8,128)(2,1)S(1)} %subtract_convert_fusion), kind=kOutput, calls=%fused_computation.23 | convolution fusion | flops 1619525632 | bytes 18874368 | tf_op jit(solution)/shard_map/ij,...jk->...ik/dot_general | solution.py:79
  211.8 15.6 %add_bitcast_fusion = (f32[1,6,64,8,512]{4,3,2,1,0:T(8,128)}, f32[1,6,64,8,512]{4,3,2,1,0:T(8,128)}, f32[512,512]{1,0:T(8,128)}, f32[512,512]{1,0:T(8,128)S(1)}, f32[512,512]{1,0:T(8,128)S(1)}) fusion(f32[1,6,512,512]{3,2,1,0:T(8,128)} %bitcast_subtract_fusion, f32[512,512]{1,0:T(8,128)S(1)} %copy-done.6, f32[512,512]{1,0:T(8,128)S(1)} %copy-done.4, ...), kind=kOutput, calls=%fused_computation.34 | convolution fusion | flops 1650196480 | bytes 42991616 | tf_op jit(solution)/shard_map/ij,...jk->...ik/dot_general | solution.py:79
  227.4 10.6 %pad_maximum_fusion = f32[2,6,64,8,512]{4,3,2,1,0:T(8,128)} fusion(f32[1,6,64,8,512]{4,3,2,1,0:T(8,128)} %get-tuple-element.28, f32[1,6,64,8,512]{4,3,2,1,0:T(8,128)} %get-tuple-element.27), kind=kLoop, calls=%fused_computation | loop fusion | flops 3145728 | bytes 25165824 | tf_op jit(solution)/shard_map/stack | solution.py:140
  238.1 11.3 %copy.71 = f32[32,2,2,6,8,512]{5,4,3,2,0,1:T(8,128)} copy(f32[32,2,2,6,8,512]{5,4,1,0,3,2:T(8,128)} %bitcast.137) | data formatting | bytes 25165824 | tf_op jit(solution)/shard_map/reshape | solution.py:48
  249.4 0.0 reduce-scatter.3.cloned.1.call-update
  249.4 0.0 reduce-scatter.5.cloned.1.call-start
  249.5 0.3 copy.88
  249.7 0.3 copy.89
  250.0 1.5 copy.90
  251.5 34.1 %reduce-scatter.3.cloned.1.call-done = f32[32,2,6,8,512]{4,3,2,1,0:T(8,128)} async-done(((f32[64,2,6,8,512]{4,3,2,1,0:T(8,128)}), f32[32,2,6,8,512]{4,3,2,1,0:T(8,128)}) %reduce-scatter.3.cloned.1.call-update) | async-done | bytes 6291472 | tf_op jit(solution)/shard_map/reduce_scatter | solution.py:49
  285.6 0.0 reduce-scatter.5.cloned.1.call-update
  285.7 0.2 pad_maximum_fusion.1
  285.9 3.4 broadcast_in_dim.10
  289.3 137.9 %all_to_all.17 = f32[2,1,786432]{2,1,0:T(1,128)} all-to-all(f32[2,1,786432]{2,1,0:T(1,128)S(1)} %broadcast_in_dim.10), channel_id=1, replica_groups=mesh['mode'=2,'scan_0'=4,'scan_1'=4,'scan_2'=2,'scan_3'=2] {'mode'}, dimensions={0} | all-to-all | bytes 12582912 | tf_op jit(solution)/shard_map/all_to_all | solution.py:20
  427.2 30.3 %reduce_sum.67 = f32[786432]{0:T(1024)S(1)} reduce(f32[2,1,786432]{2,1,0:T(1,128)} %all_to_all.17, f32[]{:T(128)} %constant.75.clone.1), dimensions={0,1}, to_apply=%region_5.6 | reduce | flops 786432 | bytes 9437188 | tf_op jit(solution)/shard_map/reduce_sum | solution.py:27
  457.5 2.1 slice_reduce_fusion
  459.6 1.4 slice.85
  461.0 1.4 slice.87
  462.5 0.8 broadcast_in_dim.8
  463.3 0.2 maximum_dynamic-update-slice_fusion
  463.5 2.6 copy-done.1
  466.2 1.5 slice.98
  467.6 7.0 %collective-permute-start.1 = (f32[2,256,1024]{2,1,0:T(8,128)}, f32[2,256,1024]{2,1,0:T(8,128)S(1)}, u32[]{:S(2)}, u32[]{:S(2)}) collective-permute-start(f32[2,256,1024]{2,1,0:T(8,128)} %slice.98), channel_id=1, source_target_pairs={{0,1},{1,2},{2,3},{3,4},{4,5},{5,6},{6,7},{7,8},{8,9},{9,10},{10,1... | collective-permute-start | bytes 6291464 | tf_op jit(solution)/shard_map/ppermute | solution.py:15
  474.7 4.8 slice.96
  479.5 44.8 %collective-permute-done.1 = f32[2,256,1024]{2,1,0:T(8,128)S(1)} collective-permute-done((f32[2,256,1024]{2,1,0:T(8,128)}, f32[2,256,1024]{2,1,0:T(8,128)S(1)}, u32[]{:S(2)}, u32[]{:S(2)}) %collective-permute-start.1) | collective-permute-done | bytes 2097184 | tf_op jit(solution)/shard_map/ppermute | solution.py:15
  524.3 3.3 fusion.29
  527.6 1.0 bitcast_add_fusion
  528.6 0.8 broadcast_in_dim.11
  529.4 3.9 all-to-all-start.2
  533.3 7.6 %divide_add_fusion = f32[2,512,1024]{2,1,0:T(8,128)} fusion(f32[2,512,1024]{2,1,0:T(8,128)} %param.8, f32[2,512,1024]{2,1,0:T(8,128)} %fusion.29, f32[]{:T(128)} %get-tuple-element.34), kind=kLoop, calls=%fused_computation.41 | loop fusion | flops 2097152 | bytes 12582916 | tf_op jit(solution)/shard_map/add | solution.py:137
  540.9 0.0 all-to-all-done.2
  540.9 0.8 fusion.30
  541.7 0.7 copy.74
  (30 shorter events, 0.1 us)
Async XLA Ops:
  7.2 278.5 %reduce-scatter.3.cloned.1.call-start = ((), (), s32[]{:S(2)}) async-start(), calls=%async_computation.5 | async-start | bytes 18874368 | tf_op jit(solution)/shard_map/reduce_scatter | solution.py:49
  10.4 28.4 %collective-permute-start = (f32[2,256,1024]{2,1,0:T(8,128)}, f32[2,256,1024]{2,1,0:T(8,128)S(1)}, u32[]{:S(2)}, u32[]{:S(2)}) collective-permute-start(f32[2,256,1024]{2,1,0:T(8,128)} %slice.80), channel_id=1, source_target_pairs={{1,0},{2,1},{3,2},{4,3},{5,4},{6,5},{7,6},{8,7},{9,8},{10,9},{11,1... | collective-permute-start | bytes 6291464 | tf_op jit(solution)/shard_map/ppermute | solution.py:15
  40.7 4.7 copy-start.3
  40.8 4.7 copy-start.5
  45.5 25.8 %copy-start.7 = (bf16[1,6,512,512]{3,2,1,0:T(8,128)(2,1)}, bf16[1,6,512,512]{3,2,1,0:T(8,128)(2,1)S(1)}, u32[]{:S(2)}) copy-start(bf16[1,6,512,512]{3,2,1,0:T(8,128)(2,1)S(1)} %get-tuple-element.33) | copy-start | bytes 9437188
  113.3 10.8 %copy-start = (f32[6,512,512]{2,1,0:T(8,128)}, f32[6,512,512]{2,1,0:T(8,128)S(1)}, u32[]{:S(2)}) copy-start(f32[6,512,512]{2,1,0:T(8,128)S(1)} %multiply_subtract_fusion) | copy-start | bytes 18874372
  155.7 12.0 %copy-start.2 = (f32[512,512]{0,1:T(8,128)S(1)}, f32[512,512]{0,1:T(8,128)}, u32[]{:S(2)}) copy-start(f32[512,512]{0,1:T(8,128)} %copy.65) | copy-start | bytes 3145732
  155.7 20.4 %slice-start.2 = ((s8[6291456]{0:T(1024)(128)(4,1)}), s8[4194304]{0:T(1024)(128)(4,1)S(1)}, s32[]{:S(2)}) async-start(s8[6291456]{0:T(1024)(128)(4,1)} %bitcast.134), calls=%async_computation.9 | async-start | bytes 8388608
  167.7 8.4 %slice-start.3 = ((s8[6291456]{0:T(1024)(128)(4,1)}), s8[2097152]{0:T(1024)(128)(4,1)S(1)}, s32[]{:S(2)}) async-start(s8[6291456]{0:T(1024)(128)(4,1)} %bitcast.134), calls=%async_computation.10 | async-start | bytes 4194304
  167.7 18.3 %slice-start = ((s8[6291456]{0:T(1024)(128)(4,1)}), s8[4194304]{0:T(1024)(128)(4,1)S(1)}, s32[]{:S(2)}) async-start(s8[6291456]{0:T(1024)(128)(4,1)} %bitcast.132), calls=%async_computation.7 | async-start | bytes 8388608
  176.1 10.0 %slice-start.1 = ((s8[6291456]{0:T(1024)(128)(4,1)}), s8[2097152]{0:T(1024)(128)(4,1)S(1)}, s32[]{:S(2)}) async-start(s8[6291456]{0:T(1024)(128)(4,1)} %bitcast.132), calls=%async_computation.8 | async-start | bytes 4194304
  199.1 12.7 %slice-start.4 = ((s8[6291456]{0:T(1024)(128)(4,1)}), s8[4194304]{0:T(1024)(128)(4,1)S(1)}, s32[]{:S(2)}) async-start(s8[6291456]{0:T(1024)(128)(4,1)} %bitcast.138), calls=%async_computation.11 | async-start | bytes 8388608
  204.5 7.3 %slice-start.5 = ((s8[6291456]{0:T(1024)(128)(4,1)}), s8[2097152]{0:T(1024)(128)(4,1)S(1)}, s32[]{:S(2)}) async-start(s8[6291456]{0:T(1024)(128)(4,1)} %bitcast.138), calls=%async_computation.12 | async-start | bytes 4194304
  204.5 7.3 %copy-start.4 = (f32[512,512]{1,0:T(8,128)S(1)}, f32[512,512]{1,0:T(8,128)}, u32[]{:S(2)}) copy-start(f32[512,512]{1,0:T(8,128)} %copy-done.3) | copy-start | bytes 3145732
  204.5 7.3 %copy-start.6 = (f32[512,512]{1,0:T(8,128)S(1)}, f32[512,512]{1,0:T(8,128)}, u32[]{:S(2)}) copy-start(f32[512,512]{1,0:T(8,128)} %copy-done.5) | copy-start | bytes 3145732
  249.4 278.2 %reduce-scatter.5.cloned.1.call-start = ((), (), s32[]{:S(2)}) async-start(), calls=%async_computation.6 | async-start | bytes 6488064 | tf_op jit(solution)/shard_map/reduce_scatter | solution.py:50
  463.5 2.6 copy-start.1
  467.6 56.7 %collective-permute-start.1 = (f32[2,256,1024]{2,1,0:T(8,128)}, f32[2,256,1024]{2,1,0:T(8,128)S(1)}, u32[]{:S(2)}, u32[]{:S(2)}) collective-permute-start(f32[2,256,1024]{2,1,0:T(8,128)} %slice.98), channel_id=1, source_target_pairs={{0,1},{1,2},{2,3},{3,4},{4,5},{5,6},{6,7},{7,8},{8,9},{9,10},{10,1... | collective-permute-start | bytes 6291464 | tf_op jit(solution)/shard_map/ppermute | solution.py:15
  529.4 11.5 %all-to-all-start.2 = ((f32[2,2,6,8,512]{4,3,2,1,0:T(8,128)}), f32[2,2,6,8,512]{4,3,2,1,0:T(8,128)S(1)}, u32[]{:S(2)}, u32[]{:S(2)}) async-start(f32[2,2,6,8,512]{4,3,2,1,0:T(8,128)} %broadcast_in_dim.11), calls=%async_computation.4 | async-start | bytes 786432 | tf_op jit(solution)/shard_map/all_to_all | solution.py:20
  533.3 7.6 %copy-start.8 = (s32[12,12]{1,0:T(8,128)S(1)}, s32[12,12]{1,0:T(8,128)}, u32[]{:S(2)}) copy-start(s32[12,12]{1,0:T(8,128)} %param.13) | copy-start | bytes 1732
Sparse Core Ops, SparseCore 0:
  249.5 36.0 reduce-scatter.2
  288.1 224.5 reduce-scatter.4
where the time goes:
time: 560 us; the launch traced here: 550 us
  blocking collectives  157 us (28%)
  matrix products  151 us (27%)
  waiting for transfers between devices  103 us (18%)
  other arithmetic  67.5 us (12%)
  local copies, waits for them, and re-layouts  40.7 us (7%)
  between operations  16.1 us (3%)
  starting transfers between devices  14.4 us (3%)
    all_to_all x2, blocking collectives, copy_for_each(): lax.all_to_all(jnp.broadcast_to(shard[None], (peers, *shard.shape)), axis...  157 us
    dot_general x8, matrix products, left_mult(): jnp.einsum('ij,...jk->...ik', first, second, preferred_element_type=jnp.f...  78.7 us
    dot_general x8, matrix products, right_mult(): jnp.einsum('...ij,jk->...ik', first, second, preferred_element_type=jnp.f...  71.5 us
    ppermute x2, waiting for transfers between devices, passed_along(): lax.ppermute(value, axis, [(source, source + steps) for source in range(l...  68.6 us
    reduce_scatter x1, waiting for transfers between devices, scatter_pairs(): pieces = lax.psum_scatter(pieces, core, scatter_dimension=0, tiled=True)  34.1 us
    reduce_sum x2, other arithmetic, over_copies(): return jnp.sum(everything, axis=0)  33.2 us
    reshape x1, local copies, waits for them, and re-layouts, scatter_pairs(): pieces = pieces.reshape(*sizes, *inside).swapaxes(0, 1).reshape(-1, *inside)  11.3 us
  transfers between devices with their start and end apart: 5, of which 3 were waited for; matrix products, arithmetic and copies ran while one was open for 11% of the time, Pallas kernels for 0%

commit v1 on v0

v1 whole, which is shorter than its diff:
```python
import functools, math
import jax, jax.numpy as jnp, numpy as np, ml_dtypes
from jax import lax
from jax.sharding import Mesh
from jax.sharding import PartitionSpec as P
from jax.experimental import pallas as pl
from jax.experimental.pallas import tpu as pltpu
f32, bf16 = jnp.float32, jnp.bfloat16
N = 512

def tables():
    i = np.arange(N, dtype=np.int32)
    ang = (i[:, None] * i[None, :] % N).astype(np.float32) * np.float32(2.0 * math.pi / N)
    f = np.float32(1.0 / math.sqrt(N))
    c = (np.cos(ang) * f).astype(ml_dtypes.bfloat16)
    s = (np.sin(ang) * f).astype(ml_dtypes.bfloat16)
    a = np.block([[c, -s], [s, c]])
    b = np.block([[c, s], [-s, c]])
    return a, b

ROWS = 64

def chunks(fn, rows=ROWS):
    def body(i, _):
        fn(pl.ds(pl.multiple_of(i * rows, rows), rows), i)
        return 0
    lax.fori_loop(0, N // rows, body, 0)

def make_exit(p_ref, m, patch_ref, rows):
    pr = p_ref[0, m, rows, :].astype(f32)
    pi = p_ref[1, m, rows, :].astype(f32)
    o_r = patch_ref[0, rows, :]
    o_i = patch_ref[1, rows, :]
    return pr, pi, o_r, o_i, (pr * o_r - pi * o_i).astype(bf16), (pr * o_i + pi * o_r).astype(bf16)

def forward_body(sc, tl, tr, bl, br, rl, rr, p_ref, a_ref, b_ref, wave_ref, sum_ref, patch_ref, x_s, h_s, *, mb):
    @pl.when(pl.program_id(0) == 0)
    def _():
        h = N // 2
        patch_ref[:, :h, :h] = tl[...]
        patch_ref[:, :h, h:] = tr[...]
        inside = sc[0] == 0
        @pl.when(inside)
        def _():
            patch_ref[:, h:, :h] = bl[...]
            patch_ref[:, h:, h:] = br[...]
        @pl.when(jnp.logical_not(inside))
        def _():
            patch_ref[:, h:, :h] = rl[...]
            patch_ref[:, h:, h:] = rr[...]
        sum_ref[...] = jnp.zeros_like(sum_ref)
    for m in range(mb):
        def one(rows, i):
            _, _, _, _, xr, xi = make_exit(p_ref, m, patch_ref, rows)
            x_s[m, rows, :N] = xr
            x_s[m, rows, N:] = xi
        chunks(one)
    for m in range(mb):
        half = jnp.dot(x_s[m], a_ref[...], preferred_element_type=f32).astype(bf16)
        h_s[:N, m * N:(m + 1) * N] = half[:, :N]
        h_s[N:, m * N:(m + 1) * N] = half[:, N:]
    for m in range(mb):
        w = jnp.dot(b_ref[...], h_s[:, m * N:(m + 1) * N], preferred_element_type=f32)
        wave_ref[0, m] = w[:N]
        wave_ref[1, m] = w[N:]
    def two(rows, i):
        acc = sum_ref[rows, :]
        for m in range(mb):
            a = wave_ref[0, m, rows, :]
            b = wave_ref[1, m, rows, :]
            acc = acc + (a * a + b * b)
        sum_ref[rows, :] = acc
    chunks(two)

def forward(sc, obj, rim, probe, a, b, mb=1):
    nm = probe.shape[1]
    q = (2, N // 2, N // 2)
    spec = lambda f: pl.BlockSpec(q, f)
    whole = lambda shp: pl.BlockSpec(shp, lambda k, sc: (0,) * len(shp))
    return pl.pallas_call(
        functools.partial(forward_body, mb=mb),
        grid_spec=pltpu.PrefetchScalarGridSpec(
            num_scalar_prefetch=1, grid=(nm // mb,),
            in_specs=[
                spec(lambda k, sc: (0, sc[0], sc[1])), spec(lambda k, sc: (0, sc[0], sc[1] + 1)),
                spec(lambda k, sc: (0, 1, sc[1])), spec(lambda k, sc: (0, 1, sc[1] + 1)),
                spec(lambda k, sc: (0, 0, sc[1])), spec(lambda k, sc: (0, 0, sc[1] + 1)),
                pl.BlockSpec((2, mb, N, N), lambda k, sc: (0, k, 0, 0)),
                whole((2 * N, 2 * N)), whole((2 * N, 2 * N))],
            out_specs=[
                pl.BlockSpec((2, mb, N, N), lambda k, sc: (0, k, 0, 0)),
                whole((N, N)), whole((2, N, N))],
            scratch_shapes=[pltpu.VMEM((mb, N, 2 * N), bf16), pltpu.VMEM((2 * N, mb * N), bf16)]),
        out_shape=[jax.ShapeDtypeStruct((2, nm, N, N), f32), jax.ShapeDtypeStruct((N, N), f32), jax.ShapeDtypeStruct((2, N, N), f32)],
        compiler_params=pltpu.CompilerParams(dimension_semantics=("arbitrary",), vmem_limit_bytes=56 << 20),
        name="forward",
    )(sc, obj, obj, obj, obj, rim, rim, probe, a, b)

def backward_body(sc, pat, s0, s1, patch_ref, p_ref, wave_ref, a_ref, b_ref, gin_ref, keep_ref, send_ref, top_ref, bot_ref, scale_s, x_s, h_s, *, mb, first):
    h = N // 2
    @pl.when(pl.program_id(0) == 0)
    def _():
        def one(rows, i):
            scale_s[rows, :] = jnp.sqrt(pat[0, rows, :]) / jnp.sqrt(jnp.maximum(s0[rows, :] + s1[rows, :], 1.0))
        chunks(one)
        if first:
            top_ref[...] = jnp.zeros_like(top_ref)
            bot_ref[...] = jnp.zeros_like(bot_ref)
        else:
            top_ref[...] = gin_ref[0][...]
            bot_ref[...] = gin_ref[1][...]
    core = sc[0]
    for m in range(mb):
        def one(rows, i):
            sc_ = scale_s[rows, :]
            x_s[rows, :N] = (wave_ref[0, m, rows, :] * sc_).astype(bf16)
            x_s[rows, N:] = (wave_ref[1, m, rows, :] * sc_).astype(bf16)
        chunks(one)
        half = jnp.dot(x_s[...], b_ref[...], preferred_element_type=f32).astype(bf16)
        h_s[:N] = half[:, :N]
        h_s[N:] = half[:, N:]
        back = jnp.dot(a_ref[...], h_s[...], preferred_element_type=f32)
        wave_ref[0, m] = back[:N]
        wave_ref[1, m] = back[N:]
        def two(rows, i, g_ref, r_out):
            pr, pi, o_r, o_i, xr, xi = make_exit(p_ref, m, patch_ref, rows)
            rr = wave_ref[0, m, rows, :] - xr.astype(f32)
            ri = wave_ref[1, m, rows, :] - xi.astype(f32)
            g_ref[0, r_out, :] += pr * rr + pi * ri
            g_ref[1, r_out, :] += pr * ri - pi * rr
            st = (o_r * rr + o_i * ri, o_r * ri - o_i * rr)
            n16 = ROWS // 16
            for c in range(2):
                v = st[c].reshape(n16, 2, 8, N)
                lo, hi = v[:, 0], v[:, 1]
                at = pl.ds(pl.multiple_of(i * n16, n16), n16)
                keep_ref[c, m, at] = jnp.where(core == 0, lo, hi)
                send_ref[c, m, at] = jnp.where(core == 0, hi, lo)
        nc = h // ROWS
        def tb(i, _):
            two(pl.ds(pl.multiple_of(i * ROWS, ROWS), ROWS), i, top_ref, pl.ds(pl.multiple_of(i * ROWS, ROWS), ROWS))
            return 0
        lax.fori_loop(0, nc, tb, 0)
        def bb(i, _):
            two(pl.ds(pl.multiple_of((i + nc) * ROWS, ROWS), ROWS), i + nc, bot_ref, pl.ds(pl.multiple_of(i * ROWS, ROWS), ROWS))
            return 0
        lax.fori_loop(0, nc, bb, 0)

def backward(sc, pat, s0, s1, patch, probe, wave, a, b, grads, first_mode, nm, mb=1):
    whole = lambda shp: pl.BlockSpec(shp, lambda k, sc: (0,) * len(shp))
    off = first_mode // mb
    first = grads is None
    def body(sc, *refs):
        refs = list(refs)
        ins = refs[:8]; refs = refs[8:]
        gin = None
        if not first:
            gin = refs[:2]; refs = refs[2:]
        backward_body(sc, *ins, gin, *refs, mb=mb, first=first)
    kshape = (2, nm, 32, 8, N)
    modes = pl.BlockSpec((2, mb, N, N), lambda k, sc: (0, k + off, 0, 0))
    half = whole((2, N // 2, N))
    return pl.pallas_call(
        body,
        grid_spec=pltpu.PrefetchScalarGridSpec(
            num_scalar_prefetch=1, grid=(nm // mb,),
            in_specs=[whole((1, N, N)), whole((N, N)), whole((N, N)), whole((2, N, N)), modes, modes,
                      whole((2 * N, 2 * N)), whole((2 * N, 2 * N))] + ([] if first else [half, half]),
            out_specs=[pl.BlockSpec((2, mb, 32, 8, N), lambda k, sc: (0, k, 0, 0, 0))] * 2 + [half, half],
            scratch_shapes=[pltpu.VMEM((N, N), f32), pltpu.VMEM((N, 2 * N), bf16), pltpu.VMEM((2 * N, N), bf16)]),
        out_shape=[jax.ShapeDtypeStruct(kshape, f32)] * 2 + [jax.ShapeDtypeStruct((2, N // 2, N), f32)] * 2,
        compiler_params=pltpu.CompilerParams(dimension_semantics=("arbitrary",), vmem_limit_bytes=56 << 20),
        name="backward",
    )(sc, pat, s0, s1, patch, probe, wave, a, b, *([] if first else grads))


SCAN = ("y", "z", "x", "core")
GROUPS = 2
VMEM = pltpu.CompilerParams(vmem_limit_bytes=56 << 20)


def shape(*dims):
    return jax.ShapeDtypeStruct(dims, f32)


def whole_spec(dims):
    return pl.BlockSpec(dims, lambda *_: (0,) * len(dims))


def along(value, axis, steps):
    count = lax.axis_size(axis)
    lo, hi = max(0, -steps), min(count, count - steps)
    return lax.ppermute(value, axis, [(i, i + steps) for i in range(lo, hi)])


def turned(value, axis, steps):
    count = lax.axis_size(axis)
    return lax.ppermute(value, axis, [(i, (i + steps) % count) for i in range(count)])


def swapped(value, axis):
    return turned(value, axis, 1)


def quarters(parts, axis):
    return [parts[0]] + [turned(parts[r], axis, r) for r in (1, 3, 2)]


def light_body(p_ref, out_ref):
    @pl.when(pl.program_id(0) == 0)
    def _():
        out_ref[...] = jnp.zeros_like(out_ref)

    def one(rows, i):
        pr = p_ref[0, 0, rows, :].astype(f32)
        pi = p_ref[1, 0, rows, :].astype(f32)
        out_ref[rows, :] += pr * pr + pi * pi

    chunks(one)


def light(probe):
    return pl.pallas_call(
        light_body,
        grid=(probe.shape[1],),
        in_specs=[pl.BlockSpec((2, 1, N, N), lambda k: (0, k, 0, 0))],
        out_specs=whole_spec((N, N)),
        out_shape=shape(N, N),
        name="light",
    )(probe)


def core_add_body(at, keep, recv, *outs):
    y, z = at[0], at[1]
    for r in range(4):
        yy = lax.rem(y + r, 4)
        zz = lax.rem(z + r, 4)
        outs[r][0] = keep[0, 0, yy] + recv[0, 0, yy]
        outs[4 + r][0] = keep[1, 0, :, zz] + recv[1, 0, :, zz]


def core_add(at, keep, recv):
    nm = keep.shape[1]
    dims = (2, nm, 4, 4, 16, N)
    spec = pl.BlockSpec((2, 1, 4, 4, 16, N), lambda k, at: (0, k, 0, 0, 0, 0))
    out = pl.BlockSpec((1, 4, 16, N), lambda k, at: (k, 0, 0, 0))
    outs = pl.pallas_call(
        core_add_body,
        grid_spec=pltpu.PrefetchScalarGridSpec(
            num_scalar_prefetch=1, grid=(nm,), in_specs=[spec, spec], out_specs=[out] * 8
        ),
        out_shape=[shape(nm, 4, 16, N)] * 8,
        compiler_params=VMEM,
        name="core_add",
    )(at, keep.reshape(dims), recv.reshape(dims))
    return outs[:4], outs[4:]


def plane_add_body(at, *refs, groups, nm):
    ins, outs = refs[: 8 * groups], refs[8 * groups :]
    y, z = at[0], at[1]
    for r in range(4):
        for part, pos in ((0, lax.rem(z + r, 4)), (1, lax.rem(y + r, 4))):
            for g in range(groups):
                a = ins[g * 8 + part * 4 : g * 8 + part * 4 + 4]
                outs[part * 4 + r][g * nm : (g + 1) * nm] = (
                    (a[0][:, pos] + a[1][:, pos]) + (a[2][:, pos] + a[3][:, pos])
                )


def plane_add(at, groups):
    nm = groups[0][0].shape[0]
    ng = len(groups)
    ins = [a for g in groups for a in g]
    outs = pl.pallas_call(
        functools.partial(plane_add_body, groups=ng, nm=nm),
        grid_spec=pltpu.PrefetchScalarGridSpec(
            num_scalar_prefetch=1,
            grid=(1,),
            in_specs=[whole_spec(a.shape) for a in ins],
            out_specs=[whole_spec((ng * nm, 16, N))] * 8,
        ),
        out_shape=[shape(ng * nm, 16, N)] * 8,
        compiler_params=VMEM,
        name="plane_add",
    )(at, *ins)
    return outs[:4], outs[4:]


def row_add_body(at, *refs):
    ins, rows, outs = refs[:8], refs[8], refs[9:]
    x = at[2]
    nm = ins[0].shape[0]
    scale = 1.0 / math.sqrt(64)
    for part in range(2):
        a = ins[part * 4 : part * 4 + 4]

        def total(xx):
            at_rows = pl.ds(pl.multiple_of(xx * 8, 8), 8)
            return ((a[0][:, at_rows] + a[1][:, at_rows]) + (a[2][:, at_rows] + a[3][:, at_rows])) * scale

        mine = total(x) + rows[part].astype(f32)
        outs[0][part] = mine
        outs[1][part] = total(1 - x)


def row_add(at, parts, rows):
    nm = rows.shape[1]
    ins = [*parts, rows]
    return pl.pallas_call(
        row_add_body,
        grid_spec=pltpu.PrefetchScalarGridSpec(
            num_scalar_prefetch=1,
            grid=(1,),
            in_specs=[whole_spec(a.shape) for a in ins],
            out_specs=[whole_spec((2, nm, 8, N))] * 2,
        ),
        out_shape=[shape(2, nm, 8, N)] * 2,
        compiler_params=VMEM,
        name="row_add",
    )(at, *ins)


def mix_body(at, w_ref, mine, b, c, d, out_ref):
    mode = at[3]
    nm = mine.shape[1]
    for part in range(2):
        own = [mine[part, j] + b[part, j] for j in range(nm)]
        far = [c[part, j] + d[part, j] for j in range(nm)]
        for k in range(nm):
            row = mode * nm + k
            acc = jnp.zeros((8, N), f32)
            for j in range(nm):
                acc += (w_ref[row, mode * nm + j].astype(f32) / 16.0) * own[j]
                acc += (w_ref[row, (1 - mode) * nm + j].astype(f32) / 16.0) * far[j]
            out_ref[part, k] = acc.astype(bf16)


def mix(at, mixing, mine, b, c, d):
    dims = mine.shape
    return pl.pallas_call(
        mix_body,
        grid_spec=pltpu.PrefetchScalarGridSpec(
            num_scalar_prefetch=2, grid=(1,), in_specs=[whole_spec(dims)] * 4, out_specs=whole_spec(dims)
        ),
        out_shape=jax.ShapeDtypeStruct(dims, bf16),
        compiler_params=VMEM,
        name="mix",
    )(at, mixing, mine, b, c, d)


def object_body(sc, lights, obj, top, top2, bot, bot2, over, out_ref):
    i, j = pl.program_id(0), pl.program_id(1)
    own_i, own_j = i - sc[0], j - sc[1]
    over_j = j - sc[3]
    out_ref[...] = obj[...]
    inv = lights[0]
    in_cols = jnp.logical_and(own_j >= 0, own_j < 2)

    @pl.when(jnp.logical_and(in_cols, own_i == 0))
    def _():
        out_ref[...] += (top[...] + top2[...]) / inv

    @pl.when(jnp.logical_and(in_cols, own_i == 1))
    def _():
        out_ref[...] += (bot[...] + bot2[...]) / inv

    @pl.when(jnp.logical_and(jnp.logical_and(i == 0, sc[2] == 1), jnp.logical_and(over_j >= 0, over_j < 2)))
    def _():
        out_ref[...] += over[...] / inv


def object_update(sc, brightest, obj, top, top2, bot, bot2, over):
    h = N // 2
    q = (2, h, h)
    own = pl.BlockSpec(q, lambda i, j, sc, li: (0, 0, jnp.clip(j - sc[1], 0, 1)))
    return pl.pallas_call(
        object_body,
        grid_spec=pltpu.PrefetchScalarGridSpec(
            num_scalar_prefetch=2,
            grid=(2, 4),
            in_specs=[pl.BlockSpec(q, lambda i, j, sc, li: (0, i, j))]
            + [own] * 4
            + [pl.BlockSpec(q, lambda i, j, sc, li: (0, 0, jnp.clip(j - sc[3], 0, 1)))],
            out_specs=pl.BlockSpec(q, lambda i, j, sc, li: (0, i, j)),
        ),
        out_shape=shape(2, N, 1024),
        compiler_params=VMEM,
        name="object_update",
    )(sc, brightest, obj, top, top2, bot, bot2, over)


def per_device(object_field, probe, patterns, row_shift, col_start, mixing):
    h = N // 2
    nm = probe.shape[1]
    a_table, b_table = tables()
    core = lax.axis_index("core")
    at = jnp.stack([lax.axis_index("y"), lax.axis_index("z"), lax.axis_index("x"), lax.axis_index("mode")])
    place = jnp.concatenate([row_shift, col_start])
    before = along(place, SCAN, 1)
    rim = along(object_field[:, :h, :], SCAN, -1)
    own_light = light(probe)
    wave, own_sum, patch = forward(place, object_field, rim, probe, a_table, b_table)
    far_sum = swapped(own_sum, "mode")
    far_light = swapped(own_light, "mode")
    brightest = jnp.max(own_light + far_light)[None]
    grads = None
    planes = []
    group = nm // GROUPS
    for g in range(GROUPS):
        keep, send, *grads = backward(
            core[None], patterns, own_sum, far_sum, patch, probe, wave, a_table, b_table, grads, g * group, group
        )
        real, imag = core_add(at, keep, swapped(send, "core"))
        planes.append(quarters(real, "y") + quarters(imag, "z"))
    top, bot = grads
    far_bot = swapped(bot, "mode")
    far_top = swapped(top, "mode")
    over = along(bot + far_bot, SCAN, 1)
    real, imag = plane_add(at, planes)
    parts = quarters(real, "z") + quarters(imag, "y")
    rows = lax.dynamic_slice_in_dim(probe, lax.axis_index(SCAN) * 8, 8, 2)
    mine, other = row_add(at, parts, rows)
    pairs = [((m, x), (m, 1 - x)) for m in range(2) for x in range(2)]
    flat = lambda m, x: 2 * m + x
    both = ("mode", "x")
    b = lax.ppermute(other, both, [(flat(m, x), flat(m, 1 - x)) for m in range(2) for x in range(2)])
    c = lax.ppermute(mine, both, [(flat(m, x), flat(1 - m, x)) for m in range(2) for x in range(2)])
    d = lax.ppermute(other, both, [(flat(m, x), flat(1 - m, 1 - x)) for m in range(2) for x in range(2)])
    probe_new = mix(at, mixing, mine, b, c, d)
    object_new = object_update(
        jnp.concatenate([place, before]), brightest, object_field, top, far_top, bot, far_bot, over
    )
    return object_new, probe_new


def solution(mesh):
    split = Mesh(mesh.devices.reshape(2, 4, 4, 2, 2), ("mode", *SCAN))
    return jax.shard_map(
        per_device,
        mesh=split,
        in_specs=(P(None, SCAN, None), P(None, "mode", None, None), P(SCAN, None, None), P(SCAN), P(SCAN), P()),
        out_specs=(P(None, SCAN, None), P(None, "mode", SCAN, None)),
        check_vma=False,
    )
```

time: 560 us -> 259 us (0.46)
  blocking collectives: 157 us -> 0 us
  matrix products: 151 us -> 0 us
  Pallas kernels: 0 us -> 103 us
  starting transfers between devices: 14.4 us -> 80 us
  other arithmetic: 67.5 us -> 5.12 us
  waiting for transfers between devices: 103 us -> 53.3 us
  local copies, waits for them, and re-layouts: 40.7 us -> 9.96 us
  between operations: 16.1 us -> 2.18 us
    all_to_all x2 -> x0, blocking collectives: 157 us -> none  [copy_for_each(): lax.all_to_all(jnp.broadcast_to(shard[None], (peers, *shard.shape)), axis...]
    dot_general x17 -> x0, matrix products: 151 us -> none  [the longest x8 78.7 us: left_mult(): jnp.einsum('ij,...jk->...ik', first, second, preferred_element_type=jnp.f...]
    pallas_call x0 -> x10, Pallas kernels: none -> 103 us  [the longest x2 38.5 us: backward(): pl.pallas_call(body, grid_spec=pltpu.PrefetchScalarGridSpec(num_scalar_pr...]
    ppermute x2 -> x30, starting transfers between devices: 10.4 us -> 80 us  [the longest x24 55.9 us: turned(): lax.ppermute(value, axis, [(i, (i + steps) % count) for i in range(count)])]
    reduce_scatter x2 -> x0, waiting for transfers between devices: 34.1 us -> none  [the longest x1 34.1 us: scatter_pairs(): pieces = lax.psum_scatter(pieces, core, scatter_dimension=0, tiled=True)]
    reduce_sum x2 -> x0, other arithmetic: 33.2 us -> none  [over_copies(): return jnp.sum(everything, axis=0)]
    ppermute x2 -> x30, waiting for transfers between devices: 68.6 us -> 53.3 us  [the longest x24 29.3 us: turned(): lax.ppermute(value, axis, [(i, (i + steps) % count) for i in range(count)])]
    reshape x1 -> x0, local copies, waits for them, and re-layouts: 11.3 us -> none  [scatter_pairs(): pieces = pieces.reshape(*sizes, *inside).swapaxes(0, 1).reshape(-1, *inside)]
  transfers between devices with their start and end apart: 5 -> 30, of which waited for: 3 -> 8; matrix products, arithmetic and copies ran while one was open for 11% -> 3% of each run, Pallas kernels for 0% -> 22%
where the time goes in v1:
time: 259 us; the launch traced here: 254 us
  Pallas kernels  103 us (40%)
  starting transfers between devices  80 us (31%)
  waiting for transfers between devices  53.3 us (21%)
  local copies, waits for them, and re-layouts  9.96 us (4%)
  other arithmetic  5.12 us (2%)
    ppermute x24, starting transfers between devices, turned(): lax.ppermute(value, axis, [(i, (i + steps) % count) for i in range(count)])  55.9 us
    pallas_call x2, Pallas kernels, backward(): pl.pallas_call(body, grid_spec=pltpu.PrefetchScalarGridSpec(num_scalar_pr...  38.5 us
    ppermute x24, waiting for transfers between devices, turned(): lax.ppermute(value, axis, [(i, (i + steps) % count) for i in range(count)])  29.3 us
    pallas_call x1, Pallas kernels, forward(): pl.pallas_call(functools.partial(forward_body, mb=mb), grid_spec=pltpu.Pr...  25.1 us
    ppermute x3, waiting for transfers between devices, along(): return lax.ppermute(value, axis, [(i, i + steps) for i in range(lo, hi)])  24 us
    ppermute x3, starting transfers between devices, along(): return lax.ppermute(value, axis, [(i, i + steps) for i in range(lo, hi)])  20 us
    pallas_call x2, Pallas kernels, core_add(): pl.pallas_call(core_add_body, grid_spec=pltpu.PrefetchScalarGridSpec(num_...  11.7 us
    pallas_call x1, Pallas kernels, object_update(): pl.pallas_call(object_body, grid_spec=pltpu.PrefetchScalarGridSpec(num_sc...  10.8 us
  transfers between devices with their start and end apart: 30, of which 8 were waited for; matrix products, arithmetic and copies ran while one was open for 3% of the time, Pallas kernels for 22%

profile of v1, /device:TPU:1, one launch (start us, length us, event | category | flops | bytes accessed | tf_op | source)
XLA Modules:
  0.0 253.5 jit_solution(10678893606158122976)
XLA Ops:
  0.6 1.7 slice.3
  2.4 3.3 %collective-permute-start.2 = (f32[2,256,1024]{2,1,0:T(8,128)S(1)}, f32[2,256,1024]{2,1,0:T(8,128)S(1)}, u32[]{:S(2)}, u32[]{:S(2)}) collective-permute-start(f32[2,256,1024]{2,1,0:T(8,128)S(1)} %slice.3), channel_id=1, source_target_pairs={{1,0},{2,1},{3,2},{4,3},{5,4},{6,5},{7,6},{8,7},{9,8},{10,9},{11,1... | collective-permute-start | bytes 6291464 | tf_op jit(solution)/shard_map/ppermute | solution.py:193
  7.0 0.7 pad_add_fusion.sc
  7.6 22.9 %collective-permute-done.2.rl.rr = f32[2,256,1024]{2,1,0:T(8,128)S(1)} collective-permute-done((f32[2,256,1024]{2,1,0:T(8,128)S(1)}, f32[2,256,1024]{2,1,0:T(8,128)S(1)}, u32[]{:S(2)}, u32[]{:S(2)}) %collective-permute-start.2) | collective-permute-done | bytes 2097184 | tf_op jit(solution)/shard_map/ppermute | solution.py:193
  30.6 1.3 copy-done
  31.9 25.1 %forward.1 = (f32[2,6,512,512]{3,2,1,0:T(8,128)}, f32[512,512]{1,0:T(8,128)}, f32[2,512,512]{2,1,0:T(8,128)}) custom-call(s32[2]{0:T(128)} %pad_add_fusion.sc, f32[2,512,1024]{2,1,0:T(8,128)} %obj.1, f32[2,512,1024]{2,1,0:T(8,128)} %obj.1, f32[2,512,1024]{2,1,0:T(8,128)} %obj.1, f32[2,512,1024]{2,1,0:T(8,128)} %obj.1, f32[2,256,1024]{2,1,0:T(8,128)} %copy-done, ...), custom_call_target="tpu_custom_call" | custom-call | tf_op jit(solution)/shard_map/forward/pallas_call | solution.py:80
  57.0 2.7 %collective-permute-start.3 = (f32[512,512]{1,0:T(8,128)}, f32[512,512]{1,0:T(8,128)S(1)}, u32[]{:S(2)}, u32[]{:S(2)}) collective-permute-start(f32[512,512]{1,0:T(8,128)} %get-tuple-element.39.refs_1_), channel_id=1, source_target_pairs={{0,64},{64,0},{1,65},{65,1},{2,66},{66,2},{3,67},{67,3},{4,68},{68... | collective-permute-start | bytes 3145736 | tf_op jit(solution)/shard_map/ppermute | solution.py:198
  59.7 12.7 %collective-permute-done.3.refs_2_ = f32[512,512]{1,0:T(8,128)S(1)} collective-permute-done((f32[512,512]{1,0:T(8,128)}, f32[512,512]{1,0:T(8,128)S(1)}, u32[]{:S(2)}, u32[]{:S(2)}) %collective-permute-start.3) | collective-permute-done | bytes 1048608 | tf_op jit(solution)/shard_map/ppermute | solution.py:198
  72.3 1.0 copy-done.4
  73.3 18.8 %backward.2 = (f32[2,3,32,8,512]{4,3,2,1,0:T(8,128)}, f32[2,3,32,8,512]{4,3,2,1,0:T(8,128)}, f32[2,256,512]{2,1,0:T(8,128)}, f32[2,256,512]{2,1,0:T(8,128)}) custom-call(s32[1]{0:T(128)} %bitcast.1.sc, f32[1,512,512]{2,1,0:T(8,128)} %refs_0_.3, f32[512,512]{1,0:T(8,128)} %get-tuple-element.39.refs_1_, f32[512,512]{1,0:T(8,128)} %copy-done.4, ...), custom_call_target="tpu_custom_call" | custom-call | tf_op jit(solution)/shard_map/backward/pallas_call | solution.py:163
  92.1 0.1 collective-permute-start.7
  92.2 19.7 %backward.3 = (f32[2,3,32,8,512]{4,3,2,1,0:T(8,128)}, f32[2,3,32,8,512]{4,3,2,1,0:T(8,128)}, f32[2,256,512]{2,1,0:T(8,128)}, f32[2,256,512]{2,1,0:T(8,128)}) custom-call(s32[1]{0:T(128)} %bitcast.1.sc, f32[1,512,512]{2,1,0:T(8,128)} %refs_0_.3, f32[512,512]{1,0:T(8,128)} %get-tuple-element.39.refs_1_, f32[512,512]{1,0:T(8,128)} %copy-done.4, ...), custom_call_target="tpu_custom_call" | custom-call | tf_op jit(solution)/shard_map/backward/pallas_call | solution.py:163
  111.9 0.6 collective-permute-start.14
  112.5 2.7 %collective-permute-start.5 = (f32[2,256,512]{2,1,0:T(8,128)}, f32[2,256,512]{2,1,0:T(8,128)S(1)}, u32[]{:S(2)}, u32[]{:S(2)}) collective-permute-start(f32[2,256,512]{2,1,0:T(8,128)} %get-tuple-element.45.bot), channel_id=1, source_target_pairs={{0,64},{64,0},{1,65},{65,1},{2,66},{66,2},{3,67},{67,3},{4,68},{68... | collective-permute-start | bytes 3145736 | tf_op jit(solution)/shard_map/ppermute | solution.py:198
  115.2 0.6 pad_add_fusion.2.at
  115.8 5.9 %core_add.2 = (f32[3,4,16,512]{3,2,1,0:T(8,128)}, f32[3,4,16,512]{3,2,1,0:T(8,128)}, f32[3,4,16,512]{3,2,1,0:T(8,128)}, f32[3,4,16,512]{3,2,1,0:T(8,128)}, f32[3...) custom-call(s32[4]{0:T(128)} %pad_add_fusion.2.at, ...), custom_call_target="tpu_custom_call" | custom-call | tf_op jit(solution)/shard_map/core_add/pallas_call | solution.py:247
  121.7 12.9 %collective-permute-start.8 = (f32[3,4,16,512]{3,2,1,0:T(8,128)}, f32[3,4,16,512]{3,2,1,0:T(8,128)S(1)}, u32[]{:S(2)}, u32[]{:S(2)}) collective-permute-start(f32[3,4,16,512]{3,2,1,0:T(8,128)} %get-tuple-element.49), channel_id=1, source_target_pairs={{0,16},{16,32},{32,48},{48,0},{1,17},{17,33},{33,49},{49,1},{2,18}... | collective-permute-start | bytes 1179656 | tf_op jit(solution)/shard_map/ppermute | solution.py:198
  134.5 1.5 collective-permute-start.9
  136.0 1.6 collective-permute-start.10
  137.5 1.4 collective-permute-done.5.bot2
  138.9 12.2 %collective-permute-start.11 = (f32[3,4,16,512]{3,2,1,0:T(8,128)}, f32[3,4,16,512]{3,2,1,0:T(8,128)S(1)}, u32[]{:S(2)}, u32[]{:S(2)}) collective-permute-start(f32[3,4,16,512]{3,2,1,0:T(8,128)} %get-tuple-element.53), channel_id=1, source_target_pairs={{0,4},{4,8},{8,12},{12,0},{1,5},{5,9},{9,13},{13,1},{2,6},{6,10},{... | collective-permute-start | bytes 1179656 | tf_op jit(solution)/shard_map/ppermute | solution.py:198
  151.1 2.7 %collective-permute-start.12 = (f32[3,4,16,512]{3,2,1,0:T(8,128)}, f32[3,4,16,512]{3,2,1,0:T(8,128)S(1)}, u32[]{:S(2)}, u32[]{:S(2)}) collective-permute-start(f32[3,4,16,512]{3,2,1,0:T(8,128)} %get-tuple-element.54), channel_id=1, source_target_pairs={{0,12},{4,0},{8,4},{12,8},{1,13},{5,1},{9,5},{13,9},{2,14},{6,2},{... | collective-permute-start | bytes 1179656 | tf_op jit(solution)/shard_map/ppermute | solution.py:198
  153.8 1.2 collective-permute-start.13
  155.0 5.9 %core_add.3 = (f32[3,4,16,512]{3,2,1,0:T(8,128)}, f32[3,4,16,512]{3,2,1,0:T(8,128)}, f32[3,4,16,512]{3,2,1,0:T(8,128)}, f32[3,4,16,512]{3,2,1,0:T(8,128)}, f32[3...) custom-call(s32[4]{0:T(128)} %pad_add_fusion.2.at, ...), custom_call_target="tpu_custom_call" | custom-call | tf_op jit(solution)/shard_map/core_add/pallas_call | solution.py:247
  160.9 1.4 collective-permute-start.15
  162.3 1.4 collective-permute-start.16
  163.7 1.6 collective-permute-start.17
  165.3 0.7 copy-done.11
  166.1 0.8 collective-permute-start.18
  166.8 5.9 %light.1 = f32[512,512]{1,0:T(8,128)} custom-call(bf16[2,6,512,512]{3,2,1,0:T(8,128)(2,1)} %refs_4_.3), custom_call_target="tpu_custom_call" | custom-call | tf_op jit(solution)/shard_map/light/pallas_call | solution.py:223
  172.8 2.3 collective-permute-start.1
  175.1 1.9 collective-permute-start.19
  177.0 0.6 collective-permute-start.20
  177.5 1.2 add.19
  178.7 2.2 collective-permute-done.17.refs_11_
  180.9 2.3 collective-permute-start.4
  183.2 9.6 %collective-permute-start.6 = (f32[2,256,512]{2,1,0:T(8,128)}, f32[2,256,512]{2,1,0:T(8,128)S(1)}, u32[]{:S(2)}, u32[]{:S(2)}) collective-permute-start(f32[2,256,512]{2,1,0:T(8,128)} %add.19), channel_id=1, source_target_pairs={{0,1},{1,2},{2,3},{3,4},{4,5},{5,6},{6,7},{7,8},{8,9},{9,10},{10,1... | collective-permute-start | bytes 3145736 | tf_op jit(solution)/shard_map/ppermute | solution.py:193
  192.9 0.7 copy-done.15
  193.6 0.1 copy-done.16
  193.7 5.0 %plane_add.1 = (f32[6,16,512]{2,1,0:T(8,128)}, f32[6,16,512]{2,1,0:T(8,128)}, f32[6,16,512]{2,1,0:T(8,128)}, f32[6,16,512]{2,1,0:T(8,128)}, f32[6,16,512]{2,1,0:...) custom-call(s32[4]{0:T(128)} %pad_add_fusion.2.at, ...), custom_call_target="tpu_custom_call" | custom-call | tf_op jit(solution)/shard_map/plane_add/pallas_call | solution.py:275
  198.8 0.1 collective-permute-start.21
  198.9 2.7 %collective-permute-start.22 = (f32[6,16,512]{2,1,0:T(8,128)}, f32[6,16,512]{2,1,0:T(8,128)S(1)}, u32[]{:S(2)}, u32[]{:S(2)}) collective-permute-start(f32[6,16,512]{2,1,0:T(8,128)} %get-tuple-element.68), channel_id=1, source_target_pairs={{0,12},{4,0},{8,4},{12,8},{1,13},{5,1},{9,5},{13,9},{2,14},{6,2},{... | collective-permute-start | bytes 589832 | tf_op jit(solution)/shard_map/ppermute | solution.py:198
  201.5 3.7 %collective-permute-done.21.refs_1_ = f32[6,16,512]{2,1,0:T(8,128)S(1)} collective-permute-done((f32[6,16,512]{2,1,0:T(8,128)}, f32[6,16,512]{2,1,0:T(8,128)S(1)}, u32[]{:S(2)}, u32[]{:S(2)}) %collective-permute-start.21) | collective-permute-done | bytes 196640 | tf_op jit(solution)/shard_map/ppermute | solution.py:198
  205.2 0.3 collective-permute-start.24
  205.5 6.2 %collective-permute-done.23.refs_3_ = f32[6,16,512]{2,1,0:T(8,128)} collective-permute-done((f32[6,16,512]{2,1,0:T(8,128)}, f32[6,16,512]{2,1,0:T(8,128)}, u32[]{:S(2)}, u32[]{:S(2)}) %collective-permute-start.23) | collective-permute-done | bytes 196640 | tf_op jit(solution)/shard_map/ppermute | solution.py:198
  211.7 2.3 collective-permute-start.25
  214.0 0.4 collective-permute-start.26
  214.4 1.5 constant_dynamic-slice_fusion.refs_8_
  215.9 3.1 %collective-permute-done.25.refs_6_ = f32[6,16,512]{2,1,0:T(8,128)} collective-permute-done((f32[6,16,512]{2,1,0:T(8,128)}, f32[6,16,512]{2,1,0:T(8,128)}, u32[]{:S(2)}, u32[]{:S(2)}) %collective-permute-start.25) | collective-permute-done | bytes 196640 | tf_op jit(solution)/shard_map/ppermute | solution.py:198
  219.0 7.1 %collective-permute-start = (s32[2]{0:T(128)S(1)}, s32[2]{0:T(128)S(1)}, u32[]{:S(2)}, u32[]{:S(2)}) collective-permute-start(s32[2]{0:T(128)S(1)} %copy-done.22), channel_id=1, source_target_pairs={{0,1},{1,2},{2,3},{3,4},{4,5},{5,6},{6,7},{7,8},{8,9},{9,10},{10,1... | collective-permute-start | bytes 32 | tf_op jit(solution)/shard_map/ppermute | solution.py:193
  226.2 3.0 %row_add.1 = (f32[2,6,8,512]{3,2,1,0:T(8,128)}, f32[2,6,8,512]{3,2,1,0:T(8,128)}) custom-call(s32[4]{0:T(128)} %pad_add_fusion.2.at, f32[6,16,512]{2,1,0:T(8,128)} %get-tuple-element.66.refs_0_, f32[6,16,512]{2,1,0:T(8,128)} %copy-done.17, f32[6,16,512]{2,1,0:T(8,128)} %copy-done.18, f32[6,16,512]{2,1,0:T(8,128)} %collective-permute-done.23.refs_3_, ...), custom_call_target="tpu_custom_call" | custom-call | tf_op jit(solution)/shard_map/row_add/pallas_call | solution.py:310
  229.2 1.8 collective-permute-start.27
  231.0 1.1 collective-permute-done
  232.0 0.7 collective-permute-start.29
  232.8 1.5 collective-permute-start.28
  234.3 0.6 pad_add_fusion.1.sc
  234.9 2.1 add_reduce_fusion
  237.0 1.0 copy-done.5
  238.0 0.4 copy-done.6
  238.3 10.8 %object_update.1 = f32[2,512,1024]{2,1,0:T(8,128)} custom-call(s32[4]{0:T(128)} %pad_add_fusion.1.sc, f32[1]{0:T(128)} %bitcast.lights, f32[2,512,1024]{2,1,0:T(8,128)} %obj.1, f32[2,256,512]{2,1,0:T(8,128)} %get-tuple-element.44.top, f32[2,256,512]{2,1,0:T(8,128)} %copy-done.5, f32[2,256,512]{2,1,0:T(8,128)} %get-tuple-element.45.bot, ...), custom_call_target="tpu_custom_call" | custom-call | tf_op jit(solution)/shard_map/object_update/pallas_call | solution.py:377
  249.2 0.6 copy-done.19
  249.8 0.1 copy-done.21
  249.9 0.7 copy-done.20
  250.6 2.9 %mix.1 = bf16[2,6,8,512]{3,2,1,0:T(8,128)(2,1)} custom-call(s32[4]{0:T(128)} %pad_add_fusion.2.at, s32[12,12]{1,0:T(8,128)} %w_ref.1, f32[2,6,8,512]{3,2,1,0:T(8,128)} %get-tuple-element.74.mine, f32[2,6,8,512]{3,2,1,0:T(8,128)} %copy-done.19, f32[2,6,8,512]{3,2,1,0:T(8,128)} %copy-done.21, f32[2,6,8,512]{3,2,1,0:T(8,128)} %copy-done.20), custom_call_target="tpu_custom_call" | custom-call | tf_op jit(solution)/shard_map/mix/pallas_call | solution.py:341
  (59 shorter events, 0.1 us)
Async XLA Ops:
  2.4 28.2 %collective-permute-start.2 = (f32[2,256,1024]{2,1,0:T(8,128)S(1)}, f32[2,256,1024]{2,1,0:T(8,128)S(1)}, u32[]{:S(2)}, u32[]{:S(2)}) collective-permute-start(f32[2,256,1024]{2,1,0:T(8,128)S(1)} %slice.3), channel_id=1, source_target_pairs={{1,0},{2,1},{3,2},{4,3},{5,4},{6,5},{7,6},{8,7},{9,8},{10,9},{11,1... | collective-permute-start | bytes 6291464 | tf_op jit(solution)/shard_map/ppermute | solution.py:193
  30.6 1.3 copy-start
  57.0 15.4 %collective-permute-start.3 = (f32[512,512]{1,0:T(8,128)}, f32[512,512]{1,0:T(8,128)S(1)}, u32[]{:S(2)}, u32[]{:S(2)}) collective-permute-start(f32[512,512]{1,0:T(8,128)} %get-tuple-element.39.refs_1_), channel_id=1, source_target_pairs={{0,64},{64,0},{1,65},{65,1},{2,66},{66,2},{3,67},{67,3},{4,68},{68... | collective-permute-start | bytes 3145736 | tf_op jit(solution)/shard_map/ppermute | solution.py:198
  72.3 1.0 copy-start.4
  92.1 23.7 %collective-permute-start.7 = (f32[2,3,32,8,512]{4,3,2,1,0:T(8,128)}, f32[2,3,32,8,512]{4,3,2,1,0:T(8,128)}, u32[]{:S(2)}, u32[]{:S(2)}) collective-permute-start(f32[2,3,32,8,512]{4,3,2,1,0:T(8,128)} %get-tuple-element.47), channel_id=1, source_target_pairs={{0,1},{1,0},{2,3},{3,2},{4,5},{5,4},{6,7},{7,6},{8,9},{9,8},{10,11... | collective-permute-start | bytes 9437192 | tf_op jit(solution)/shard_map/ppermute | solution.py:198
  111.9 39.2 %collective-permute-start.14 = (f32[2,3,32,8,512]{4,3,2,1,0:T(8,128)}, f32[2,3,32,8,512]{4,3,2,1,0:T(8,128)}, u32[]{:S(2)}, u32[]{:S(2)}) collective-permute-start(f32[2,3,32,8,512]{4,3,2,1,0:T(8,128)} %get-tuple-element.57), channel_id=1, source_target_pairs={{0,1},{1,0},{2,3},{3,2},{4,5},{5,4},{6,7},{7,6},{8,9},{9,8},{10,11... | collective-permute-start | bytes 9437192 | tf_op jit(solution)/shard_map/ppermute | solution.py:198
  112.5 26.4 %collective-permute-start.5 = (f32[2,256,512]{2,1,0:T(8,128)}, f32[2,256,512]{2,1,0:T(8,128)S(1)}, u32[]{:S(2)}, u32[]{:S(2)}) collective-permute-start(f32[2,256,512]{2,1,0:T(8,128)} %get-tuple-element.45.bot), channel_id=1, source_target_pairs={{0,64},{64,0},{1,65},{65,1},{2,66},{66,2},{3,67},{67,3},{4,68},{68... | collective-permute-start | bytes 3145736 | tf_op jit(solution)/shard_map/ppermute | solution.py:198
  121.7 32.1 %collective-permute-start.8 = (f32[3,4,16,512]{3,2,1,0:T(8,128)}, f32[3,4,16,512]{3,2,1,0:T(8,128)S(1)}, u32[]{:S(2)}, u32[]{:S(2)}) collective-permute-start(f32[3,4,16,512]{3,2,1,0:T(8,128)} %get-tuple-element.49), channel_id=1, source_target_pairs={{0,16},{16,32},{32,48},{48,0},{1,17},{17,33},{33,49},{49,1},{2,18}... | collective-permute-start | bytes 1179656 | tf_op jit(solution)/shard_map/ppermute | solution.py:198
  134.5 26.4 %collective-permute-start.9 = (f32[3,4,16,512]{3,2,1,0:T(8,128)}, f32[3,4,16,512]{3,2,1,0:T(8,128)S(1)}, u32[]{:S(2)}, u32[]{:S(2)}) collective-permute-start(f32[3,4,16,512]{3,2,1,0:T(8,128)} %get-tuple-element.50), channel_id=1, source_target_pairs={{0,48},{16,0},{32,16},{48,32},{1,49},{17,1},{33,17},{49,33},{2,50}... | collective-permute-start | bytes 1179656 | tf_op jit(solution)/shard_map/ppermute | solution.py:198
  136.0 26.3 %collective-permute-start.10 = (f32[3,4,16,512]{3,2,1,0:T(8,128)}, f32[3,4,16,512]{3,2,1,0:T(8,128)S(1)}, u32[]{:S(2)}, u32[]{:S(2)}) collective-permute-start(f32[3,4,16,512]{3,2,1,0:T(8,128)} %get-tuple-element.51), channel_id=1, source_target_pairs={{0,32},{16,48},{32,0},{48,16},{1,33},{17,49},{33,1},{49,17},{2,34}... | collective-permute-start | bytes 1179656 | tf_op jit(solution)/shard_map/ppermute | solution.py:198
  138.9 38.6 %copy-start.3 = (f32[2,256,512]{2,1,0:T(8,128)}, f32[2,256,512]{2,1,0:T(8,128)S(1)}, u32[]{:S(2)}) copy-start(f32[2,256,512]{2,1,0:T(8,128)S(1)} %collective-permute-done.5.bot2) | copy-start | bytes 3145732
  138.9 24.8 %collective-permute-start.11 = (f32[3,4,16,512]{3,2,1,0:T(8,128)}, f32[3,4,16,512]{3,2,1,0:T(8,128)S(1)}, u32[]{:S(2)}, u32[]{:S(2)}) collective-permute-start(f32[3,4,16,512]{3,2,1,0:T(8,128)} %get-tuple-element.53), channel_id=1, source_target_pairs={{0,4},{4,8},{8,12},{12,0},{1,5},{5,9},{9,13},{13,1},{2,6},{6,10},{... | collective-permute-start | bytes 1179656 | tf_op jit(solution)/shard_map/ppermute | solution.py:198
  151.1 14.2 %collective-permute-start.12 = (f32[3,4,16,512]{3,2,1,0:T(8,128)}, f32[3,4,16,512]{3,2,1,0:T(8,128)S(1)}, u32[]{:S(2)}, u32[]{:S(2)}) collective-permute-start(f32[3,4,16,512]{3,2,1,0:T(8,128)} %get-tuple-element.54), channel_id=1, source_target_pairs={{0,12},{4,0},{8,4},{12,8},{1,13},{5,1},{9,5},{13,9},{2,14},{6,2},{... | collective-permute-start | bytes 1179656 | tf_op jit(solution)/shard_map/ppermute | solution.py:198
  153.8 7.1 %copy-start.7 = (f32[3,4,16,512]{3,2,1,0:T(8,128)}, f32[3,4,16,512]{3,2,1,0:T(8,128)S(1)}, u32[]{:S(2)}) copy-start(f32[3,4,16,512]{3,2,1,0:T(8,128)S(1)} %collective-permute-done.8.refs_1_) | copy-start | bytes 1179652
  153.8 19.0 %collective-permute-start.13 = (f32[3,4,16,512]{3,2,1,0:T(8,128)}, f32[3,4,16,512]{3,2,1,0:T(8,128)S(1)}, u32[]{:S(2)}, u32[]{:S(2)}) collective-permute-start(f32[3,4,16,512]{3,2,1,0:T(8,128)} %get-tuple-element.55), channel_id=1, source_target_pairs={{0,8},{4,12},{8,0},{12,4},{1,9},{5,13},{9,1},{13,5},{2,10},{6,14},... | collective-permute-start | bytes 1179656 | tf_op jit(solution)/shard_map/ppermute | solution.py:198
  160.9 4.4 %copy-start.8 = (f32[3,4,16,512]{3,2,1,0:T(8,128)}, f32[3,4,16,512]{3,2,1,0:T(8,128)S(1)}, u32[]{:S(2)}) copy-start(f32[3,4,16,512]{3,2,1,0:T(8,128)S(1)} %collective-permute-done.9.refs_2_) | copy-start | bytes 1179652
  160.9 14.2 %collective-permute-start.15 = (f32[3,4,16,512]{3,2,1,0:T(8,128)}, f32[3,4,16,512]{3,2,1,0:T(8,128)S(1)}, u32[]{:S(2)}, u32[]{:S(2)}) collective-permute-start(f32[3,4,16,512]{3,2,1,0:T(8,128)} %get-tuple-element.59), channel_id=1, source_target_pairs={{0,16},{16,32},{32,48},{48,0},{1,17},{17,33},{33,49},{49,1},{2,18}... | collective-permute-start | bytes 1179656 | tf_op jit(solution)/shard_map/ppermute | solution.py:198
  162.3 3.0 %copy-start.9 = (f32[3,4,16,512]{3,2,1,0:T(8,128)}, f32[3,4,16,512]{3,2,1,0:T(8,128)S(1)}, u32[]{:S(2)}) copy-start(f32[3,4,16,512]{3,2,1,0:T(8,128)S(1)} %collective-permute-done.10.refs_3_) | copy-start | bytes 1179652
  162.3 14.6 %collective-permute-start.16 = (f32[3,4,16,512]{3,2,1,0:T(8,128)}, f32[3,4,16,512]{3,2,1,0:T(8,128)S(1)}, u32[]{:S(2)}, u32[]{:S(2)}) collective-permute-start(f32[3,4,16,512]{3,2,1,0:T(8,128)} %get-tuple-element.60), channel_id=1, source_target_pairs={{0,48},{16,0},{32,16},{48,32},{1,49},{17,1},{33,17},{49,33},{2,50}... | collective-permute-start | bytes 1179656 | tf_op jit(solution)/shard_map/ppermute | solution.py:198
  163.7 1.6 copy-start.10
  163.7 17.2 %collective-permute-start.17 = (f32[3,4,16,512]{3,2,1,0:T(8,128)}, f32[3,4,16,512]{3,2,1,0:T(8,128)}, u32[]{:S(2)}, u32[]{:S(2)}) collective-permute-start(f32[3,4,16,512]{3,2,1,0:T(8,128)} %get-tuple-element.61), channel_id=1, source_target_pairs={{0,32},{16,48},{32,0},{48,16},{1,33},{17,49},{33,1},{49,17},{2,34}... | collective-permute-start | bytes 1179656 | tf_op jit(solution)/shard_map/ppermute | solution.py:198
  165.3 0.8 copy-start.11
  166.1 11.5 %copy-start.2 = (f32[2,256,512]{2,1,0:T(8,128)S(1)}, f32[2,256,512]{2,1,0:T(8,128)}, u32[]{:S(2)}) copy-start(f32[2,256,512]{2,1,0:T(8,128)} %get-tuple-element.45.bot) | copy-start | bytes 3145732
  166.1 17.1 %collective-permute-start.18 = (f32[3,4,16,512]{3,2,1,0:T(8,128)}, f32[3,4,16,512]{3,2,1,0:T(8,128)}, u32[]{:S(2)}, u32[]{:S(2)}) collective-permute-start(f32[3,4,16,512]{3,2,1,0:T(8,128)} %get-tuple-element.63), channel_id=1, source_target_pairs={{0,4},{4,8},{8,12},{12,0},{1,5},{5,9},{9,13},{13,1},{2,6},{6,10},{... | collective-permute-start | bytes 1179656 | tf_op jit(solution)/shard_map/ppermute | solution.py:198
  172.8 20.1 %copy-start.12 = (f32[3,4,16,512]{3,2,1,0:T(8,128)}, f32[3,4,16,512]{3,2,1,0:T(8,128)S(1)}, u32[]{:S(2)}) copy-start(f32[3,4,16,512]{3,2,1,0:T(8,128)S(1)} %collective-permute-done.13.refs_7_) | copy-start | bytes 1179652
  172.8 60.0 %collective-permute-start.1 = (f32[512,512]{1,0:T(8,128)}, f32[512,512]{1,0:T(8,128)}, u32[]{:S(2)}, u32[]{:S(2)}) collective-permute-start(f32[512,512]{1,0:T(8,128)} %light.1), channel_id=1, source_target_pairs={{0,64},{64,0},{1,65},{65,1},{2,66},{66,2},{3,67},{67,3},{4,68},{68... | collective-permute-start | bytes 3145736 | tf_op jit(solution)/shard_map/ppermute | solution.py:198
  175.1 17.8 %copy-start.13 = (f32[3,4,16,512]{3,2,1,0:T(8,128)}, f32[3,4,16,512]{3,2,1,0:T(8,128)S(1)}, u32[]{:S(2)}) copy-start(f32[3,4,16,512]{3,2,1,0:T(8,128)S(1)} %collective-permute-done.15.refs_9_) | copy-start | bytes 1179652
  175.1 17.8 %collective-permute-start.19 = (f32[3,4,16,512]{3,2,1,0:T(8,128)}, f32[3,4,16,512]{3,2,1,0:T(8,128)S(1)}, u32[]{:S(2)}, u32[]{:S(2)}) collective-permute-start(f32[3,4,16,512]{3,2,1,0:T(8,128)} %get-tuple-element.64), channel_id=1, source_target_pairs={{0,12},{4,0},{8,4},{12,8},{1,13},{5,1},{9,5},{13,9},{2,14},{6,2},{... | collective-permute-start | bytes 1179656 | tf_op jit(solution)/shard_map/ppermute | solution.py:198
  177.0 15.9 %copy-start.14 = (f32[3,4,16,512]{3,2,1,0:T(8,128)}, f32[3,4,16,512]{3,2,1,0:T(8,128)S(1)}, u32[]{:S(2)}) copy-start(f32[3,4,16,512]{3,2,1,0:T(8,128)S(1)} %collective-permute-done.16.refs_10_) | copy-start | bytes 1179652
  177.0 15.9 %collective-permute-start.20 = (f32[3,4,16,512]{3,2,1,0:T(8,128)}, f32[3,4,16,512]{3,2,1,0:T(8,128)S(1)}, u32[]{:S(2)}, u32[]{:S(2)}) collective-permute-start(f32[3,4,16,512]{3,2,1,0:T(8,128)} %get-tuple-element.65), channel_id=1, source_target_pairs={{0,8},{4,12},{8,0},{12,4},{1,9},{5,13},{9,1},{13,5},{2,10},{6,14},... | collective-permute-start | bytes 1179656 | tf_op jit(solution)/shard_map/ppermute | solution.py:198
  180.9 56.1 %collective-permute-start.4 = (f32[2,256,512]{2,1,0:T(8,128)}, f32[2,256,512]{2,1,0:T(8,128)S(1)}, u32[]{:S(2)}, u32[]{:S(2)}) collective-permute-start(f32[2,256,512]{2,1,0:T(8,128)} %get-tuple-element.44.top), channel_id=1, source_target_pairs={{0,64},{64,0},{1,65},{65,1},{2,66},{66,2},{3,67},{67,3},{4,68},{68... | collective-permute-start | bytes 3145736 | tf_op jit(solution)/shard_map/ppermute | solution.py:198
  183.2 53.8 %collective-permute-start.6 = (f32[2,256,512]{2,1,0:T(8,128)}, f32[2,256,512]{2,1,0:T(8,128)S(1)}, u32[]{:S(2)}, u32[]{:S(2)}) collective-permute-start(f32[2,256,512]{2,1,0:T(8,128)} %add.19), channel_id=1, source_target_pairs={{0,1},{1,2},{2,3},{3,4},{4,5},{5,6},{6,7},{7,8},{8,9},{9,10},{10,1... | collective-permute-start | bytes 3145736 | tf_op jit(solution)/shard_map/ppermute | solution.py:193
  192.8 0.8 copy-start.15
  192.8 0.9 copy-start.16
  193.7 25.3 %copy-start.22 = (s32[2]{0:T(128)S(1)}, s32[2]{0:T(128)}, u32[]{:S(2)}) copy-start(s32[2]{0:T(128)} %pad_add_fusion.sc) | copy-start | bytes 28
  193.7 41.1 %copy-start.1 = (f32[512,512]{1,0:T(8,128)S(1)}, f32[512,512]{1,0:T(8,128)}, u32[]{:S(2)}) copy-start(f32[512,512]{1,0:T(8,128)} %light.1) | copy-start | bytes 3145732
  198.8 6.4 %collective-permute-start.21 = (f32[6,16,512]{2,1,0:T(8,128)}, f32[6,16,512]{2,1,0:T(8,128)S(1)}, u32[]{:S(2)}, u32[]{:S(2)}) collective-permute-start(f32[6,16,512]{2,1,0:T(8,128)} %get-tuple-element.67), channel_id=1, source_target_pairs={{0,4},{4,8},{8,12},{12,0},{1,5},{5,9},{9,13},{13,1},{2,6},{6,10},{... | collective-permute-start | bytes 589832 | tf_op jit(solution)/shard_map/ppermute | solution.py:198
  198.9 6.3 %collective-permute-start.22 = (f32[6,16,512]{2,1,0:T(8,128)}, f32[6,16,512]{2,1,0:T(8,128)S(1)}, u32[]{:S(2)}, u32[]{:S(2)}) collective-permute-start(f32[6,16,512]{2,1,0:T(8,128)} %get-tuple-element.68), channel_id=1, source_target_pairs={{0,12},{4,0},{8,4},{12,8},{1,13},{5,1},{9,5},{13,9},{2,14},{6,2},{... | collective-permute-start | bytes 589832 | tf_op jit(solution)/shard_map/ppermute | solution.py:198
  205.2 21.0 %copy-start.17 = (f32[6,16,512]{2,1,0:T(8,128)}, f32[6,16,512]{2,1,0:T(8,128)S(1)}, u32[]{:S(2)}) copy-start(f32[6,16,512]{2,1,0:T(8,128)S(1)} %collective-permute-done.21.refs_1_) | copy-start | bytes 589828
  205.2 6.5 %collective-permute-start.23 = (f32[6,16,512]{2,1,0:T(8,128)}, f32[6,16,512]{2,1,0:T(8,128)}, u32[]{:S(2)}, u32[]{:S(2)}) collective-permute-start(f32[6,16,512]{2,1,0:T(8,128)} %get-tuple-element.69), channel_id=1, source_target_pairs={{0,8},{4,12},{8,0},{12,4},{1,9},{5,13},{9,1},{13,5},{2,10},{6,14},... | collective-permute-start | bytes 589832 | tf_op jit(solution)/shard_map/ppermute | solution.py:198
  205.2 21.0 %copy-start.18 = (f32[6,16,512]{2,1,0:T(8,128)}, f32[6,16,512]{2,1,0:T(8,128)S(1)}, u32[]{:S(2)}) copy-start(f32[6,16,512]{2,1,0:T(8,128)S(1)} %collective-permute-done.22.refs_2_) | copy-start | bytes 589828
  205.2 8.8 %collective-permute-start.24 = (f32[6,16,512]{2,1,0:T(8,128)}, f32[6,16,512]{2,1,0:T(8,128)}, u32[]{:S(2)}, u32[]{:S(2)}) collective-permute-start(f32[6,16,512]{2,1,0:T(8,128)} %get-tuple-element.71), channel_id=1, source_target_pairs={{0,16},{16,32},{32,48},{48,0},{1,17},{17,33},{33,49},{49,1},{2,18}... | collective-permute-start | bytes 589832 | tf_op jit(solution)/shard_map/ppermute | solution.py:198
  211.7 7.3 %collective-permute-start.25 = (f32[6,16,512]{2,1,0:T(8,128)}, f32[6,16,512]{2,1,0:T(8,128)}, u32[]{:S(2)}, u32[]{:S(2)}) collective-permute-start(f32[6,16,512]{2,1,0:T(8,128)} %get-tuple-element.72), channel_id=1, source_target_pairs={{0,48},{16,0},{32,16},{48,32},{1,49},{17,1},{33,17},{49,33},{2,50}... | collective-permute-start | bytes 589832 | tf_op jit(solution)/shard_map/ppermute | solution.py:198
  214.0 12.2 %collective-permute-start.26 = (f32[6,16,512]{2,1,0:T(8,128)}, f32[6,16,512]{2,1,0:T(8,128)}, u32[]{:S(2)}, u32[]{:S(2)}) collective-permute-start(f32[6,16,512]{2,1,0:T(8,128)} %get-tuple-element.73), channel_id=1, source_target_pairs={{0,32},{16,48},{32,0},{48,16},{1,33},{17,49},{33,1},{49,17},{2,34}... | collective-permute-start | bytes 589832 | tf_op jit(solution)/shard_map/ppermute | solution.py:198
  219.0 13.0 %collective-permute-start = (s32[2]{0:T(128)S(1)}, s32[2]{0:T(128)S(1)}, u32[]{:S(2)}, u32[]{:S(2)}) collective-permute-start(s32[2]{0:T(128)S(1)} %copy-done.22), channel_id=1, source_target_pairs={{0,1},{1,2},{2,3},{3,4},{4,5},{5,6},{6,7},{7,8},{8,9},{9,10},{10,1... | collective-permute-start | bytes 32 | tf_op jit(solution)/shard_map/ppermute | solution.py:193
  229.2 20.0 %collective-permute-start.27 = (f32[2,6,8,512]{3,2,1,0:T(8,128)}, f32[2,6,8,512]{3,2,1,0:T(8,128)S(1)}, u32[]{:S(2)}, u32[]{:S(2)}) collective-permute-start(f32[2,6,8,512]{3,2,1,0:T(8,128)} %get-tuple-element.75), channel_id=1, source_target_pairs={{0,2},{2,0},{64,66},{66,64},{1,3},{3,1},{65,67},{67,65},{4,6},{6,4... | collective-permute-start | bytes 589832 | tf_op jit(solution)/shard_map/ppermute | solution.py:427
  232.0 17.1 %collective-permute-start.29 = (f32[2,6,8,512]{3,2,1,0:T(8,128)}, f32[2,6,8,512]{3,2,1,0:T(8,128)S(1)}, u32[]{:S(2)}, u32[]{:S(2)}) collective-permute-start(f32[2,6,8,512]{3,2,1,0:T(8,128)} %get-tuple-element.75), channel_id=1, source_target_pairs={{0,66},{2,64},{64,2},{66,0},{1,67},{3,65},{65,3},{67,1},{4,70},{6,... | collective-permute-start | bytes 589832 | tf_op jit(solution)/shard_map/ppermute | solution.py:429
  232.8 16.4 %collective-permute-start.28 = (f32[2,6,8,512]{3,2,1,0:T(8,128)}, f32[2,6,8,512]{3,2,1,0:T(8,128)S(1)}, u32[]{:S(2)}, u32[]{:S(2)}) collective-permute-start(f32[2,6,8,512]{3,2,1,0:T(8,128)} %get-tuple-element.74.mine), channel_id=1, source_target_pairs={{0,64},{2,66},{64,0},{66,2},{1,65},{3,67},{65,1},{67,3},{4,68},{6,... | collective-permute-start | bytes 589832 | tf_op jit(solution)/shard_map/ppermute | solution.py:428
  237.0 1.0 copy-start.5
  237.0 1.3 copy-start.6
  249.2 0.7 copy-start.19
  249.2 0.7 copy-start.21
  249.9 0.7 copy-start.20

commit v2 on v0

v2 whole, which is shorter than its diff:
```python
import functools
import math

import jax
import jax.numpy as jnp
import ml_dtypes
import numpy as np
from jax import lax
from jax.experimental import pallas as pl
from jax.experimental.pallas import tpu as pltpu
from jax.sharding import Mesh
from jax.sharding import PartitionSpec as P

f32, bf16 = jnp.float32, jnp.bfloat16
N = 512
H = 256
CHUNK = 32
VMEM_MIB = 56


def tables():
    i = np.arange(N, dtype=np.int32)
    angle = (i[:, None] * i[None, :] % N).astype(np.float32) * np.float32(2.0 * math.pi / N)
    factor = np.float32(1.0 / math.sqrt(N))
    c = (np.cos(angle) * factor).astype(ml_dtypes.bfloat16)
    s = (np.sin(angle) * factor).astype(ml_dtypes.bfloat16)
    minus = np.block([[c, -s], [s, c]])
    plus = np.block([[c, s], [-s, c]])

    def stacked(table):
        return table.reshape(2 * N, 2, 2, H).swapaxes(1, 2).reshape(2, N, 2 * N)

    wave_rows = stacked(plus).reshape(2, 2, H, 2 * N).swapaxes(0, 1).reshape(2, N, 2 * N)
    back_rows = stacked(minus).reshape(2, 16, 2, 16, 2 * N).transpose(2, 0, 1, 3, 4).reshape(2, N, 2 * N)
    return minus, plus, np.ascontiguousarray(wave_rows), np.ascontiguousarray(back_rows)


def params(mib):
    return pltpu.CompilerParams(vmem_limit_bytes=mib << 20)


def cost(us):
    return pl.CostEstimate(flops=int(us * 1.1e9), transcendentals=0, bytes_accessed=int(us * 3e6))


def shape(*dims, dtype=f32):
    return jax.ShapeDtypeStruct(dims, dtype)


def whole(*dims):
    return pl.BlockSpec(dims, lambda *_: (0,) * len(dims))


def loop(count, fn):
    def body(i, carry):
        fn(i)
        return carry

    lax.fori_loop(0, count, body, 0)


def at(i, size):
    return pl.ds(pl.multiple_of(i * size, size), size)


def exit_rows(p_ref, m, rows, o_r, o_i):
    pr = p_ref[0, m, rows, :].astype(f32)
    pi = p_ref[1, m, rows, :].astype(f32)
    return pr, pi, (pr * o_r - pi * o_i).astype(bf16), (pr * o_i + pi * o_r).astype(bf16)


def exit_half(p_ref, m, patch, x_s):
    def one(i):
        rows = at(i, CHUNK)
        _, _, xr, xi = exit_rows(p_ref, m, rows, patch[0, rows, :], patch[1, rows, :])
        x_s[m, rows, :N] = xr
        x_s[m, rows, N:] = xi

    loop(H // CHUNK, one)


def along_rows(x_s, table, out):
    nm = x_s.shape[0]
    x = x_s[...].reshape(nm * H, 2 * N)
    half = jnp.dot(x, table[...], preferred_element_type=f32).astype(bf16)
    for m in range(nm):
        out[m, :H] = half[m * H : (m + 1) * H, :N]
        out[m, H:] = half[m * H : (m + 1) * H, N:]


def top_body(sc, left, right, p_ref, table, half_ref, patch_ref, x_s):
    @pl.when(pl.program_id(0) == 0)
    def _():
        patch_ref[:, :, :H] = left[...]
        patch_ref[:, :, H:] = right[...]

    for m in range(x_s.shape[0]):
        exit_half(p_ref, m, patch_ref, x_s)
    along_rows(x_s, table, half_ref)


def top_half(sc, obj, probe, table, mb=2):
    nm = probe.shape[1]
    return pl.pallas_call(
        top_body,
        grid_spec=pltpu.PrefetchScalarGridSpec(
            num_scalar_prefetch=1,
            grid=(nm // mb,),
            in_specs=[
                pl.BlockSpec((2, H, H), lambda k, sc: (0, sc[0], sc[1])),
                pl.BlockSpec((2, H, H), lambda k, sc: (0, sc[0], sc[1] + 1)),
                pl.BlockSpec((2, mb, H, N), lambda k, sc: (0, k, 0, 0)),
                whole(2 * N, 2 * N),
            ],
            out_specs=[pl.BlockSpec((mb, N, N), lambda k, sc: (k, 0, 0)), whole(2, H, N)],
            scratch_shapes=[pltpu.VMEM((mb, H, 2 * N), bf16)],
        ),
        out_shape=[shape(nm, N, N, dtype=bf16), shape(2, H, N)],
        compiler_params=params(50),
        name="top_half",
        cost_estimate=cost(6),
    )(sc, obj, obj, probe, table)


def wave_half(wave_ref, sum_ref, wt, top, bot):
    nm = top.shape[0]
    for m in range(nm):
        wave_ref[m] = jnp.dot(wt[0, :, :N], top[m], preferred_element_type=f32) + jnp.dot(
            wt[0, :, N:], bot[m], preferred_element_type=f32
        )

    def one(i):
        rows = at(i, CHUNK)
        low = pl.ds(pl.multiple_of(i * CHUNK + H, CHUNK), CHUNK)
        acc = sum_ref[rows, :]
        for m in range(nm):
            a = wave_ref[m, rows, :]
            b = wave_ref[m, low, :]
            acc = acc + (a * a + b * b)
        sum_ref[rows, :] = acc

    loop(H // CHUNK, one)


def bottom_body(sc, left, right, rim, p_ref, table, wt, top, half_ref, patch_ref, wave_ref, sum_ref, x_s):
    @pl.when(pl.program_id(0) == 0)
    def _():
        @pl.when(sc[0] == 0)
        def _():
            patch_ref[:, :, :H] = left[...]
            patch_ref[:, :, H:] = right[...]

        @pl.when(sc[0] != 0)
        def _():
            patch_ref[...] = rim[...]

        sum_ref[...] = jnp.zeros_like(sum_ref)

    for m in range(x_s.shape[0]):
        exit_half(p_ref, m, patch_ref, x_s)
    along_rows(x_s, table, half_ref)
    wave_half(wave_ref, sum_ref, wt, top, half_ref)


def bottom_half(sc, obj, rim, probe, table, wave_rows, top, mb=2):
    nm = probe.shape[1]
    halves = pl.BlockSpec((mb, N, N), lambda k, sc: (k, 0, 0))
    return pl.pallas_call(
        bottom_body,
        grid_spec=pltpu.PrefetchScalarGridSpec(
            num_scalar_prefetch=1,
            grid=(nm // mb,),
            in_specs=[
                pl.BlockSpec((2, H, H), lambda k, sc: (0, 1, sc[1])),
                pl.BlockSpec((2, H, H), lambda k, sc: (0, 1, sc[1] + 1)),
                whole(2, H, N),
                pl.BlockSpec((2, mb, H, N), lambda k, sc: (0, k, 1, 0)),
                whole(2 * N, 2 * N),
                pl.BlockSpec((1, N, 2 * N), lambda k, sc: (0, 0, 0)),
                halves,
            ],
            out_specs=[halves, whole(2, H, N), halves, whole(H, N)],
            scratch_shapes=[pltpu.VMEM((mb, H, 2 * N), bf16)],
        ),
        out_shape=[shape(nm, N, N, dtype=bf16), shape(2, H, N), shape(nm, N, N), shape(H, N)],
        compiler_params=params(50),
        name="bottom_half",
        cost_estimate=cost(11),
    )(sc, obj, obj, rim, probe, table, wave_rows, top)


def low_wave_body(wt, top, bot, wave_ref, sum_ref):
    @pl.when(pl.program_id(0) == 0)
    def _():
        sum_ref[...] = jnp.zeros_like(sum_ref)

    wave_half(wave_ref, sum_ref, wt, top, bot)


def low_wave(wave_rows, top, bot, mb=2):
    nm = top.shape[0]
    halves = pl.BlockSpec((mb, N, N), lambda k: (k, 0, 0))
    return pl.pallas_call(
        low_wave_body,
        grid=(nm // mb,),
        in_specs=[pl.BlockSpec((1, N, 2 * N), lambda k: (1, 0, 0)), halves, halves],
        out_specs=[halves, whole(H, N)],
        out_shape=[shape(nm, N, N), shape(H, N)],
        compiler_params=params(50),
        name="low_wave",
        cost_estimate=cost(5),
    )(wave_rows, top, bot)


def fixed_half(pat, s0, s1, wave_ref, table, half_ref, scale_s, x_s):
    @pl.when(pl.program_id(0) == 0)
    def _():
        def one(i):
            rows = at(i, CHUNK)
            scale_s[rows, :] = jnp.sqrt(pat[0, rows, :]) / jnp.sqrt(jnp.maximum(s0[rows, :] + s1[rows, :], 1.0))

        loop(H // CHUNK, one)

    for m in range(x_s.shape[0]):

        def one(i):
            rows = at(i, CHUNK)
            low = pl.ds(pl.multiple_of(i * CHUNK + H, CHUNK), CHUNK)
            factor = scale_s[rows, :]
            x_s[m, rows, :N] = (wave_ref[m, rows, :] * factor).astype(bf16)
            x_s[m, rows, N:] = (wave_ref[m, low, :] * factor).astype(bf16)

        loop(H // CHUNK, one)
    along_rows(x_s, table, half_ref)


def fixed_top(pat, s0, s1, wave, table, mb=2):
    nm = wave.shape[0]
    halves = pl.BlockSpec((mb, N, N), lambda k: (k, 0, 0))
    return pl.pallas_call(
        fixed_half,
        grid=(nm // mb,),
        in_specs=[pl.BlockSpec((1, H, N), lambda k: (0, 0, 0)), whole(H, N), whole(H, N), halves, whole(2 * N, 2 * N)],
        out_specs=halves,
        out_shape=shape(nm, N, N, dtype=bf16),
        scratch_shapes=[pltpu.VMEM((H, N), f32), pltpu.VMEM((mb, H, 2 * N), bf16)],
        compiler_params=params(50),
        name="fixed_top",
        cost_estimate=cost(5),
    )(pat, s0, s1, wave, table)


def gradients(sc, block, bt, top, bot, patch_top, patch_bot, p_ref, keep_ref, send_ref, gtop, gbot, back_s):
    core = sc[0]

    @pl.when(pl.program_id(0) == 0)
    def _():
        gtop[...] = jnp.zeros_like(gtop)
        gbot[...] = jnp.zeros_like(gbot)

    for m in range(p_ref.shape[1]):
        back_s[...] = jnp.dot(bt[0, :, :N], top[m], preferred_element_type=f32) + jnp.dot(
            bt[0, :, N:], bot[m], preferred_element_type=f32
        )
        for patch, g_ref, base in ((patch_top, gtop, 0), (patch_bot, gbot, 8)):

            def one(i):
                g = i + base
                rows = pl.ds(pl.multiple_of(i * 32 + block * 16, 16), 16)
                full = pl.ds(pl.multiple_of(g * 32 + block * 16, 16), 16)
                o_r = patch[0, rows, :]
                o_i = patch[1, rows, :]
                pr, pi, xr, xi = exit_rows(p_ref, m, full, o_r, o_i)
                rr = back_s[at(g, 16), :] - xr.astype(f32)
                ri = back_s[pl.ds(pl.multiple_of(g * 16 + H, 16), 16), :] - xi.astype(f32)
                g_ref[0, i] += pr * rr + pi * ri
                g_ref[1, i] += pr * ri - pi * rr
                st0 = o_r * rr + o_i * ri
                st1 = o_r * ri - o_i * rr
                turned_g = (g % 4) * 4 + g // 4
                keep_ref[m, jnp.where(core == 0, g, turned_g)] = jnp.where(core == 0, st0, st1)
                send_ref[m, jnp.where(core == 0, turned_g, g)] = jnp.where(core == 0, st1, st0)

            loop(8, one)


def first_block_body(sc, pat, s0, s1, wave_ref, table, bt, top, ptop, pbot, p_ref, half_ref, keep, send, gtop, gbot, scale_s, x_s, back_s):
    fixed_half(pat, s0, s1, wave_ref, table, half_ref, scale_s, x_s)
    gradients(sc, 0, bt, top, half_ref, ptop, pbot, p_ref, keep, send, gtop, gbot, back_s)


GRADS = [shape(2, 8, 16, N)] * 2


def grad_specs(mb):
    return [pl.BlockSpec((mb, 16, 16, N), lambda k, sc: (k, 0, 0, 0))] * 2 + [whole(2, 8, 16, N)] * 2


def first_block(sc, pat, s0, s1, wave, table, back_rows, top, ptop, pbot, probe, mb=2):
    nm = wave.shape[0]
    halves = pl.BlockSpec((mb, N, N), lambda k, sc: (k, 0, 0))
    return pl.pallas_call(
        first_block_body,
        grid_spec=pltpu.PrefetchScalarGridSpec(
            num_scalar_prefetch=1,
            grid=(nm // mb,),
            in_specs=[
                pl.BlockSpec((1, H, N), lambda k, sc: (0, 1, 0)),
                whole(H, N),
                whole(H, N),
                halves,
                whole(2 * N, 2 * N),
                pl.BlockSpec((1, N, 2 * N), lambda k, sc: (0, 0, 0)),
                halves,
                whole(2, H, N),
                whole(2, H, N),
                pl.BlockSpec((2, mb, N, N), lambda k, sc: (0, k, 0, 0)),
            ],
            out_specs=[halves] + grad_specs(mb),
            scratch_shapes=[pltpu.VMEM((H, N), f32), pltpu.VMEM((mb, H, 2 * N), bf16), pltpu.VMEM((N, N), f32)],
        ),
        out_shape=[shape(nm, N, N, dtype=bf16)] + [shape(nm, 16, 16, N)] * 2 + GRADS,
        compiler_params=params(50),
        name="first_block",
        cost_estimate=cost(16),
    )(sc, pat, s0, s1, wave, table, back_rows, top, ptop, pbot, probe)


def second_block_body(sc, bt, top, bot, ptop, pbot, p_ref, keep, send, gtop, gbot, back_s):
    gradients(sc, 1, bt, top, bot, ptop, pbot, p_ref, keep, send, gtop, gbot, back_s)


def second_block(sc, back_rows, top, bot, ptop, pbot, probe, mb=2):
    nm = top.shape[0]
    halves = pl.BlockSpec((mb, N, N), lambda k, sc: (k, 0, 0))
    return pl.pallas_call(
        second_block_body,
        grid_spec=pltpu.PrefetchScalarGridSpec(
            num_scalar_prefetch=1,
            grid=(nm // mb,),
            in_specs=[
                pl.BlockSpec((1, N, 2 * N), lambda k, sc: (1, 0, 0)),
                halves,
                halves,
                whole(2, H, N),
                whole(2, H, N),
                pl.BlockSpec((2, mb, N, N), lambda k, sc: (0, k, 0, 0)),
            ],
            out_specs=grad_specs(mb),
            scratch_shapes=[pltpu.VMEM((N, N), f32)],
        ),
        out_shape=[shape(nm, 16, 16, N)] * 2 + GRADS,
        compiler_params=params(50),
        name="second_block",
        cost_estimate=cost(9),
    )(sc, back_rows, top, bot, ptop, pbot, probe)


SCAN = ("y", "z", "x", "core")
RING = ("y", "z", "core")


def along(value, steps):
    count = lax.axis_size(SCAN)
    lo, hi = max(0, -steps), min(count, count - steps)
    return lax.ppermute(value, SCAN, [(i, i + steps) for i in range(lo, hi)])


def swapped(value, axis):
    return lax.ppermute(value, axis, [(0, 1), (1, 0)])


def turned(value, steps, first):
    flat = lambda y, z, core: (y * 4 + z) * 2 + core
    pairs = []
    for y in range(4):
        for z in range(4):
            for core in range(2):
                on_y = (core == 0) == first
                to = ((y + steps) % 4, z) if on_y else (y, (z + steps) % 4)
                pairs.append((flat(y, z, core), flat(*to, core)))
    return lax.ppermute(value, RING, pairs)


def across(value, flip_mode, flip_x):
    pairs = [(2 * m + x, 2 * (m ^ flip_mode) + (x ^ flip_x)) for m in range(2) for x in range(2)]
    return lax.ppermute(value, ("mode", "x"), pairs)


def rim_body(sc, a, out):
    out[...] = a[...]


def rim_rows(sc, obj):
    return pl.pallas_call(
        rim_body,
        grid_spec=pltpu.PrefetchScalarGridSpec(
            num_scalar_prefetch=1,
            grid=(2,),
            in_specs=[pl.BlockSpec((2, H, H), lambda k, sc: (0, 0, sc[1] + k))],
            out_specs=pl.BlockSpec((2, H, H), lambda k, sc: (0, 0, k)),
        ),
        out_shape=shape(2, H, N),
        compiler_params=params(8),
        name="rim_rows",
        cost_estimate=cost(2),
    )(sc, obj)


def light_body(p_ref, out_ref):
    @pl.when(pl.program_id(0) == 0)
    def _():
        out_ref[...] = jnp.zeros_like(out_ref)

    def one(i):
        rows = at(i, 16)
        acc = out_ref[rows, :]
        for m in range(p_ref.shape[1]):
            pr = p_ref[0, m, rows, :].astype(f32)
            pi = p_ref[1, m, rows, :].astype(f32)
            acc = acc + (pr * pr + pi * pi)
        out_ref[rows, :] = acc

    loop(N // 16, one)


def light(probe):
    nm = probe.shape[1]
    return pl.pallas_call(
        light_body,
        grid=(3,),
        in_specs=[pl.BlockSpec((2, nm // 3, N, N), lambda k: (0, k, 0, 0))],
        out_specs=whole(N, N),
        out_shape=shape(N, N),
        compiler_params=params(12),
        name="light",
        cost_estimate=cost(3),
    )(probe)


def core_add_body(sc, k0, k1, r0, r1, own, near, back, far0, far1):
    me = sc[0]
    for j, (k, r) in enumerate(((k0, r0), (k1, r1))):
        for out, turn in ((own, 0), (near, 1), (back, 3)):
            a = lax.rem(me + turn, 4)
            out[j, 0] = k[0, a] + r[0, a]
        a = lax.rem(me + 2, 4)
        (far0, far1)[j][0] = k[0, a] + r[0, a]


def core_add(sc, keep, recv):
    nm = keep.shape[0]
    n2 = nm // 2
    keep, recv = (v.reshape(nm, 4, 4, 16, N) for v in (keep, recv))
    low = pl.BlockSpec((1, 4, 4, 16, N), lambda k, sc: (k, 0, 0, 0, 0))
    high = pl.BlockSpec((1, 4, 4, 16, N), lambda k, sc: (k + n2, 0, 0, 0, 0))
    pair = pl.BlockSpec((2, 1, 4, 16, N), lambda k, sc: (0, k, 0, 0, 0))
    one = pl.BlockSpec((1, 4, 16, N), lambda k, sc: (k, 0, 0, 0))
    return pl.pallas_call(
        core_add_body,
        grid_spec=pltpu.PrefetchScalarGridSpec(
            num_scalar_prefetch=1,
            grid=(n2,),
            in_specs=[low, high, low, high],
            out_specs=[pair, pair, pair, one, one],
        ),
        out_shape=[shape(2, n2, 4, 16, N)] * 3 + [shape(n2, 4, 16, N)] * 2,
        compiler_params=params(16),
        name="core_add",
        cost_estimate=cost(4),
    )(sc, keep, keep, recv, recv)


def relay_body(a, b, ra, rb, oa, ob):
    oa[...] = a[...] + ra[...]
    ob[...] = b[...] + rb[...]


def relay_add(near, back, ra, rb):
    n2 = near.shape[1]
    low = pl.BlockSpec((None, 1, 4, 16, N), lambda k: (0, k, 0, 0, 0))
    high = pl.BlockSpec((None, 1, 4, 16, N), lambda k: (1, k, 0, 0, 0))
    one = pl.BlockSpec((1, 4, 16, N), lambda k: (k, 0, 0, 0))
    return pl.pallas_call(
        relay_body,
        grid=(n2,),
        in_specs=[low, high, one, one],
        out_specs=[low, high],
        out_shape=[shape(2, n2, 4, 16, N)] * 2,
        input_output_aliases={0: 0, 1: 1},
        compiler_params=params(8),
        name="relay_add",
        cost_estimate=cost(2),
    )(near, back, ra, rb)


def plane_add_body(sc, *refs):
    me = sc[1]
    for block in range(2):
        own, ra, rb = refs[3 * block : 3 * block + 3]
        for turn in range(4):
            b = lax.rem(me + turn, 4)
            refs[6 + turn][block, :, 0] = own[:, 0, b] + (ra[:, 0, b] + rb[:, 0, b])


def plane_add(sc, blocks):
    n2 = blocks[0][0].shape[1]
    ins = pl.BlockSpec((2, 1, 4, 16, N), lambda k, sc: (0, k, 0, 0, 0))
    outs = pl.BlockSpec((2, 2, 1, 16, N), lambda k, sc: (0, 0, k, 0, 0))
    return pl.pallas_call(
        plane_add_body,
        grid_spec=pltpu.PrefetchScalarGridSpec(
            num_scalar_prefetch=1, grid=(n2,), in_specs=[ins] * 6, out_specs=[outs] * 4
        ),
        out_shape=[shape(2, 2, n2, 16, N)] * 4,
        compiler_params=params(16),
        name="plane_add",
        cost_estimate=cost(3),
    )(sc, *blocks[0], *blocks[1])


def line_add_body(sc, a, b, c, d, keep, send):
    core = sc[2]
    mine = pl.ds(pl.multiple_of(core * 8, 8), 8)
    other = pl.ds(pl.multiple_of((1 - core) * 8, 8), 8)
    for out, rows in ((keep, mine), (send, other)):
        for block in range(2):
            for j in range(2):
                out[block, j] = (a[block, j, :, rows] + b[block, j, :, rows]) + (
                    c[block, j, :, rows] + d[block, j, :, rows]
                )


def line_add(sc, arrays):
    dims = arrays[0].shape
    small = (*dims[:3], 8, N)
    return pl.pallas_call(
        line_add_body,
        grid_spec=pltpu.PrefetchScalarGridSpec(
            num_scalar_prefetch=1, grid=(1,), in_specs=[whole(*dims)] * 4, out_specs=[whole(*small)] * 2
        ),
        out_shape=[shape(*small)] * 2,
        compiler_params=params(16),
        name="line_add",
        cost_estimate=cost(2),
    )(sc, *arrays)


def pixel_body(sc, keep, recv, rows, mine, other):
    core, x = sc[2], sc[3]
    scale = 1.0 / math.sqrt(64)
    nm = mine.shape[1]

    def fill(part, ref):
        mine[part] = ref[x] * scale + rows[part].astype(f32)
        other[part] = ref[1 - x] * scale

    @pl.when(core == 0)
    def _():
        fill(0, keep)
        fill(1, recv)

    @pl.when(core != 0)
    def _():
        fill(0, recv)
        fill(1, keep)


def pixel_step(sc, keep, recv, rows):
    nm = rows.shape[1]
    dims = (2, nm, 8, N)
    return pl.pallas_call(
        pixel_body,
        grid_spec=pltpu.PrefetchScalarGridSpec(
            num_scalar_prefetch=1, grid=(1,), in_specs=[whole(*dims)] * 3, out_specs=[whole(*dims)] * 2
        ),
        out_shape=[shape(*dims)] * 2,
        compiler_params=params(8),
        name="pixel_step",
        cost_estimate=cost(2),
    )(sc, keep.reshape(dims), recv.reshape(dims), rows)


def mix_body(sc, w_ref, mine, b, c, d, out_ref):
    mode = sc[4]
    nm = mine.shape[1]
    for part in range(2):
        own = [mine[part, j] + b[part, j] for j in range(nm)]
        far = [c[part, j] + d[part, j] for j in range(nm)]
        for k in range(nm):
            row = mode * nm + k
            acc = jnp.zeros((8, N), f32)
            for j in range(nm):
                acc += (w_ref[row, mode * nm + j].astype(f32) / 16.0) * own[j]
                acc += (w_ref[row, (1 - mode) * nm + j].astype(f32) / 16.0) * far[j]
            out_ref[part, k] = acc.astype(bf16)


def mix(sc, mixing, mine, b, c, d):
    dims = mine.shape
    return pl.pallas_call(
        mix_body,
        grid_spec=pltpu.PrefetchScalarGridSpec(
            num_scalar_prefetch=2, grid=(1,), in_specs=[whole(*dims)] * 4, out_specs=whole(*dims)
        ),
        out_shape=shape(*dims, dtype=bf16),
        compiler_params=params(8),
        name="mix",
        cost_estimate=cost(2),
    )(sc, mixing, mine, b, c, d)


def object_body(sc, lights, obj, t0, t0f, t1, t1f, b0, b0f, b1, b1f, over0, over1, out_ref):
    i, j = pl.program_id(0), pl.program_id(1)
    own_i, own_j = i - sc[0], j - sc[1]
    over_j = j - sc[3]
    out_ref[...] = obj[...]
    most = lights[0]
    in_cols = jnp.logical_and(own_j >= 0, own_j < 2)

    def add(even, odd):
        for g in range(8):
            for block, values in ((0, even), (1, odd)):
                rows = slice(g * 32 + block * 16, g * 32 + block * 16 + 16)
                total = values[0][:, g]
                for v in values[1:]:
                    total = total + v[:, g]
                out_ref[:, rows, :] += total / most

    @pl.when(jnp.logical_and(in_cols, own_i == 0))
    def _():
        add((t0, t0f), (t1, t1f))

    @pl.when(jnp.logical_and(in_cols, own_i == 1))
    def _():
        add((b0, b0f), (b1, b1f))

    @pl.when(jnp.logical_and(jnp.logical_and(i == 0, sc[2] == 1), jnp.logical_and(over_j >= 0, over_j < 2)))
    def _():
        add((over0,), (over1,))


def object_update(sc, most, obj, pieces, over):
    own = pl.BlockSpec((2, 8, 16, H), lambda i, j, sc, li: (0, 0, 0, jnp.clip(j - sc[1], 0, 1)))
    specs = [
        pl.BlockSpec((None, 2, 8, 16, H), lambda i, j, sc, li, b=b: (b, 0, 0, 0, jnp.clip(j - sc[3], 0, 1)))
        for b in range(2)
    ]
    band = pl.BlockSpec((2, H, H), lambda i, j, sc, li: (0, i, j))
    return pl.pallas_call(
        object_body,
        grid_spec=pltpu.PrefetchScalarGridSpec(
            num_scalar_prefetch=2, grid=(2, 4), in_specs=[band] + [own] * 8 + specs, out_specs=band
        ),
        out_shape=shape(2, N, 4 * H),
        compiler_params=params(24),
        name="object_update",
        cost_estimate=cost(6),
    )(sc, most, obj, *pieces, over, over)


def over_body(b0, b0f, b1, b1f, out):
    out[0] = b0[...] + b0f[...]
    out[1] = b1[...] + b1f[...]


def over_sum(b0, b0f, b1, b1f):
    spec = pl.BlockSpec((2, 2, 16, N), lambda k: (0, k, 0, 0))
    return pl.pallas_call(
        over_body,
        grid=(4,),
        in_specs=[spec] * 4,
        out_specs=pl.BlockSpec((2, 2, 2, 16, N), lambda k: (0, 0, k, 0, 0)),
        out_shape=shape(2, 2, 8, 16, N),
        compiler_params=params(8),
        name="over_sum",
        cost_estimate=cost(2),
    )(b0, b0f, b1, b1f)


def tied(*values):
    return lax.optimization_barrier(values)


def per_device(object_field, probe, patterns, row_shift, col_start, mixing):
    minus, plus, wave_rows, back_rows = tables()
    y, z, x, core = (lax.axis_index(a) for a in SCAN)
    mode = lax.axis_index("mode")
    first = jnp.where(core == 0, y, z)
    second = jnp.where(core == 0, z, y)
    sc = jnp.stack([first, second, core, x, mode])
    core = core[None]
    place = jnp.concatenate([row_shift, col_start])
    before = along(place, 1)
    rim = along(rim_rows(before, object_field), -1)
    half_top, patch_top = top_half(place, object_field, probe, minus)
    own_light = light(probe)
    half_top, own_light = tied(half_top, own_light)
    half_bot, patch_bot, wave_top, sum_top = bottom_half(
        place, object_field, rim, probe, minus, wave_rows, half_top
    )
    far_top = swapped(sum_top, "mode")
    wave_bot, sum_bot = low_wave(wave_rows, half_top, half_bot)
    far_bot = swapped(sum_bot, "mode")
    fixed = fixed_top(patterns, sum_top, far_top, wave_top, plus)
    low, keep0, send0, top0, bot0 = first_block(
        core, patterns, sum_bot, far_bot, wave_bot, plus, back_rows, fixed, patch_top, patch_bot, probe
    )
    recv0 = swapped(send0, "core")
    bot0_far = swapped(bot0, "mode")
    top0_far = swapped(top0, "mode")
    keep1, send1, top1, bot1 = second_block(core, back_rows, fixed, low, patch_top, patch_bot, probe)
    bot1_far = swapped(bot1, "mode")
    top1_far = swapped(top1, "mode")
    far_light = swapped(own_light, "mode")
    recv1 = swapped(send1, "core")
    own0, near0, back0, far0a, far0b = core_add(sc, keep0, recv0)
    ra0, rb0 = turned(far0a, 1, True), turned(far0b, -1, True)
    keep1, recv1, bot0_far = tied(keep1, recv1, bot0_far)
    own1, near1, back1, far1a, far1b = core_add(sc, keep1, recv1)
    near0, back0 = relay_add(near0, back0, ra0, rb0)
    ra1, rb1 = turned(far1a, 1, True), turned(far1b, -1, True)
    plane0 = (own0, turned(near0, 1, True), turned(back0, -1, True))
    ra1, rb1, bot1_far = tied(ra1, rb1, bot1_far)
    over = along(over_sum(bot0, bot0_far, bot1, bot1_far), 1)
    near1, back1 = relay_add(near1, back1, ra1, rb1)
    plane1 = (own1, turned(near1, 1, True), turned(back1, -1, True))
    *plane1, top0_far = tied(*plane1, top0_far)
    line = plane_add(sc, (plane0, plane1))
    line = [line[0]] + [turned(line[r], r, False) for r in (1, 3, 2)]
    *line, top1_far = tied(*line, top1_far)
    keep, send = line_add(sc, line)
    rows = lax.dynamic_slice_in_dim(probe, lax.axis_index(SCAN) * 8, 8, 2)
    keep, far_light = tied(keep, far_light)
    most = jnp.max(own_light + far_light)[None]
    mine, other = pixel_step(sc, keep, swapped(send, "core"), rows)
    probe_new = mix(sc, mixing, mine, across(other, 0, 1), across(mine, 1, 0), across(other, 1, 1))
    pieces = (top0, top0_far, top1, top1_far, bot0, bot0_far, bot1, bot1_far)
    object_new = object_update(jnp.concatenate([place, before]), most, object_field, pieces, over)
    return object_new, probe_new


def solution(mesh):
    split = Mesh(mesh.devices.reshape(2, 4, 4, 2, 2), ("mode", *SCAN))
    return jax.shard_map(
        per_device,
        mesh=split,
        in_specs=(P(None, SCAN, None), P(None, "mode", None, None), P(SCAN, None, None), P(SCAN), P(SCAN), P()),
        out_specs=(P(None, SCAN, None), P(None, "mode", SCAN, None)),
        check_vma=False,
    )
```

time: 560 us -> 218 us (0.39)
  the two profiles are of different devices: /device:TPU:1 before, /device:TPU:40 now
where the time goes in v2:
time: 218 us; the launch traced here: 217 us
  Pallas kernels  98 us (45%)
  waiting for transfers between devices  65 us (30%)
  starting transfers between devices  38.8 us (18%)
  local copies, waits for them, and re-layouts  11 us (5%)
  between operations  2.28 us (1%)
  other arithmetic  2.25 us (1%)
    ppermute x10, waiting for transfers between devices, swapped(): return lax.ppermute(value, axis, [(0, 1), (1, 0)])  45 us
    pallas_call x1, Pallas kernels, first_block(): pl.pallas_call(first_block_body, grid_spec=pltpu.PrefetchScalarGridSpec(n...  18.7 us
    pallas_call x1, Pallas kernels, bottom_half(): pl.pallas_call(bottom_body, grid_spec=pltpu.PrefetchScalarGridSpec(num_sc...  15.1 us
    ppermute x10, starting transfers between devices, swapped(): return lax.ppermute(value, axis, [(0, 1), (1, 0)])  14.4 us
    ppermute x11, starting transfers between devices, turned(): return lax.ppermute(value, RING, pairs)  13.9 us
    ppermute x3, waiting for transfers between devices, along(): return lax.ppermute(value, SCAN, [(i, i + steps) for i in range(lo, hi)])  13 us
    pallas_call x1, Pallas kernels, second_block(): pl.pallas_call(second_block_body, grid_spec=pltpu.PrefetchScalarGridSpec(...  12.5 us
    unnamed x66, local copies, waits for them, and re-layouts  10 us
  transfers between devices with their start and end apart: 27, of which 14 were waited for; matrix products, arithmetic and copies ran while one was open for 1% of the time, Pallas kernels for 23%

profile of v2, /device:TPU:40, one launch (start us, length us, event | category | flops | bytes accessed | tf_op | source)
XLA Modules:
  0.0 217.2 jit_solution(772901259750072241)
XLA Ops:
  2.0 2.3 %collective-permute-start = (s32[2]{0:T(128)S(1)}, s32[2]{0:T(128)S(1)}, u32[]{:S(2)}, u32[]{:S(2)}) collective-permute-start(s32[2]{0:T(128)S(1)} %pad_add_fusion.sc), channel_id=1, source_target_pairs={{0,1},{1,2},{2,3},{3,4},{4,5},{5,6},{6,7},{7,8},{8,9},{9,10},{10,1... | collective-permute-start | bytes 32 | tf_op jit(solution)/shard_map/ppermute | solution.py:366
  4.3 3.7 %collective-permute-done.sc = s32[2]{0:T(128)S(1)} collective-permute-done((s32[2]{0:T(128)S(1)}, s32[2]{0:T(128)S(1)}, u32[]{:S(2)}, u32[]{:S(2)}) %collective-permute-start) | collective-permute-done | bytes 40 | tf_op jit(solution)/shard_map/ppermute | solution.py:366
  8.0 2.2 %copy-done.1 = f32[2,512,1024]{2,1,0:T(8,128)S(1)} copy-done((f32[2,512,1024]{2,1,0:T(8,128)S(1)}, f32[2,512,1024]{2,1,0:T(8,128)}, u32[]{:S(2)}) %copy-start.1) | copy-done | bytes 4194328
  10.2 0.8 rim_rows.1
  11.1 2.1 collective-permute-start.1
  13.1 2.3 %light.1 = f32[512,512]{1,0:T(8,128)S(1)} custom-call(bf16[2,6,512,512]{3,2,1,0:T(8,128)(2,1)S(1)} %copy-done), custom_call_target="tpu_custom_call" | custom-call | flops 3300000000 | bytes 9000000 | tf_op jit(solution)/shard_map/light/pallas_call | solution.py:429
  15.5 8.4 %top_half.1 = (bf16[6,512,512]{2,1,0:T(8,128)(2,1)}, f32[2,256,512]{2,1,0:T(8,128)S(1)}) custom-call(s32[2]{0:T(128)S(1)} %pad_add_fusion.sc, f32[2,512,1024]{2,1,0:T(8,128)} %obj.1, f32[2,512,1024]{2,1,0:T(8,128)} %obj.1, bf16[2,6,512,512]{3,2,1,0:T(8,128)(2,1)} %p_ref.9, bf16[1024,1024]{1,0:T(8,128)(2,1)S(1)} %copy-done.26), custom_call_target="tpu_custom_call" | custom-call | flops 6600000000 | bytes 18000000 | tf_op jit(solution)/shard_map/top_half/pallas_call | solution.py:104
  23.9 1.0 copy-done.27
  24.9 0.5 collective-permute-done.1.rim
  25.4 15.1 %bottom_half.1 = (bf16[6,512,512]{2,1,0:T(8,128)(2,1)}, f32[2,256,512]{2,1,0:T(8,128)S(1)}, f32[6,512,512]{2,1,0:T(8,128)}, f32[256,512]{1,0:T(8,128)S(1)}) custom-call(s32[2]{0:T(128)S(1)} %pad_add_fusion.sc, f32[2,512,1024]{2,1,0:T(8,128)} %obj.1, f32[2,512,1024]{2,1,0:T(8,128)} %obj.1, f32[2,256,512]{2,1,0:T(8,128)S(1)} %collective-permute-done.1.rim, ...), custom_call_target="tpu_custom_call" | custom-call | flops 12099999744 | bytes 33000000 | tf_op jit(solution)/shard_map/bottom_half/pallas_call | solution.py:168
  40.5 1.0 copy-done.31
  41.5 3.0 %collective-permute-start.3 = (f32[256,512]{1,0:T(8,128)S(1)}, f32[256,512]{1,0:T(8,128)}, u32[]{:S(2)}, u32[]{:S(2)}) collective-permute-start(f32[256,512]{1,0:T(8,128)S(1)} %get-tuple-element.66.s0), channel_id=1, source_target_pairs={{0,64},{64,0},{1,65},{65,1},{2,66},{66,2},{3,67},{67,3},{4,68},{68... | collective-permute-start | bytes 1572872 | tf_op jit(solution)/shard_map/ppermute | solution.py:370
  44.6 8.3 %low_wave.1 = (f32[6,512,512]{2,1,0:T(8,128)}, f32[256,512]{1,0:T(8,128)S(1)}) custom-call(bf16[2,512,1024]{2,1,0:T(8,128)(2,1)S(1)} %copy-done.25, bf16[6,512,512]{2,1,0:T(8,128)(2,1)} %get-tuple-element.62.top, bf16[6,512,512]{2,1,0:T(8,128)(2,1)} %get-tuple-element.63.bot), custom_call_target="tpu_custom_call" | custom-call | flops 5500000256 | bytes 15000000 | tf_op jit(solution)/shard_map/low_wave/pallas_call | solution.py:203
  52.8 0.5 collective-permute-start.2
  53.3 3.9 %collective-permute-done.3.s1 = f32[256,512]{1,0:T(8,128)} collective-permute-done((f32[256,512]{1,0:T(8,128)S(1)}, f32[256,512]{1,0:T(8,128)}, u32[]{:S(2)}, u32[]{:S(2)}) %collective-permute-start.3) | collective-permute-done | bytes 524320 | tf_op jit(solution)/shard_map/ppermute | solution.py:370
  57.3 8.7 %fixed_top.1.top = bf16[6,512,512]{2,1,0:T(8,128)(2,1)} custom-call(f32[1,512,512]{2,1,0:T(8,128)S(1)} %copy-done.3, f32[256,512]{1,0:T(8,128)S(1)} %get-tuple-element.66.s0, f32[256,512]{1,0:T(8,128)} %collective-permute-done.3.s1, f32[6,512,512]{2,1,0:T(8,128)} %get-tuple-element.67.wave_ref, bf16[1024,1024]{1,0:T(8,128)(2,1)} %constant.43.clone.table), custom_call_target="tpu_custom_call" | custom-call | flops 5500000256 | bytes 15000000 | tf_op jit(solution)/shard_map/fixed_top/pallas_call | solution.py:240
  66.0 2.5 %collective-permute-done.2.s1 = f32[256,512]{1,0:T(8,128)} collective-permute-done((f32[256,512]{1,0:T(8,128)S(1)}, f32[256,512]{1,0:T(8,128)}, u32[]{:S(2)}, u32[]{:S(2)}) %collective-permute-start.2) | collective-permute-done | bytes 524320 | tf_op jit(solution)/shard_map/ppermute | solution.py:370
  68.5 1.0 copy-done.21
  69.5 18.7 %first_block.1 = (bf16[6,512,512]{2,1,0:T(8,128)(2,1)}, f32[6,16,16,512]{3,2,1,0:T(8,128)}, f32[6,16,16,512]{3,2,1,0:T(8,128)}, f32[2,8,16,512]{3,2,1,0:T(8,128)S(1)}, f32[2,8,16,512]{3,2,1,0:T(8,128)S(1)}) custom-call(s32[1]{0:T(128)} %bitcast.2.sc, f32[1,512,512]{2,1,0:T(8,128)S(1)} %copy-done.3, f32[256,512]{1,0:T(8,128)S(1)} %copy-done.21, ...), custom_call_target="tpu_custom_call" | custom-call | flops 17600000000 | bytes 48000000 | tf_op jit(solution)/shard_map/first_block/pallas_call | solution.py:302
  88.3 12.5 %second_block.1 = (f32[6,16,16,512]{3,2,1,0:T(8,128)}, f32[6,16,16,512]{3,2,1,0:T(8,128)}, f32[2,8,16,512]{3,2,1,0:T(8,128)S(1)}, f32[2,8,16,512]{3,2,1,0:T(8,128)S(1)}) custom-call(s32[1]{0:T(128)} %bitcast.2.sc, bf16[2,512,1024]{2,1,0:T(8,128)(2,1)} %constant.44.clone.bt, bf16[6,512,512]{2,1,0:T(8,128)(2,1)} %fixed_top.1.top, ...), custom_call_target="tpu_custom_call" | custom-call | flops 9900000256 | bytes 27000000 | tf_op jit(solution)/shard_map/second_block/pallas_call | solution.py:336
  100.9 0.5 collective-permute-start.4
  101.6 3.2 %collective-permute-start.10 = (f32[2,8,16,512]{3,2,1,0:T(8,128)S(1)}, f32[2,8,16,512]{3,2,1,0:T(8,128)}, u32[]{:S(2)}, u32[]{:S(2)}) collective-permute-start(f32[2,8,16,512]{3,2,1,0:T(8,128)S(1)} %get-tuple-element.82.b0), channel_id=1, source_target_pairs={{0,64},{64,0},{1,65},{65,1},{2,66},{66,2},{3,67},{67,3},{4,68},{68... | collective-permute-start | bytes 1572872 | tf_op jit(solution)/shard_map/ppermute | solution.py:370
  104.9 0.4 collective-permute-start.13
  105.2 12.8 %collective-permute-done.10.b0f = f32[2,8,16,512]{3,2,1,0:T(8,128)} collective-permute-done((f32[2,8,16,512]{3,2,1,0:T(8,128)S(1)}, f32[2,8,16,512]{3,2,1,0:T(8,128)}, u32[]{:S(2)}, u32[]{:S(2)}) %collective-permute-start.10) | collective-permute-done | bytes 524320 | tf_op jit(solution)/shard_map/ppermute | solution.py:370
  118.0 1.9 copy-done.24
  119.9 3.6 %core_add.3 = (f32[2,3,4,16,512]{4,3,2,1,0:T(8,128)S(1)}, f32[2,3,4,16,512]{4,3,2,1,0:T(8,128)S(1)}, f32[2,3,4,16,512]{4,3,2,1,0:T(8,128)S(1)}, f32[3,4,16,512]{3,2,1,0:T(8,128)S(1)}, f32[3,4,16,512]{3,2,1,0:T(8,128)S(1)}) custom-call(s32[5]{0:T(128)S(1)} %stack.23.sc, f32[6,4,4,16,512]{4,3,2,1,0:T(8,128)S(1)} %bitcast.15, ...), custom_call_target="tpu_custom_call" | custom-call | flops 4400000000 | bytes 12000000 | tf_op jit(solution)/shard_map/core_add/pallas_call | solution.py:459
  123.5 1.7 collective-permute-start.11
  125.2 0.4 collective-permute-start.12
  125.6 3.4 %core_add.2 = (f32[2,3,4,16,512]{4,3,2,1,0:T(8,128)S(1)}, f32[2,3,4,16,512]{4,3,2,1,0:T(8,128)S(1)}, f32[2,3,4,16,512]{4,3,2,1,0:T(8,128)S(1)}, f32[3,4,16,512]{3,2,1,0:T(8,128)S(1)}, f32[3,4,16,512]{3,2,1,0:T(8,128)S(1)}) custom-call(s32[5]{0:T(128)S(1)} %stack.23.sc, f32[6,4,4,16,512]{4,3,2,1,0:T(8,128)S(1)} %bitcast.13, ...), custom_call_target="tpu_custom_call" | custom-call | flops 4400000000 | bytes 12000000 | tf_op jit(solution)/shard_map/core_add/pallas_call | solution.py:459
  129.0 1.7 collective-permute-start.5
  130.7 0.4 collective-permute-start.6
  131.4 1.6 collective-permute-done.12.rb
  133.1 1.3 collective-permute-start.14
  134.5 0.8 collective-permute-start.15
  135.2 1.6 collective-permute-done.5.ra
  136.9 1.6 collective-permute-done.6.rb
  138.6 1.3 collective-permute-start.7
  139.9 0.8 collective-permute-start.8
  140.7 3.1 %collective-permute-start.16 = (f32[2,8,16,512]{3,2,1,0:T(8,128)S(1)}, f32[2,8,16,512]{3,2,1,0:T(8,128)S(1)}, u32[]{:S(2)}, u32[]{:S(2)}) collective-permute-start(f32[2,8,16,512]{3,2,1,0:T(8,128)S(1)} %get-tuple-element.95.t0), channel_id=1, source_target_pairs={{0,64},{64,0},{1,65},{65,1},{2,66},{66,2},{3,67},{67,3},{4,68},{68... | collective-permute-start | bytes 1572872 | tf_op jit(solution)/shard_map/ppermute | solution.py:370
  143.8 8.8 %collective-permute-done.16.t0f = f32[2,8,16,512]{3,2,1,0:T(8,128)S(1)} collective-permute-done((f32[2,8,16,512]{3,2,1,0:T(8,128)S(1)}, f32[2,8,16,512]{3,2,1,0:T(8,128)S(1)}, u32[]{:S(2)}, u32[]{:S(2)}) %collective-permute-start.16) | collective-permute-done | bytes 524320 | tf_op jit(solution)/shard_map/ppermute | solution.py:370
  152.6 0.8 copy-done.16
  153.4 3.0 %collective-permute-start.20 = (f32[2,8,16,512]{3,2,1,0:T(8,128)S(1)}, f32[2,8,16,512]{3,2,1,0:T(8,128)S(1)}, u32[]{:S(2)}, u32[]{:S(2)}) collective-permute-start(f32[2,8,16,512]{3,2,1,0:T(8,128)S(1)} %get-tuple-element.103.t1), channel_id=1, source_target_pairs={{0,64},{64,0},{1,65},{65,1},{2,66},{66,2},{3,67},{67,3},{4,68},{68... | collective-permute-start | bytes 1572872 | tf_op jit(solution)/shard_map/ppermute | solution.py:370
  156.4 0.5 collective-permute-start.21
  157.0 2.4 %plane_add.1 = (f32[2,2,3,16,512]{4,3,2,1,0:T(8,128)S(1)}, f32[2,2,3,16,512]{4,3,2,1,0:T(8,128)}, f32[2,2,3,16,512]{4,3,2,1,0:T(8,128)S(1)}, f32[2,2,3,16,512]{4,3,2,1,0:T(8,128)}) custom-call(s32[5]{0:T(128)S(1)} %stack.23.sc, f32[2,3,4,16,512]{4,3,2,1,0:T(8,128)S(1)} %get-tuple-element.72.refs_0_, ...), custom_call_target="tpu_custom_call" | custom-call | flops 3300000000 | bytes 9000000 | tf_op jit(solution)/shard_map/plane_add/pallas_call | solution.py:510
  159.4 2.3 %collective-permute-start.17 = (f32[2,2,3,16,512]{4,3,2,1,0:T(8,128)}, f32[2,2,3,16,512]{4,3,2,1,0:T(8,128)}, u32[]{:S(2)}, u32[]{:S(2)}) collective-permute-start(f32[2,2,3,16,512]{4,3,2,1,0:T(8,128)} %get-tuple-element.100), channel_id=1, source_target_pairs={{0,4},{1,17},{4,8},{5,21},{8,12},{9,25},{12,0},{13,29},{16,20},{17... | collective-permute-start | bytes 1179656 | tf_op jit(solution)/shard_map/ppermute | solution.py:382
  161.7 0.7 collective-permute-start.18
  162.4 2.5 %collective-permute-start.19 = (f32[2,2,3,16,512]{4,3,2,1,0:T(8,128)S(1)}, f32[2,2,3,16,512]{4,3,2,1,0:T(8,128)}, u32[]{:S(2)}, u32[]{:S(2)}) collective-permute-start(f32[2,2,3,16,512]{4,3,2,1,0:T(8,128)S(1)} %get-tuple-element.102), channel_id=1, source_target_pairs={{0,8},{1,33},{4,12},{5,37},{8,0},{9,41},{12,4},{13,45},{16,24},{17... | collective-permute-start | bytes 1179656 | tf_op jit(solution)/shard_map/ppermute | solution.py:382
  164.9 2.1 over_sum.1
  167.0 2.8 %collective-permute-done.20.t1f = f32[2,8,16,512]{3,2,1,0:T(8,128)S(1)} collective-permute-done((f32[2,8,16,512]{3,2,1,0:T(8,128)S(1)}, f32[2,8,16,512]{3,2,1,0:T(8,128)S(1)}, u32[]{:S(2)}, u32[]{:S(2)}) %collective-permute-start.20) | collective-permute-done | bytes 524320 | tf_op jit(solution)/shard_map/ppermute | solution.py:370
  169.8 0.8 copy-done.18
  170.6 1.9 collective-permute-start.22
  172.5 0.9 constant_dynamic-slice_fusion.rows
  173.4 1.7 collective-permute-done.19.d
  175.1 1.0 copy-done.30
  176.1 1.8 line_add.1
  178.2 14.2 %collective-permute-done.21 = f32[512,512]{1,0:T(8,128)} collective-permute-done((f32[512,512]{1,0:T(8,128)S(1)}, f32[512,512]{1,0:T(8,128)}, u32[]{:S(2)}, u32[]{:S(2)}) %collective-permute-start.21) | collective-permute-done | bytes 1048608 | tf_op jit(solution)/shard_map/ppermute | solution.py:370
  192.4 2.1 add_reduce_fusion
  194.5 0.6 pixel_step.1
  195.1 1.5 collective-permute-start.24
  196.6 2.2 collective-permute-start.26
  198.8 0.6 collective-permute-start.25
  199.3 8.8 %collective-permute-done.22.over0.over1 = f32[2,2,8,16,512]{4,3,2,1,0:T(8,128)S(1)} collective-permute-done((f32[2,2,8,16,512]{4,3,2,1,0:T(8,128)S(1)}, f32[2,2,8,16,512]{4,3,2,1,0:T(8,128)S(1)}, u32[]{:S(2)}, u32[]{:S(2)}) %collective-permute-start.22) | collective-permute-done | bytes 1048608 | tf_op jit(solution)/shard_map/ppermute | solution.py:366
  208.2 7.4 %object_update.1 = f32[2,512,1024]{2,1,0:T(8,128)} custom-call(s32[4]{0:T(128)S(1)} %pad_add_fusion.1.sc, f32[1]{0:T(128)} %bitcast.9.lights, f32[2,512,1024]{2,1,0:T(8,128)S(1)} %copy-done.2, f32[2,8,16,512]{3,2,1,0:T(8,128)S(1)} %copy-done.5, f32[2,8,16,512]{3,2,1,0:T(8,128)S(1)} %copy-done.17, f32[2,8,16,512]{3,2,1,0:T(8,128)S(1)} %copy-done.10, ...), custom_call_target="tpu_custom_call" | custom-call | flops 6600000000 | bytes 18000000 | tf_op jit(solution)/shard_map/object_update/pallas_call | solution.py:650
  215.6 1.6 mix.1
  (79 shorter events, 1.3 us)
Async XLA Ops:
  2.0 11.1 %copy-start = (bf16[2,6,512,512]{3,2,1,0:T(8,128)(2,1)S(1)}, bf16[2,6,512,512]{3,2,1,0:T(8,128)(2,1)}, u32[]{:S(2)}) copy-start(bf16[2,6,512,512]{3,2,1,0:T(8,128)(2,1)} %p_ref.9) | copy-start | bytes 18874372
  2.0 6.0 %collective-permute-start = (s32[2]{0:T(128)S(1)}, s32[2]{0:T(128)S(1)}, u32[]{:S(2)}, u32[]{:S(2)}) collective-permute-start(s32[2]{0:T(128)S(1)} %pad_add_fusion.sc), channel_id=1, source_target_pairs={{0,1},{1,2},{2,3},{3,4},{4,5},{5,6},{6,7},{7,8},{8,9},{9,10},{10,1... | collective-permute-start | bytes 32 | tf_op jit(solution)/shard_map/ppermute | solution.py:366
  8.0 2.2 %copy-start.1 = (f32[2,512,1024]{2,1,0:T(8,128)S(1)}, f32[2,512,1024]{2,1,0:T(8,128)}, u32[]{:S(2)}) copy-start(f32[2,512,1024]{2,1,0:T(8,128)} %obj.1) | copy-start | bytes 12582916
  11.0 4.4 %copy-start.26 = (bf16[1024,1024]{1,0:T(8,128)(2,1)S(1)}, bf16[1024,1024]{1,0:T(8,128)(2,1)}, u32[]{:S(2)}) copy-start(bf16[1024,1024]{1,0:T(8,128)(2,1)} %constant.41.clone.table) | copy-start | bytes 6291460
  11.1 14.4 %collective-permute-start.1 = (f32[2,256,512]{2,1,0:T(8,128)S(1)}, f32[2,256,512]{2,1,0:T(8,128)S(1)}, u32[]{:S(2)}, u32[]{:S(2)}) collective-permute-start(f32[2,256,512]{2,1,0:T(8,128)S(1)} %rim_rows.1), channel_id=1, source_target_pairs={{1,0},{2,1},{3,2},{4,3},{5,4},{6,5},{7,6},{8,7},{9,8},{10,9},{11,1... | collective-permute-start | bytes 3145736 | tf_op jit(solution)/shard_map/ppermute | solution.py:366
  23.9 1.0 copy-start.27
  24.9 19.7 %copy-start.25 = (bf16[2,512,1024]{2,1,0:T(8,128)(2,1)S(1)}, bf16[2,512,1024]{2,1,0:T(8,128)(2,1)}, u32[]{:S(2)}) copy-start(bf16[2,512,1024]{2,1,0:T(8,128)(2,1)} %constant.42.clone.wt) | copy-start | bytes 6291460
  40.5 1.0 copy-start.31
  41.5 15.7 %collective-permute-start.3 = (f32[256,512]{1,0:T(8,128)S(1)}, f32[256,512]{1,0:T(8,128)}, u32[]{:S(2)}, u32[]{:S(2)}) collective-permute-start(f32[256,512]{1,0:T(8,128)S(1)} %get-tuple-element.66.s0), channel_id=1, source_target_pairs={{0,64},{64,0},{1,65},{65,1},{2,66},{66,2},{3,67},{67,3},{4,68},{68... | collective-permute-start | bytes 1572872 | tf_op jit(solution)/shard_map/ppermute | solution.py:370
  44.6 12.7 %copy-start.3 = (f32[1,512,512]{2,1,0:T(8,128)S(1)}, f32[1,512,512]{2,1,0:T(8,128)}, u32[]{:S(2)}) copy-start(f32[1,512,512]{2,1,0:T(8,128)} %pat.3) | copy-start | bytes 3145732
  52.8 13.1 %copy-start.20 = (f32[256,512]{1,0:T(8,128)}, f32[256,512]{1,0:T(8,128)S(1)}, u32[]{:S(2)}) copy-start(f32[256,512]{1,0:T(8,128)S(1)} %get-tuple-element.64.s0) | copy-start | bytes 1572868
  52.8 15.7 %collective-permute-start.2 = (f32[256,512]{1,0:T(8,128)S(1)}, f32[256,512]{1,0:T(8,128)}, u32[]{:S(2)}, u32[]{:S(2)}) collective-permute-start(f32[256,512]{1,0:T(8,128)S(1)} %get-tuple-element.64.s0), channel_id=1, source_target_pairs={{0,64},{64,0},{1,65},{65,1},{2,66},{66,2},{3,67},{67,3},{4,68},{68... | collective-permute-start | bytes 1572872 | tf_op jit(solution)/shard_map/ppermute | solution.py:370
  68.5 1.0 copy-start.21
  69.5 18.8 %copy-start.28 = (f32[2,256,512]{2,1,0:T(8,128)S(1)}, f32[2,256,512]{2,1,0:T(8,128)}, u32[]{:S(2)}) copy-start(f32[2,256,512]{2,1,0:T(8,128)} %copy-done.27) | copy-start | bytes 3145732
  69.5 18.8 %copy-start.32 = (f32[2,256,512]{2,1,0:T(8,128)S(1)}, f32[2,256,512]{2,1,0:T(8,128)}, u32[]{:S(2)}) copy-start(f32[2,256,512]{2,1,0:T(8,128)} %copy-done.31) | copy-start | bytes 3145732
  88.3 13.3 %copy-start.6 = (f32[2,8,16,512]{3,2,1,0:T(8,128)}, f32[2,8,16,512]{3,2,1,0:T(8,128)S(1)}, u32[]{:S(2)}) copy-start(f32[2,8,16,512]{3,2,1,0:T(8,128)S(1)} %get-tuple-element.82.b0) | copy-start | bytes 1572868
  88.3 52.4 %copy-start.4 = (f32[2,8,16,512]{3,2,1,0:T(8,128)}, f32[2,8,16,512]{3,2,1,0:T(8,128)S(1)}, u32[]{:S(2)}) copy-start(f32[2,8,16,512]{3,2,1,0:T(8,128)S(1)} %get-tuple-element.95.t0) | copy-start | bytes 1572868
  100.8 0.8 copy-start.11
  100.8 52.6 %copy-start.9 = (f32[2,8,16,512]{3,2,1,0:T(8,128)}, f32[2,8,16,512]{3,2,1,0:T(8,128)S(1)}, u32[]{:S(2)}) copy-start(f32[2,8,16,512]{3,2,1,0:T(8,128)S(1)} %get-tuple-element.103.t1) | copy-start | bytes 1572868
  100.8 17.2 %collective-permute-start.9 = (f32[6,16,16,512]{3,2,1,0:T(8,128)}, f32[6,16,16,512]{3,2,1,0:T(8,128)}, u32[]{:S(2)}, u32[]{:S(2)}) collective-permute-start(f32[6,16,16,512]{3,2,1,0:T(8,128)} %get-tuple-element.81), channel_id=1, source_target_pairs={{0,1},{1,0},{2,3},{3,2},{4,5},{5,4},{6,7},{7,6},{8,9},{9,8},{10,11... | collective-permute-start | bytes 9437192 | tf_op jit(solution)/shard_map/ppermute | solution.py:370
  100.9 24.7 %collective-permute-start.4 = (f32[6,16,16,512]{3,2,1,0:T(8,128)}, f32[6,16,16,512]{3,2,1,0:T(8,128)}, u32[]{:S(2)}, u32[]{:S(2)}) collective-permute-start(f32[6,16,16,512]{3,2,1,0:T(8,128)} %get-tuple-element.71), channel_id=1, source_target_pairs={{0,1},{1,0},{2,3},{3,2},{4,5},{5,4},{6,7},{7,6},{8,9},{9,8},{10,11... | collective-permute-start | bytes 9437192 | tf_op jit(solution)/shard_map/ppermute | solution.py:370
  101.6 16.4 %collective-permute-start.10 = (f32[2,8,16,512]{3,2,1,0:T(8,128)S(1)}, f32[2,8,16,512]{3,2,1,0:T(8,128)}, u32[]{:S(2)}, u32[]{:S(2)}) collective-permute-start(f32[2,8,16,512]{3,2,1,0:T(8,128)S(1)} %get-tuple-element.82.b0), channel_id=1, source_target_pairs={{0,64},{64,0},{1,65},{65,1},{2,66},{66,2},{3,67},{67,3},{4,68},{68... | collective-permute-start | bytes 1572872 | tf_op jit(solution)/shard_map/ppermute | solution.py:370
  104.9 26.2 %collective-permute-start.13 = (f32[2,8,16,512]{3,2,1,0:T(8,128)}, f32[2,8,16,512]{3,2,1,0:T(8,128)S(1)}, u32[]{:S(2)}, u32[]{:S(2)}) collective-permute-start(f32[2,8,16,512]{3,2,1,0:T(8,128)} %copy-done.11), channel_id=1, source_target_pairs={{0,64},{64,0},{1,65},{65,1},{2,66},{66,2},{3,67},{67,3},{4,68},{68... | collective-permute-start | bytes 1572872 | tf_op jit(solution)/shard_map/ppermute | solution.py:370
  118.0 1.9 copy-start.24
  119.9 5.7 %copy-start.23 = (f32[6,16,16,512]{3,2,1,0:T(8,128)S(1)}, f32[6,16,16,512]{3,2,1,0:T(8,128)}, u32[]{:S(2)}) copy-start(f32[6,16,16,512]{3,2,1,0:T(8,128)} %get-tuple-element.70) | copy-start | bytes 9437188
  123.5 7.8 %collective-permute-start.11 = (f32[3,4,16,512]{3,2,1,0:T(8,128)S(1)}, f32[3,4,16,512]{3,2,1,0:T(8,128)S(1)}, u32[]{:S(2)}, u32[]{:S(2)}) collective-permute-start(f32[3,4,16,512]{3,2,1,0:T(8,128)S(1)} %get-tuple-element.88), channel_id=1, source_target_pairs={{0,16},{1,5},{4,20},{5,9},{8,24},{9,13},{12,28},{13,1},{16,32},{17... | collective-permute-start | bytes 1179656 | tf_op jit(solution)/shard_map/ppermute | solution.py:382
  125.2 7.8 %collective-permute-start.12 = (f32[3,4,16,512]{3,2,1,0:T(8,128)S(1)}, f32[3,4,16,512]{3,2,1,0:T(8,128)S(1)}, u32[]{:S(2)}, u32[]{:S(2)}) collective-permute-start(f32[3,4,16,512]{3,2,1,0:T(8,128)S(1)} %get-tuple-element.89), channel_id=1, source_target_pairs={{0,48},{1,13},{4,52},{5,1},{8,56},{9,5},{12,60},{13,9},{16,0},{17,... | collective-permute-start | bytes 1179656 | tf_op jit(solution)/shard_map/ppermute | solution.py:382
  129.0 7.8 %collective-permute-start.5 = (f32[3,4,16,512]{3,2,1,0:T(8,128)S(1)}, f32[3,4,16,512]{3,2,1,0:T(8,128)S(1)}, u32[]{:S(2)}, u32[]{:S(2)}) collective-permute-start(f32[3,4,16,512]{3,2,1,0:T(8,128)S(1)} %get-tuple-element.75), channel_id=1, source_target_pairs={{0,16},{1,5},{4,20},{5,9},{8,24},{9,13},{12,28},{13,1},{16,32},{17... | collective-permute-start | bytes 1179656 | tf_op jit(solution)/shard_map/ppermute | solution.py:382
  130.7 7.8 %collective-permute-start.6 = (f32[3,4,16,512]{3,2,1,0:T(8,128)S(1)}, f32[3,4,16,512]{3,2,1,0:T(8,128)S(1)}, u32[]{:S(2)}, u32[]{:S(2)}) collective-permute-start(f32[3,4,16,512]{3,2,1,0:T(8,128)S(1)} %get-tuple-element.76), channel_id=1, source_target_pairs={{0,48},{1,13},{4,52},{5,1},{8,56},{9,5},{12,60},{13,9},{16,0},{17,... | collective-permute-start | bytes 1179656 | tf_op jit(solution)/shard_map/ppermute | solution.py:382
  131.1 33.8 %copy-start.14 = (f32[2,8,16,512]{3,2,1,0:T(8,128)}, f32[2,8,16,512]{3,2,1,0:T(8,128)S(1)}, u32[]{:S(2)}) copy-start(f32[2,8,16,512]{3,2,1,0:T(8,128)S(1)} %collective-permute-done.13.b1f) | copy-start | bytes 1572868
  133.1 23.3 %collective-permute-start.14 = (f32[2,3,4,16,512]{4,3,2,1,0:T(8,128)S(1)}, f32[2,3,4,16,512]{4,3,2,1,0:T(8,128)S(1)}, u32[]{:S(2)}, u32[]{:S(2)}) collective-permute-start(f32[2,3,4,16,512]{4,3,2,1,0:T(8,128)S(1)} %get-tuple-element.93), channel_id=1, source_target_pairs={{0,16},{1,5},{4,20},{5,9},{8,24},{9,13},{12,28},{13,1},{16,32},{17... | collective-permute-start | bytes 2359304 | tf_op jit(solution)/shard_map/ppermute | solution.py:382
  134.5 22.5 %collective-permute-start.15 = (f32[2,3,4,16,512]{4,3,2,1,0:T(8,128)S(1)}, f32[2,3,4,16,512]{4,3,2,1,0:T(8,128)S(1)}, u32[]{:S(2)}, u32[]{:S(2)}) collective-permute-start(f32[2,3,4,16,512]{4,3,2,1,0:T(8,128)S(1)} %get-tuple-element.94), channel_id=1, source_target_pairs={{0,48},{1,13},{4,52},{5,1},{8,56},{9,5},{12,60},{13,9},{16,0},{17,... | collective-permute-start | bytes 2359304 | tf_op jit(solution)/shard_map/ppermute | solution.py:382
  138.6 18.4 %collective-permute-start.7 = (f32[2,3,4,16,512]{4,3,2,1,0:T(8,128)S(1)}, f32[2,3,4,16,512]{4,3,2,1,0:T(8,128)S(1)}, u32[]{:S(2)}, u32[]{:S(2)}) collective-permute-start(f32[2,3,4,16,512]{4,3,2,1,0:T(8,128)S(1)} %get-tuple-element.77), channel_id=1, source_target_pairs={{0,16},{1,5},{4,20},{5,9},{8,24},{9,13},{12,28},{13,1},{16,32},{17... | collective-permute-start | bytes 2359304 | tf_op jit(solution)/shard_map/ppermute | solution.py:382
  139.9 17.0 %collective-permute-start.8 = (f32[2,3,4,16,512]{4,3,2,1,0:T(8,128)S(1)}, f32[2,3,4,16,512]{4,3,2,1,0:T(8,128)S(1)}, u32[]{:S(2)}, u32[]{:S(2)}) collective-permute-start(f32[2,3,4,16,512]{4,3,2,1,0:T(8,128)S(1)} %get-tuple-element.78), channel_id=1, source_target_pairs={{0,48},{1,13},{4,52},{5,1},{8,56},{9,5},{12,60},{13,9},{16,0},{17,... | collective-permute-start | bytes 2359304 | tf_op jit(solution)/shard_map/ppermute | solution.py:382
  140.7 11.9 %collective-permute-start.16 = (f32[2,8,16,512]{3,2,1,0:T(8,128)S(1)}, f32[2,8,16,512]{3,2,1,0:T(8,128)S(1)}, u32[]{:S(2)}, u32[]{:S(2)}) collective-permute-start(f32[2,8,16,512]{3,2,1,0:T(8,128)S(1)} %get-tuple-element.95.t0), channel_id=1, source_target_pairs={{0,64},{64,0},{1,65},{65,1},{2,66},{66,2},{3,67},{67,3},{4,68},{68... | collective-permute-start | bytes 1572872 | tf_op jit(solution)/shard_map/ppermute | solution.py:370
  152.6 0.8 copy-start.16
  153.4 16.4 %collective-permute-start.20 = (f32[2,8,16,512]{3,2,1,0:T(8,128)S(1)}, f32[2,8,16,512]{3,2,1,0:T(8,128)S(1)}, u32[]{:S(2)}, u32[]{:S(2)}) collective-permute-start(f32[2,8,16,512]{3,2,1,0:T(8,128)S(1)} %get-tuple-element.103.t1), channel_id=1, source_target_pairs={{0,64},{64,0},{1,65},{65,1},{2,66},{66,2},{3,67},{67,3},{4,68},{68... | collective-permute-start | bytes 1572872 | tf_op jit(solution)/shard_map/ppermute | solution.py:370
  156.4 35.9 %collective-permute-start.21 = (f32[512,512]{1,0:T(8,128)S(1)}, f32[512,512]{1,0:T(8,128)}, u32[]{:S(2)}, u32[]{:S(2)}) collective-permute-start(f32[512,512]{1,0:T(8,128)S(1)} %light.1), channel_id=1, source_target_pairs={{0,64},{64,0},{1,65},{65,1},{2,66},{66,2},{3,67},{67,3},{4,68},{68... | collective-permute-start | bytes 3145736 | tf_op jit(solution)/shard_map/ppermute | solution.py:370
  157.0 7.9 %copy-start.7 = (f32[2,8,16,512]{3,2,1,0:T(8,128)S(1)}, f32[2,8,16,512]{3,2,1,0:T(8,128)}, u32[]{:S(2)}) copy-start(f32[2,8,16,512]{3,2,1,0:T(8,128)} %copy-done.6) | copy-start | bytes 1572868
  157.0 7.9 %copy-start.12 = (f32[2,8,16,512]{3,2,1,0:T(8,128)S(1)}, f32[2,8,16,512]{3,2,1,0:T(8,128)}, u32[]{:S(2)}) copy-start(f32[2,8,16,512]{3,2,1,0:T(8,128)} %copy-done.11) | copy-start | bytes 1572868
  159.4 7.6 %copy-start.29 = (f32[2,2,3,16,512]{4,3,2,1,0:T(8,128)}, f32[2,2,3,16,512]{4,3,2,1,0:T(8,128)S(1)}, u32[]{:S(2)}) copy-start(f32[2,2,3,16,512]{4,3,2,1,0:T(8,128)S(1)} %get-tuple-element.104.a) | copy-start | bytes 1179652
  159.4 14.0 %collective-permute-start.17 = (f32[2,2,3,16,512]{4,3,2,1,0:T(8,128)}, f32[2,2,3,16,512]{4,3,2,1,0:T(8,128)}, u32[]{:S(2)}, u32[]{:S(2)}) collective-permute-start(f32[2,2,3,16,512]{4,3,2,1,0:T(8,128)} %get-tuple-element.100), channel_id=1, source_target_pairs={{0,4},{1,17},{4,8},{5,21},{8,12},{9,25},{12,0},{13,29},{16,20},{17... | collective-permute-start | bytes 1179656 | tf_op jit(solution)/shard_map/ppermute | solution.py:382
  161.7 11.8 %collective-permute-start.18 = (f32[2,2,3,16,512]{4,3,2,1,0:T(8,128)}, f32[2,2,3,16,512]{4,3,2,1,0:T(8,128)}, u32[]{:S(2)}, u32[]{:S(2)}) collective-permute-start(f32[2,2,3,16,512]{4,3,2,1,0:T(8,128)} %get-tuple-element.101), channel_id=1, source_target_pairs={{0,12},{1,49},{4,0},{5,53},{8,4},{9,57},{12,8},{13,61},{16,28},{17... | collective-permute-start | bytes 1179656 | tf_op jit(solution)/shard_map/ppermute | solution.py:382
  162.4 12.8 %collective-permute-start.19 = (f32[2,2,3,16,512]{4,3,2,1,0:T(8,128)S(1)}, f32[2,2,3,16,512]{4,3,2,1,0:T(8,128)}, u32[]{:S(2)}, u32[]{:S(2)}) collective-permute-start(f32[2,2,3,16,512]{4,3,2,1,0:T(8,128)S(1)} %get-tuple-element.102), channel_id=1, source_target_pairs={{0,8},{1,33},{4,12},{5,37},{8,0},{9,41},{12,4},{13,45},{16,24},{17... | collective-permute-start | bytes 1179656 | tf_op jit(solution)/shard_map/ppermute | solution.py:382
  169.8 0.8 copy-start.18
  170.6 37.6 %collective-permute-start.22 = (f32[2,2,8,16,512]{4,3,2,1,0:T(8,128)S(1)}, f32[2,2,8,16,512]{4,3,2,1,0:T(8,128)S(1)}, u32[]{:S(2)}, u32[]{:S(2)}) collective-permute-start(f32[2,2,8,16,512]{4,3,2,1,0:T(8,128)S(1)} %over_sum.1), channel_id=1, source_target_pairs={{0,1},{1,2},{2,3},{3,4},{4,5},{5,6},{6,7},{7,8},{8,9},{9,10},{10,1... | collective-permute-start | bytes 3145736 | tf_op jit(solution)/shard_map/ppermute | solution.py:366
  175.1 1.0 copy-start.30
  178.0 16.5 %collective-permute-start.23 = (f32[2,2,3,8,512]{4,3,2,1,0:T(8,128)S(1)}, f32[2,2,3,8,512]{4,3,2,1,0:T(8,128)S(1)}, u32[]{:S(2)}, u32[]{:S(2)}) collective-permute-start(f32[2,2,3,8,512]{4,3,2,1,0:T(8,128)S(1)} %get-tuple-element.115), channel_id=1, source_target_pairs={{0,1},{1,0},{2,3},{3,2},{4,5},{5,4},{6,7},{7,6},{8,9},{9,8},{10,11... | collective-permute-start | bytes 589832 | tf_op jit(solution)/shard_map/ppermute | solution.py:370
  194.5 13.7 %copy-start.2 = (f32[2,512,1024]{2,1,0:T(8,128)S(1)}, f32[2,512,1024]{2,1,0:T(8,128)}, u32[]{:S(2)}) copy-start(f32[2,512,1024]{2,1,0:T(8,128)} %obj.1) | copy-start | bytes 12582916
  194.5 13.7 %copy-start.5 = (f32[2,8,16,512]{3,2,1,0:T(8,128)S(1)}, f32[2,8,16,512]{3,2,1,0:T(8,128)}, u32[]{:S(2)}) copy-start(f32[2,8,16,512]{3,2,1,0:T(8,128)} %copy-done.4) | copy-start | bytes 1572868
  194.5 13.7 %copy-start.8 = (f32[2,8,16,512]{3,2,1,0:T(8,128)S(1)}, f32[2,8,16,512]{3,2,1,0:T(8,128)}, u32[]{:S(2)}) copy-start(f32[2,8,16,512]{3,2,1,0:T(8,128)} %copy-done.6) | copy-start | bytes 1572868
  194.5 13.7 %copy-start.10 = (f32[2,8,16,512]{3,2,1,0:T(8,128)S(1)}, f32[2,8,16,512]{3,2,1,0:T(8,128)}, u32[]{:S(2)}) copy-start(f32[2,8,16,512]{3,2,1,0:T(8,128)} %copy-done.9) | copy-start | bytes 1572868
  194.5 13.7 %copy-start.13 = (f32[2,8,16,512]{3,2,1,0:T(8,128)S(1)}, f32[2,8,16,512]{3,2,1,0:T(8,128)}, u32[]{:S(2)}) copy-start(f32[2,8,16,512]{3,2,1,0:T(8,128)} %copy-done.11) | copy-start | bytes 1572868
  194.5 13.7 %copy-start.15 = (f32[2,8,16,512]{3,2,1,0:T(8,128)S(1)}, f32[2,8,16,512]{3,2,1,0:T(8,128)}, u32[]{:S(2)}) copy-start(f32[2,8,16,512]{3,2,1,0:T(8,128)} %copy-done.14) | copy-start | bytes 1572868
  194.5 13.7 %copy-start.17 = (f32[2,8,16,512]{3,2,1,0:T(8,128)S(1)}, f32[2,8,16,512]{3,2,1,0:T(8,128)}, u32[]{:S(2)}) copy-start(f32[2,8,16,512]{3,2,1,0:T(8,128)} %copy-done.16) | copy-start | bytes 1572868
  194.5 13.7 %copy-start.19 = (f32[2,8,16,512]{3,2,1,0:T(8,128)S(1)}, f32[2,8,16,512]{3,2,1,0:T(8,128)}, u32[]{:S(2)}) copy-start(f32[2,8,16,512]{3,2,1,0:T(8,128)} %copy-done.18) | copy-start | bytes 1572868
  195.1 20.5 %collective-permute-start.24 = (f32[2,6,8,512]{3,2,1,0:T(8,128)S(1)}, f32[2,6,8,512]{3,2,1,0:T(8,128)S(1)}, u32[]{:S(2)}, u32[]{:S(2)}) collective-permute-start(f32[2,6,8,512]{3,2,1,0:T(8,128)S(1)} %get-tuple-element.117), channel_id=1, source_target_pairs={{0,2},{2,0},{64,66},{66,64},{1,3},{3,1},{65,67},{67,65},{4,6},{6,4... | collective-permute-start | bytes 589832 | tf_op jit(solution)/shard_map/ppermute | solution.py:387
  196.6 19.0 %collective-permute-start.26 = (f32[2,6,8,512]{3,2,1,0:T(8,128)S(1)}, f32[2,6,8,512]{3,2,1,0:T(8,128)S(1)}, u32[]{:S(2)}, u32[]{:S(2)}) collective-permute-start(f32[2,6,8,512]{3,2,1,0:T(8,128)S(1)} %get-tuple-element.117), channel_id=1, source_target_pairs={{0,66},{2,64},{64,2},{66,0},{1,67},{3,65},{65,3},{67,1},{4,70},{6,... | collective-permute-start | bytes 589832 | tf_op jit(solution)/shard_map/ppermute | solution.py:387
  198.8 16.8 %collective-permute-start.25 = (f32[2,6,8,512]{3,2,1,0:T(8,128)S(1)}, f32[2,6,8,512]{3,2,1,0:T(8,128)S(1)}, u32[]{:S(2)}, u32[]{:S(2)}) collective-permute-start(f32[2,6,8,512]{3,2,1,0:T(8,128)S(1)} %get-tuple-element.116.mine), channel_id=1, source_target_pairs={{0,64},{2,66},{64,0},{66,2},{1,65},{3,67},{65,1},{67,3},{4,68},{6,... | collective-permute-start | bytes 589832 | tf_op jit(solution)/shard_map/ppermute | solution.py:387
  208.2 7.4 %copy-start.22 = (s32[12,12]{1,0:T(8,128)S(1)}, s32[12,12]{1,0:T(8,128)}, u32[]{:S(2)}) copy-start(s32[12,12]{1,0:T(8,128)} %w_ref.1) | copy-start | bytes 1732

commit v3 on v0

v3 whole, which is shorter than its diff:
```python
import functools
import math

import jax
import jax.numpy as jnp
import ml_dtypes
import numpy as np
from jax import lax
from jax.experimental import pallas as pl
from jax.experimental.pallas import tpu as pltpu
from jax.sharding import Mesh
from jax.sharding import PartitionSpec as P

f32, bf16 = jnp.float32, jnp.bfloat16
N = 512
H = 256
CHUNK = 32
PAIR = 2


def tables():
    i = np.arange(N, dtype=np.int32)
    angle = (i[:, None] * i[None, :] % N).astype(np.float32) * np.float32(2.0 * math.pi / N)
    factor = np.float32(1.0 / math.sqrt(N))
    c = (np.cos(angle) * factor).astype(ml_dtypes.bfloat16)
    s = (np.sin(angle) * factor).astype(ml_dtypes.bfloat16)
    minus = np.block([[c, -s], [s, c]])
    plus = np.block([[c, s], [-s, c]])

    def stacked(table):
        return table.reshape(2 * N, 2, 2, H).swapaxes(1, 2).reshape(2 * N, 2 * N)

    wave_rows = stacked(plus).reshape(2, 2, H, 2 * N).swapaxes(0, 1).reshape(2, N, 2 * N)
    back_rows = stacked(minus).reshape(2, 16, 2, 16, 2 * N).transpose(2, 0, 1, 3, 4).reshape(2, N, 2 * N)
    return minus, plus, wave_rows[0], wave_rows[1], back_rows[0], back_rows[1]


def shape(*dims, dtype=f32):
    return jax.ShapeDtypeStruct(dims, dtype)


def whole(*dims):
    return pl.BlockSpec(dims, lambda *_: (0,) * len(dims))


def params(mib):
    return pltpu.CompilerParams(vmem_limit_bytes=mib << 20)


SCALARS = pl.BlockSpec(memory_space=pltpu.SMEM)
LOCAL = pl.BlockSpec(memory_space=pltpu.VMEM)
FAR = pl.BlockSpec(memory_space=pltpu.HBM)


def local_call(body, name, ins, outs, scratch, mib, alias=None):
    def call(*args):
        return pl.pallas_call(
            body,
            in_specs=ins,
            out_specs=[LOCAL] * len(outs),
            out_shape=outs,
            scratch_shapes=scratch,
            compiler_params=params(mib),
            input_output_aliases=alias or {},
            name=name,
        )(*args)

    return call


def loop(count, fn, unroll=1):
    def body(i, carry):
        fn(i)
        return carry

    lax.fori_loop(0, count, body, 0, unroll=unroll)


def at(i, size, base=0):
    return pl.ds(pl.multiple_of(i * size + base, min(size, base) if base else size), size)


def exit_rows(p_ref, m, rows, o_r, o_i):
    pr = p_ref[0, m, rows, :].astype(f32)
    pi = p_ref[1, m, rows, :].astype(f32)
    return pr, pi, (pr * o_r - pi * o_i).astype(bf16), (pr * o_i + pi * o_r).astype(bf16)


def exit_half(p_ref, m, j, base, patch, x_s):
    def one(i):
        rows = at(i, CHUNK)
        _, _, xr, xi = exit_rows(p_ref, m, at(i, CHUNK, base), patch[0, rows, :], patch[1, rows, :])
        x_s[j, rows, :N] = xr
        x_s[j, rows, N:] = xi

    loop(H // CHUNK, one, 2)


def along_rows(x_s, table, out, m0):
    x = x_s[...].reshape(PAIR * H, 2 * N)
    half = jnp.dot(x, table[...], preferred_element_type=f32).astype(bf16)
    for j in range(PAIR):
        out[m0 + j, :H] = half[j * H : (j + 1) * H, :N]
        out[m0 + j, H:] = half[j * H : (j + 1) * H, N:]


def pairs(p_ref, fn):
    nm = p_ref
    loop(nm // PAIR, lambda k: fn(k * PAIR))


def top_body(sc, patch, p_ref, table, half_ref, own_half, far_half, x_s):
    base = sc[2] * H

    def lit(i):
        rows = pl.ds(pl.multiple_of(base + i * CHUNK, CHUNK), CHUNK)
        acc = jnp.zeros((CHUNK, N), f32)
        for m in range(p_ref.shape[1]):
            pr = p_ref[0, m, rows, :].astype(f32)
            pi = p_ref[1, m, rows, :].astype(f32)
            acc = acc + (pr * pr + pi * pi)
        own_half[at(i, CHUNK), :] = acc
        far_half[at(i, CHUNK), :] = acc

    loop(H // CHUNK, lit)

    def step(m0):
        for j in range(PAIR):
            exit_half(p_ref, m0 + j, j, 0, patch, x_s)
        along_rows(x_s, table, half_ref, m0)

    pairs(p_ref.shape[1], step)


def top_half(sc, patch, probe, table):
    nm = probe.shape[1]
    return local_call(
        top_body,
        "top_half",
        [SCALARS, LOCAL, LOCAL, LOCAL],
        [shape(nm, N, N, dtype=bf16), shape(H, N), shape(H, N)],
        [pltpu.VMEM((PAIR, H, 2 * N), bf16)],
        6,
    )(sc, patch, probe, table)


def wave_half(wave_ref, sum_ref, wt, top, bot, m0):
    for j in range(PAIR):
        m = m0 + j
        wave_ref[m] = jnp.dot(wt[:, :N], top[m], preferred_element_type=f32) + jnp.dot(
            wt[:, N:], bot[m], preferred_element_type=f32
        )

    def one(i):
        rows = at(i, CHUNK)
        low = at(i, CHUNK, H)
        acc = sum_ref[rows, :]
        for j in range(PAIR):
            a = wave_ref[m0 + j, rows, :]
            b = wave_ref[m0 + j, low, :]
            acc = acc + (a * a + b * b)
        sum_ref[rows, :] = acc

    loop(H // CHUNK, one, 2)


def bottom_body(place, own, rim, p_ref, table, wt, top, half_ref, patch_ref, wave_ref, sum_ref, x_s):
    @pl.when(place[0] == 0)
    def _():
        patch_ref[...] = own[...]

    @pl.when(place[0] != 0)
    def _():
        patch_ref[...] = rim[...]

    sum_ref[...] = jnp.zeros_like(sum_ref)

    def step(m0):
        for j in range(PAIR):
            exit_half(p_ref, m0 + j, j, H, patch_ref, x_s)
        along_rows(x_s, table, half_ref, m0)
        wave_half(wave_ref, sum_ref, wt, top, half_ref, m0)

    pairs(p_ref.shape[1], step)


def bottom_half(place, own, rim, probe, table, wave_rows, top):
    nm = probe.shape[1]
    return local_call(
        bottom_body,
        "bottom_half",
        [SCALARS] + [LOCAL] * 6,
        [shape(nm, N, N, dtype=bf16), shape(2, H, N), shape(nm, N, N), shape(H, N)],
        [pltpu.VMEM((PAIR, H, 2 * N), bf16)],
        8,
    )(place, own, rim, probe, table, wave_rows, top)


def low_wave_body(wt, top, bot, wave_ref, sum_ref):
    sum_ref[...] = jnp.zeros_like(sum_ref)
    pairs(top.shape[0], lambda m0: wave_half(wave_ref, sum_ref, wt, top, bot, m0))


def low_wave(wave_rows, top, bot):
    nm = top.shape[0]
    return local_call(
        low_wave_body, "low_wave", [LOCAL] * 3, [shape(nm, N, N), shape(H, N)], [], 5
    )(wave_rows, top, bot)


def set_scale(pat, base, s0, s1, scale_s):
    def one(i):
        rows = at(i, CHUNK)
        total = jnp.maximum(s0[rows, :] + s1[rows, :], 1.0)
        scale_s[rows, :] = jnp.sqrt(pat[0, at(i, CHUNK, base), :]) / jnp.sqrt(total)

    loop(H // CHUNK, one)


def fixed_half(wave_ref, table, half_ref, scale_s, x_s, m0):
    for j in range(PAIR):

        def one(i):
            rows = at(i, CHUNK)
            low = at(i, CHUNK, H)
            factor = scale_s[rows, :]
            x_s[j, rows, :N] = (wave_ref[m0 + j, rows, :] * factor).astype(bf16)
            x_s[j, rows, N:] = (wave_ref[m0 + j, low, :] * factor).astype(bf16)

        loop(H // CHUNK, one, 2)
    along_rows(x_s, table, half_ref, m0)


def fixed_top_body(pat, s0, s1, wave_ref, table, half_ref, scale_s, x_s):
    set_scale(pat, 0, s0, s1, scale_s)
    pairs(wave_ref.shape[0], lambda m0: fixed_half(wave_ref, table, half_ref, scale_s, x_s, m0))


SCALE = [pltpu.VMEM((H, N), f32), pltpu.VMEM((PAIR, H, 2 * N), bf16)]


def fixed_top(pat, s0, s1, wave, table):
    nm = wave.shape[0]
    return local_call(
        fixed_top_body, "fixed_top", [LOCAL] * 5, [shape(nm, N, N, dtype=bf16)], SCALE, 6
    )(pat, s0, s1, wave, table)[0]


def gradients(core, block, bt, top, bot, patch_top, patch_bot, p_ref, keep_ref, send_ref, gtop, gbot, back_s, m):
    back_s[...] = jnp.dot(bt[:, :N], top[m], preferred_element_type=f32) + jnp.dot(
        bt[:, N:], bot[m], preferred_element_type=f32
    )
    for patch, g_ref, base in ((patch_top, gtop, 0), (patch_bot, gbot, 8)):

        def one(i):
            g = i + base
            rows = pl.ds(pl.multiple_of(i * 32 + block * 16, 16), 16)
            full = pl.ds(pl.multiple_of(g * 32 + block * 16, 16), 16)
            o_r = patch[0, rows, :]
            o_i = patch[1, rows, :]
            pr, pi, xr, xi = exit_rows(p_ref, m, full, o_r, o_i)
            rr = back_s[at(g, 16), :] - xr.astype(f32)
            ri = back_s[pl.ds(pl.multiple_of(g * 16 + H, 16), 16), :] - xi.astype(f32)
            g_ref[0, i] += pr * rr + pi * ri
            g_ref[1, i] += pr * ri - pi * rr
            st0 = o_r * rr + o_i * ri
            st1 = o_r * ri - o_i * rr
            turned_g = (g % 4) * 4 + g // 4
            keep_ref[m, jnp.where(core == 0, g, turned_g)] = jnp.where(core == 0, st0, st1)
            send_ref[m, jnp.where(core == 0, turned_g, g)] = jnp.where(core == 0, st1, st0)

        loop(8, one, UNROLL)


UNROLL = 8
LIMIT = 4
GRADS = [shape(2, 8, 16, N)] * 2


def first_block_body(core, pat, s0, s1, wave_ref, table, bt, top, ptop, pbot, p_ref, half_ref, keep, send, gtop, gbot, scale_s, x_s, back_s):
    set_scale(pat, H, s0, s1, scale_s)
    gtop[...] = jnp.zeros_like(gtop)
    gbot[...] = jnp.zeros_like(gbot)

    def step(m0):
        fixed_half(wave_ref, table, half_ref, scale_s, x_s, m0)
        for j in range(PAIR):
            gradients(core[2], 0, bt, top, half_ref, ptop, pbot, p_ref, keep, send, gtop, gbot, back_s, m0 + j)

    pairs(wave_ref.shape[0], step)


def first_block(core, pat, s0, s1, wave, table, back_rows, top, ptop, pbot, probe):
    nm = wave.shape[0]
    return local_call(
        first_block_body,
        "first_block",
        [SCALARS] + [LOCAL] * 10,
        [shape(nm, N, N, dtype=bf16)] + [shape(nm, 16, 16, N)] * 2 + GRADS,
        SCALE + [pltpu.VMEM((N, N), f32)],
        9,
    )(core, pat, s0, s1, wave, table, back_rows, top, ptop, pbot, probe)


def second_block(core, back_rows, top, bot, ptop, pbot, probe, first, count, grads=None):
    nm = top.shape[0]
    half = [shape(2, 8, 16, N)] * 2

    def body(core, bt, top, bot, ptop, pbot, p_ref, *refs):
        if grads is None:
            keep, send, gtop, gbot, back_s = refs
            gtop[...] = jnp.zeros_like(gtop)
            gbot[...] = jnp.zeros_like(gbot)
        else:
            kin, sin, tin, bin_, keep, send, gtop, gbot, back_s = refs
        loop(
            count,
            lambda m: gradients(
                core[2], 1, bt, top, bot, ptop, pbot, p_ref, keep, send, gtop, gbot, back_s, m + first
            ),
        )

    given = [] if grads is None else grads
    return local_call(
        body,
        "second_block",
        [SCALARS] + [LOCAL] * (6 + len(given)),
        [shape(nm, 16, 16, N)] * 2 + half,
        [pltpu.VMEM((N, N), f32)],
        6,
        {7 + i: i for i in range(len(given))},
    )(core, back_rows, top, bot, ptop, pbot, probe, *given)


SCAN = ("y", "z", "x", "core")
RING = ("y", "z", "core")


def along(value, steps):
    count = lax.axis_size(SCAN)
    lo, hi = max(0, -steps), min(count, count - steps)
    return lax.ppermute(value, SCAN, [(i, i + steps) for i in range(lo, hi)])


def swapped(value, axis):
    return lax.ppermute(value, axis, [(0, 1), (1, 0)])


def turned(value, steps, first):
    flat = lambda y, z, core: (y * 4 + z) * 2 + core
    pairs = []
    for y in range(4):
        for z in range(4):
            for core in range(2):
                on_y = (core == 0) == first
                to = ((y + steps) % 4, z) if on_y else (y, (z + steps) % 4)
                pairs.append((flat(y, z, core), flat(*to, core)))
    return lax.ppermute(value, RING, pairs)


def across(value, flip_mode, flip_x):
    pairs = [(2 * m + x, 2 * (m ^ flip_mode) + (x ^ flip_x)) for m in range(2) for x in range(2)]
    return lax.ppermute(value, ("mode", "x"), pairs)


def window(obj, first, place):
    return obj.at[:, pl.ds(pl.multiple_of(first * H, H), H), pl.ds(pl.multiple_of(place[1] * H, H), N)]


def rim_body(place, obj, out, sem):
    copy = pltpu.make_async_copy(window(obj, 0, place), out, sem)
    copy.start()
    copy.wait()


def rim_rows(place, obj):
    return local_call(rim_body, "rim_rows", [SCALARS, FAR], [shape(2, H, N)], [pltpu.SemaphoreType.DMA], 60)(
        place, obj
    )[0]


def own_body(place, obj, top, bot, sems):
    copies = [
        pltpu.make_async_copy(window(obj, place[0], place), top, sems.at[0]),
        pltpu.make_async_copy(window(obj, 1, place), bot, sems.at[1]),
    ]
    for copy in copies:
        copy.start()
    for copy in copies:
        copy.wait()


def own_rows(place, obj):
    outs = [shape(2, H, N)] * 2
    return local_call(own_body, "own_rows", [SCALARS, FAR], outs, [pltpu.SemaphoreType.DMA((2,))], 60)(place, obj)


def brightest_body(own, far, out):
    def one(i, acc):
        return jnp.maximum(acc, own[at(i, 8), :] + far[at(i, 8), :])

    out[...] = lax.fori_loop(0, H // 8, one, jnp.zeros((8, N), f32))


def brightest(own, far):
    return local_call(brightest_body, "brightest", [LOCAL, LOCAL], [shape(8, N)], [], LIMIT)(own, far)[0]


def core_add_body(sc, keep, recv, own, near, back, far0, far1):
    me = sc[0]
    n2 = own.shape[1]
    for m in range(2 * n2):
        j, k = m // n2, m % n2
        for out, turn in ((own, 0), (near, 1), (back, 3)):
            a = at(lax.rem(me + turn, 4), 4)
            out[j, k] = keep[m, a] + recv[m, a]
        a = at(lax.rem(me + 2, 4), 4)
        (far0, far1)[j][k] = keep[m, a] + recv[m, a]


def core_add(sc, keep, recv):
    n2 = keep.shape[0] // 2
    outs = [shape(2, n2, 4, 16, N)] * 3 + [shape(n2, 4, 16, N)] * 2
    return local_call(core_add_body, "core_add", [SCALARS, LOCAL, LOCAL], outs, [], LIMIT)(sc, keep, recv)


def relay_body(a, b, ra, rb, oa, ob):
    oa[0] = a[0] + ra[...]
    ob[1] = b[1] + rb[...]


def relay_add(near, back, ra, rb):
    outs = [shape(*near.shape)] * 2
    return local_call(relay_body, "relay_add", [LOCAL] * 4, outs, [], LIMIT, {0: 0, 1: 1})(near, back, ra, rb)


def plane_add_body(sc, *refs):
    me = sc[1]
    for block in range(2):
        own, ra, rb = refs[3 * block : 3 * block + 3]
        for turn in range(4):
            b = lax.rem(me + turn, 4)
            refs[6 + turn][block] = own[:, :, b] + (ra[:, :, b] + rb[:, :, b])


def plane_add(sc, blocks):
    n2 = blocks[0][0].shape[1]
    outs = [shape(2, 2, n2, 16, N)] * 4
    return local_call(plane_add_body, "plane_add", [SCALARS] + [LOCAL] * 6, outs, [], LIMIT)(
        sc, *blocks[0], *blocks[1]
    )


def line_add_body(sc, a, b, c, d, keep, send):
    core = sc[2]
    for out, side in ((keep, core), (send, 1 - core)):
        rows = at(side, 8)
        for block in range(2):
            for j in range(2):
                out[block, j] = (a[block, j, :, rows] + b[block, j, :, rows]) + (
                    c[block, j, :, rows] + d[block, j, :, rows]
                )


def line_add(sc, arrays):
    dims = arrays[0].shape
    outs = [shape(*dims[:3], 8, N)] * 2
    return local_call(line_add_body, "line_add", [SCALARS] + [LOCAL] * 4, outs, [], LIMIT)(sc, *arrays)


def pixel_body(sc, keep, recv, rows, mine, other):
    core, x = sc[2], sc[3]
    scale = 1.0 / math.sqrt(64)

    def fill(part, ref):
        mine[part] = ref[x] * scale + rows[part].astype(f32)
        other[part] = ref[1 - x] * scale

    @pl.when(core == 0)
    def _():
        fill(0, keep)
        fill(1, recv)

    @pl.when(core != 0)
    def _():
        fill(0, recv)
        fill(1, keep)


def pixel_step(sc, keep, recv, rows):
    dims = rows.shape
    return local_call(pixel_body, "pixel_step", [SCALARS] + [LOCAL] * 3, [shape(*dims)] * 2, [], LIMIT)(
        sc, keep.reshape(dims), recv.reshape(dims), rows
    )


def mix_body(sc, w_ref, mine, b, c, d, out_ref):
    mode = sc[4]
    nm = mine.shape[1]
    for part in range(2):
        own = [mine[part, j] + b[part, j] for j in range(nm)]
        far = [c[part, j] + d[part, j] for j in range(nm)]
        for k in range(nm):
            row = mode * nm + k
            acc = jnp.zeros((8, N), f32)
            for j in range(nm):
                acc += (w_ref[row, mode * nm + j].astype(f32) / 16.0) * own[j]
                acc += (w_ref[row, (1 - mode) * nm + j].astype(f32) / 16.0) * far[j]
            out_ref[part, k] = acc.astype(bf16)


def mix(sc, mixing, mine, b, c, d):
    outs = [shape(*mine.shape, dtype=bf16)]
    return local_call(mix_body, "mix", [SCALARS] * 2 + [LOCAL] * 4, outs, [], LIMIT)(sc, mixing, mine, b, c, d)[0]


def object_body(place, before, near_max, far_max, obj, t0, t0f, t1, t1f, b0, b0f, b1, b1f, over, out, new, sems):
    shift, col = place[0], pl.multiple_of(place[1] * H, H)
    over_shift, over_col = before[0], pl.multiple_of(before[1] * H, H)
    largest = jnp.max(jnp.maximum(near_max[...], far_max[...]))
    copies = []
    for half in range(2):
        base = half * H

        def start(i):
            rows = at(i, CHUNK, base)
            new[:, rows, :] = obj[:, rows, :]

        loop(H // CHUNK, start, 2)

        def add(column, even, odd):
            def one(g):
                for block, values in ((0, even), (1, odd)):
                    rows = pl.ds(pl.multiple_of(g * 32 + base + block * 16, 16), 16)
                    total = values[0][:, g]
                    for v in values[1:]:
                        total = total + v[:, g]
                    new[:, rows, pl.ds(column, N)] += total / largest

            loop(8, one, 2)

        @pl.when(shift == half)
        def _():
            add(col, (t0, t0f), (t1, t1f))

        if half == 1:

            @pl.when(shift == 0)
            def _():
                add(col, (b0, b0f), (b1, b1f))

        else:

            @pl.when(over_shift == 1)
            def _():
                add(over_col, (over.at[0],), (over.at[1],))

        copy = pltpu.make_async_copy(new.at[:, pl.ds(base, H), :], out.at[:, pl.ds(base, H), :], sems.at[half])
        copy.start()
        copies.append(copy)
    for copy in copies:
        copy.wait()


def object_update(place, before, near_max, far_max, obj, pieces, over):
    return pl.pallas_call(
        object_body,
        in_specs=[SCALARS] * 2 + [LOCAL] * 12,
        out_specs=FAR,
        out_shape=shape(2, N, 4 * H),
        scratch_shapes=[pltpu.VMEM((2, N, 4 * H), f32), pltpu.SemaphoreType.DMA((2,))],
        compiler_params=params(10),
        name="object_update",
    )(place, before, near_max, far_max, obj, *pieces, over)


def over_body(b0, b0f, b1, b1f, out):
    out[0] = b0[...] + b0f[...]
    out[1] = b1[...] + b1f[...]


def over_sum(b0, b0f, b1, b1f):
    return local_call(over_body, "over_sum", [LOCAL] * 4, [shape(2, 2, 8, 16, N)], [], LIMIT)(b0, b0f, b1, b1f)[0]


def tied(*values):
    return lax.optimization_barrier(values)


def per_device(object_field, probe, patterns, row_shift, col_start, mixing):
    minus, plus, wave_top_rows, wave_bot_rows, back_rows0, back_rows1 = tables()
    y, z, x, core = (lax.axis_index(a) for a in SCAN)
    mode = lax.axis_index("mode")
    first = jnp.where(core == 0, y, z)
    second = jnp.where(core == 0, z, y)
    sc = jnp.stack([first, second, core, x, mode])
    place = jnp.concatenate([row_shift, col_start])
    before = along(place, 1)
    rows = lax.dynamic_slice_in_dim(probe, lax.axis_index(SCAN) * 8, 8, 2)
    before, place, sc, rows = tied(before, place, sc, rows)
    rim = along(rim_rows(before, object_field), -1)
    patch_top, own_bot = own_rows(place, object_field)
    half_top, own_light, light_out = top_half(sc, patch_top, probe, minus)
    rim, light_out, half_top = tied(rim, light_out, half_top)
    far_light = swapped(light_out, "mode")
    half_bot, patch_bot, wave_top, sum_top = bottom_half(
        place, own_bot, rim, probe, minus, wave_top_rows, half_top
    )
    far_top = swapped(sum_top, "mode")
    half_bot, far_light = tied(half_bot, far_light)
    wave_bot, sum_bot = low_wave(wave_bot_rows, half_top, half_bot)
    far_bot = swapped(sum_bot, "mode")
    fixed = fixed_top(patterns, sum_top, far_top, wave_top, plus)
    half_max = brightest(own_light, far_light)
    low, keep0, send0, top0, bot0 = first_block(
        sc, patterns, sum_bot, far_bot, wave_bot, plus, back_rows0, fixed, patch_top, patch_bot, probe
    )
    recv0 = swapped(send0, "core")
    bot0_far = swapped(bot0, "mode")
    top0_far = swapped(top0, "mode")
    part1 = second_block(sc, back_rows1, fixed, low, patch_top, patch_bot, probe, 0, 3)
    own0, near0, back0, far0a, far0b = core_add(sc, keep0, recv0)
    ra0, rb0 = turned(far0a, 1, True), turned(far0b, -1, True)
    *part1, near0 = tied(*part1, near0)
    keep1, send1, top1, bot1 = second_block(
        sc, back_rows1, fixed, low, patch_top, patch_bot, probe, 3, 3, part1
    )
    bot1_far = swapped(bot1, "mode")
    top1_far = swapped(top1, "mode")
    recv1 = swapped(send1, "core")
    near0, back0 = relay_add(near0, back0, ra0, rb0)
    keep1, near0, back0 = tied(keep1, near0, back0)
    own1, near1, back1, far1a, far1b = core_add(sc, keep1, recv1)
    ra1, rb1 = turned(far1a, 1, True), turned(far1b, -1, True)
    plane0 = (own0, turned(near0, 1, True), turned(back0, -1, True))
    ra1, rb1, bot0_far, *plane0 = tied(ra1, rb1, bot0_far, *plane0)
    near1, back1 = relay_add(near1, back1, ra1, rb1)
    plane1 = (own1, turned(near1, 1, True), turned(back1, -1, True))
    *plane1, bot1_far = tied(*plane1, bot1_far)
    over = along(over_sum(bot0, bot0_far, bot1, bot1_far), 1)
    line = plane_add(sc, (plane0, plane1))
    line = [line[0]] + [turned(line[r], r, False) for r in (1, 3, 2)]
    *line, top0_far = tied(*line, top0_far)
    keep, send = line_add(sc, line)
    far_max = swapped(half_max, "core")
    mine, other = pixel_step(sc, keep, swapped(send, "core"), rows)
    mine, other, over = tied(mine, other, over)
    probe_new = mix(sc, mixing, mine, across(other, 0, 1), across(mine, 1, 0), across(other, 1, 1))
    pieces = (top0, top0_far, top1, top1_far, bot0, bot0_far, bot1, bot1_far)
    object_new = object_update(place, before, half_max, far_max, object_field, pieces, over)
    return object_new, probe_new


def solution(mesh):
    split = Mesh(mesh.devices.reshape(2, 4, 4, 2, 2), ("mode", *SCAN))
    return jax.shard_map(
        per_device,
        mesh=split,
        in_specs=(P(None, SCAN, None), P(None, "mode", None, None), P(SCAN, None, None), P(SCAN), P(SCAN), P()),
        out_specs=(P(None, SCAN, None), P(None, "mode", SCAN, None)),
        check_vma=False,
    )
```

time: 560 us -> 190 us (0.34); the launches traced: 550 us -> 188 us
  blocking collectives: 157 us -> 0 us
  matrix products: 151 us -> 0 us
  other arithmetic: 67.5 us -> 0.08 us
  Pallas kernels: 0 us -> 59.6 us
  waiting for transfers between devices: 103 us -> 64 us
  starting transfers between devices: 14.4 us -> 52.6 us
  local copies, waits for them, and re-layouts: 40.7 us -> 9.83 us
  between operations: 16.1 us -> 2.35 us
    all_to_all x2 -> x0, blocking collectives: 157 us -> none  [copy_for_each(): lax.all_to_all(jnp.broadcast_to(shard[None], (peers, *shard.shape)), axis...]
    dot_general x17 -> x0, matrix products: 151 us -> none  [the longest x8 78.7 us: left_mult(): jnp.einsum('ij,...jk->...ik', first, second, preferred_element_type=jnp.f...]
    pallas_call x0 -> x20, Pallas kernels: none -> 59.6 us  [the longest x19 56.5 us: call(): pl.pallas_call(body, in_specs=ins, out_specs=[LOCAL] * len(outs), out_sha...]
    ppermute x2 -> x28, starting transfers between devices: 10.4 us -> 52.6 us  [the longest x11 21 us: turned(): return lax.ppermute(value, RING, pairs)]
    reduce_scatter x2 -> x0, waiting for transfers between devices: 34.1 us -> none  [the longest x1 34.1 us: scatter_pairs(): pieces = lax.psum_scatter(pieces, core, scatter_dimension=0, tiled=True)]
    reduce_sum x2 -> x0, other arithmetic: 33.2 us -> none  [over_copies(): return jnp.sum(everything, axis=0)]
    slice x5 -> x0, local copies, waits for them, and re-layouts: 12.3 us -> none  [the longest x1 4.82 us: per_device(): own_rows = accum[:, :tile_size, :]]
    reshape x1 -> x0, local copies, waits for them, and re-layouts: 11.3 us -> none  [scatter_pairs(): pieces = pieces.reshape(*sizes, *inside).swapaxes(0, 1).reshape(-1, *inside)]
  transfers between devices with their start and end apart: 5 -> 28, of which waited for: 3 -> 14; matrix products, arithmetic and copies ran while one was open for 11% -> 1% of each run, Pallas kernels for 0% -> 21%
where the time goes in v3:
time: 190 us; the launch traced here: 188 us
  waiting for transfers between devices  64 us (34%)
  Pallas kernels  59.6 us (31%)
  starting transfers between devices  52.6 us (28%)
  local copies, waits for them, and re-layouts  9.83 us (5%)
  between operations  2.35 us (1%)
    pallas_call x19, Pallas kernels, call(): pl.pallas_call(body, in_specs=ins, out_specs=[LOCAL] * len(outs), out_sha...  56.5 us
    ppermute x11, waiting for transfers between devices, swapped(): return lax.ppermute(value, axis, [(0, 1), (1, 0)])  52.4 us
    ppermute x11, starting transfers between devices, turned(): return lax.ppermute(value, RING, pairs)  21 us
    ppermute x11, starting transfers between devices, swapped(): return lax.ppermute(value, axis, [(0, 1), (1, 0)])  13.5 us
    ppermute x3, starting transfers between devices, along(): return lax.ppermute(value, SCAN, [(i, i + steps) for i in range(lo, hi)])  12.8 us
    unnamed x46, local copies, waits for them, and re-layouts  8.84 us
    ppermute x11, waiting for transfers between devices, turned(): return lax.ppermute(value, RING, pairs)  7.23 us
    ppermute x3, starting transfers between devices, across(): return lax.ppermute(value, ('mode', 'x'), pairs)  5.25 us
  transfers between devices with their start and end apart: 28, of which 14 were waited for; matrix products, arithmetic and copies ran while one was open for 1% of the time, Pallas kernels for 21%

profile of v3, /device:TPU:1, one launch (start us, length us, event | category | flops | bytes accessed | tf_op | source)
XLA Modules:
  0.0 188.4 jit_solution(11013840116057872293)
XLA Ops:
  2.0 4.5 %collective-permute-start = (s32[2]{0:T(128)S(1)}, s32[2]{0:T(128)S(1)}, u32[]{:S(2)}, u32[]{:S(2)}) collective-permute-start(s32[2]{0:T(128)S(1)} %pad_add_fusion.place), channel_id=1, source_target_pairs={{0,1},{1,2},{2,3},{3,4},{4,5},{5,6},{6,7},{7,8},{8,9},{9,10},{10,1... | collective-permute-start | bytes 32 | tf_op jit(solution)/shard_map/ppermute | solution.py:342
  6.5 0.9 constant_dynamic-slice_fusion.rows
  7.5 0.5 copy-done.17
  8.1 2.9 %rim_rows.1 = f32[2,256,512]{2,1,0:T(8,128)} custom-call(s32[2]{0:T(128)} %copy-done.17, f32[2,512,1024]{2,1,0:T(8,128)} %obj.5), custom_call_target="tpu_custom_call" | custom-call | tf_op jit(solution)/shard_map/rim_rows/pallas_call | solution.py:57
  11.0 1.9 %collective-permute-start.1 = (f32[2,256,512]{2,1,0:T(8,128)}, f32[2,256,512]{2,1,0:T(8,128)S(1)}, u32[]{:S(2)}, u32[]{:S(2)}) collective-permute-start(f32[2,256,512]{2,1,0:T(8,128)} %rim_rows.1), channel_id=1, source_target_pairs={{1,0},{2,1},{3,2},{4,3},{5,4},{6,5},{7,6},{8,7},{9,8},{10,9},{11,1... | collective-permute-start | bytes 3145736 | tf_op jit(solution)/shard_map/ppermute | solution.py:342
  12.9 3.7 %own_rows.1 = (f32[2,256,512]{2,1,0:T(8,128)}, f32[2,256,512]{2,1,0:T(8,128)}) custom-call(s32[2]{0:T(128)} %copy-done.15, f32[2,512,1024]{2,1,0:T(8,128)} %obj.5), custom_call_target="tpu_custom_call" | custom-call | tf_op jit(solution)/shard_map/own_rows/pallas_call | solution.py:57
  16.7 2.8 %copy-done = bf16[2,6,512,512]{3,2,1,0:T(8,128)(2,1)S(1)} copy-done((bf16[2,6,512,512]{3,2,1,0:T(8,128)(2,1)S(1)}, bf16[2,6,512,512]{3,2,1,0:T(8,128)(2,1)}, u32[]{:S(2)}) %copy-start) | copy-done | bytes 6291480
  19.4 1.2 copy-done.2
  20.7 1.6 copy-done.5
  22.3 6.2 %top_half.1 = (bf16[6,512,512]{2,1,0:T(8,128)(2,1)S(1)}, f32[256,512]{1,0:T(8,128)S(1)}, f32[256,512]{1,0:T(8,128)S(1)}) custom-call(s32[5]{0:T(128)S(1)} %stack.23.sc.core, f32[2,256,512]{2,1,0:T(8,128)S(1)} %copy-done.2, bf16[2,6,512,512]{3,2,1,0:T(8,128)(2,1)S(1)} %copy-done, bf16[1024,1024]{1,0:T(8,128)(2,1)S(1)} %copy-done.5), custom_call_target="tpu_custom_call" | custom-call | tf_op jit(solution)/shard_map/top_half/pallas_call | solution.py:57
  28.5 2.5 %collective-permute-start.2 = (f32[256,512]{1,0:T(8,128)S(1)}, f32[256,512]{1,0:T(8,128)S(1)}, u32[]{:S(2)}, u32[]{:S(2)}) collective-permute-start(f32[256,512]{1,0:T(8,128)S(1)} %get-tuple-element.94), channel_id=1, source_target_pairs={{0,64},{64,0},{1,65},{65,1},{2,66},{66,2},{3,67},{67,3},{4,68},{68... | collective-permute-start | bytes 1572872 | tf_op jit(solution)/shard_map/ppermute | solution.py:346
  31.1 9.5 %bottom_half.1 = (bf16[6,512,512]{2,1,0:T(8,128)(2,1)S(1)}, f32[2,256,512]{2,1,0:T(8,128)S(1)}, f32[6,512,512]{2,1,0:T(8,128)S(1)}, f32[256,512]{1,0:T(8,128)S(1)}) custom-call(s32[2]{0:T(128)S(1)} %copy-done.16, f32[2,256,512]{2,1,0:T(8,128)S(1)} %copy-done.13, f32[2,256,512]{2,1,0:T(8,128)S(1)} %collective-permute-done.1.rim, ...), custom_call_target="tpu_custom_call" | custom-call | tf_op jit(solution)/shard_map/bottom_half/pallas_call | solution.py:57
  40.6 0.6 collective-permute-start.5
  41.2 1.6 collective-permute-done.2.far
  42.8 4.3 %low_wave.1 = (f32[6,512,512]{2,1,0:T(8,128)S(1)}, f32[256,512]{1,0:T(8,128)S(1)}) custom-call(bf16[512,1024]{1,0:T(8,128)(2,1)S(1)} %copy-done.11, bf16[6,512,512]{2,1,0:T(8,128)(2,1)S(1)} %get-tuple-element.92.top, bf16[6,512,512]{2,1,0:T(8,128)(2,1)S(1)} %get-tuple-element.96.bot), custom_call_target="tpu_custom_call" | custom-call | tf_op jit(solution)/shard_map/low_wave/pallas_call | solution.py:57
  47.2 2.6 %copy-done.7 = f32[6,512,512]{2,1,0:T(8,128)} copy-done((f32[6,512,512]{2,1,0:T(8,128)}, f32[6,512,512]{2,1,0:T(8,128)S(1)}, u32[]{:S(2)}) %copy-start.7) | copy-done | bytes 6291480
  49.8 3.7 %collective-permute-start.4 = (f32[256,512]{1,0:T(8,128)S(1)}, f32[256,512]{1,0:T(8,128)S(1)}, u32[]{:S(2)}, u32[]{:S(2)}) collective-permute-start(f32[256,512]{1,0:T(8,128)S(1)} %get-tuple-element.97.s0), channel_id=1, source_target_pairs={{0,64},{64,0},{1,65},{65,1},{2,66},{66,2},{3,67},{67,3},{4,68},{68... | collective-permute-start | bytes 1572872 | tf_op jit(solution)/shard_map/ppermute | solution.py:346
  53.5 2.6 %collective-permute-done.5.s1 = f32[256,512]{1,0:T(8,128)S(1)} collective-permute-done((f32[256,512]{1,0:T(8,128)S(1)}, f32[256,512]{1,0:T(8,128)S(1)}, u32[]{:S(2)}, u32[]{:S(2)}) %collective-permute-start.5) | collective-permute-done | bytes 524320 | tf_op jit(solution)/shard_map/ppermute | solution.py:346
  56.2 4.9 %fixed_top.1.top = bf16[6,512,512]{2,1,0:T(8,128)(2,1)S(1)} custom-call(f32[1,512,512]{2,1,0:T(8,128)S(1)} %copy-done.9, f32[256,512]{1,0:T(8,128)S(1)} %get-tuple-element.99.s0, f32[256,512]{1,0:T(8,128)S(1)} %collective-permute-done.5.s1, f32[6,512,512]{2,1,0:T(8,128)S(1)} %get-tuple-element.100.wave_ref, bf16[1024,1024]{1,0:T(8,128)(2,1)S(1)} %copy-done.4), custom_call_target="tpu_custom_call" | custom-call | tf_op jit(solution)/shard_map/fixed_top/pallas_call | solution.py:57
  61.1 5.1 %collective-permute-done.4.s1 = f32[256,512]{1,0:T(8,128)S(1)} collective-permute-done((f32[256,512]{1,0:T(8,128)S(1)}, f32[256,512]{1,0:T(8,128)S(1)}, u32[]{:S(2)}, u32[]{:S(2)}) %collective-permute-start.4) | collective-permute-done | bytes 524320 | tf_op jit(solution)/shard_map/ppermute | solution.py:346
  66.3 11.3 %first_block.1 = (bf16[6,512,512]{2,1,0:T(8,128)(2,1)S(1)}, f32[6,16,16,512]{3,2,1,0:T(8,128)S(1)}, f32[6,16,16,512]{3,2,1,0:T(8,128)S(1)}, f32[2,8,16,512]{3,2,1,0:T(8,128)S(1)}, f32[2,8,16,512]{3,2,1,0:T(8,128)S(1)}) custom-call(s32[5]{0:T(128)S(1)} %stack.23.sc.core, f32[1,512,512]{2,1,0:T(8,128)S(1)} %copy-done.9, f32[256,512]{1,0:T(8,128)S(1)} %get-tuple-element.97.s0, ...), custom_call_target="tpu_custom_call" | custom-call | tf_op jit(solution)/shard_map/first_block/pallas_call | solution.py:57
  77.7 3.9 %second_block.2 = (f32[6,16,16,512]{3,2,1,0:T(8,128)S(1)}, f32[6,16,16,512]{3,2,1,0:T(8,128)S(1)}, f32[2,8,16,512]{3,2,1,0:T(8,128)S(1)}, f32[2,8,16,512]{3,2,1,0:T(8,128)S(1)}) custom-call(s32[5]{0:T(128)S(1)} %stack.23.sc.core, bf16[512,1024]{1,0:T(8,128)(2,1)S(1)} %copy-done.8, bf16[6,512,512]{2,1,0:T(8,128)(2,1)S(1)} %fixed_top.1.top, ...), custom_call_target="tpu_custom_call" | custom-call | tf_op jit(solution)/shard_map/second_block/pallas_call | solution.py:57
  81.6 1.7 collective-permute-done.6.recv
  83.4 0.9 core_add.2
  84.2 3.8 %second_block.3 = (f32[6,16,16,512]{3,2,1,0:T(8,128)S(1)}, f32[6,16,16,512]{3,2,1,0:T(8,128)S(1)}, f32[2,8,16,512]{3,2,1,0:T(8,128)S(1)}, f32[2,8,16,512]{3,2,1,0:T(8,128)S(1)}) custom-call(s32[5]{0:T(128)S(1)} %stack.23.sc.core, bf16[512,1024]{1,0:T(8,128)(2,1)S(1)} %copy-done.8, ...), custom_call_target="tpu_custom_call", output_to_operand_aliasing={{0}: (7, {}), {1}: (8, {}), {2}: (9, {}), {3}: (10, {})} | custom-call | tf_op jit(solution)/shard_map/second_block/pallas_call | solution.py:57
  88.1 0.2 collective-permute-start.9
  88.3 5.1 %collective-permute-start.7 = (f32[3,4,16,512]{3,2,1,0:T(8,128)S(1)}, f32[3,4,16,512]{3,2,1,0:T(8,128)S(1)}, u32[]{:S(2)}, u32[]{:S(2)}) collective-permute-start(f32[3,4,16,512]{3,2,1,0:T(8,128)S(1)} %get-tuple-element.118), channel_id=1, source_target_pairs={{0,16},{1,5},{4,20},{5,9},{8,24},{9,13},{12,28},{13,1},{16,32},{17... | collective-permute-start | bytes 1179656 | tf_op jit(solution)/shard_map/ppermute | solution.py:358
  93.3 2.2 %collective-permute-start.8 = (f32[3,4,16,512]{3,2,1,0:T(8,128)S(1)}, f32[3,4,16,512]{3,2,1,0:T(8,128)S(1)}, u32[]{:S(2)}, u32[]{:S(2)}) collective-permute-start(f32[3,4,16,512]{3,2,1,0:T(8,128)S(1)} %get-tuple-element.119), channel_id=1, source_target_pairs={{0,48},{1,13},{4,52},{5,1},{8,56},{9,5},{12,60},{13,9},{16,0},{17,... | collective-permute-start | bytes 1179656 | tf_op jit(solution)/shard_map/ppermute | solution.py:358
  95.6 5.5 %collective-permute-done.7.ra = f32[3,4,16,512]{3,2,1,0:T(8,128)S(1)} collective-permute-done((f32[3,4,16,512]{3,2,1,0:T(8,128)S(1)}, f32[3,4,16,512]{3,2,1,0:T(8,128)S(1)}, u32[]{:S(2)}, u32[]{:S(2)}) %collective-permute-start.7) | collective-permute-done | bytes 393248 | tf_op jit(solution)/shard_map/ppermute | solution.py:358
  101.0 0.1 relay_add.2
  101.2 0.9 collective-permute-start.13
  102.1 1.9 %collective-permute-start.14 = (f32[2,3,4,16,512]{4,3,2,1,0:T(8,128)S(1)}, f32[2,3,4,16,512]{4,3,2,1,0:T(8,128)S(1)}, u32[]{:S(2)}, u32[]{:S(2)}) collective-permute-start(f32[2,3,4,16,512]{4,3,2,1,0:T(8,128)S(1)} %get-tuple-element.129), channel_id=1, source_target_pairs={{0,48},{1,13},{4,52},{5,1},{8,56},{9,5},{12,60},{13,9},{16,0},{17,... | collective-permute-start | bytes 2359304 | tf_op jit(solution)/shard_map/ppermute | solution.py:358
  104.0 1.6 collective-permute-start.12
  105.6 0.9 core_add.3
  106.6 2.7 %collective-permute-start.11 = (f32[3,4,16,512]{3,2,1,0:T(8,128)S(1)}, f32[3,4,16,512]{3,2,1,0:T(8,128)S(1)}, u32[]{:S(2)}, u32[]{:S(2)}) collective-permute-start(f32[3,4,16,512]{3,2,1,0:T(8,128)S(1)} %get-tuple-element.125), channel_id=1, source_target_pairs={{0,48},{1,13},{4,52},{5,1},{8,56},{9,5},{12,60},{13,9},{16,0},{17,... | collective-permute-start | bytes 1179656 | tf_op jit(solution)/shard_map/ppermute | solution.py:358
  109.2 6.8 %collective-permute-done.12.b0f = f32[2,8,16,512]{3,2,1,0:T(8,128)S(1)} collective-permute-done((f32[2,8,16,512]{3,2,1,0:T(8,128)S(1)}, f32[2,8,16,512]{3,2,1,0:T(8,128)S(1)}, u32[]{:S(2)}, u32[]{:S(2)}) %collective-permute-start.12) | collective-permute-done | bytes 524320 | tf_op jit(solution)/shard_map/ppermute | solution.py:346
  116.1 1.8 collective-permute-done.10.ra
  117.8 0.1 relay_add.3
  118.0 1.2 collective-permute-start.15
  119.1 1.7 collective-permute-start.16
  120.9 1.6 collective-permute-start.17
  122.5 9.2 %collective-permute-done.17.b1f = f32[2,8,16,512]{3,2,1,0:T(8,128)S(1)} collective-permute-done((f32[2,8,16,512]{3,2,1,0:T(8,128)S(1)}, f32[2,8,16,512]{3,2,1,0:T(8,128)S(1)}, u32[]{:S(2)}, u32[]{:S(2)}) %collective-permute-start.17) | collective-permute-done | bytes 524320 | tf_op jit(solution)/shard_map/ppermute | solution.py:346
  131.7 0.1 over_sum.1
  131.8 6.4 %collective-permute-start.24 = (f32[2,2,8,16,512]{4,3,2,1,0:T(8,128)S(1)}, f32[2,2,8,16,512]{4,3,2,1,0:T(8,128)S(1)}, u32[]{:S(2)}, u32[]{:S(2)}) collective-permute-start(f32[2,2,8,16,512]{4,3,2,1,0:T(8,128)S(1)} %over_sum.1), channel_id=1, source_target_pairs={{0,1},{1,2},{2,3},{3,4},{4,5},{5,6},{6,7},{7,8},{8,9},{9,10},{10,1... | collective-permute-start | bytes 3145736 | tf_op jit(solution)/shard_map/ppermute | solution.py:342
  138.2 2.3 %collective-permute-start.21 = (f32[2,8,16,512]{3,2,1,0:T(8,128)S(1)}, f32[2,8,16,512]{3,2,1,0:T(8,128)S(1)}, u32[]{:S(2)}, u32[]{:S(2)}) collective-permute-start(f32[2,8,16,512]{3,2,1,0:T(8,128)S(1)} %get-tuple-element.102.t0), channel_id=1, source_target_pairs={{0,64},{64,0},{1,65},{65,1},{2,66},{66,2},{3,67},{67,3},{4,68},{68... | collective-permute-start | bytes 1572872 | tf_op jit(solution)/shard_map/ppermute | solution.py:346
  140.5 0.8 plane_add.1
  141.3 2.1 %collective-permute-start.18 = (f32[2,2,3,16,512]{4,3,2,1,0:T(8,128)S(1)}, f32[2,2,3,16,512]{4,3,2,1,0:T(8,128)S(1)}, u32[]{:S(2)}, u32[]{:S(2)}) collective-permute-start(f32[2,2,3,16,512]{4,3,2,1,0:T(8,128)S(1)} %get-tuple-element.145), channel_id=1, source_target_pairs={{0,4},{1,17},{4,8},{5,21},{8,12},{9,25},{12,0},{13,29},{16,20},{17... | collective-permute-start | bytes 1179656 | tf_op jit(solution)/shard_map/ppermute | solution.py:358
  143.4 2.1 %collective-permute-start.19 = (f32[2,2,3,16,512]{4,3,2,1,0:T(8,128)S(1)}, f32[2,2,3,16,512]{4,3,2,1,0:T(8,128)S(1)}, u32[]{:S(2)}, u32[]{:S(2)}) collective-permute-start(f32[2,2,3,16,512]{4,3,2,1,0:T(8,128)S(1)} %get-tuple-element.146), channel_id=1, source_target_pairs={{0,12},{1,49},{4,0},{5,53},{8,4},{9,57},{12,8},{13,61},{16,28},{17... | collective-permute-start | bytes 1179656 | tf_op jit(solution)/shard_map/ppermute | solution.py:358
  145.5 1.1 collective-permute-start.20
  146.6 22.2 %collective-permute-done.21.t0f = f32[2,8,16,512]{3,2,1,0:T(8,128)S(1)} collective-permute-done((f32[2,8,16,512]{3,2,1,0:T(8,128)S(1)}, f32[2,8,16,512]{3,2,1,0:T(8,128)S(1)}, u32[]{:S(2)}, u32[]{:S(2)}) %collective-permute-start.21) | collective-permute-done | bytes 524320 | tf_op jit(solution)/shard_map/ppermute | solution.py:346
  168.8 0.6 line_add.1
  169.5 1.4 collective-permute-done.23
  171.0 0.6 pixel_step.1
  171.6 2.8 %collective-permute-start.25 = (f32[2,6,8,512]{3,2,1,0:T(8,128)S(1)}, f32[2,6,8,512]{3,2,1,0:T(8,128)S(1)}, u32[]{:S(2)}, u32[]{:S(2)}) collective-permute-start(f32[2,6,8,512]{3,2,1,0:T(8,128)S(1)} %get-tuple-element.163), channel_id=1, source_target_pairs={{0,2},{2,0},{64,66},{66,64},{1,3},{3,1},{65,67},{67,65},{4,6},{6,4... | collective-permute-start | bytes 589832 | tf_op jit(solution)/shard_map/ppermute | solution.py:363
  174.3 1.2 collective-permute-start.26
  175.6 1.3 collective-permute-start.27
  176.8 0.2 brightest.1.near_max
  177.0 0.8 collective-permute-start.3
  177.8 0.8 collective-permute-done.3.far_max
  178.7 0.8 collective-permute-done.22.t1f
  179.5 3.0 %object_update.1 = f32[2,512,1024]{2,1,0:T(8,128)} custom-call(s32[2]{0:T(128)S(1)} %copy-done.16, s32[2]{0:T(128)S(1)} %copy-done.18, f32[8,512]{1,0:T(8,128)S(1)} %brightest.1.near_max, f32[8,512]{1,0:T(8,128)S(1)} %collective-permute-done.3.far_max, f32[2,512,1024]{2,1,0:T(8,128)S(1)} %copy-done.1, f32[2,8,16,512]{3,2,1,0:T(8,128)S(1)} %get-tuple-element.102.t0, ...), custom_call_target="tpu_custom_call" | custom-call | tf_op jit(solution)/shard_map/object_update/pallas_call | solution.py:566
  182.5 2.2 %collective-permute-done.25.b = f32[2,6,8,512]{3,2,1,0:T(8,128)S(1)} collective-permute-done((f32[2,6,8,512]{3,2,1,0:T(8,128)S(1)}, f32[2,6,8,512]{3,2,1,0:T(8,128)S(1)}, u32[]{:S(2)}, u32[]{:S(2)}) %collective-permute-start.25) | collective-permute-done | bytes 196640 | tf_op jit(solution)/shard_map/ppermute | solution.py:363
  184.7 2.2 %collective-permute-done.26.c = f32[2,6,8,512]{3,2,1,0:T(8,128)S(1)} collective-permute-done((f32[2,6,8,512]{3,2,1,0:T(8,128)S(1)}, f32[2,6,8,512]{3,2,1,0:T(8,128)S(1)}, u32[]{:S(2)}, u32[]{:S(2)}) %collective-permute-start.26) | collective-permute-done | bytes 196640 | tf_op jit(solution)/shard_map/ppermute | solution.py:363
  186.9 1.6 mix.1
  (63 shorter events, 0.5 us)
Async XLA Ops:
  2.0 10.9 %copy-start.15 = (s32[2]{0:T(128)}, s32[2]{0:T(128)S(1)}, u32[]{:S(2)}) copy-start(s32[2]{0:T(128)S(1)} %pad_add_fusion.place) | copy-start | bytes 28
  2.0 5.5 %collective-permute-start = (s32[2]{0:T(128)S(1)}, s32[2]{0:T(128)S(1)}, u32[]{:S(2)}, u32[]{:S(2)}) collective-permute-start(s32[2]{0:T(128)S(1)} %pad_add_fusion.place), channel_id=1, source_target_pairs={{0,1},{1,2},{2,3},{3,4},{4,5},{5,6},{6,7},{7,8},{8,9},{9,10},{10,1... | collective-permute-start | bytes 32 | tf_op jit(solution)/shard_map/ppermute | solution.py:342
  7.5 0.5 copy-start.17
  11.0 17.6 %collective-permute-start.1 = (f32[2,256,512]{2,1,0:T(8,128)}, f32[2,256,512]{2,1,0:T(8,128)S(1)}, u32[]{:S(2)}, u32[]{:S(2)}) collective-permute-start(f32[2,256,512]{2,1,0:T(8,128)} %rim_rows.1), channel_id=1, source_target_pairs={{1,0},{2,1},{3,2},{4,3},{5,4},{6,5},{7,6},{8,7},{9,8},{10,9},{11,1... | collective-permute-start | bytes 3145736 | tf_op jit(solution)/shard_map/ppermute | solution.py:342
  12.9 18.2 %slice-start = ((s8[6291456]{0:T(1024)(128)(4,1)}), s8[2097152]{0:T(1024)(128)(4,1)S(1)}, s32[]{:S(2)}) async-start(s8[6291456]{0:T(1024)(128)(4,1)} %bitcast.7), calls=%async_computation | async-start | bytes 4194304
  16.7 2.8 %copy-start = (bf16[2,6,512,512]{3,2,1,0:T(8,128)(2,1)S(1)}, bf16[2,6,512,512]{3,2,1,0:T(8,128)(2,1)}, u32[]{:S(2)}) copy-start(bf16[2,6,512,512]{3,2,1,0:T(8,128)(2,1)} %p_ref.9) | copy-start | bytes 18874372
  19.4 1.2 copy-start.2
  20.7 1.6 copy-start.5
  22.3 8.8 %slice-start.1 = ((s8[6291456]{0:T(1024)(128)(4,1)}), s8[4194304]{0:T(1024)(128)(4,1)S(1)}, s32[]{:S(2)}) async-start(s8[6291456]{0:T(1024)(128)(4,1)} %bitcast.7), calls=%async_computation.1 | async-start | bytes 8388608
  22.3 8.8 %copy-start.6 = (bf16[1024,1024]{1,0:T(8,128)(2,1)S(1)}, bf16[1024,1024]{1,0:T(8,128)(2,1)}, u32[]{:S(2)}) copy-start(bf16[1024,1024]{1,0:T(8,128)(2,1)} %constant.43.clone.table) | copy-start | bytes 6291460
  22.3 8.8 %copy-start.12 = (bf16[512,1024]{1,0:T(8,128)(2,1)S(1)}, bf16[512,1024]{1,0:T(8,128)(2,1)}, u32[]{:S(2)}) copy-start(bf16[512,1024]{1,0:T(8,128)(2,1)} %constant.44.clone.wt) | copy-start | bytes 3145732
  22.3 8.8 %copy-start.13 = (f32[2,256,512]{2,1,0:T(8,128)S(1)}, f32[2,256,512]{2,1,0:T(8,128)}, u32[]{:S(2)}) copy-start(f32[2,256,512]{2,1,0:T(8,128)} %get-tuple-element.88.own) | copy-start | bytes 3145732
  22.3 8.8 %copy-start.16 = (s32[2]{0:T(128)S(1)}, s32[2]{0:T(128)}, u32[]{:S(2)}) copy-start(s32[2]{0:T(128)} %copy-done.15) | copy-start | bytes 28
  28.5 14.3 %collective-permute-start.2 = (f32[256,512]{1,0:T(8,128)S(1)}, f32[256,512]{1,0:T(8,128)S(1)}, u32[]{:S(2)}, u32[]{:S(2)}) collective-permute-start(f32[256,512]{1,0:T(8,128)S(1)} %get-tuple-element.94), channel_id=1, source_target_pairs={{0,64},{64,0},{1,65},{65,1},{2,66},{66,2},{3,67},{67,3},{4,68},{68... | collective-permute-start | bytes 1572872 | tf_op jit(solution)/shard_map/ppermute | solution.py:346
  31.1 11.7 %copy-start.11 = (bf16[512,1024]{1,0:T(8,128)(2,1)S(1)}, bf16[512,1024]{1,0:T(8,128)(2,1)}, u32[]{:S(2)}) copy-start(bf16[512,1024]{1,0:T(8,128)(2,1)} %constant.45.clone.wt) | copy-start | bytes 3145732
  40.6 15.5 %collective-permute-start.5 = (f32[256,512]{1,0:T(8,128)S(1)}, f32[256,512]{1,0:T(8,128)S(1)}, u32[]{:S(2)}, u32[]{:S(2)}) collective-permute-start(f32[256,512]{1,0:T(8,128)S(1)} %get-tuple-element.99.s0), channel_id=1, source_target_pairs={{0,64},{64,0},{1,65},{65,1},{2,66},{66,2},{3,67},{67,3},{4,68},{68... | collective-permute-start | bytes 1572872 | tf_op jit(solution)/shard_map/ppermute | solution.py:346
  42.8 13.3 %copy-start.4 = (bf16[1024,1024]{1,0:T(8,128)(2,1)S(1)}, bf16[1024,1024]{1,0:T(8,128)(2,1)}, u32[]{:S(2)}) copy-start(bf16[1024,1024]{1,0:T(8,128)(2,1)} %constant.46.clone.table) | copy-start | bytes 6291460
  42.8 13.3 %copy-start.9 = (f32[1,512,512]{2,1,0:T(8,128)S(1)}, f32[1,512,512]{2,1,0:T(8,128)}, u32[]{:S(2)}) copy-start(f32[1,512,512]{2,1,0:T(8,128)} %pat.3) | copy-start | bytes 3145732
  47.2 2.6 %copy-start.7 = (f32[6,512,512]{2,1,0:T(8,128)}, f32[6,512,512]{2,1,0:T(8,128)S(1)}, u32[]{:S(2)}) copy-start(f32[6,512,512]{2,1,0:T(8,128)S(1)} %get-tuple-element.98.wave_ref) | copy-start | bytes 18874372
  49.8 16.4 %collective-permute-start.4 = (f32[256,512]{1,0:T(8,128)S(1)}, f32[256,512]{1,0:T(8,128)S(1)}, u32[]{:S(2)}, u32[]{:S(2)}) collective-permute-start(f32[256,512]{1,0:T(8,128)S(1)} %get-tuple-element.97.s0), channel_id=1, source_target_pairs={{0,64},{64,0},{1,65},{65,1},{2,66},{66,2},{3,67},{67,3},{4,68},{68... | collective-permute-start | bytes 1572872 | tf_op jit(solution)/shard_map/ppermute | solution.py:346
  56.1 10.1 %slice-start.2 = ((s8[6291456]{0:T(1024)(128)(4,1)}), s8[4194304]{0:T(1024)(128)(4,1)S(1)}, s32[]{:S(2)}) async-start(s8[6291456]{0:T(1024)(128)(4,1)} %bitcast.9), calls=%async_computation.2 | async-start | bytes 8388608
  56.1 10.1 %copy-start.3 = (f32[2,256,512]{2,1,0:T(8,128)S(1)}, f32[2,256,512]{2,1,0:T(8,128)}, u32[]{:S(2)}) copy-start(f32[2,256,512]{2,1,0:T(8,128)} %get-tuple-element.86.patch.ptop) | copy-start | bytes 3145732
  56.1 10.1 %slice-start.3 = ((s8[6291456]{0:T(1024)(128)(4,1)}), s8[2097152]{0:T(1024)(128)(4,1)S(1)}, s32[]{:S(2)}) async-start(s8[6291456]{0:T(1024)(128)(4,1)} %bitcast.9), calls=%async_computation.3 | async-start | bytes 4194304
  56.1 10.1 %copy-start.10 = (bf16[512,1024]{1,0:T(8,128)(2,1)S(1)}, bf16[512,1024]{1,0:T(8,128)(2,1)}, u32[]{:S(2)}) copy-start(bf16[512,1024]{1,0:T(8,128)(2,1)} %constant.47.clone.bt) | copy-start | bytes 3145732
  66.3 11.5 %copy-start.8 = (bf16[512,1024]{1,0:T(8,128)(2,1)S(1)}, bf16[512,1024]{1,0:T(8,128)(2,1)}, u32[]{:S(2)}) copy-start(bf16[512,1024]{1,0:T(8,128)(2,1)} %constant.48.clone.bt) | copy-start | bytes 3145732
  77.6 5.7 %collective-permute-start.6 = (f32[6,16,16,512]{3,2,1,0:T(8,128)S(1)}, f32[6,16,16,512]{3,2,1,0:T(8,128)S(1)}, u32[]{:S(2)}, u32[]{:S(2)}) collective-permute-start(f32[6,16,16,512]{3,2,1,0:T(8,128)S(1)} %get-tuple-element.109), channel_id=1, source_target_pairs={{0,1},{1,0},{2,3},{3,2},{4,5},{5,4},{6,7},{7,6},{8,9},{9,8},{10,11... | collective-permute-start | bytes 9437192 | tf_op jit(solution)/shard_map/ppermute | solution.py:346
  88.1 17.6 %collective-permute-start.9 = (f32[6,16,16,512]{3,2,1,0:T(8,128)S(1)}, f32[6,16,16,512]{3,2,1,0:T(8,128)S(1)}, u32[]{:S(2)}, u32[]{:S(2)}) collective-permute-start(f32[6,16,16,512]{3,2,1,0:T(8,128)S(1)} %get-tuple-element.123), channel_id=1, source_target_pairs={{0,1},{1,0},{2,3},{3,2},{4,5},{5,4},{6,7},{7,6},{8,9},{9,8},{10,11... | collective-permute-start | bytes 9437192 | tf_op jit(solution)/shard_map/ppermute | solution.py:346
  88.3 12.8 %collective-permute-start.7 = (f32[3,4,16,512]{3,2,1,0:T(8,128)S(1)}, f32[3,4,16,512]{3,2,1,0:T(8,128)S(1)}, u32[]{:S(2)}, u32[]{:S(2)}) collective-permute-start(f32[3,4,16,512]{3,2,1,0:T(8,128)S(1)} %get-tuple-element.118), channel_id=1, source_target_pairs={{0,16},{1,5},{4,20},{5,9},{8,24},{9,13},{12,28},{13,1},{16,32},{17... | collective-permute-start | bytes 1179656 | tf_op jit(solution)/shard_map/ppermute | solution.py:358
  93.3 7.7 %collective-permute-start.8 = (f32[3,4,16,512]{3,2,1,0:T(8,128)S(1)}, f32[3,4,16,512]{3,2,1,0:T(8,128)S(1)}, u32[]{:S(2)}, u32[]{:S(2)}) collective-permute-start(f32[3,4,16,512]{3,2,1,0:T(8,128)S(1)} %get-tuple-element.119), channel_id=1, source_target_pairs={{0,48},{1,13},{4,52},{5,1},{8,56},{9,5},{12,60},{13,9},{16,0},{17,... | collective-permute-start | bytes 1179656 | tf_op jit(solution)/shard_map/ppermute | solution.py:358
  101.2 14.9 %collective-permute-start.13 = (f32[2,3,4,16,512]{4,3,2,1,0:T(8,128)S(1)}, f32[2,3,4,16,512]{4,3,2,1,0:T(8,128)S(1)}, u32[]{:S(2)}, u32[]{:S(2)}) collective-permute-start(f32[2,3,4,16,512]{4,3,2,1,0:T(8,128)S(1)} %get-tuple-element.128), channel_id=1, source_target_pairs={{0,16},{1,5},{4,20},{5,9},{8,24},{9,13},{12,28},{13,1},{16,32},{17... | collective-permute-start | bytes 2359304 | tf_op jit(solution)/shard_map/ppermute | solution.py:358
  102.1 13.9 %collective-permute-start.14 = (f32[2,3,4,16,512]{4,3,2,1,0:T(8,128)S(1)}, f32[2,3,4,16,512]{4,3,2,1,0:T(8,128)S(1)}, u32[]{:S(2)}, u32[]{:S(2)}) collective-permute-start(f32[2,3,4,16,512]{4,3,2,1,0:T(8,128)S(1)} %get-tuple-element.129), channel_id=1, source_target_pairs={{0,48},{1,13},{4,52},{5,1},{8,56},{9,5},{12,60},{13,9},{16,0},{17,... | collective-permute-start | bytes 2359304 | tf_op jit(solution)/shard_map/ppermute | solution.py:358
  104.0 12.0 %collective-permute-start.12 = (f32[2,8,16,512]{3,2,1,0:T(8,128)S(1)}, f32[2,8,16,512]{3,2,1,0:T(8,128)S(1)}, u32[]{:S(2)}, u32[]{:S(2)}) collective-permute-start(f32[2,8,16,512]{3,2,1,0:T(8,128)S(1)} %get-tuple-element.126.b0), channel_id=1, source_target_pairs={{0,64},{64,0},{1,65},{65,1},{2,66},{66,2},{3,67},{67,3},{4,68},{68... | collective-permute-start | bytes 1572872 | tf_op jit(solution)/shard_map/ppermute | solution.py:346
  106.5 11.3 %collective-permute-start.10 = (f32[3,4,16,512]{3,2,1,0:T(8,128)S(1)}, f32[3,4,16,512]{3,2,1,0:T(8,128)S(1)}, u32[]{:S(2)}, u32[]{:S(2)}) collective-permute-start(f32[3,4,16,512]{3,2,1,0:T(8,128)S(1)} %get-tuple-element.124), channel_id=1, source_target_pairs={{0,16},{1,5},{4,20},{5,9},{8,24},{9,13},{12,28},{13,1},{16,32},{17... | collective-permute-start | bytes 1179656 | tf_op jit(solution)/shard_map/ppermute | solution.py:358
  106.6 11.2 %collective-permute-start.11 = (f32[3,4,16,512]{3,2,1,0:T(8,128)S(1)}, f32[3,4,16,512]{3,2,1,0:T(8,128)S(1)}, u32[]{:S(2)}, u32[]{:S(2)}) collective-permute-start(f32[3,4,16,512]{3,2,1,0:T(8,128)S(1)} %get-tuple-element.125), channel_id=1, source_target_pairs={{0,48},{1,13},{4,52},{5,1},{8,56},{9,5},{12,60},{13,9},{16,0},{17,... | collective-permute-start | bytes 1179656 | tf_op jit(solution)/shard_map/ppermute | solution.py:358
  118.0 13.7 %collective-permute-start.15 = (f32[2,3,4,16,512]{4,3,2,1,0:T(8,128)S(1)}, f32[2,3,4,16,512]{4,3,2,1,0:T(8,128)S(1)}, u32[]{:S(2)}, u32[]{:S(2)}) collective-permute-start(f32[2,3,4,16,512]{4,3,2,1,0:T(8,128)S(1)} %get-tuple-element.138), channel_id=1, source_target_pairs={{0,16},{1,5},{4,20},{5,9},{8,24},{9,13},{12,28},{13,1},{16,32},{17... | collective-permute-start | bytes 2359304 | tf_op jit(solution)/shard_map/ppermute | solution.py:358
  119.1 12.5 %collective-permute-start.16 = (f32[2,3,4,16,512]{4,3,2,1,0:T(8,128)S(1)}, f32[2,3,4,16,512]{4,3,2,1,0:T(8,128)S(1)}, u32[]{:S(2)}, u32[]{:S(2)}) collective-permute-start(f32[2,3,4,16,512]{4,3,2,1,0:T(8,128)S(1)} %get-tuple-element.139), channel_id=1, source_target_pairs={{0,48},{1,13},{4,52},{5,1},{8,56},{9,5},{12,60},{13,9},{16,0},{17,... | collective-permute-start | bytes 2359304 | tf_op jit(solution)/shard_map/ppermute | solution.py:358
  120.9 10.8 %collective-permute-start.17 = (f32[2,8,16,512]{3,2,1,0:T(8,128)S(1)}, f32[2,8,16,512]{3,2,1,0:T(8,128)S(1)}, u32[]{:S(2)}, u32[]{:S(2)}) collective-permute-start(f32[2,8,16,512]{3,2,1,0:T(8,128)S(1)} %get-tuple-element.140.b1), channel_id=1, source_target_pairs={{0,64},{64,0},{1,65},{65,1},{2,66},{66,2},{3,67},{67,3},{4,68},{68... | collective-permute-start | bytes 1572872 | tf_op jit(solution)/shard_map/ppermute | solution.py:346
  131.8 39.8 %collective-permute-start.24 = (f32[2,2,8,16,512]{4,3,2,1,0:T(8,128)S(1)}, f32[2,2,8,16,512]{4,3,2,1,0:T(8,128)S(1)}, u32[]{:S(2)}, u32[]{:S(2)}) collective-permute-start(f32[2,2,8,16,512]{4,3,2,1,0:T(8,128)S(1)} %over_sum.1), channel_id=1, source_target_pairs={{0,1},{1,2},{2,3},{3,4},{4,5},{5,6},{6,7},{7,8},{8,9},{9,10},{10,1... | collective-permute-start | bytes 3145736 | tf_op jit(solution)/shard_map/ppermute | solution.py:342
  138.2 41.3 %copy-start.1 = (f32[2,512,1024]{2,1,0:T(8,128)S(1)}, f32[2,512,1024]{2,1,0:T(8,128)}, u32[]{:S(2)}) copy-start(f32[2,512,1024]{2,1,0:T(8,128)} %obj.5) | copy-start | bytes 12582916
  138.2 41.3 %copy-start.18 = (s32[2]{0:T(128)S(1)}, s32[2]{0:T(128)}, u32[]{:S(2)}) copy-start(s32[2]{0:T(128)} %copy-done.17) | copy-start | bytes 28
  138.2 30.6 %collective-permute-start.21 = (f32[2,8,16,512]{3,2,1,0:T(8,128)S(1)}, f32[2,8,16,512]{3,2,1,0:T(8,128)S(1)}, u32[]{:S(2)}, u32[]{:S(2)}) collective-permute-start(f32[2,8,16,512]{3,2,1,0:T(8,128)S(1)} %get-tuple-element.102.t0), channel_id=1, source_target_pairs={{0,64},{64,0},{1,65},{65,1},{2,66},{66,2},{3,67},{67,3},{4,68},{68... | collective-permute-start | bytes 1572872 | tf_op jit(solution)/shard_map/ppermute | solution.py:346
  141.3 27.5 %collective-permute-start.18 = (f32[2,2,3,16,512]{4,3,2,1,0:T(8,128)S(1)}, f32[2,2,3,16,512]{4,3,2,1,0:T(8,128)S(1)}, u32[]{:S(2)}, u32[]{:S(2)}) collective-permute-start(f32[2,2,3,16,512]{4,3,2,1,0:T(8,128)S(1)} %get-tuple-element.145), channel_id=1, source_target_pairs={{0,4},{1,17},{4,8},{5,21},{8,12},{9,25},{12,0},{13,29},{16,20},{17... | collective-permute-start | bytes 1179656 | tf_op jit(solution)/shard_map/ppermute | solution.py:358
  143.4 25.4 %collective-permute-start.19 = (f32[2,2,3,16,512]{4,3,2,1,0:T(8,128)S(1)}, f32[2,2,3,16,512]{4,3,2,1,0:T(8,128)S(1)}, u32[]{:S(2)}, u32[]{:S(2)}) collective-permute-start(f32[2,2,3,16,512]{4,3,2,1,0:T(8,128)S(1)} %get-tuple-element.146), channel_id=1, source_target_pairs={{0,12},{1,49},{4,0},{5,53},{8,4},{9,57},{12,8},{13,61},{16,28},{17... | collective-permute-start | bytes 1179656 | tf_op jit(solution)/shard_map/ppermute | solution.py:358
  145.5 23.4 %collective-permute-start.20 = (f32[2,2,3,16,512]{4,3,2,1,0:T(8,128)S(1)}, f32[2,2,3,16,512]{4,3,2,1,0:T(8,128)S(1)}, u32[]{:S(2)}, u32[]{:S(2)}) collective-permute-start(f32[2,2,3,16,512]{4,3,2,1,0:T(8,128)S(1)} %get-tuple-element.147), channel_id=1, source_target_pairs={{0,8},{1,33},{4,12},{5,37},{8,0},{9,41},{12,4},{13,45},{16,24},{17... | collective-permute-start | bytes 1179656 | tf_op jit(solution)/shard_map/ppermute | solution.py:358
  168.8 10.7 %collective-permute-start.22 = (f32[2,8,16,512]{3,2,1,0:T(8,128)S(1)}, f32[2,8,16,512]{3,2,1,0:T(8,128)S(1)}, u32[]{:S(2)}, u32[]{:S(2)}) collective-permute-start(f32[2,8,16,512]{3,2,1,0:T(8,128)S(1)} %get-tuple-element.149.t1), channel_id=1, source_target_pairs={{0,64},{64,0},{1,65},{65,1},{2,66},{66,2},{3,67},{67,3},{4,68},{68... | collective-permute-start | bytes 1572872 | tf_op jit(solution)/shard_map/ppermute | solution.py:346
  169.4 1.5 collective-permute-start.23
  171.6 13.1 %collective-permute-start.25 = (f32[2,6,8,512]{3,2,1,0:T(8,128)S(1)}, f32[2,6,8,512]{3,2,1,0:T(8,128)S(1)}, u32[]{:S(2)}, u32[]{:S(2)}) collective-permute-start(f32[2,6,8,512]{3,2,1,0:T(8,128)S(1)} %get-tuple-element.163), channel_id=1, source_target_pairs={{0,2},{2,0},{64,66},{66,64},{1,3},{3,1},{65,67},{67,65},{4,6},{6,4... | collective-permute-start | bytes 589832 | tf_op jit(solution)/shard_map/ppermute | solution.py:363
  174.3 12.5 %collective-permute-start.26 = (f32[2,6,8,512]{3,2,1,0:T(8,128)S(1)}, f32[2,6,8,512]{3,2,1,0:T(8,128)S(1)}, u32[]{:S(2)}, u32[]{:S(2)}) collective-permute-start(f32[2,6,8,512]{3,2,1,0:T(8,128)S(1)} %get-tuple-element.162.mine), channel_id=1, source_target_pairs={{0,64},{2,66},{64,0},{66,2},{1,65},{3,67},{65,1},{67,3},{4,68},{6,... | collective-permute-start | bytes 589832 | tf_op jit(solution)/shard_map/ppermute | solution.py:363
  175.6 11.3 %collective-permute-start.27 = (f32[2,6,8,512]{3,2,1,0:T(8,128)S(1)}, f32[2,6,8,512]{3,2,1,0:T(8,128)S(1)}, u32[]{:S(2)}, u32[]{:S(2)}) collective-permute-start(f32[2,6,8,512]{3,2,1,0:T(8,128)S(1)} %get-tuple-element.163), channel_id=1, source_target_pairs={{0,66},{2,64},{64,2},{66,0},{1,67},{3,65},{65,3},{67,1},{4,70},{6,... | collective-permute-start | bytes 589832 | tf_op jit(solution)/shard_map/ppermute | solution.py:363
  177.0 9.8 %copy-start.14 = (s32[12,12]{1,0:T(8,128)S(1)}, s32[12,12]{1,0:T(8,128)}, u32[]{:S(2)}) copy-start(s32[12,12]{1,0:T(8,128)} %w_ref.1) | copy-start | bytes 1732
  177.0 1.6 collective-permute-start.3

commit v4 on v3

--- a/solution.py
+++ b/solution.py
@@ -52,7 +52,7 @@
 FAR = pl.BlockSpec(memory_space=pltpu.HBM)
 
 
-def local_call(body, name, ins, outs, scratch, mib, alias=None):
+def local_call(body, name, ins, outs, scratch, mib, alias=None, cost=None):
     def call(*args):
         return pl.pallas_call(
             body,
@@ -63,6 +63,7 @@
             compiler_params=params(mib),
             input_output_aliases=alias or {},
             name=name,
+            cost_estimate=cost,
         )(*args)
 
     return call
@@ -78,6 +79,11 @@
 
 def at(i, size, base=0):
     return pl.ds(pl.multiple_of(i * size + base, min(size, base) if base else size), size)
+
+
+def here():
+    y, z, x, core, mode = (lax.axis_index(a) for a in ("y", "z", "x", "core", "mode"))
+    return jnp.where(core == 0, y, z), jnp.where(core == 0, z, y), core, x, mode
 
 
 def exit_rows(p_ref, m, rows, o_r, o_i):
@@ -109,8 +115,38 @@
     loop(nm // PAIR, lambda k: fn(k * PAIR))
 
 
-def top_body(sc, patch, p_ref, table, half_ref, own_half, far_half, x_s):
-    base = sc[2] * H
+def window(place):
+    return pl.ds(pl.multiple_of(place[1] * H, H), N)
+
+
+def own_body(place, obj, top_ref, bot_ref, first_ref):
+    columns = window(place)
+    top = place[0] * H
+
+    def take(i):
+        rows = at(i, CHUNK)
+        top_ref[:, rows, :] = obj[:, pl.ds(pl.multiple_of(top + i * CHUNK, CHUNK), CHUNK), columns]
+        bot_ref[:, rows, :] = obj[:, at(i, CHUNK, H), columns]
+        first_ref[:, rows, :] = obj[:, rows, :]
+
+    loop(H // CHUNK, take, 2)
+
+
+def own_rows(place, obj):
+    return local_call(own_body, "own_rows", [SCALARS, LOCAL], [shape(2, H, N)] * 2 + [shape(2, H, 2 * N)], [], LIMIT)(
+        place, obj
+    )
+
+
+def top_body(patch_ref, p_ref, table, half_ref, own_half, far_half, rows_ref, x_s):
+    def step(m0):
+        for j in range(PAIR):
+            exit_half(p_ref, m0 + j, j, 0, patch_ref, x_s)
+        along_rows(x_s, table, half_ref, m0)
+
+    pairs(p_ref.shape[1], step)
+    core = lax.axis_index("core")
+    base = core * H
 
     def lit(i):
         rows = pl.ds(pl.multiple_of(base + i * CHUNK, CHUNK), CHUNK)
@@ -123,25 +159,23 @@
         far_half[at(i, CHUNK), :] = acc
 
     loop(H // CHUNK, lit)
-
-    def step(m0):
-        for j in range(PAIR):
-            exit_half(p_ref, m0 + j, j, 0, patch, x_s)
-        along_rows(x_s, table, half_ref, m0)
-
-    pairs(p_ref.shape[1], step)
-
-
-def top_half(sc, patch, probe, table):
+    chip = (lax.axis_index("y") * 4 + lax.axis_index("z")) * 2 + lax.axis_index("x")
+    for part in range(2):
+        for m in range(p_ref.shape[1]):
+            both = p_ref[part, m, at(chip, 16), :].astype(f32)
+            rows_ref[part, m] = jnp.where(core == 0, both[:8], both[8:])
+
+
+def top_half(patch, probe, table):
     nm = probe.shape[1]
     return local_call(
         top_body,
         "top_half",
-        [SCALARS, LOCAL, LOCAL, LOCAL],
-        [shape(nm, N, N, dtype=bf16), shape(H, N), shape(H, N)],
+        [LOCAL, LOCAL, LOCAL],
+        [shape(nm, N, N, dtype=bf16), shape(H, N), shape(H, N), shape(2, nm, 8, N)],
         [pltpu.VMEM((PAIR, H, 2 * N), bf16)],
         6,
-    )(sc, patch, probe, table)
+    )(patch, probe, table)
 
 
 def wave_half(wave_ref, sum_ref, wt, top, bot, m0):
@@ -274,10 +308,11 @@
 
 UNROLL = 8
 LIMIT = 4
+STAGE = pl.CostEstimate(flops=int(5e9), transcendentals=0, bytes_accessed=int(15e6))
 GRADS = [shape(2, 8, 16, N)] * 2
 
 
-def first_block_body(core, pat, s0, s1, wave_ref, table, bt, top, ptop, pbot, p_ref, half_ref, keep, send, gtop, gbot, scale_s, x_s, back_s):
+def first_block_body(pat, s0, s1, wave_ref, table, bt, top, ptop, pbot, p_ref, half_ref, keep, send, gtop, gbot, scale_s, x_s, back_s):
     set_scale(pat, H, s0, s1, scale_s)
     gtop[...] = jnp.zeros_like(gtop)
     gbot[...] = jnp.zeros_like(gbot)
@@ -285,28 +320,28 @@
     def step(m0):
         fixed_half(wave_ref, table, half_ref, scale_s, x_s, m0)
         for j in range(PAIR):
-            gradients(core[2], 0, bt, top, half_ref, ptop, pbot, p_ref, keep, send, gtop, gbot, back_s, m0 + j)
+            gradients(lax.axis_index("core"), 0, bt, top, half_ref, ptop, pbot, p_ref, keep, send, gtop, gbot, back_s, m0 + j)
 
     pairs(wave_ref.shape[0], step)
 
 
-def first_block(core, pat, s0, s1, wave, table, back_rows, top, ptop, pbot, probe):
+def first_block(pat, s0, s1, wave, table, back_rows, top, ptop, pbot, probe):
     nm = wave.shape[0]
     return local_call(
         first_block_body,
         "first_block",
-        [SCALARS] + [LOCAL] * 10,
+        [LOCAL] * 10,
         [shape(nm, N, N, dtype=bf16)] + [shape(nm, 16, 16, N)] * 2 + GRADS,
         SCALE + [pltpu.VMEM((N, N), f32)],
         9,
-    )(core, pat, s0, s1, wave, table, back_rows, top, ptop, pbot, probe)
-
-
-def second_block(core, back_rows, top, bot, ptop, pbot, probe, first, count, grads=None):
+    )(pat, s0, s1, wave, table, back_rows, top, ptop, pbot, probe)
+
+
+def second_block(back_rows, top, bot, ptop, pbot, probe, first, count, grads=None):
     nm = top.shape[0]
     half = [shape(2, 8, 16, N)] * 2
 
-    def body(core, bt, top, bot, ptop, pbot, p_ref, *refs):
+    def body(bt, top, bot, ptop, pbot, p_ref, *refs):
         if grads is None:
             keep, send, gtop, gbot, back_s = refs
             gtop[...] = jnp.zeros_like(gtop)
@@ -316,7 +351,7 @@
         loop(
             count,
             lambda m: gradients(
-                core[2], 1, bt, top, bot, ptop, pbot, p_ref, keep, send, gtop, gbot, back_s, m + first
+                lax.axis_index("core"), 1, bt, top, bot, ptop, pbot, p_ref, keep, send, gtop, gbot, back_s, m + first
             ),
         )
 
@@ -324,12 +359,12 @@
     return local_call(
         body,
         "second_block",
-        [SCALARS] + [LOCAL] * (6 + len(given)),
+        [LOCAL] * (6 + len(given)),
         [shape(nm, 16, 16, N)] * 2 + half,
         [pltpu.VMEM((N, N), f32)],
         6,
-        {7 + i: i for i in range(len(given))},
-    )(core, back_rows, top, bot, ptop, pbot, probe, *given)
+        {6 + i: i for i in range(len(given))},
+    )(back_rows, top, bot, ptop, pbot, probe, *given)
 
 
 SCAN = ("y", "z", "x", "core")
@@ -363,36 +398,18 @@
     return lax.ppermute(value, ("mode", "x"), pairs)
 
 
-def window(obj, first, place):
-    return obj.at[:, pl.ds(pl.multiple_of(first * H, H), H), pl.ds(pl.multiple_of(place[1] * H, H), N)]
-
-
-def rim_body(place, obj, out, sem):
-    copy = pltpu.make_async_copy(window(obj, 0, place), out, sem)
-    copy.start()
-    copy.wait()
+def rim_body(place, obj, out):
+    columns = window(place)
+
+    def take(i):
+        rows = at(i, CHUNK)
+        out[:, rows, :] = obj[:, rows, columns]
+
+    loop(H // CHUNK, take, 2)
 
 
 def rim_rows(place, obj):
-    return local_call(rim_body, "rim_rows", [SCALARS, FAR], [shape(2, H, N)], [pltpu.SemaphoreType.DMA], 60)(
-        place, obj
-    )[0]
-
-
-def own_body(place, obj, top, bot, sems):
-    copies = [
-        pltpu.make_async_copy(window(obj, place[0], place), top, sems.at[0]),
-        pltpu.make_async_copy(window(obj, 1, place), bot, sems.at[1]),
-    ]
-    for copy in copies:
-        copy.start()
-    for copy in copies:
-        copy.wait()
-
-
-def own_rows(place, obj):
-    outs = [shape(2, H, N)] * 2
-    return local_call(own_body, "own_rows", [SCALARS, FAR], outs, [pltpu.SemaphoreType.DMA((2,))], 60)(place, obj)
+    return local_call(rim_body, "rim_rows", [SCALARS, LOCAL], [shape(2, H, N)], [], LIMIT)(place, obj)[0]
 
 
 def brightest_body(own, far, out):
@@ -403,11 +420,11 @@
 
 
 def brightest(own, far):
-    return local_call(brightest_body, "brightest", [LOCAL, LOCAL], [shape(8, N)], [], LIMIT)(own, far)[0]
-
-
-def core_add_body(sc, keep, recv, own, near, back, far0, far1):
-    me = sc[0]
+    return local_call(brightest_body, "brightest", [LOCAL, LOCAL], [shape(8, N)], [], LIMIT, cost=STAGE)(own, far)[0]
+
+
+def core_add_body(keep, recv, own, near, back, far0, far1):
+    me = here()[0]
     n2 = own.shape[1]
     for m in range(2 * n2):
         j, k = m // n2, m % n2
@@ -418,10 +435,10 @@
         (far0, far1)[j][k] = keep[m, a] + recv[m, a]
 
 
-def core_add(sc, keep, recv):
+def core_add(keep, recv):
     n2 = keep.shape[0] // 2
     outs = [shape(2, n2, 4, 16, N)] * 3 + [shape(n2, 4, 16, N)] * 2
-    return local_call(core_add_body, "core_add", [SCALARS, LOCAL, LOCAL], outs, [], LIMIT)(sc, keep, recv)
+    return local_call(core_add_body, "core_add", [LOCAL, LOCAL], outs, [], LIMIT, cost=STAGE)(keep, recv)
 
 
 def relay_body(a, b, ra, rb, oa, ob):
@@ -431,11 +448,11 @@
 
 def relay_add(near, back, ra, rb):
     outs = [shape(*near.shape)] * 2
-    return local_call(relay_body, "relay_add", [LOCAL] * 4, outs, [], LIMIT, {0: 0, 1: 1})(near, back, ra, rb)
-
-
-def plane_add_body(sc, *refs):
-    me = sc[1]
+    return local_call(relay_body, "relay_add", [LOCAL] * 4, outs, [], LIMIT, {0: 0, 1: 1}, cost=STAGE)(near, back, ra, rb)
+
+
+def plane_add_body(*refs):
+    me = here()[1]
     for block in range(2):
         own, ra, rb = refs[3 * block : 3 * block + 3]
         for turn in range(4):
@@ -443,16 +460,16 @@
             refs[6 + turn][block] = own[:, :, b] + (ra[:, :, b] + rb[:, :, b])
 
 
-def plane_add(sc, blocks):
+def plane_add(blocks):
     n2 = blocks[0][0].shape[1]
     outs = [shape(2, 2, n2, 16, N)] * 4
-    return local_call(plane_add_body, "plane_add", [SCALARS] + [LOCAL] * 6, outs, [], LIMIT)(
-        sc, *blocks[0], *blocks[1]
+    return local_call(plane_add_body, "plane_add", [LOCAL] * 6, outs, [], LIMIT, cost=STAGE)(
+        *blocks[0], *blocks[1]
     )
 
 
-def line_add_body(sc, a, b, c, d, keep, send):
-    core = sc[2]
+def line_add_body(a, b, c, d, keep, send):
+    core = here()[2]
     for out, side in ((keep, core), (send, 1 - core)):
         rows = at(side, 8)
         for block in range(2):
@@ -462,18 +479,18 @@
                 )
 
 
-def line_add(sc, arrays):
+def line_add(arrays):
     dims = arrays[0].shape
     outs = [shape(*dims[:3], 8, N)] * 2
-    return local_call(line_add_body, "line_add", [SCALARS] + [LOCAL] * 4, outs, [], LIMIT)(sc, *arrays)
-
-
-def pixel_body(sc, keep, recv, rows, mine, other):
-    core, x = sc[2], sc[3]
+    return local_call(line_add_body, "line_add", [LOCAL] * 4, outs, [], LIMIT, cost=STAGE)(*arrays)
+
+
+def pixel_body(keep, recv, rows, mine, other):
+    core, x = here()[2:4]
     scale = 1.0 / math.sqrt(64)
 
     def fill(part, ref):
-        mine[part] = ref[x] * scale + rows[part].astype(f32)
+        mine[part] = ref[x] * scale + rows[part]
         other[part] = ref[1 - x] * scale
 
     @pl.when(core == 0)
@@ -487,15 +504,15 @@
         fill(1, keep)
 
 
-def pixel_step(sc, keep, recv, rows):
+def pixel_step(keep, recv, rows):
     dims = rows.shape
-    return local_call(pixel_body, "pixel_step", [SCALARS] + [LOCAL] * 3, [shape(*dims)] * 2, [], LIMIT)(
-        sc, keep.reshape(dims), recv.reshape(dims), rows
+    return local_call(pixel_body, "pixel_step", [LOCAL] * 3, [shape(*dims)] * 2, [], LIMIT, cost=STAGE)(
+        keep.reshape(dims), recv.reshape(dims), rows
     )
 
 
-def mix_body(sc, w_ref, mine, b, c, d, out_ref):
-    mode = sc[4]
+def mix_body(w_ref, mine, b, c, d, out_ref):
+    mode = here()[4]
     nm = mine.shape[1]
     for part in range(2):
         own = [mine[part, j] + b[part, j] for j in range(nm)]
@@ -509,9 +526,9 @@
             out_ref[part, k] = acc.astype(bf16)
 
 
-def mix(sc, mixing, mine, b, c, d):
+def mix(mixing, mine, b, c, d):
     outs = [shape(*mine.shape, dtype=bf16)]
-    return local_call(mix_body, "mix", [SCALARS] * 2 + [LOCAL] * 4, outs, [], LIMIT)(sc, mixing, mine, b, c, d)[0]
+    return local_call(mix_body, "mix", [SCALARS] + [LOCAL] * 4, outs, [], LIMIT)(mixing, mine, b, c, d)[0]
 
 
 def object_body(place, before, near_max, far_max, obj, t0, t0f, t1, t1f, b0, b0f, b1, b1f, over, out, new, sems):
@@ -580,7 +597,7 @@
 
 
 def over_sum(b0, b0f, b1, b1f):
-    return local_call(over_body, "over_sum", [LOCAL] * 4, [shape(2, 2, 8, 16, N)], [], LIMIT)(b0, b0f, b1, b1f)[0]
+    return local_call(over_body, "over_sum", [LOCAL] * 4, [shape(2, 2, 8, 16, N)], [], LIMIT, cost=STAGE)(b0, b0f, b1, b1f)[0]
 
 
 def tied(*values):
@@ -589,63 +606,58 @@
 
 def per_device(object_field, probe, patterns, row_shift, col_start, mixing):
     minus, plus, wave_top_rows, wave_bot_rows, back_rows0, back_rows1 = tables()
-    y, z, x, core = (lax.axis_index(a) for a in SCAN)
-    mode = lax.axis_index("mode")
-    first = jnp.where(core == 0, y, z)
-    second = jnp.where(core == 0, z, y)
-    sc = jnp.stack([first, second, core, x, mode])
     place = jnp.concatenate([row_shift, col_start])
     before = along(place, 1)
-    rows = lax.dynamic_slice_in_dim(probe, lax.axis_index(SCAN) * 8, 8, 2)
-    before, place, sc, rows = tied(before, place, sc, rows)
-    rim = along(rim_rows(before, object_field), -1)
-    patch_top, own_bot = own_rows(place, object_field)
-    half_top, own_light, light_out = top_half(sc, patch_top, probe, minus)
-    rim, light_out, half_top = tied(rim, light_out, half_top)
+    patch_top, own_bot, first_rows = own_rows(place, object_field)
+    before, patch_top = tied(before, patch_top)
+    rim = along(rim_rows(before, first_rows), -1)
+    half_top, own_light, light_out, rows = top_half(patch_top, probe, minus)
+    rim, half_top, light_out = tied(rim, half_top, light_out)
     far_light = swapped(light_out, "mode")
     half_bot, patch_bot, wave_top, sum_top = bottom_half(
         place, own_bot, rim, probe, minus, wave_top_rows, half_top
     )
     far_top = swapped(sum_top, "mode")
-    half_bot, far_light = tied(half_bot, far_light)
     wave_bot, sum_bot = low_wave(wave_bot_rows, half_top, half_bot)
     far_bot = swapped(sum_bot, "mode")
+    wave_top, far_light = tied(wave_top, far_light)
     fixed = fixed_top(patterns, sum_top, far_top, wave_top, plus)
-    half_max = brightest(own_light, far_light)
     low, keep0, send0, top0, bot0 = first_block(
-        sc, patterns, sum_bot, far_bot, wave_bot, plus, back_rows0, fixed, patch_top, patch_bot, probe
+        patterns, sum_bot, far_bot, wave_bot, plus, back_rows0, fixed, patch_top, patch_bot, probe
     )
     recv0 = swapped(send0, "core")
     bot0_far = swapped(bot0, "mode")
-    top0_far = swapped(top0, "mode")
-    part1 = second_block(sc, back_rows1, fixed, low, patch_top, patch_bot, probe, 0, 3)
-    own0, near0, back0, far0a, far0b = core_add(sc, keep0, recv0)
+    half_max = brightest(own_light, far_light)
+    far_max = swapped(half_max, "core")
+    part1 = second_block(back_rows1, fixed, low, patch_top, patch_bot, probe, 0, 3)
+    own0, near0, back0, far0a, far0b = core_add(keep0, recv0)
     ra0, rb0 = turned(far0a, 1, True), turned(far0b, -1, True)
     *part1, near0 = tied(*part1, near0)
-    keep1, send1, top1, bot1 = second_block(
-        sc, back_rows1, fixed, low, patch_top, patch_bot, probe, 3, 3, part1
-    )
-    bot1_far = swapped(bot1, "mode")
-    top1_far = swapped(top1, "mode")
+    keep1, send1, top1, bot1 = second_block(back_rows1, fixed, low, patch_top, patch_bot, probe, 3, 3, part1)
     recv1 = swapped(send1, "core")
     near0, back0 = relay_add(near0, back0, ra0, rb0)
-    keep1, near0, back0 = tied(keep1, near0, back0)
-    own1, near1, back1, far1a, far1b = core_add(sc, keep1, recv1)
+    top0_next, bot0_far, _ = tied(top0, bot0_far, near0)
+    top0_far = swapped(top0_next, "mode")
+    bot1_next, top0_far = tied(bot1, top0_far)
+    bot1_far = swapped(bot1_next, "mode")
+    keep1, _, bot0_far = tied(keep1, near0, bot0_far)
+    own1, near1, back1, far1a, far1b = core_add(keep1, recv1)
     ra1, rb1 = turned(far1a, 1, True), turned(far1b, -1, True)
     plane0 = (own0, turned(near0, 1, True), turned(back0, -1, True))
-    ra1, rb1, bot0_far, *plane0 = tied(ra1, rb1, bot0_far, *plane0)
+    ra1, rb1, top0_far, *plane0 = tied(ra1, rb1, top0_far, *plane0)
     near1, back1 = relay_add(near1, back1, ra1, rb1)
     plane1 = (own1, turned(near1, 1, True), turned(back1, -1, True))
     *plane1, bot1_far = tied(*plane1, bot1_far)
+    top1_next, _ = tied(top1, plane1[1])
+    top1_far = swapped(top1_next, "mode")
     over = along(over_sum(bot0, bot0_far, bot1, bot1_far), 1)
-    line = plane_add(sc, (plane0, plane1))
+    line = plane_add((plane0, plane1))
     line = [line[0]] + [turned(line[r], r, False) for r in (1, 3, 2)]
-    *line, top0_far = tied(*line, top0_far)
-    keep, send = line_add(sc, line)
-    far_max = swapped(half_max, "core")
-    mine, other = pixel_step(sc, keep, swapped(send, "core"), rows)
+    *line, top1_far, far_max = tied(*line, top1_far, far_max)
+    keep, send = line_add(line)
+    mine, other = pixel_step(keep, swapped(send, "core"), rows)
     mine, other, over = tied(mine, other, over)
-    probe_new = mix(sc, mixing, mine, across(other, 0, 1), across(mine, 1, 0), across(other, 1, 1))
+    probe_new = mix(mixing, mine, across(other, 0, 1), across(mine, 1, 0), across(other, 1, 1))
     pieces = (top0, top0_far, top1, top1_far, bot0, bot0_far, bot1, bot1_far)
     object_new = object_update(place, before, half_max, far_max, object_field, pieces, over)
     return object_new, probe_new

time: 190 us -> 184 us (0.968)
  starting transfers between devices: 52.6 us -> 63.2 us
  Pallas kernels: 59.6 us -> 50 us
  local copies, waits for them, and re-layouts: 9.83 us -> 3.81 us
    ppermute x11, waiting for transfers between devices: 52.4 us -> 38.2 us  [swapped(): return lax.ppermute(value, axis, [(0, 1), (1, 0)])]
    ppermute x11, starting transfers between devices: 13.5 us -> 27.4 us  [swapped(): return lax.ppermute(value, axis, [(0, 1), (1, 0)])]
    pallas_call x19, Pallas kernels: 56.5 us -> 46.9 us  [call(): pl.pallas_call(body, in_specs=ins, out_specs=[LOCAL] * len(outs), out_sha...]
    ppermute x3, waiting for transfers between devices: 0.01 us -> 7.14 us  [along(): return lax.ppermute(value, SCAN, [(i, i + steps) for i in range(lo, hi)])]
    unnamed x46 -> x24, local copies, waits for them, and re-layouts: 8.84 us -> 3.81 us
    ppermute x11, waiting for transfers between devices: 7.23 us -> 12.2 us  [turned(): return lax.ppermute(value, RING, pairs)]
    ppermute x3, starting transfers between devices: 12.8 us -> 9.63 us  [along(): return lax.ppermute(value, SCAN, [(i, i + steps) for i in range(lo, hi)])]
  transfers between devices with their start and end apart: 28 -> 28, of which waited for: 14 -> 15; matrix products, arithmetic and copies ran while one was open for 1% -> 0% of each run, Pallas kernels for 21% -> 18%
where the time goes in v4:
time: 184 us; the launch traced here: 183 us
  waiting for transfers between devices  63.5 us (35%)
  starting transfers between devices  63.2 us (34%)
  Pallas kernels  50 us (27%)
  local copies, waits for them, and re-layouts  3.81 us (2%)
  between operations  2.19 us (1%)
    pallas_call x19, Pallas kernels, call(): pl.pallas_call(body, in_specs=ins, out_specs=[LOCAL] * len(outs), out_sha...  46.9 us
    ppermute x11, waiting for transfers between devices, swapped(): return lax.ppermute(value, axis, [(0, 1), (1, 0)])  38.2 us
    ppermute x11, starting transfers between devices, swapped(): return lax.ppermute(value, axis, [(0, 1), (1, 0)])  27.4 us
    ppermute x11, starting transfers between devices, turned(): return lax.ppermute(value, RING, pairs)  22.3 us
    ppermute x11, waiting for transfers between devices, turned(): return lax.ppermute(value, RING, pairs)  12.2 us
    ppermute x3, starting transfers between devices, along(): return lax.ppermute(value, SCAN, [(i, i + steps) for i in range(lo, hi)])  9.63 us
    ppermute x3, waiting for transfers between devices, along(): return lax.ppermute(value, SCAN, [(i, i + steps) for i in range(lo, hi)])  7.14 us
    ppermute x3, waiting for transfers between devices, across(): return lax.ppermute(value, ('mode', 'x'), pairs)  5.9 us
  transfers between devices with their start and end apart: 28, of which 15 were waited for; matrix products, arithmetic and copies ran while one was open for 0% of the time, Pallas kernels for 18%

profile of v4, /device:TPU:1, one launch (start us, length us, event | category | flops | bytes accessed | tf_op | source)
XLA Modules:
  0.0 182.8 jit_solution(5637434271746338280)
XLA Ops:
  1.9 0.1 pad_add_fusion.place
  2.0 4.8 %collective-permute-start = (s32[2]{0:T(128)S(1)}, s32[2]{0:T(128)S(1)}, u32[]{:S(2)}, u32[]{:S(2)}) collective-permute-start(s32[2]{0:T(128)S(1)} %pad_add_fusion.place), channel_id=1, source_target_pairs={{0,1},{1,2},{2,3},{3,4},{4,5},{5,6},{6,7},{7,8},{8,9},{9,10},{10,1... | collective-permute-start | bytes 32 | tf_op jit(solution)/shard_map/ppermute | solution.py:377
  6.8 2.2 %copy-done.1 = f32[2,512,1024]{2,1,0:T(8,128)S(1)} copy-done((f32[2,512,1024]{2,1,0:T(8,128)S(1)}, f32[2,512,1024]{2,1,0:T(8,128)}, u32[]{:S(2)}) %copy-start.1) | copy-done | bytes 4194328
  9.0 0.8 own_rows.1
  9.8 0.6 rim_rows.1
  10.4 1.9 %collective-permute-start.1 = (f32[2,256,512]{2,1,0:T(8,128)S(1)}, f32[2,256,512]{2,1,0:T(8,128)S(1)}, u32[]{:S(2)}, u32[]{:S(2)}) collective-permute-start(f32[2,256,512]{2,1,0:T(8,128)S(1)} %rim_rows.1), channel_id=1, source_target_pairs={{1,0},{2,1},{3,2},{4,3},{5,4},{6,5},{7,6},{8,7},{9,8},{10,9},{11,1... | collective-permute-start | bytes 3145736 | tf_op jit(solution)/shard_map/ppermute | solution.py:377
  12.4 1.6 copy-done.3
  14.0 5.7 %top_half.1 = (bf16[6,512,512]{2,1,0:T(8,128)(2,1)S(1)}, f32[256,512]{1,0:T(8,128)S(1)}, f32[256,512]{1,0:T(8,128)S(1)}, f32[2,6,8,512]{3,2,1,0:T(8,128)S(1)}) custom-call(f32[2,256,512]{2,1,0:T(8,128)S(1)} %get-tuple-element.90.patch_ref.ptop, bf16[2,6,512,512]{3,2,1,0:T(8,128)(2,1)S(1)} %copy-done, bf16[1024,1024]{1,0:T(8,128)(2,1)S(1)} %copy-done.3), custom_call_target="tpu_custom_call" | custom-call | tf_op jit(solution)/shard_map/top_half/pallas_call | solution.py:57
  19.7 7.1 %collective-permute-done.1.rim = f32[2,256,512]{2,1,0:T(8,128)S(1)} collective-permute-done((f32[2,256,512]{2,1,0:T(8,128)S(1)}, f32[2,256,512]{2,1,0:T(8,128)S(1)}, u32[]{:S(2)}, u32[]{:S(2)}) %collective-permute-start.1) | collective-permute-done | bytes 1048608 | tf_op jit(solution)/shard_map/ppermute | solution.py:377
  26.9 2.5 %collective-permute-start.2 = (f32[256,512]{1,0:T(8,128)S(1)}, f32[256,512]{1,0:T(8,128)S(1)}, u32[]{:S(2)}, u32[]{:S(2)}) collective-permute-start(f32[256,512]{1,0:T(8,128)S(1)} %get-tuple-element.99), channel_id=1, source_target_pairs={{0,64},{64,0},{1,65},{65,1},{2,66},{66,2},{3,67},{67,3},{4,68},{68... | collective-permute-start | bytes 1572872 | tf_op jit(solution)/shard_map/ppermute | solution.py:381
  29.3 9.6 %bottom_half.1 = (bf16[6,512,512]{2,1,0:T(8,128)(2,1)S(1)}, f32[2,256,512]{2,1,0:T(8,128)S(1)}, f32[6,512,512]{2,1,0:T(8,128)S(1)}, f32[256,512]{1,0:T(8,128)S(1)}) custom-call(s32[2]{0:T(128)S(1)} %pad_add_fusion.place, f32[2,256,512]{2,1,0:T(8,128)S(1)} %get-tuple-element.92.own, f32[2,256,512]{2,1,0:T(8,128)S(1)} %collective-permute-done.1.rim, ...), custom_call_target="tpu_custom_call" | custom-call | tf_op jit(solution)/shard_map/bottom_half/pallas_call | solution.py:57
  38.9 0.6 collective-permute-start.3
  39.5 4.3 %low_wave.1 = (f32[6,512,512]{2,1,0:T(8,128)S(1)}, f32[256,512]{1,0:T(8,128)S(1)}) custom-call(bf16[512,1024]{1,0:T(8,128)(2,1)S(1)} %copy-done.9, bf16[6,512,512]{2,1,0:T(8,128)(2,1)S(1)} %get-tuple-element.97.top, bf16[6,512,512]{2,1,0:T(8,128)(2,1)S(1)} %get-tuple-element.103.bot), custom_call_target="tpu_custom_call" | custom-call | tf_op jit(solution)/shard_map/low_wave/pallas_call | solution.py:57
  43.8 2.5 %collective-permute-start.4 = (f32[256,512]{1,0:T(8,128)S(1)}, f32[256,512]{1,0:T(8,128)S(1)}, u32[]{:S(2)}, u32[]{:S(2)}) collective-permute-start(f32[256,512]{1,0:T(8,128)S(1)} %get-tuple-element.104.s0), channel_id=1, source_target_pairs={{0,64},{64,0},{1,65},{65,1},{2,66},{66,2},{3,67},{67,3},{4,68},{68... | collective-permute-start | bytes 1572872 | tf_op jit(solution)/shard_map/ppermute | solution.py:381
  46.4 6.9 %collective-permute-done.3.s1 = f32[256,512]{1,0:T(8,128)S(1)} collective-permute-done((f32[256,512]{1,0:T(8,128)S(1)}, f32[256,512]{1,0:T(8,128)S(1)}, u32[]{:S(2)}, u32[]{:S(2)}) %collective-permute-start.3) | collective-permute-done | bytes 524320 | tf_op jit(solution)/shard_map/ppermute | solution.py:381
  53.2 4.8 %fixed_top.1.top = bf16[6,512,512]{2,1,0:T(8,128)(2,1)S(1)} custom-call(f32[1,512,512]{2,1,0:T(8,128)S(1)} %copy-done.6, f32[256,512]{1,0:T(8,128)S(1)} %get-tuple-element.101.s0, f32[256,512]{1,0:T(8,128)S(1)} %collective-permute-done.3.s1, f32[6,512,512]{2,1,0:T(8,128)S(1)} %get-tuple-element.102.wave_ref, bf16[1024,1024]{1,0:T(8,128)(2,1)S(1)} %copy-done.5), custom_call_target="tpu_custom_call" | custom-call | tf_op jit(solution)/shard_map/fixed_top/pallas_call | solution.py:57
  58.1 0.8 collective-permute-done.4.s1
  58.9 11.0 %first_block.1 = (bf16[6,512,512]{2,1,0:T(8,128)(2,1)S(1)}, f32[6,16,16,512]{3,2,1,0:T(8,128)S(1)}, f32[6,16,16,512]{3,2,1,0:T(8,128)S(1)}, f32[2,8,16,512]{3,2,1,0:T(8,128)S(1)}, f32[2,8,16,512]{3,2,1,0:T(8,128)S(1)}) custom-call(f32[1,512,512]{2,1,0:T(8,128)S(1)} %copy-done.6, f32[256,512]{1,0:T(8,128)S(1)} %get-tuple-element.104.s0, ...), custom_call_target="tpu_custom_call" | custom-call | tf_op jit(solution)/shard_map/first_block/pallas_call | solution.py:57
  69.8 0.1 collective-permute-start.5
  69.9 3.4 %second_block.2 = (f32[6,16,16,512]{3,2,1,0:T(8,128)S(1)}, f32[6,16,16,512]{3,2,1,0:T(8,128)S(1)}, f32[2,8,16,512]{3,2,1,0:T(8,128)S(1)}, f32[2,8,16,512]{3,2,1,0:T(8,128)S(1)}) custom-call(bf16[512,1024]{1,0:T(8,128)(2,1)S(1)} %copy-done.7, bf16[6,512,512]{2,1,0:T(8,128)(2,1)S(1)} %fixed_top.1.top, bf16[6,512,512]{2,1,0:T(8,128)(2,1)S(1)} %get-tuple-element.107.bot, ...), custom_call_target="tpu_custom_call" | custom-call | tf_op jit(solution)/shard_map/second_block/pallas_call | solution.py:57
  73.4 2.2 %collective-permute-done.5.recv = f32[6,16,16,512]{3,2,1,0:T(8,128)S(1)} collective-permute-done((f32[6,16,16,512]{3,2,1,0:T(8,128)S(1)}, f32[6,16,16,512]{3,2,1,0:T(8,128)S(1)}, u32[]{:S(2)}, u32[]{:S(2)}) %collective-permute-start.5) | collective-permute-done | bytes 3145760 | tf_op jit(solution)/shard_map/ppermute | solution.py:381
  75.6 0.3 core_add.2
  75.9 3.4 %second_block.3 = (f32[6,16,16,512]{3,2,1,0:T(8,128)S(1)}, f32[6,16,16,512]{3,2,1,0:T(8,128)S(1)}, f32[2,8,16,512]{3,2,1,0:T(8,128)S(1)}, f32[2,8,16,512]{3,2,1,0:T(8,128)S(1)}) custom-call(bf16[512,1024]{1,0:T(8,128)(2,1)S(1)} %copy-done.7, ...), custom_call_target="tpu_custom_call", output_to_operand_aliasing={{0}: (6, {}), {1}: (7, {}), {2}: (8, {}), {3}: (9, {})} | custom-call | tf_op jit(solution)/shard_map/second_block/pallas_call | solution.py:57
  79.3 0.2 collective-permute-start.9
  79.5 8.4 %collective-permute-start.6 = (f32[3,4,16,512]{3,2,1,0:T(8,128)S(1)}, f32[3,4,16,512]{3,2,1,0:T(8,128)S(1)}, u32[]{:S(2)}, u32[]{:S(2)}) collective-permute-start(f32[3,4,16,512]{3,2,1,0:T(8,128)S(1)} %get-tuple-element.122), channel_id=1, source_target_pairs={{0,16},{1,5},{4,20},{5,9},{8,24},{9,13},{12,28},{13,1},{16,32},{17... | collective-permute-start | bytes 1179656 | tf_op jit(solution)/shard_map/ppermute | solution.py:393
  87.9 2.1 %collective-permute-start.7 = (f32[3,4,16,512]{3,2,1,0:T(8,128)S(1)}, f32[3,4,16,512]{3,2,1,0:T(8,128)S(1)}, u32[]{:S(2)}, u32[]{:S(2)}) collective-permute-start(f32[3,4,16,512]{3,2,1,0:T(8,128)S(1)} %get-tuple-element.123), channel_id=1, source_target_pairs={{0,48},{1,13},{4,52},{5,1},{8,56},{9,5},{12,60},{13,9},{16,0},{17,... | collective-permute-start | bytes 1179656 | tf_op jit(solution)/shard_map/ppermute | solution.py:393
  90.0 1.6 collective-permute-start.8
  91.6 3.9 %collective-permute-done.6.ra = f32[3,4,16,512]{3,2,1,0:T(8,128)S(1)} collective-permute-done((f32[3,4,16,512]{3,2,1,0:T(8,128)S(1)}, f32[3,4,16,512]{3,2,1,0:T(8,128)S(1)}, u32[]{:S(2)}, u32[]{:S(2)}) %collective-permute-start.6) | collective-permute-done | bytes 393248 | tf_op jit(solution)/shard_map/ppermute | solution.py:393
  95.5 0.1 relay_add.2
  95.6 1.1 collective-permute-start.13
  96.7 8.7 %collective-permute-done.8.b0f = f32[2,8,16,512]{3,2,1,0:T(8,128)S(1)} collective-permute-done((f32[2,8,16,512]{3,2,1,0:T(8,128)S(1)}, f32[2,8,16,512]{3,2,1,0:T(8,128)S(1)}, u32[]{:S(2)}, u32[]{:S(2)}) %collective-permute-start.8) | collective-permute-done | bytes 524320 | tf_op jit(solution)/shard_map/ppermute | solution.py:381
  105.4 1.5 collective-permute-start.12
  107.0 0.3 core_add.3
  107.3 1.5 collective-permute-start.10
  108.8 1.2 collective-permute-start.11
  110.0 9.9 %collective-permute-done.12.t0f = f32[2,8,16,512]{3,2,1,0:T(8,128)S(1)} collective-permute-done((f32[2,8,16,512]{3,2,1,0:T(8,128)S(1)}, f32[2,8,16,512]{3,2,1,0:T(8,128)S(1)}, u32[]{:S(2)}, u32[]{:S(2)}) %collective-permute-start.12) | collective-permute-done | bytes 524320 | tf_op jit(solution)/shard_map/ppermute | solution.py:381
  120.0 2.3 %collective-permute-done.11.rb = f32[3,4,16,512]{3,2,1,0:T(8,128)S(1)} collective-permute-done((f32[3,4,16,512]{3,2,1,0:T(8,128)S(1)}, f32[3,4,16,512]{3,2,1,0:T(8,128)S(1)}, u32[]{:S(2)}, u32[]{:S(2)}) %collective-permute-start.11) | collective-permute-done | bytes 393248 | tf_op jit(solution)/shard_map/ppermute | solution.py:393
  122.3 0.1 relay_add.3
  122.4 0.1 collective-permute-start.15
  122.5 2.7 %collective-permute-start.16 = (f32[2,3,4,16,512]{4,3,2,1,0:T(8,128)S(1)}, f32[2,3,4,16,512]{4,3,2,1,0:T(8,128)S(1)}, u32[]{:S(2)}, u32[]{:S(2)}) collective-permute-start(f32[2,3,4,16,512]{4,3,2,1,0:T(8,128)S(1)} %get-tuple-element.146), channel_id=1, source_target_pairs={{0,48},{1,13},{4,52},{5,1},{8,56},{9,5},{12,60},{13,9},{16,0},{17,... | collective-permute-start | bytes 2359304 | tf_op jit(solution)/shard_map/ppermute | solution.py:393
  125.2 1.4 collective-permute-start.17
  126.6 0.2 brightest.1.near_max
  126.8 2.5 %collective-permute-start.22 = (f32[8,512]{1,0:T(8,128)S(1)}, f32[8,512]{1,0:T(8,128)S(1)}, u32[]{:S(2)}, u32[]{:S(2)}) collective-permute-start(f32[8,512]{1,0:T(8,128)S(1)} %brightest.1.near_max), channel_id=1, source_target_pairs={{0,1},{1,0},{2,3},{3,2},{4,5},{5,4},{6,7},{7,6},{8,9},{9,8},{10,11... | collective-permute-start | bytes 49160 | tf_op jit(solution)/shard_map/ppermute | solution.py:381
  129.3 8.6 %collective-permute-done.17.b1f = f32[2,8,16,512]{3,2,1,0:T(8,128)S(1)} collective-permute-done((f32[2,8,16,512]{3,2,1,0:T(8,128)S(1)}, f32[2,8,16,512]{3,2,1,0:T(8,128)S(1)}, u32[]{:S(2)}, u32[]{:S(2)}) %collective-permute-start.17) | collective-permute-done | bytes 524320 | tf_op jit(solution)/shard_map/ppermute | solution.py:381
  138.0 1.4 collective-permute-start.21
  139.4 0.3 plane_add.1
  139.7 1.6 collective-permute-start.18
  141.3 1.9 %collective-permute-start.19 = (f32[2,2,3,16,512]{4,3,2,1,0:T(8,128)S(1)}, f32[2,2,3,16,512]{4,3,2,1,0:T(8,128)S(1)}, u32[]{:S(2)}, u32[]{:S(2)}) collective-permute-start(f32[2,2,3,16,512]{4,3,2,1,0:T(8,128)S(1)} %get-tuple-element.153), channel_id=1, source_target_pairs={{0,12},{1,49},{4,0},{5,53},{8,4},{9,57},{12,8},{13,61},{16,28},{17... | collective-permute-start | bytes 1179656 | tf_op jit(solution)/shard_map/ppermute | solution.py:393
  143.2 1.7 collective-permute-start.20
  144.9 0.1 over_sum.1
  145.0 2.9 %collective-permute-start.24 = (f32[2,2,8,16,512]{4,3,2,1,0:T(8,128)S(1)}, f32[2,2,8,16,512]{4,3,2,1,0:T(8,128)S(1)}, u32[]{:S(2)}, u32[]{:S(2)}) collective-permute-start(f32[2,2,8,16,512]{4,3,2,1,0:T(8,128)S(1)} %over_sum.1), channel_id=1, source_target_pairs={{0,1},{1,2},{2,3},{3,4},{4,5},{5,6},{6,7},{7,8},{8,9},{9,10},{10,1... | collective-permute-start | bytes 3145736 | tf_op jit(solution)/shard_map/ppermute | solution.py:377
  147.9 0.6 collective-permute-done.18.b
  148.5 3.6 %collective-permute-done.19.c = f32[2,2,3,16,512]{4,3,2,1,0:T(8,128)S(1)} collective-permute-done((f32[2,2,3,16,512]{4,3,2,1,0:T(8,128)S(1)}, f32[2,2,3,16,512]{4,3,2,1,0:T(8,128)S(1)}, u32[]{:S(2)}, u32[]{:S(2)}) %collective-permute-start.19) | collective-permute-done | bytes 393248 | tf_op jit(solution)/shard_map/ppermute | solution.py:393
  152.1 1.8 %collective-permute-done.20.d = f32[2,2,3,16,512]{4,3,2,1,0:T(8,128)S(1)} collective-permute-done((f32[2,2,3,16,512]{4,3,2,1,0:T(8,128)S(1)}, f32[2,2,3,16,512]{4,3,2,1,0:T(8,128)S(1)}, u32[]{:S(2)}, u32[]{:S(2)}) %collective-permute-start.20) | collective-permute-done | bytes 393248 | tf_op jit(solution)/shard_map/ppermute | solution.py:393
  153.9 0.1 line_add.1
  154.0 13.0 %collective-permute-start.23 = (f32[2,2,3,8,512]{4,3,2,1,0:T(8,128)S(1)}, f32[2,2,3,8,512]{4,3,2,1,0:T(8,128)S(1)}, u32[]{:S(2)}, u32[]{:S(2)}) collective-permute-start(f32[2,2,3,8,512]{4,3,2,1,0:T(8,128)S(1)} %get-tuple-element.167), channel_id=1, source_target_pairs={{0,1},{1,0},{2,3},{3,2},{4,5},{5,4},{6,7},{7,6},{8,9},{9,8},{10,11... | collective-permute-start | bytes 589832 | tf_op jit(solution)/shard_map/ppermute | solution.py:381
  167.1 1.1 collective-permute-done.23
  168.2 0.1 collective-permute-start.25
  168.3 1.6 collective-permute-start.26
  169.9 2.2 %collective-permute-start.27 = (f32[2,6,8,512]{3,2,1,0:T(8,128)S(1)}, f32[2,6,8,512]{3,2,1,0:T(8,128)S(1)}, u32[]{:S(2)}, u32[]{:S(2)}) collective-permute-start(f32[2,6,8,512]{3,2,1,0:T(8,128)S(1)} %get-tuple-element.173), channel_id=1, source_target_pairs={{0,66},{2,64},{64,2},{66,0},{1,67},{3,65},{65,3},{67,1},{4,70},{6,... | collective-permute-start | bytes 589832 | tf_op jit(solution)/shard_map/ppermute | solution.py:398
  172.1 3.2 %object_update.1 = f32[2,512,1024]{2,1,0:T(8,128)} custom-call(s32[2]{0:T(128)S(1)} %pad_add_fusion.place, s32[2]{0:T(128)S(1)} %collective-permute-done.place.before, f32[8,512]{1,0:T(8,128)S(1)} %brightest.1.near_max, f32[8,512]{1,0:T(8,128)S(1)} %collective-permute-done.22.far_max, f32[2,512,1024]{2,1,0:T(8,128)S(1)} %copy-done.2, ...), custom_call_target="tpu_custom_call" | custom-call | tf_op jit(solution)/shard_map/object_update/pallas_call | solution.py:583
  175.3 3.7 %collective-permute-done.26.c = f32[2,6,8,512]{3,2,1,0:T(8,128)S(1)} collective-permute-done((f32[2,6,8,512]{3,2,1,0:T(8,128)S(1)}, f32[2,6,8,512]{3,2,1,0:T(8,128)S(1)}, u32[]{:S(2)}, u32[]{:S(2)}) %collective-permute-start.26) | collective-permute-done | bytes 196640 | tf_op jit(solution)/shard_map/ppermute | solution.py:398
  179.1 2.2 %collective-permute-done.27.d = f32[2,6,8,512]{3,2,1,0:T(8,128)S(1)} collective-permute-done((f32[2,6,8,512]{3,2,1,0:T(8,128)S(1)}, f32[2,6,8,512]{3,2,1,0:T(8,128)S(1)}, u32[]{:S(2)}, u32[]{:S(2)}) %collective-permute-start.27) | collective-permute-done | bytes 196640 | tf_op jit(solution)/shard_map/ppermute | solution.py:398
  181.2 1.6 mix.1
  (37 shorter events, 0.1 us)
Async XLA Ops:
  2.0 10.4 %copy-start = (bf16[2,6,512,512]{3,2,1,0:T(8,128)(2,1)S(1)}, bf16[2,6,512,512]{3,2,1,0:T(8,128)(2,1)}, u32[]{:S(2)}) copy-start(bf16[2,6,512,512]{3,2,1,0:T(8,128)(2,1)} %p_ref.9) | copy-start | bytes 18874372
  2.0 7.8 %collective-permute-start = (s32[2]{0:T(128)S(1)}, s32[2]{0:T(128)S(1)}, u32[]{:S(2)}, u32[]{:S(2)}) collective-permute-start(s32[2]{0:T(128)S(1)} %pad_add_fusion.place), channel_id=1, source_target_pairs={{0,1},{1,2},{2,3},{3,4},{4,5},{5,6},{6,7},{7,8},{8,9},{9,10},{10,1... | collective-permute-start | bytes 32 | tf_op jit(solution)/shard_map/ppermute | solution.py:377
  6.8 2.2 %copy-start.1 = (f32[2,512,1024]{2,1,0:T(8,128)S(1)}, f32[2,512,1024]{2,1,0:T(8,128)}, u32[]{:S(2)}) copy-start(f32[2,512,1024]{2,1,0:T(8,128)} %obj.3) | copy-start | bytes 12582916
  10.4 16.4 %collective-permute-start.1 = (f32[2,256,512]{2,1,0:T(8,128)S(1)}, f32[2,256,512]{2,1,0:T(8,128)S(1)}, u32[]{:S(2)}, u32[]{:S(2)}) collective-permute-start(f32[2,256,512]{2,1,0:T(8,128)S(1)} %rim_rows.1), channel_id=1, source_target_pairs={{1,0},{2,1},{3,2},{4,3},{5,4},{6,5},{7,6},{8,7},{9,8},{10,9},{11,1... | collective-permute-start | bytes 3145736 | tf_op jit(solution)/shard_map/ppermute | solution.py:377
  12.4 1.6 copy-start.3
  14.0 15.3 %copy-start.4 = (bf16[1024,1024]{1,0:T(8,128)(2,1)S(1)}, bf16[1024,1024]{1,0:T(8,128)(2,1)}, u32[]{:S(2)}) copy-start(bf16[1024,1024]{1,0:T(8,128)(2,1)} %constant.12.clone.table) | copy-start | bytes 6291460
  14.0 15.3 %copy-start.10 = (bf16[512,1024]{1,0:T(8,128)(2,1)S(1)}, bf16[512,1024]{1,0:T(8,128)(2,1)}, u32[]{:S(2)}) copy-start(bf16[512,1024]{1,0:T(8,128)(2,1)} %constant.13.clone.wt) | copy-start | bytes 3145732
  26.9 19.5 %collective-permute-start.2 = (f32[256,512]{1,0:T(8,128)S(1)}, f32[256,512]{1,0:T(8,128)S(1)}, u32[]{:S(2)}, u32[]{:S(2)}) collective-permute-start(f32[256,512]{1,0:T(8,128)S(1)} %get-tuple-element.99), channel_id=1, source_target_pairs={{0,64},{64,0},{1,65},{65,1},{2,66},{66,2},{3,67},{67,3},{4,68},{68... | collective-permute-start | bytes 1572872 | tf_op jit(solution)/shard_map/ppermute | solution.py:381
  29.3 10.2 %copy-start.9 = (bf16[512,1024]{1,0:T(8,128)(2,1)S(1)}, bf16[512,1024]{1,0:T(8,128)(2,1)}, u32[]{:S(2)}) copy-start(bf16[512,1024]{1,0:T(8,128)(2,1)} %constant.14.clone.wt) | copy-start | bytes 3145732
  38.9 14.3 %collective-permute-start.3 = (f32[256,512]{1,0:T(8,128)S(1)}, f32[256,512]{1,0:T(8,128)S(1)}, u32[]{:S(2)}, u32[]{:S(2)}) collective-permute-start(f32[256,512]{1,0:T(8,128)S(1)} %get-tuple-element.101.s0), channel_id=1, source_target_pairs={{0,64},{64,0},{1,65},{65,1},{2,66},{66,2},{3,67},{67,3},{4,68},{68... | collective-permute-start | bytes 1572872 | tf_op jit(solution)/shard_map/ppermute | solution.py:381
  39.5 13.7 %copy-start.5 = (bf16[1024,1024]{1,0:T(8,128)(2,1)S(1)}, bf16[1024,1024]{1,0:T(8,128)(2,1)}, u32[]{:S(2)}) copy-start(bf16[1024,1024]{1,0:T(8,128)(2,1)} %constant.15.clone.table) | copy-start | bytes 6291460
  39.5 13.7 %copy-start.6 = (f32[1,512,512]{2,1,0:T(8,128)S(1)}, f32[1,512,512]{2,1,0:T(8,128)}, u32[]{:S(2)}) copy-start(f32[1,512,512]{2,1,0:T(8,128)} %pat.3) | copy-start | bytes 3145732
  43.8 15.0 %collective-permute-start.4 = (f32[256,512]{1,0:T(8,128)S(1)}, f32[256,512]{1,0:T(8,128)S(1)}, u32[]{:S(2)}, u32[]{:S(2)}) collective-permute-start(f32[256,512]{1,0:T(8,128)S(1)} %get-tuple-element.104.s0), channel_id=1, source_target_pairs={{0,64},{64,0},{1,65},{65,1},{2,66},{66,2},{3,67},{67,3},{4,68},{68... | collective-permute-start | bytes 1572872 | tf_op jit(solution)/shard_map/ppermute | solution.py:381
  46.4 12.5 %copy-start.8 = (bf16[512,1024]{1,0:T(8,128)(2,1)S(1)}, bf16[512,1024]{1,0:T(8,128)(2,1)}, u32[]{:S(2)}) copy-start(bf16[512,1024]{1,0:T(8,128)(2,1)} %constant.16.clone.bt) | copy-start | bytes 3145732
  58.9 11.1 %copy-start.7 = (bf16[512,1024]{1,0:T(8,128)(2,1)S(1)}, bf16[512,1024]{1,0:T(8,128)(2,1)}, u32[]{:S(2)}) copy-start(bf16[512,1024]{1,0:T(8,128)(2,1)} %constant.17.clone.bt) | copy-start | bytes 3145732
  69.8 5.7 %collective-permute-start.5 = (f32[6,16,16,512]{3,2,1,0:T(8,128)S(1)}, f32[6,16,16,512]{3,2,1,0:T(8,128)S(1)}, u32[]{:S(2)}, u32[]{:S(2)}) collective-permute-start(f32[6,16,16,512]{3,2,1,0:T(8,128)S(1)} %get-tuple-element.113), channel_id=1, source_target_pairs={{0,1},{1,0},{2,3},{3,2},{4,5},{5,4},{6,7},{7,6},{8,9},{9,8},{10,11... | collective-permute-start | bytes 9437192 | tf_op jit(solution)/shard_map/ppermute | solution.py:381
  79.3 27.7 %collective-permute-start.9 = (f32[6,16,16,512]{3,2,1,0:T(8,128)S(1)}, f32[6,16,16,512]{3,2,1,0:T(8,128)S(1)}, u32[]{:S(2)}, u32[]{:S(2)}) collective-permute-start(f32[6,16,16,512]{3,2,1,0:T(8,128)S(1)} %get-tuple-element.129), channel_id=1, source_target_pairs={{0,1},{1,0},{2,3},{3,2},{4,5},{5,4},{6,7},{7,6},{8,9},{9,8},{10,11... | collective-permute-start | bytes 9437192 | tf_op jit(solution)/shard_map/ppermute | solution.py:381
  79.5 16.0 %collective-permute-start.6 = (f32[3,4,16,512]{3,2,1,0:T(8,128)S(1)}, f32[3,4,16,512]{3,2,1,0:T(8,128)S(1)}, u32[]{:S(2)}, u32[]{:S(2)}) collective-permute-start(f32[3,4,16,512]{3,2,1,0:T(8,128)S(1)} %get-tuple-element.122), channel_id=1, source_target_pairs={{0,16},{1,5},{4,20},{5,9},{8,24},{9,13},{12,28},{13,1},{16,32},{17... | collective-permute-start | bytes 1179656 | tf_op jit(solution)/shard_map/ppermute | solution.py:393
  87.9 7.6 %collective-permute-start.7 = (f32[3,4,16,512]{3,2,1,0:T(8,128)S(1)}, f32[3,4,16,512]{3,2,1,0:T(8,128)S(1)}, u32[]{:S(2)}, u32[]{:S(2)}) collective-permute-start(f32[3,4,16,512]{3,2,1,0:T(8,128)S(1)} %get-tuple-element.123), channel_id=1, source_target_pairs={{0,48},{1,13},{4,52},{5,1},{8,56},{9,5},{12,60},{13,9},{16,0},{17,... | collective-permute-start | bytes 1179656 | tf_op jit(solution)/shard_map/ppermute | solution.py:393
  90.0 15.4 %collective-permute-start.8 = (f32[2,8,16,512]{3,2,1,0:T(8,128)S(1)}, f32[2,8,16,512]{3,2,1,0:T(8,128)S(1)}, u32[]{:S(2)}, u32[]{:S(2)}) collective-permute-start(f32[2,8,16,512]{3,2,1,0:T(8,128)S(1)} %get-tuple-element.126.b0), channel_id=1, source_target_pairs={{0,64},{64,0},{1,65},{65,1},{2,66},{66,2},{3,67},{67,3},{4,68},{68... | collective-permute-start | bytes 1572872 | tf_op jit(solution)/shard_map/ppermute | solution.py:381
  95.6 24.3 %collective-permute-start.13 = (f32[2,3,4,16,512]{4,3,2,1,0:T(8,128)S(1)}, f32[2,3,4,16,512]{4,3,2,1,0:T(8,128)S(1)}, u32[]{:S(2)}, u32[]{:S(2)}) collective-permute-start(f32[2,3,4,16,512]{4,3,2,1,0:T(8,128)S(1)} %get-tuple-element.124), channel_id=1, source_target_pairs={{0,16},{1,5},{4,20},{5,9},{8,24},{9,13},{12,28},{13,1},{16,32},{17... | collective-permute-start | bytes 2359304 | tf_op jit(solution)/shard_map/ppermute | solution.py:393
  105.4 14.5 %collective-permute-start.12 = (f32[2,8,16,512]{3,2,1,0:T(8,128)S(1)}, f32[2,8,16,512]{3,2,1,0:T(8,128)S(1)}, u32[]{:S(2)}, u32[]{:S(2)}) collective-permute-start(f32[2,8,16,512]{3,2,1,0:T(8,128)S(1)} %get-tuple-element.133.t0), channel_id=1, source_target_pairs={{0,64},{64,0},{1,65},{65,1},{2,66},{66,2},{3,67},{67,3},{4,68},{68... | collective-permute-start | bytes 1572872 | tf_op jit(solution)/shard_map/ppermute | solution.py:381
  107.0 13.0 %collective-permute-start.14 = (f32[2,3,4,16,512]{4,3,2,1,0:T(8,128)S(1)}, f32[2,3,4,16,512]{4,3,2,1,0:T(8,128)S(1)}, u32[]{:S(2)}, u32[]{:S(2)}) collective-permute-start(f32[2,3,4,16,512]{4,3,2,1,0:T(8,128)S(1)} %get-tuple-element.136), channel_id=1, source_target_pairs={{0,48},{1,13},{4,52},{5,1},{8,56},{9,5},{12,60},{13,9},{16,0},{17,... | collective-permute-start | bytes 2359304 | tf_op jit(solution)/shard_map/ppermute | solution.py:393
  107.3 12.7 %collective-permute-start.10 = (f32[3,4,16,512]{3,2,1,0:T(8,128)S(1)}, f32[3,4,16,512]{3,2,1,0:T(8,128)S(1)}, u32[]{:S(2)}, u32[]{:S(2)}) collective-permute-start(f32[3,4,16,512]{3,2,1,0:T(8,128)S(1)} %get-tuple-element.130), channel_id=1, source_target_pairs={{0,16},{1,5},{4,20},{5,9},{8,24},{9,13},{12,28},{13,1},{16,32},{17... | collective-permute-start | bytes 1179656 | tf_op jit(solution)/shard_map/ppermute | solution.py:393
  108.8 13.5 %collective-permute-start.11 = (f32[3,4,16,512]{3,2,1,0:T(8,128)S(1)}, f32[3,4,16,512]{3,2,1,0:T(8,128)S(1)}, u32[]{:S(2)}, u32[]{:S(2)}) collective-permute-start(f32[3,4,16,512]{3,2,1,0:T(8,128)S(1)} %get-tuple-element.131), channel_id=1, source_target_pairs={{0,48},{1,13},{4,52},{5,1},{8,56},{9,5},{12,60},{13,9},{16,0},{17,... | collective-permute-start | bytes 1179656 | tf_op jit(solution)/shard_map/ppermute | solution.py:393
  122.4 15.5 %collective-permute-start.15 = (f32[2,3,4,16,512]{4,3,2,1,0:T(8,128)S(1)}, f32[2,3,4,16,512]{4,3,2,1,0:T(8,128)S(1)}, u32[]{:S(2)}, u32[]{:S(2)}) collective-permute-start(f32[2,3,4,16,512]{4,3,2,1,0:T(8,128)S(1)} %get-tuple-element.145), channel_id=1, source_target_pairs={{0,16},{1,5},{4,20},{5,9},{8,24},{9,13},{12,28},{13,1},{16,32},{17... | collective-permute-start | bytes 2359304 | tf_op jit(solution)/shard_map/ppermute | solution.py:393
  122.5 15.4 %collective-permute-start.16 = (f32[2,3,4,16,512]{4,3,2,1,0:T(8,128)S(1)}, f32[2,3,4,16,512]{4,3,2,1,0:T(8,128)S(1)}, u32[]{:S(2)}, u32[]{:S(2)}) collective-permute-start(f32[2,3,4,16,512]{4,3,2,1,0:T(8,128)S(1)} %get-tuple-element.146), channel_id=1, source_target_pairs={{0,48},{1,13},{4,52},{5,1},{8,56},{9,5},{12,60},{13,9},{16,0},{17,... | collective-permute-start | bytes 2359304 | tf_op jit(solution)/shard_map/ppermute | solution.py:393
  125.2 12.8 %collective-permute-start.17 = (f32[2,8,16,512]{3,2,1,0:T(8,128)S(1)}, f32[2,8,16,512]{3,2,1,0:T(8,128)S(1)}, u32[]{:S(2)}, u32[]{:S(2)}) collective-permute-start(f32[2,8,16,512]{3,2,1,0:T(8,128)S(1)} %get-tuple-element.147.b1), channel_id=1, source_target_pairs={{0,64},{64,0},{1,65},{65,1},{2,66},{66,2},{3,67},{67,3},{4,68},{68... | collective-permute-start | bytes 1572872 | tf_op jit(solution)/shard_map/ppermute | solution.py:381
  126.8 18.2 %collective-permute-start.22 = (f32[8,512]{1,0:T(8,128)S(1)}, f32[8,512]{1,0:T(8,128)S(1)}, u32[]{:S(2)}, u32[]{:S(2)}) collective-permute-start(f32[8,512]{1,0:T(8,128)S(1)} %brightest.1.near_max), channel_id=1, source_target_pairs={{0,1},{1,0},{2,3},{3,2},{4,5},{5,4},{6,7},{7,6},{8,9},{9,8},{10,11... | collective-permute-start | bytes 49160 | tf_op jit(solution)/shard_map/ppermute | solution.py:381
  138.0 16.0 %collective-permute-start.21 = (f32[2,8,16,512]{3,2,1,0:T(8,128)S(1)}, f32[2,8,16,512]{3,2,1,0:T(8,128)S(1)}, u32[]{:S(2)}, u32[]{:S(2)}) collective-permute-start(f32[2,8,16,512]{3,2,1,0:T(8,128)S(1)} %get-tuple-element.156.t1), channel_id=1, source_target_pairs={{0,64},{64,0},{1,65},{65,1},{2,66},{66,2},{3,67},{67,3},{4,68},{68... | collective-permute-start | bytes 1572872 | tf_op jit(solution)/shard_map/ppermute | solution.py:381
  139.7 8.9 %collective-permute-start.18 = (f32[2,2,3,16,512]{4,3,2,1,0:T(8,128)S(1)}, f32[2,2,3,16,512]{4,3,2,1,0:T(8,128)S(1)}, u32[]{:S(2)}, u32[]{:S(2)}) collective-permute-start(f32[2,2,3,16,512]{4,3,2,1,0:T(8,128)S(1)} %get-tuple-element.152), channel_id=1, source_target_pairs={{0,4},{1,17},{4,8},{5,21},{8,12},{9,25},{12,0},{13,29},{16,20},{17... | collective-permute-start | bytes 1179656 | tf_op jit(solution)/shard_map/ppermute | solution.py:393
  141.3 10.8 %collective-permute-start.19 = (f32[2,2,3,16,512]{4,3,2,1,0:T(8,128)S(1)}, f32[2,2,3,16,512]{4,3,2,1,0:T(8,128)S(1)}, u32[]{:S(2)}, u32[]{:S(2)}) collective-permute-start(f32[2,2,3,16,512]{4,3,2,1,0:T(8,128)S(1)} %get-tuple-element.153), channel_id=1, source_target_pairs={{0,12},{1,49},{4,0},{5,53},{8,4},{9,57},{12,8},{13,61},{16,28},{17... | collective-permute-start | bytes 1179656 | tf_op jit(solution)/shard_map/ppermute | solution.py:393
  143.2 10.8 %collective-permute-start.20 = (f32[2,2,3,16,512]{4,3,2,1,0:T(8,128)S(1)}, f32[2,2,3,16,512]{4,3,2,1,0:T(8,128)S(1)}, u32[]{:S(2)}, u32[]{:S(2)}) collective-permute-start(f32[2,2,3,16,512]{4,3,2,1,0:T(8,128)S(1)} %get-tuple-element.154), channel_id=1, source_target_pairs={{0,8},{1,33},{4,12},{5,37},{8,0},{9,41},{12,4},{13,45},{16,24},{17... | collective-permute-start | bytes 1179656 | tf_op jit(solution)/shard_map/ppermute | solution.py:393
  145.0 23.2 %collective-permute-start.24 = (f32[2,2,8,16,512]{4,3,2,1,0:T(8,128)S(1)}, f32[2,2,8,16,512]{4,3,2,1,0:T(8,128)S(1)}, u32[]{:S(2)}, u32[]{:S(2)}) collective-permute-start(f32[2,2,8,16,512]{4,3,2,1,0:T(8,128)S(1)} %over_sum.1), channel_id=1, source_target_pairs={{0,1},{1,2},{2,3},{3,4},{4,5},{5,6},{6,7},{7,8},{8,9},{9,10},{10,1... | collective-permute-start | bytes 3145736 | tf_op jit(solution)/shard_map/ppermute | solution.py:377
  154.0 14.1 %collective-permute-start.23 = (f32[2,2,3,8,512]{4,3,2,1,0:T(8,128)S(1)}, f32[2,2,3,8,512]{4,3,2,1,0:T(8,128)S(1)}, u32[]{:S(2)}, u32[]{:S(2)}) collective-permute-start(f32[2,2,3,8,512]{4,3,2,1,0:T(8,128)S(1)} %get-tuple-element.167), channel_id=1, source_target_pairs={{0,1},{1,0},{2,3},{3,2},{4,5},{5,4},{6,7},{7,6},{8,9},{9,8},{10,11... | collective-permute-start | bytes 589832 | tf_op jit(solution)/shard_map/ppermute | solution.py:381
  168.1 4.0 %copy-start.2 = (f32[2,512,1024]{2,1,0:T(8,128)S(1)}, f32[2,512,1024]{2,1,0:T(8,128)}, u32[]{:S(2)}) copy-start(f32[2,512,1024]{2,1,0:T(8,128)} %obj.3) | copy-start | bytes 12582916
  168.2 13.0 %copy-start.11 = (s32[12,12]{1,0:T(8,128)S(1)}, s32[12,12]{1,0:T(8,128)}, u32[]{:S(2)}) copy-start(s32[12,12]{1,0:T(8,128)} %w_ref.1) | copy-start | bytes 1732
  168.2 7.1 %collective-permute-start.25 = (f32[2,6,8,512]{3,2,1,0:T(8,128)S(1)}, f32[2,6,8,512]{3,2,1,0:T(8,128)S(1)}, u32[]{:S(2)}, u32[]{:S(2)}) collective-permute-start(f32[2,6,8,512]{3,2,1,0:T(8,128)S(1)} %get-tuple-element.173), channel_id=1, source_target_pairs={{0,2},{2,0},{64,66},{66,64},{1,3},{3,1},{65,67},{67,65},{4,6},{6,4... | collective-permute-start | bytes 589832 | tf_op jit(solution)/shard_map/ppermute | solution.py:398
  168.3 10.8 %collective-permute-start.26 = (f32[2,6,8,512]{3,2,1,0:T(8,128)S(1)}, f32[2,6,8,512]{3,2,1,0:T(8,128)S(1)}, u32[]{:S(2)}, u32[]{:S(2)}) collective-permute-start(f32[2,6,8,512]{3,2,1,0:T(8,128)S(1)} %get-tuple-element.172.mine), channel_id=1, source_target_pairs={{0,64},{2,66},{64,0},{66,2},{1,65},{3,67},{65,1},{67,3},{4,68},{6,... | collective-permute-start | bytes 589832 | tf_op jit(solution)/shard_map/ppermute | solution.py:398
  169.9 11.3 %collective-permute-start.27 = (f32[2,6,8,512]{3,2,1,0:T(8,128)S(1)}, f32[2,6,8,512]{3,2,1,0:T(8,128)S(1)}, u32[]{:S(2)}, u32[]{:S(2)}) collective-permute-start(f32[2,6,8,512]{3,2,1,0:T(8,128)S(1)} %get-tuple-element.173), channel_id=1, source_target_pairs={{0,66},{2,64},{64,2},{66,0},{1,67},{3,65},{65,3},{67,1},{4,70},{6,... | collective-permute-start | bytes 589832 | tf_op jit(solution)/shard_map/ppermute | solution.py:398

commit v5 on v4

--- a/solution.py
+++ b/solution.py
@@ -280,11 +280,11 @@
     )(pat, s0, s1, wave, table)[0]
 
 
-def gradients(core, block, bt, top, bot, patch_top, patch_bot, p_ref, keep_ref, send_ref, gtop, gbot, back_s, m):
+def gradients(core, block, bt, top, bot, patch_top, patch_bot, p_ref, keep_ref, send_ref, grad, back_s, m):
     back_s[...] = jnp.dot(bt[:, :N], top[m], preferred_element_type=f32) + jnp.dot(
         bt[:, N:], bot[m], preferred_element_type=f32
     )
-    for patch, g_ref, base in ((patch_top, gtop, 0), (patch_bot, gbot, 8)):
+    for patch, side, base in ((patch_top, 0, 0), (patch_bot, 1, 8)):
 
         def one(i):
             g = i + base
@@ -295,8 +295,8 @@
             pr, pi, xr, xi = exit_rows(p_ref, m, full, o_r, o_i)
             rr = back_s[at(g, 16), :] - xr.astype(f32)
             ri = back_s[pl.ds(pl.multiple_of(g * 16 + H, 16), 16), :] - xi.astype(f32)
-            g_ref[0, i] += pr * rr + pi * ri
-            g_ref[1, i] += pr * ri - pi * rr
+            grad[side, 0, i] += pr * rr + pi * ri
+            grad[side, 1, i] += pr * ri - pi * rr
             st0 = o_r * rr + o_i * ri
             st1 = o_r * ri - o_i * rr
             turned_g = (g % 4) * 4 + g // 4
@@ -308,19 +308,18 @@
 
 UNROLL = 8
 LIMIT = 4
-STAGE = pl.CostEstimate(flops=int(5e9), transcendentals=0, bytes_accessed=int(15e6))
-GRADS = [shape(2, 8, 16, N)] * 2
-
-
-def first_block_body(pat, s0, s1, wave_ref, table, bt, top, ptop, pbot, p_ref, half_ref, keep, send, gtop, gbot, scale_s, x_s, back_s):
+STAGE = pl.CostEstimate(flops=int(5 * 1e9), transcendentals=0, bytes_accessed=int(5 * 3e6))
+GRADS = [shape(2, 2, 8, 16, N)]
+
+
+def first_block_body(pat, s0, s1, wave_ref, table, bt, top, ptop, pbot, p_ref, half_ref, keep, send, grad, scale_s, x_s, back_s):
     set_scale(pat, H, s0, s1, scale_s)
-    gtop[...] = jnp.zeros_like(gtop)
-    gbot[...] = jnp.zeros_like(gbot)
+    grad[...] = jnp.zeros_like(grad)
 
     def step(m0):
         fixed_half(wave_ref, table, half_ref, scale_s, x_s, m0)
         for j in range(PAIR):
-            gradients(lax.axis_index("core"), 0, bt, top, half_ref, ptop, pbot, p_ref, keep, send, gtop, gbot, back_s, m0 + j)
+            gradients(lax.axis_index("core"), 0, bt, top, half_ref, ptop, pbot, p_ref, keep, send, grad, back_s, m0 + j)
 
     pairs(wave_ref.shape[0], step)
 
@@ -339,19 +338,18 @@
 
 def second_block(back_rows, top, bot, ptop, pbot, probe, first, count, grads=None):
     nm = top.shape[0]
-    half = [shape(2, 8, 16, N)] * 2
+    half = GRADS
 
     def body(bt, top, bot, ptop, pbot, p_ref, *refs):
         if grads is None:
-            keep, send, gtop, gbot, back_s = refs
-            gtop[...] = jnp.zeros_like(gtop)
-            gbot[...] = jnp.zeros_like(gbot)
+            keep, send, grad, back_s = refs
+            grad[...] = jnp.zeros_like(grad)
         else:
-            kin, sin, tin, bin_, keep, send, gtop, gbot, back_s = refs
+            keep, send, grad, back_s = refs[3:]
         loop(
             count,
             lambda m: gradients(
-                lax.axis_index("core"), 1, bt, top, bot, ptop, pbot, p_ref, keep, send, gtop, gbot, back_s, m + first
+                lax.axis_index("core"), 1, bt, top, bot, ptop, pbot, p_ref, keep, send, grad, back_s, m + first
             ),
         )
 
@@ -531,7 +529,7 @@
     return local_call(mix_body, "mix", [SCALARS] + [LOCAL] * 4, outs, [], LIMIT)(mixing, mine, b, c, d)[0]
 
 
-def object_body(place, before, near_max, far_max, obj, t0, t0f, t1, t1f, b0, b0f, b1, b1f, over, out, new, sems):
+def object_body(place, before, near_max, far_max, obj, g0, g0f, g1, g1f, over, out, new, sems):
     shift, col = place[0], pl.multiple_of(place[1] * H, H)
     over_shift, over_col = before[0], pl.multiple_of(before[1] * H, H)
     largest = jnp.max(jnp.maximum(near_max[...], far_max[...]))
@@ -558,13 +556,13 @@
 
         @pl.when(shift == half)
         def _():
-            add(col, (t0, t0f), (t1, t1f))
+            add(col, (g0.at[0], g0f.at[0]), (g1.at[0], g1f.at[0]))
 
         if half == 1:
 
             @pl.when(shift == 0)
             def _():
-                add(col, (b0, b0f), (b1, b1f))
+                add(col, (g0.at[1], g0f.at[1]), (g1.at[1], g1f.at[1]))
 
         else:
 
@@ -582,7 +580,7 @@
 def object_update(place, before, near_max, far_max, obj, pieces, over):
     return pl.pallas_call(
         object_body,
-        in_specs=[SCALARS] * 2 + [LOCAL] * 12,
+        in_specs=[SCALARS] * 2 + [LOCAL] * 8,
         out_specs=FAR,
         out_shape=shape(2, N, 4 * H),
         scratch_shapes=[pltpu.VMEM((2, N, 4 * H), f32), pltpu.SemaphoreType.DMA((2,))],
@@ -591,13 +589,14 @@
     )(place, before, near_max, far_max, obj, *pieces, over)
 
 
-def over_body(b0, b0f, b1, b1f, out):
-    out[0] = b0[...] + b0f[...]
-    out[1] = b1[...] + b1f[...]
-
-
-def over_sum(b0, b0f, b1, b1f):
-    return local_call(over_body, "over_sum", [LOCAL] * 4, [shape(2, 2, 8, 16, N)], [], LIMIT, cost=STAGE)(b0, b0f, b1, b1f)[0]
+def over_body(g0, g0f, g1, g1f, out):
+    out[0] = g0[1] + g0f[1]
+    out[1] = g1[1] + g1f[1]
+
+
+def over_sum(*pieces):
+    outs = [shape(2, 2, 8, 16, N)]
+    return local_call(over_body, "over_sum", [LOCAL] * 4, outs, [], LIMIT, cost=STAGE)(*pieces)[0]
 
 
 def tied(*values):
@@ -622,44 +621,39 @@
     far_bot = swapped(sum_bot, "mode")
     wave_top, far_light = tied(wave_top, far_light)
     fixed = fixed_top(patterns, sum_top, far_top, wave_top, plus)
-    low, keep0, send0, top0, bot0 = first_block(
+    low, keep0, send0, grad0 = first_block(
         patterns, sum_bot, far_bot, wave_bot, plus, back_rows0, fixed, patch_top, patch_bot, probe
     )
     recv0 = swapped(send0, "core")
-    bot0_far = swapped(bot0, "mode")
-    half_max = brightest(own_light, far_light)
-    far_max = swapped(half_max, "core")
+    grad0_far = swapped(grad0, "mode")
     part1 = second_block(back_rows1, fixed, low, patch_top, patch_bot, probe, 0, 3)
     own0, near0, back0, far0a, far0b = core_add(keep0, recv0)
     ra0, rb0 = turned(far0a, 1, True), turned(far0b, -1, True)
     *part1, near0 = tied(*part1, near0)
-    keep1, send1, top1, bot1 = second_block(back_rows1, fixed, low, patch_top, patch_bot, probe, 3, 3, part1)
+    keep1, send1, grad1 = second_block(back_rows1, fixed, low, patch_top, patch_bot, probe, 3, 3, part1)
     recv1 = swapped(send1, "core")
     near0, back0 = relay_add(near0, back0, ra0, rb0)
-    top0_next, bot0_far, _ = tied(top0, bot0_far, near0)
-    top0_far = swapped(top0_next, "mode")
-    bot1_next, top0_far = tied(bot1, top0_far)
-    bot1_far = swapped(bot1_next, "mode")
-    keep1, _, bot0_far = tied(keep1, near0, bot0_far)
+    keep1, _ = tied(keep1, near0)
     own1, near1, back1, far1a, far1b = core_add(keep1, recv1)
     ra1, rb1 = turned(far1a, 1, True), turned(far1b, -1, True)
     plane0 = (own0, turned(near0, 1, True), turned(back0, -1, True))
-    ra1, rb1, top0_far, *plane0 = tied(ra1, rb1, top0_far, *plane0)
+    ra1, rb1, grad0_far, *plane0 = tied(ra1, rb1, grad0_far, *plane0)
+    grad1_next, _ = tied(grad1, grad0_far)
+    grad1_far = swapped(grad1_next, "mode")
     near1, back1 = relay_add(near1, back1, ra1, rb1)
     plane1 = (own1, turned(near1, 1, True), turned(back1, -1, True))
-    *plane1, bot1_far = tied(*plane1, bot1_far)
-    top1_next, _ = tied(top1, plane1[1])
-    top1_far = swapped(top1_next, "mode")
-    over = along(over_sum(bot0, bot0_far, bot1, bot1_far), 1)
+    half_max = brightest(own_light, far_light)
+    far_max = swapped(half_max, "core")
     line = plane_add((plane0, plane1))
     line = [line[0]] + [turned(line[r], r, False) for r in (1, 3, 2)]
-    *line, top1_far, far_max = tied(*line, top1_far, far_max)
+    *line, far_max, grad1_far = tied(*line, far_max, grad1_far)
+    over = along(over_sum(grad0, grad0_far, grad1, grad1_far), 1)
     keep, send = line_add(line)
     mine, other = pixel_step(keep, swapped(send, "core"), rows)
-    mine, other, over = tied(mine, other, over)
     probe_new = mix(mixing, mine, across(other, 0, 1), across(mine, 1, 0), across(other, 1, 1))
-    pieces = (top0, top0_far, top1, top1_far, bot0, bot0_far, bot1, bot1_far)
-    object_new = object_update(place, before, half_max, far_max, object_field, pieces, over)
+    object_new = object_update(
+        place, before, half_max, far_max, object_field, (grad0, grad0_far, grad1, grad1_far), over
+    )
     return object_new, probe_new
 
 

time: 184 us -> 176 us (0.957)
  starting transfers between devices: 63.2 us -> 47.4 us
  waiting for transfers between devices: 63.5 us -> 72.1 us
    ppermute x11 -> x9, starting transfers between devices: 27.4 us -> 11.3 us  [swapped(): return lax.ppermute(value, axis, [(0, 1), (1, 0)])]
    ppermute x3, waiting for transfers between devices: 5.9 us -> 16.3 us  [across(): return lax.ppermute(value, ('mode', 'x'), pairs)]
    ppermute x11 -> x9, waiting for transfers between devices: 38.2 us -> 36.7 us  [swapped(): return lax.ppermute(value, axis, [(0, 1), (1, 0)])]
  transfers between devices with their start and end apart: 28 -> 26, of which waited for: 15 -> 12; matrix products, arithmetic and copies ran while one was open for 0% -> 0% of each run, Pallas kernels for 18% -> 18%
where the time goes in v5:
time: 176 us
  waiting for transfers between devices  72.1 us (41%)
  Pallas kernels  49.8 us (28%)
  starting transfers between devices  47.4 us (27%)
  local copies, waits for them, and re-layouts  3.81 us (2%)
  between operations  2.33 us (1%)
    pallas_call x19, Pallas kernels, call(): pl.pallas_call(body, in_specs=ins, out_specs=[LOCAL] * len(outs), out_sha...  46.7 us
    ppermute x9, waiting for transfers between devices, swapped(): return lax.ppermute(value, axis, [(0, 1), (1, 0)])  36.7 us
    ppermute x11, starting transfers between devices, turned(): return lax.ppermute(value, RING, pairs)  22 us
    ppermute x3, waiting for transfers between devices, across(): return lax.ppermute(value, ('mode', 'x'), pairs)  16.3 us
    ppermute x11, waiting for transfers between devices, turned(): return lax.ppermute(value, RING, pairs)  12 us
    ppermute x9, starting transfers between devices, swapped(): return lax.ppermute(value, axis, [(0, 1), (1, 0)])  11.3 us
    ppermute x3, starting transfers between devices, along(): return lax.ppermute(value, SCAN, [(i, i + steps) for i in range(lo, hi)])  10.1 us
    ppermute x3, waiting for transfers between devices, along(): return lax.ppermute(value, SCAN, [(i, i + steps) for i in range(lo, hi)])  7.14 us
  transfers between devices with their start and end apart: 26, of which 12 were waited for; matrix products, arithmetic and copies ran while one was open for 0% of the time, Pallas kernels for 18%

profile of v5, /device:TPU:1, one launch (start us, length us, event | category | flops | bytes accessed | tf_op | source)
XLA Modules:
  0.0 175.6 jit_solution(14127726779961754954)
XLA Ops:
  1.9 0.1 pad_add_fusion.place
  2.0 4.8 %collective-permute-start = (s32[2]{0:T(128)S(1)}, s32[2]{0:T(128)S(1)}, u32[]{:S(2)}, u32[]{:S(2)}) collective-permute-start(s32[2]{0:T(128)S(1)} %pad_add_fusion.place), channel_id=1, source_target_pairs={{0,1},{1,2},{2,3},{3,4},{4,5},{5,6},{6,7},{7,8},{8,9},{9,10},{10,1... | collective-permute-start | bytes 32 | tf_op jit(solution)/shard_map/ppermute | solution.py:375
  6.8 0.0 copy-start.1
  6.8 2.2 %copy-done.1 = f32[2,512,1024]{2,1,0:T(8,128)S(1)} copy-done((f32[2,512,1024]{2,1,0:T(8,128)S(1)}, f32[2,512,1024]{2,1,0:T(8,128)}, u32[]{:S(2)}) %copy-start.1) | copy-done | bytes 4194328
  9.0 0.8 own_rows.1
  9.8 0.6 rim_rows.1
  10.4 1.9 %collective-permute-start.1 = (f32[2,256,512]{2,1,0:T(8,128)S(1)}, f32[2,256,512]{2,1,0:T(8,128)S(1)}, u32[]{:S(2)}, u32[]{:S(2)}) collective-permute-start(f32[2,256,512]{2,1,0:T(8,128)S(1)} %rim_rows.1), channel_id=1, source_target_pairs={{1,0},{2,1},{3,2},{4,3},{5,4},{6,5},{7,6},{8,7},{9,8},{10,9},{11,1... | collective-permute-start | bytes 3145736 | tf_op jit(solution)/shard_map/ppermute | solution.py:375
  12.4 0.0 copy-start.3
  12.4 1.6 copy-done.3
  14.0 5.7 %top_half.1 = (bf16[6,512,512]{2,1,0:T(8,128)(2,1)S(1)}, f32[256,512]{1,0:T(8,128)S(1)}, f32[256,512]{1,0:T(8,128)S(1)}, f32[2,6,8,512]{3,2,1,0:T(8,128)S(1)}) custom-call(f32[2,256,512]{2,1,0:T(8,128)S(1)} %get-tuple-element.74.patch_ref.ptop, bf16[2,6,512,512]{3,2,1,0:T(8,128)(2,1)S(1)} %copy-done, bf16[1024,1024]{1,0:T(8,128)(2,1)S(1)} %copy-done.3), custom_call_target="tpu_custom_call" | custom-call | tf_op jit(solution)/shard_map/top_half/pallas_call | solution.py:57
  19.7 7.1 %collective-permute-done.1.rim = f32[2,256,512]{2,1,0:T(8,128)S(1)} collective-permute-done((f32[2,256,512]{2,1,0:T(8,128)S(1)}, f32[2,256,512]{2,1,0:T(8,128)S(1)}, u32[]{:S(2)}, u32[]{:S(2)}) %collective-permute-start.1) | collective-permute-done | bytes 1048608 | tf_op jit(solution)/shard_map/ppermute | solution.py:375
  26.9 2.5 %collective-permute-start.2 = (f32[256,512]{1,0:T(8,128)S(1)}, f32[256,512]{1,0:T(8,128)S(1)}, u32[]{:S(2)}, u32[]{:S(2)}) collective-permute-start(f32[256,512]{1,0:T(8,128)S(1)} %get-tuple-element.83), channel_id=1, source_target_pairs={{0,64},{64,0},{1,65},{65,1},{2,66},{66,2},{3,67},{67,3},{4,68},{68... | collective-permute-start | bytes 1572872 | tf_op jit(solution)/shard_map/ppermute | solution.py:379
  29.3 9.6 %bottom_half.1 = (bf16[6,512,512]{2,1,0:T(8,128)(2,1)S(1)}, f32[2,256,512]{2,1,0:T(8,128)S(1)}, f32[6,512,512]{2,1,0:T(8,128)S(1)}, f32[256,512]{1,0:T(8,128)S(1)}) custom-call(s32[2]{0:T(128)S(1)} %pad_add_fusion.place, f32[2,256,512]{2,1,0:T(8,128)S(1)} %get-tuple-element.76.own, f32[2,256,512]{2,1,0:T(8,128)S(1)} %collective-permute-done.1.rim, ...), custom_call_target="tpu_custom_call" | custom-call | tf_op jit(solution)/shard_map/bottom_half/pallas_call | solution.py:57
  38.9 0.6 collective-permute-start.3
  39.5 4.3 %low_wave.1 = (f32[6,512,512]{2,1,0:T(8,128)S(1)}, f32[256,512]{1,0:T(8,128)S(1)}) custom-call(bf16[512,1024]{1,0:T(8,128)(2,1)S(1)} %copy-done.9, bf16[6,512,512]{2,1,0:T(8,128)(2,1)S(1)} %get-tuple-element.81.top, bf16[6,512,512]{2,1,0:T(8,128)(2,1)S(1)} %get-tuple-element.87.bot), custom_call_target="tpu_custom_call" | custom-call | tf_op jit(solution)/shard_map/low_wave/pallas_call | solution.py:57
  43.8 2.5 %collective-permute-start.4 = (f32[256,512]{1,0:T(8,128)S(1)}, f32[256,512]{1,0:T(8,128)S(1)}, u32[]{:S(2)}, u32[]{:S(2)}) collective-permute-start(f32[256,512]{1,0:T(8,128)S(1)} %get-tuple-element.88.s0), channel_id=1, source_target_pairs={{0,64},{64,0},{1,65},{65,1},{2,66},{66,2},{3,67},{67,3},{4,68},{68... | collective-permute-start | bytes 1572872 | tf_op jit(solution)/shard_map/ppermute | solution.py:379
  46.4 0.0 collective-permute-done.2.far
  46.4 6.9 %collective-permute-done.3.s1 = f32[256,512]{1,0:T(8,128)S(1)} collective-permute-done((f32[256,512]{1,0:T(8,128)S(1)}, f32[256,512]{1,0:T(8,128)S(1)}, u32[]{:S(2)}, u32[]{:S(2)}) %collective-permute-start.3) | collective-permute-done | bytes 524320 | tf_op jit(solution)/shard_map/ppermute | solution.py:379
  53.2 4.8 %fixed_top.1.top = bf16[6,512,512]{2,1,0:T(8,128)(2,1)S(1)} custom-call(f32[1,512,512]{2,1,0:T(8,128)S(1)} %copy-done.6, f32[256,512]{1,0:T(8,128)S(1)} %get-tuple-element.85.s0, f32[256,512]{1,0:T(8,128)S(1)} %collective-permute-done.3.s1, f32[6,512,512]{2,1,0:T(8,128)S(1)} %get-tuple-element.86.wave_ref, bf16[1024,1024]{1,0:T(8,128)(2,1)S(1)} %copy-done.5), custom_call_target="tpu_custom_call" | custom-call | tf_op jit(solution)/shard_map/fixed_top/pallas_call | solution.py:57
  58.1 0.8 collective-permute-done.4.s1
  58.9 11.0 %first_block.1 = (bf16[6,512,512]{2,1,0:T(8,128)(2,1)S(1)}, f32[6,16,16,512]{3,2,1,0:T(8,128)S(1)}, f32[6,16,16,512]{3,2,1,0:T(8,128)S(1)}, f32[2,2,8,16,512]{4,3,2,1,0:T(8,128)S(1)}) custom-call(f32[1,512,512]{2,1,0:T(8,128)S(1)} %copy-done.6, f32[256,512]{1,0:T(8,128)S(1)} %get-tuple-element.88.s0, f32[256,512]{1,0:T(8,128)S(1)} %collective-permute-done.4.s1, ...), custom_call_target="tpu_custom_call" | custom-call | tf_op jit(solution)/shard_map/first_block/pallas_call | solution.py:57
  69.8 0.1 collective-permute-start.5
  69.9 3.4 %second_block.2 = (f32[6,16,16,512]{3,2,1,0:T(8,128)S(1)}, f32[6,16,16,512]{3,2,1,0:T(8,128)S(1)}, f32[2,2,8,16,512]{4,3,2,1,0:T(8,128)S(1)}) custom-call(bf16[512,1024]{1,0:T(8,128)(2,1)S(1)} %copy-done.7, bf16[6,512,512]{2,1,0:T(8,128)(2,1)S(1)} %fixed_top.1.top, bf16[6,512,512]{2,1,0:T(8,128)(2,1)S(1)} %get-tuple-element.91.bot, ...), custom_call_target="tpu_custom_call" | custom-call | tf_op jit(solution)/shard_map/second_block/pallas_call | solution.py:57
  73.3 2.3 %collective-permute-done.5.recv = f32[6,16,16,512]{3,2,1,0:T(8,128)S(1)} collective-permute-done((f32[6,16,16,512]{3,2,1,0:T(8,128)S(1)}, f32[6,16,16,512]{3,2,1,0:T(8,128)S(1)}, u32[]{:S(2)}, u32[]{:S(2)}) %collective-permute-start.5) | collective-permute-done | bytes 3145760 | tf_op jit(solution)/shard_map/ppermute | solution.py:379
  75.6 0.3 core_add.2
  75.9 3.3 %second_block.3 = (f32[6,16,16,512]{3,2,1,0:T(8,128)S(1)}, f32[6,16,16,512]{3,2,1,0:T(8,128)S(1)}, f32[2,2,8,16,512]{4,3,2,1,0:T(8,128)S(1)}) custom-call(bf16[512,1024]{1,0:T(8,128)(2,1)S(1)} %copy-done.7, bf16[6,512,512]{2,1,0:T(8,128)(2,1)S(1)} %fixed_top.1.top, ...), custom_call_target="tpu_custom_call", output_to_operand_aliasing={{0}: (6, {}), {1}: (7, {}), {2}: (8, {})} | custom-call | tf_op jit(solution)/shard_map/second_block/pallas_call | solution.py:57
  79.2 0.2 collective-permute-start.8
  79.4 8.4 %collective-permute-start.6 = (f32[3,4,16,512]{3,2,1,0:T(8,128)S(1)}, f32[3,4,16,512]{3,2,1,0:T(8,128)S(1)}, u32[]{:S(2)}, u32[]{:S(2)}) collective-permute-start(f32[3,4,16,512]{3,2,1,0:T(8,128)S(1)} %get-tuple-element.104), channel_id=1, source_target_pairs={{0,16},{1,5},{4,20},{5,9},{8,24},{9,13},{12,28},{13,1},{16,32},{17... | collective-permute-start | bytes 1179656 | tf_op jit(solution)/shard_map/ppermute | solution.py:391
  87.8 2.1 %collective-permute-start.7 = (f32[3,4,16,512]{3,2,1,0:T(8,128)S(1)}, f32[3,4,16,512]{3,2,1,0:T(8,128)S(1)}, u32[]{:S(2)}, u32[]{:S(2)}) collective-permute-start(f32[3,4,16,512]{3,2,1,0:T(8,128)S(1)} %get-tuple-element.105), channel_id=1, source_target_pairs={{0,48},{1,13},{4,52},{5,1},{8,56},{9,5},{12,60},{13,9},{16,0},{17,... | collective-permute-start | bytes 1179656 | tf_op jit(solution)/shard_map/ppermute | solution.py:391
  89.9 1.6 collective-permute-start.11
  91.5 3.9 %collective-permute-done.6.ra = f32[3,4,16,512]{3,2,1,0:T(8,128)S(1)} collective-permute-done((f32[3,4,16,512]{3,2,1,0:T(8,128)S(1)}, f32[3,4,16,512]{3,2,1,0:T(8,128)S(1)}, u32[]{:S(2)}, u32[]{:S(2)}) %collective-permute-start.6) | collective-permute-done | bytes 393248 | tf_op jit(solution)/shard_map/ppermute | solution.py:391
  95.4 0.1 relay_add.2
  95.5 1.0 collective-permute-start.12
  96.6 1.8 %collective-permute-start.13 = (f32[2,3,4,16,512]{4,3,2,1,0:T(8,128)S(1)}, f32[2,3,4,16,512]{4,3,2,1,0:T(8,128)S(1)}, u32[]{:S(2)}, u32[]{:S(2)}) collective-permute-start(f32[2,3,4,16,512]{4,3,2,1,0:T(8,128)S(1)} %get-tuple-element.113), channel_id=1, source_target_pairs={{0,48},{1,13},{4,52},{5,1},{8,56},{9,5},{12,60},{13,9},{16,0},{17,... | collective-permute-start | bytes 2359304 | tf_op jit(solution)/shard_map/ppermute | solution.py:391
  98.4 0.0 collective-permute-done.8.recv
  98.4 0.3 core_add.3
  98.7 0.1 collective-permute-start.9
  98.8 2.7 %collective-permute-start.10 = (f32[3,4,16,512]{3,2,1,0:T(8,128)S(1)}, f32[3,4,16,512]{3,2,1,0:T(8,128)S(1)}, u32[]{:S(2)}, u32[]{:S(2)}) collective-permute-start(f32[3,4,16,512]{3,2,1,0:T(8,128)S(1)} %get-tuple-element.110), channel_id=1, source_target_pairs={{0,48},{1,13},{4,52},{5,1},{8,56},{9,5},{12,60},{13,9},{16,0},{17,... | collective-permute-start | bytes 1179656 | tf_op jit(solution)/shard_map/ppermute | solution.py:391
  101.4 15.1 %collective-permute-done.11.g0f = f32[2,2,8,16,512]{4,3,2,1,0:T(8,128)S(1)} collective-permute-done((f32[2,2,8,16,512]{4,3,2,1,0:T(8,128)S(1)}, f32[2,2,8,16,512]{4,3,2,1,0:T(8,128)S(1)}, u32[]{:S(2)}, u32[]{:S(2)}) %collective-permute-start.11) | collective-permute-done | bytes 1048608 | tf_op jit(solution)/shard_map/ppermute | solution.py:379
  116.6 0.1 relay_add.3
  116.7 0.1 collective-permute-start.14
  116.8 2.7 %collective-permute-start.15 = (f32[2,3,4,16,512]{4,3,2,1,0:T(8,128)S(1)}, f32[2,3,4,16,512]{4,3,2,1,0:T(8,128)S(1)}, u32[]{:S(2)}, u32[]{:S(2)}) collective-permute-start(f32[2,3,4,16,512]{4,3,2,1,0:T(8,128)S(1)} %get-tuple-element.123), channel_id=1, source_target_pairs={{0,48},{1,13},{4,52},{5,1},{8,56},{9,5},{12,60},{13,9},{16,0},{17,... | collective-permute-start | bytes 2359304 | tf_op jit(solution)/shard_map/ppermute | solution.py:391
  119.5 1.6 collective-permute-start.20
  121.0 8.1 %collective-permute-done.14.refs_4_ = f32[2,3,4,16,512]{4,3,2,1,0:T(8,128)S(1)} collective-permute-done((f32[2,3,4,16,512]{4,3,2,1,0:T(8,128)S(1)}, f32[2,3,4,16,512]{4,3,2,1,0:T(8,128)S(1)}, u32[]{:S(2)}, u32[]{:S(2)}) %collective-permute-start.14) | collective-permute-done | bytes 786464 | tf_op jit(solution)/shard_map/ppermute | solution.py:391
  129.1 0.2 plane_add.1
  129.4 0.1 collective-permute-start.16
  129.5 2.6 %collective-permute-start.17 = (f32[2,2,3,16,512]{4,3,2,1,0:T(8,128)S(1)}, f32[2,2,3,16,512]{4,3,2,1,0:T(8,128)S(1)}, u32[]{:S(2)}, u32[]{:S(2)}) collective-permute-start(f32[2,2,3,16,512]{4,3,2,1,0:T(8,128)S(1)} %get-tuple-element.126), channel_id=1, source_target_pairs={{0,12},{1,49},{4,0},{5,53},{8,4},{9,57},{12,8},{13,61},{16,28},{17... | collective-permute-start | bytes 1179656 | tf_op jit(solution)/shard_map/ppermute | solution.py:391
  132.1 0.5 collective-permute-start.18
  132.6 0.2 brightest.1.near_max
  132.8 2.2 %collective-permute-start.19 = (f32[8,512]{1,0:T(8,128)S(1)}, f32[8,512]{1,0:T(8,128)S(1)}, u32[]{:S(2)}, u32[]{:S(2)}) collective-permute-start(f32[8,512]{1,0:T(8,128)S(1)} %brightest.1.near_max), channel_id=1, source_target_pairs={{0,1},{1,0},{2,3},{3,2},{4,5},{5,4},{6,7},{7,6},{8,9},{9,8},{10,11... | collective-permute-start | bytes 49160 | tf_op jit(solution)/shard_map/ppermute | solution.py:379
  135.0 0.8 collective-permute-done.19.far_max
  135.8 8.8 %collective-permute-done.20.g1f = f32[2,2,8,16,512]{4,3,2,1,0:T(8,128)S(1)} collective-permute-done((f32[2,2,8,16,512]{4,3,2,1,0:T(8,128)S(1)}, f32[2,2,8,16,512]{4,3,2,1,0:T(8,128)S(1)}, u32[]{:S(2)}, u32[]{:S(2)}) %collective-permute-start.20) | collective-permute-done | bytes 1048608 | tf_op jit(solution)/shard_map/ppermute | solution.py:379
  144.6 0.1 over_sum.1
  144.7 3.4 %collective-permute-start.21 = (f32[2,2,8,16,512]{4,3,2,1,0:T(8,128)S(1)}, f32[2,2,8,16,512]{4,3,2,1,0:T(8,128)S(1)}, u32[]{:S(2)}, u32[]{:S(2)}) collective-permute-start(f32[2,2,8,16,512]{4,3,2,1,0:T(8,128)S(1)} %over_sum.1), channel_id=1, source_target_pairs={{0,1},{1,2},{2,3},{3,4},{4,5},{5,6},{6,7},{7,8},{8,9},{9,10},{10,1... | collective-permute-start | bytes 3145736 | tf_op jit(solution)/shard_map/ppermute | solution.py:375
  148.2 0.1 line_add.1
  148.3 0.1 collective-permute-start.22
  148.4 2.0 %collective-permute-done.22 = f32[2,2,3,8,512]{4,3,2,1,0:T(8,128)S(1)} collective-permute-done((f32[2,2,3,8,512]{4,3,2,1,0:T(8,128)S(1)}, f32[2,2,3,8,512]{4,3,2,1,0:T(8,128)S(1)}, u32[]{:S(2)}, u32[]{:S(2)}) %collective-permute-start.22) | collective-permute-done | bytes 196640 | tf_op jit(solution)/shard_map/ppermute | solution.py:379
  150.4 0.4 collective-permute-start.23
  150.9 1.9 %collective-permute-start.24 = (f32[2,6,8,512]{3,2,1,0:T(8,128)S(1)}, f32[2,6,8,512]{3,2,1,0:T(8,128)S(1)}, u32[]{:S(2)}, u32[]{:S(2)}) collective-permute-start(f32[2,6,8,512]{3,2,1,0:T(8,128)S(1)} %get-tuple-element.140.mine), channel_id=1, source_target_pairs={{0,64},{2,66},{64,0},{66,2},{1,65},{3,67},{65,1},{67,3},{4,68},{6,... | collective-permute-start | bytes 589832 | tf_op jit(solution)/shard_map/ppermute | solution.py:396
  152.7 1.6 collective-permute-start.25
  154.4 12.6 %collective-permute-done.23.b = f32[2,6,8,512]{3,2,1,0:T(8,128)S(1)} collective-permute-done((f32[2,6,8,512]{3,2,1,0:T(8,128)S(1)}, f32[2,6,8,512]{3,2,1,0:T(8,128)S(1)}, u32[]{:S(2)}, u32[]{:S(2)}) %collective-permute-start.23) | collective-permute-done | bytes 196640 | tf_op jit(solution)/shard_map/ppermute | solution.py:396
  167.0 3.6 %collective-permute-done.24.c = f32[2,6,8,512]{3,2,1,0:T(8,128)S(1)} collective-permute-done((f32[2,6,8,512]{3,2,1,0:T(8,128)S(1)}, f32[2,6,8,512]{3,2,1,0:T(8,128)S(1)}, u32[]{:S(2)}, u32[]{:S(2)}) %collective-permute-start.24) | collective-permute-done | bytes 196640 | tf_op jit(solution)/shard_map/ppermute | solution.py:396
  170.7 1.6 mix.1
  172.3 3.1 %object_update.1 = f32[2,512,1024]{2,1,0:T(8,128)} custom-call(s32[2]{0:T(128)S(1)} %pad_add_fusion.place, s32[2]{0:T(128)S(1)} %collective-permute-done.place.before, f32[8,512]{1,0:T(8,128)S(1)} %brightest.1.near_max, f32[8,512]{1,0:T(8,128)S(1)} %collective-permute-done.19.far_max, f32[2,512,1024]{2,1,0:T(8,128)S(1)} %copy-done.2, ...), custom_call_target="tpu_custom_call" | custom-call | tf_op jit(solution)/shard_map/object_update/pallas_call | solution.py:581
  (33 shorter events, 0.1 us)
Async XLA Ops:
  2.0 10.4 %copy-start = (bf16[2,6,512,512]{3,2,1,0:T(8,128)(2,1)S(1)}, bf16[2,6,512,512]{3,2,1,0:T(8,128)(2,1)}, u32[]{:S(2)}) copy-start(bf16[2,6,512,512]{3,2,1,0:T(8,128)(2,1)} %p_ref.9) | copy-start | bytes 18874372
  2.0 7.8 %collective-permute-start = (s32[2]{0:T(128)S(1)}, s32[2]{0:T(128)S(1)}, u32[]{:S(2)}, u32[]{:S(2)}) collective-permute-start(s32[2]{0:T(128)S(1)} %pad_add_fusion.place), channel_id=1, source_target_pairs={{0,1},{1,2},{2,3},{3,4},{4,5},{5,6},{6,7},{7,8},{8,9},{9,10},{10,1... | collective-permute-start | bytes 32 | tf_op jit(solution)/shard_map/ppermute | solution.py:375
  6.8 2.2 %copy-start.1 = (f32[2,512,1024]{2,1,0:T(8,128)S(1)}, f32[2,512,1024]{2,1,0:T(8,128)}, u32[]{:S(2)}) copy-start(f32[2,512,1024]{2,1,0:T(8,128)} %obj.3) | copy-start | bytes 12582916
  10.4 16.4 %collective-permute-start.1 = (f32[2,256,512]{2,1,0:T(8,128)S(1)}, f32[2,256,512]{2,1,0:T(8,128)S(1)}, u32[]{:S(2)}, u32[]{:S(2)}) collective-permute-start(f32[2,256,512]{2,1,0:T(8,128)S(1)} %rim_rows.1), channel_id=1, source_target_pairs={{1,0},{2,1},{3,2},{4,3},{5,4},{6,5},{7,6},{8,7},{9,8},{10,9},{11,1... | collective-permute-start | bytes 3145736 | tf_op jit(solution)/shard_map/ppermute | solution.py:375
  12.4 1.6 copy-start.3
  14.0 15.3 %copy-start.4 = (bf16[1024,1024]{1,0:T(8,128)(2,1)S(1)}, bf16[1024,1024]{1,0:T(8,128)(2,1)}, u32[]{:S(2)}) copy-start(bf16[1024,1024]{1,0:T(8,128)(2,1)} %constant.12.clone.table) | copy-start | bytes 6291460
  14.0 15.3 %copy-start.10 = (bf16[512,1024]{1,0:T(8,128)(2,1)S(1)}, bf16[512,1024]{1,0:T(8,128)(2,1)}, u32[]{:S(2)}) copy-start(bf16[512,1024]{1,0:T(8,128)(2,1)} %constant.13.clone.wt) | copy-start | bytes 3145732
  26.9 19.5 %collective-permute-start.2 = (f32[256,512]{1,0:T(8,128)S(1)}, f32[256,512]{1,0:T(8,128)S(1)}, u32[]{:S(2)}, u32[]{:S(2)}) collective-permute-start(f32[256,512]{1,0:T(8,128)S(1)} %get-tuple-element.83), channel_id=1, source_target_pairs={{0,64},{64,0},{1,65},{65,1},{2,66},{66,2},{3,67},{67,3},{4,68},{68... | collective-permute-start | bytes 1572872 | tf_op jit(solution)/shard_map/ppermute | solution.py:379
  29.3 10.2 %copy-start.9 = (bf16[512,1024]{1,0:T(8,128)(2,1)S(1)}, bf16[512,1024]{1,0:T(8,128)(2,1)}, u32[]{:S(2)}) copy-start(bf16[512,1024]{1,0:T(8,128)(2,1)} %constant.14.clone.wt) | copy-start | bytes 3145732
  38.9 14.3 %collective-permute-start.3 = (f32[256,512]{1,0:T(8,128)S(1)}, f32[256,512]{1,0:T(8,128)S(1)}, u32[]{:S(2)}, u32[]{:S(2)}) collective-permute-start(f32[256,512]{1,0:T(8,128)S(1)} %get-tuple-element.85.s0), channel_id=1, source_target_pairs={{0,64},{64,0},{1,65},{65,1},{2,66},{66,2},{3,67},{67,3},{4,68},{68... | collective-permute-start | bytes 1572872 | tf_op jit(solution)/shard_map/ppermute | solution.py:379
  39.5 13.7 %copy-start.5 = (bf16[1024,1024]{1,0:T(8,128)(2,1)S(1)}, bf16[1024,1024]{1,0:T(8,128)(2,1)}, u32[]{:S(2)}) copy-start(bf16[1024,1024]{1,0:T(8,128)(2,1)} %constant.15.clone.table) | copy-start | bytes 6291460
  39.5 13.7 %copy-start.6 = (f32[1,512,512]{2,1,0:T(8,128)S(1)}, f32[1,512,512]{2,1,0:T(8,128)}, u32[]{:S(2)}) copy-start(f32[1,512,512]{2,1,0:T(8,128)} %pat.3) | copy-start | bytes 3145732
  43.8 15.0 %collective-permute-start.4 = (f32[256,512]{1,0:T(8,128)S(1)}, f32[256,512]{1,0:T(8,128)S(1)}, u32[]{:S(2)}, u32[]{:S(2)}) collective-permute-start(f32[256,512]{1,0:T(8,128)S(1)} %get-tuple-element.88.s0), channel_id=1, source_target_pairs={{0,64},{64,0},{1,65},{65,1},{2,66},{66,2},{3,67},{67,3},{4,68},{68... | collective-permute-start | bytes 1572872 | tf_op jit(solution)/shard_map/ppermute | solution.py:379
  46.4 12.5 %copy-start.8 = (bf16[512,1024]{1,0:T(8,128)(2,1)S(1)}, bf16[512,1024]{1,0:T(8,128)(2,1)}, u32[]{:S(2)}) copy-start(bf16[512,1024]{1,0:T(8,128)(2,1)} %constant.16.clone.bt) | copy-start | bytes 3145732
  58.9 11.1 %copy-start.7 = (bf16[512,1024]{1,0:T(8,128)(2,1)S(1)}, bf16[512,1024]{1,0:T(8,128)(2,1)}, u32[]{:S(2)}) copy-start(bf16[512,1024]{1,0:T(8,128)(2,1)} %constant.17.clone.bt) | copy-start | bytes 3145732
  69.8 5.7 %collective-permute-start.5 = (f32[6,16,16,512]{3,2,1,0:T(8,128)S(1)}, f32[6,16,16,512]{3,2,1,0:T(8,128)S(1)}, u32[]{:S(2)}, u32[]{:S(2)}) collective-permute-start(f32[6,16,16,512]{3,2,1,0:T(8,128)S(1)} %get-tuple-element.96), channel_id=1, source_target_pairs={{0,1},{1,0},{2,3},{3,2},{4,5},{5,4},{6,7},{7,6},{8,9},{9,8},{10,11... | collective-permute-start | bytes 9437192 | tf_op jit(solution)/shard_map/ppermute | solution.py:379
  79.2 19.2 %collective-permute-start.8 = (f32[6,16,16,512]{3,2,1,0:T(8,128)S(1)}, f32[6,16,16,512]{3,2,1,0:T(8,128)S(1)}, u32[]{:S(2)}, u32[]{:S(2)}) collective-permute-start(f32[6,16,16,512]{3,2,1,0:T(8,128)S(1)} %get-tuple-element.108), channel_id=1, source_target_pairs={{0,1},{1,0},{2,3},{3,2},{4,5},{5,4},{6,7},{7,6},{8,9},{9,8},{10,11... | collective-permute-start | bytes 9437192 | tf_op jit(solution)/shard_map/ppermute | solution.py:379
  79.4 16.0 %collective-permute-start.6 = (f32[3,4,16,512]{3,2,1,0:T(8,128)S(1)}, f32[3,4,16,512]{3,2,1,0:T(8,128)S(1)}, u32[]{:S(2)}, u32[]{:S(2)}) collective-permute-start(f32[3,4,16,512]{3,2,1,0:T(8,128)S(1)} %get-tuple-element.104), channel_id=1, source_target_pairs={{0,16},{1,5},{4,20},{5,9},{8,24},{9,13},{12,28},{13,1},{16,32},{17... | collective-permute-start | bytes 1179656 | tf_op jit(solution)/shard_map/ppermute | solution.py:391
  87.8 7.6 %collective-permute-start.7 = (f32[3,4,16,512]{3,2,1,0:T(8,128)S(1)}, f32[3,4,16,512]{3,2,1,0:T(8,128)S(1)}, u32[]{:S(2)}, u32[]{:S(2)}) collective-permute-start(f32[3,4,16,512]{3,2,1,0:T(8,128)S(1)} %get-tuple-element.105), channel_id=1, source_target_pairs={{0,48},{1,13},{4,52},{5,1},{8,56},{9,5},{12,60},{13,9},{16,0},{17,... | collective-permute-start | bytes 1179656 | tf_op jit(solution)/shard_map/ppermute | solution.py:391
  89.9 26.6 %collective-permute-start.11 = (f32[2,2,8,16,512]{4,3,2,1,0:T(8,128)S(1)}, f32[2,2,8,16,512]{4,3,2,1,0:T(8,128)S(1)}, u32[]{:S(2)}, u32[]{:S(2)}) collective-permute-start(f32[2,2,8,16,512]{4,3,2,1,0:T(8,128)S(1)} %get-tuple-element.111.g0), channel_id=1, source_target_pairs={{0,64},{64,0},{1,65},{65,1},{2,66},{66,2},{3,67},{67,3},{4,68},{68... | collective-permute-start | bytes 3145736 | tf_op jit(solution)/shard_map/ppermute | solution.py:379
  95.5 21.0 %collective-permute-start.12 = (f32[2,3,4,16,512]{4,3,2,1,0:T(8,128)S(1)}, f32[2,3,4,16,512]{4,3,2,1,0:T(8,128)S(1)}, u32[]{:S(2)}, u32[]{:S(2)}) collective-permute-start(f32[2,3,4,16,512]{4,3,2,1,0:T(8,128)S(1)} %get-tuple-element.106), channel_id=1, source_target_pairs={{0,16},{1,5},{4,20},{5,9},{8,24},{9,13},{12,28},{13,1},{16,32},{17... | collective-permute-start | bytes 2359304 | tf_op jit(solution)/shard_map/ppermute | solution.py:391
  96.6 20.0 %collective-permute-start.13 = (f32[2,3,4,16,512]{4,3,2,1,0:T(8,128)S(1)}, f32[2,3,4,16,512]{4,3,2,1,0:T(8,128)S(1)}, u32[]{:S(2)}, u32[]{:S(2)}) collective-permute-start(f32[2,3,4,16,512]{4,3,2,1,0:T(8,128)S(1)} %get-tuple-element.113), channel_id=1, source_target_pairs={{0,48},{1,13},{4,52},{5,1},{8,56},{9,5},{12,60},{13,9},{16,0},{17,... | collective-permute-start | bytes 2359304 | tf_op jit(solution)/shard_map/ppermute | solution.py:391
  98.7 17.9 %collective-permute-start.9 = (f32[3,4,16,512]{3,2,1,0:T(8,128)S(1)}, f32[3,4,16,512]{3,2,1,0:T(8,128)S(1)}, u32[]{:S(2)}, u32[]{:S(2)}) collective-permute-start(f32[3,4,16,512]{3,2,1,0:T(8,128)S(1)} %get-tuple-element.109), channel_id=1, source_target_pairs={{0,16},{1,5},{4,20},{5,9},{8,24},{9,13},{12,28},{13,1},{16,32},{17... | collective-permute-start | bytes 1179656 | tf_op jit(solution)/shard_map/ppermute | solution.py:391
  98.8 17.8 %collective-permute-start.10 = (f32[3,4,16,512]{3,2,1,0:T(8,128)S(1)}, f32[3,4,16,512]{3,2,1,0:T(8,128)S(1)}, u32[]{:S(2)}, u32[]{:S(2)}) collective-permute-start(f32[3,4,16,512]{3,2,1,0:T(8,128)S(1)} %get-tuple-element.110), channel_id=1, source_target_pairs={{0,48},{1,13},{4,52},{5,1},{8,56},{9,5},{12,60},{13,9},{16,0},{17,... | collective-permute-start | bytes 1179656 | tf_op jit(solution)/shard_map/ppermute | solution.py:391
  116.7 12.4 %collective-permute-start.14 = (f32[2,3,4,16,512]{4,3,2,1,0:T(8,128)S(1)}, f32[2,3,4,16,512]{4,3,2,1,0:T(8,128)S(1)}, u32[]{:S(2)}, u32[]{:S(2)}) collective-permute-start(f32[2,3,4,16,512]{4,3,2,1,0:T(8,128)S(1)} %get-tuple-element.122), channel_id=1, source_target_pairs={{0,16},{1,5},{4,20},{5,9},{8,24},{9,13},{12,28},{13,1},{16,32},{17... | collective-permute-start | bytes 2359304 | tf_op jit(solution)/shard_map/ppermute | solution.py:391
  116.8 12.3 %collective-permute-start.15 = (f32[2,3,4,16,512]{4,3,2,1,0:T(8,128)S(1)}, f32[2,3,4,16,512]{4,3,2,1,0:T(8,128)S(1)}, u32[]{:S(2)}, u32[]{:S(2)}) collective-permute-start(f32[2,3,4,16,512]{4,3,2,1,0:T(8,128)S(1)} %get-tuple-element.123), channel_id=1, source_target_pairs={{0,48},{1,13},{4,52},{5,1},{8,56},{9,5},{12,60},{13,9},{16,0},{17,... | collective-permute-start | bytes 2359304 | tf_op jit(solution)/shard_map/ppermute | solution.py:391
  119.5 25.1 %collective-permute-start.20 = (f32[2,2,8,16,512]{4,3,2,1,0:T(8,128)S(1)}, f32[2,2,8,16,512]{4,3,2,1,0:T(8,128)S(1)}, u32[]{:S(2)}, u32[]{:S(2)}) collective-permute-start(f32[2,2,8,16,512]{4,3,2,1,0:T(8,128)S(1)} %get-tuple-element.130.g1), channel_id=1, source_target_pairs={{0,64},{64,0},{1,65},{65,1},{2,66},{66,2},{3,67},{67,3},{4,68},{68... | collective-permute-start | bytes 3145736 | tf_op jit(solution)/shard_map/ppermute | solution.py:379
  129.4 15.2 %collective-permute-start.16 = (f32[2,2,3,16,512]{4,3,2,1,0:T(8,128)S(1)}, f32[2,2,3,16,512]{4,3,2,1,0:T(8,128)S(1)}, u32[]{:S(2)}, u32[]{:S(2)}) collective-permute-start(f32[2,2,3,16,512]{4,3,2,1,0:T(8,128)S(1)} %get-tuple-element.125), channel_id=1, source_target_pairs={{0,4},{1,17},{4,8},{5,21},{8,12},{9,25},{12,0},{13,29},{16,20},{17... | collective-permute-start | bytes 1179656 | tf_op jit(solution)/shard_map/ppermute | solution.py:391
  129.5 15.1 %collective-permute-start.17 = (f32[2,2,3,16,512]{4,3,2,1,0:T(8,128)S(1)}, f32[2,2,3,16,512]{4,3,2,1,0:T(8,128)S(1)}, u32[]{:S(2)}, u32[]{:S(2)}) collective-permute-start(f32[2,2,3,16,512]{4,3,2,1,0:T(8,128)S(1)} %get-tuple-element.126), channel_id=1, source_target_pairs={{0,12},{1,49},{4,0},{5,53},{8,4},{9,57},{12,8},{13,61},{16,28},{17... | collective-permute-start | bytes 1179656 | tf_op jit(solution)/shard_map/ppermute | solution.py:391
  132.1 12.5 %collective-permute-start.18 = (f32[2,2,3,16,512]{4,3,2,1,0:T(8,128)S(1)}, f32[2,2,3,16,512]{4,3,2,1,0:T(8,128)S(1)}, u32[]{:S(2)}, u32[]{:S(2)}) collective-permute-start(f32[2,2,3,16,512]{4,3,2,1,0:T(8,128)S(1)} %get-tuple-element.127), channel_id=1, source_target_pairs={{0,8},{1,33},{4,12},{5,37},{8,0},{9,41},{12,4},{13,45},{16,24},{17... | collective-permute-start | bytes 1179656 | tf_op jit(solution)/shard_map/ppermute | solution.py:391
  132.8 3.1 %collective-permute-start.19 = (f32[8,512]{1,0:T(8,128)S(1)}, f32[8,512]{1,0:T(8,128)S(1)}, u32[]{:S(2)}, u32[]{:S(2)}) collective-permute-start(f32[8,512]{1,0:T(8,128)S(1)} %brightest.1.near_max), channel_id=1, source_target_pairs={{0,1},{1,0},{2,3},{3,2},{4,5},{5,4},{6,7},{7,6},{8,9},{9,8},{10,11... | collective-permute-start | bytes 49160 | tf_op jit(solution)/shard_map/ppermute | solution.py:379
  144.7 27.5 %collective-permute-start.21 = (f32[2,2,8,16,512]{4,3,2,1,0:T(8,128)S(1)}, f32[2,2,8,16,512]{4,3,2,1,0:T(8,128)S(1)}, u32[]{:S(2)}, u32[]{:S(2)}) collective-permute-start(f32[2,2,8,16,512]{4,3,2,1,0:T(8,128)S(1)} %over_sum.1), channel_id=1, source_target_pairs={{0,1},{1,2},{2,3},{3,4},{4,5},{5,6},{6,7},{7,8},{8,9},{9,10},{10,1... | collective-permute-start | bytes 3145736 | tf_op jit(solution)/shard_map/ppermute | solution.py:375
  148.3 2.1 %collective-permute-start.22 = (f32[2,2,3,8,512]{4,3,2,1,0:T(8,128)S(1)}, f32[2,2,3,8,512]{4,3,2,1,0:T(8,128)S(1)}, u32[]{:S(2)}, u32[]{:S(2)}) collective-permute-start(f32[2,2,3,8,512]{4,3,2,1,0:T(8,128)S(1)} %get-tuple-element.138), channel_id=1, source_target_pairs={{0,1},{1,0},{2,3},{3,2},{4,5},{5,4},{6,7},{7,6},{8,9},{9,8},{10,11... | collective-permute-start | bytes 589832 | tf_op jit(solution)/shard_map/ppermute | solution.py:379
  150.4 20.3 %copy-start.11 = (s32[12,12]{1,0:T(8,128)S(1)}, s32[12,12]{1,0:T(8,128)}, u32[]{:S(2)}) copy-start(s32[12,12]{1,0:T(8,128)} %w_ref.1) | copy-start | bytes 1732
  150.4 21.9 %copy-start.2 = (f32[2,512,1024]{2,1,0:T(8,128)S(1)}, f32[2,512,1024]{2,1,0:T(8,128)}, u32[]{:S(2)}) copy-start(f32[2,512,1024]{2,1,0:T(8,128)} %obj.3) | copy-start | bytes 12582916
  150.4 16.6 %collective-permute-start.23 = (f32[2,6,8,512]{3,2,1,0:T(8,128)S(1)}, f32[2,6,8,512]{3,2,1,0:T(8,128)S(1)}, u32[]{:S(2)}, u32[]{:S(2)}) collective-permute-start(f32[2,6,8,512]{3,2,1,0:T(8,128)S(1)} %get-tuple-element.141), channel_id=1, source_target_pairs={{0,2},{2,0},{64,66},{66,64},{1,3},{3,1},{65,67},{67,65},{4,6},{6,4... | collective-permute-start | bytes 589832 | tf_op jit(solution)/shard_map/ppermute | solution.py:396
  150.9 19.8 %collective-permute-start.24 = (f32[2,6,8,512]{3,2,1,0:T(8,128)S(1)}, f32[2,6,8,512]{3,2,1,0:T(8,128)S(1)}, u32[]{:S(2)}, u32[]{:S(2)}) collective-permute-start(f32[2,6,8,512]{3,2,1,0:T(8,128)S(1)} %get-tuple-element.140.mine), channel_id=1, source_target_pairs={{0,64},{2,66},{64,0},{66,2},{1,65},{3,67},{65,1},{67,3},{4,68},{6,... | collective-permute-start | bytes 589832 | tf_op jit(solution)/shard_map/ppermute | solution.py:396
  152.7 17.9 %collective-permute-start.25 = (f32[2,6,8,512]{3,2,1,0:T(8,128)S(1)}, f32[2,6,8,512]{3,2,1,0:T(8,128)S(1)}, u32[]{:S(2)}, u32[]{:S(2)}) collective-permute-start(f32[2,6,8,512]{3,2,1,0:T(8,128)S(1)} %get-tuple-element.141), channel_id=1, source_target_pairs={{0,66},{2,64},{64,2},{66,0},{1,67},{3,65},{65,3},{67,1},{4,70},{6,... | collective-permute-start | bytes 589832 | tf_op jit(solution)/shard_map/ppermute | solution.py:396

commit v6 on v4

--- a/solution.py
+++ b/solution.py
@@ -15,6 +15,7 @@
 N = 512
 H = 256
 CHUNK = 32
+QUARTER = 128
 PAIR = 2
 
 
@@ -138,15 +139,15 @@
     )
 
 
-def top_body(patch_ref, p_ref, table, half_ref, own_half, far_half, rows_ref, x_s):
+def top_body(patch_ref, p_ref, table, half_ref, own_part, far_part, rows_ref, x_s):
     def step(m0):
         for j in range(PAIR):
             exit_half(p_ref, m0 + j, j, 0, patch_ref, x_s)
         along_rows(x_s, table, half_ref, m0)
 
     pairs(p_ref.shape[1], step)
-    core = lax.axis_index("core")
-    base = core * H
+    core, x = lax.axis_index("core"), lax.axis_index("x")
+    base = (core * 2 + x) * QUARTER
 
     def lit(i):
         rows = pl.ds(pl.multiple_of(base + i * CHUNK, CHUNK), CHUNK)
@@ -155,10 +156,10 @@
             pr = p_ref[0, m, rows, :].astype(f32)
             pi = p_ref[1, m, rows, :].astype(f32)
             acc = acc + (pr * pr + pi * pi)
-        own_half[at(i, CHUNK), :] = acc
-        far_half[at(i, CHUNK), :] = acc
-
-    loop(H // CHUNK, lit)
+        own_part[at(i, CHUNK), :] = acc
+        far_part[at(i, CHUNK), :] = acc
+
+    loop(QUARTER // CHUNK, lit)
     chip = (lax.axis_index("y") * 4 + lax.axis_index("z")) * 2 + lax.axis_index("x")
     for part in range(2):
         for m in range(p_ref.shape[1]):
@@ -172,18 +173,29 @@
         top_body,
         "top_half",
         [LOCAL, LOCAL, LOCAL],
-        [shape(nm, N, N, dtype=bf16), shape(H, N), shape(H, N), shape(2, nm, 8, N)],
+        [shape(nm, N, N, dtype=bf16), shape(QUARTER, N), shape(QUARTER, N), shape(2, nm, 8, N)],
         [pltpu.VMEM((PAIR, H, 2 * N), bf16)],
         6,
     )(patch, probe, table)
 
 
-def wave_half(wave_ref, sum_ref, wt, top, bot, m0):
+def first_terms_body(wt0, wt1, top, wave0, wave1):
+    def step(m):
+        wave0[m] = jnp.dot(wt0[:, :N], top[m], preferred_element_type=f32)
+        wave1[m] = jnp.dot(wt1[:, :N], top[m], preferred_element_type=f32)
+
+    loop(top.shape[0], step)
+
+
+def first_terms(wt0, wt1, top):
+    nm = top.shape[0]
+    return local_call(first_terms_body, "first_terms", [LOCAL] * 3, [shape(nm, N, N)] * 2, [], 5)(wt0, wt1, top)
+
+
+def wave_half(wave_ref, sum_ref, wt, bot, m0):
     for j in range(PAIR):
         m = m0 + j
-        wave_ref[m] = jnp.dot(wt[:, :N], top[m], preferred_element_type=f32) + jnp.dot(
-            wt[:, N:], bot[m], preferred_element_type=f32
-        )
+        wave_ref[m] += jnp.dot(wt[:, N:], bot[m], preferred_element_type=f32)
 
     def one(i):
         rows = at(i, CHUNK)
@@ -198,7 +210,7 @@
     loop(H // CHUNK, one, 2)
 
 
-def bottom_body(place, own, rim, p_ref, table, wt, top, half_ref, patch_ref, wave_ref, sum_ref, x_s):
+def bottom_body(place, own, rim, p_ref, table, wt, _, half_ref, patch_ref, wave_ref, sum_ref, x_s):
     @pl.when(place[0] == 0)
     def _():
         patch_ref[...] = own[...]
@@ -213,12 +225,12 @@
         for j in range(PAIR):
             exit_half(p_ref, m0 + j, j, H, patch_ref, x_s)
         along_rows(x_s, table, half_ref, m0)
-        wave_half(wave_ref, sum_ref, wt, top, half_ref, m0)
+        wave_half(wave_ref, sum_ref, wt, half_ref, m0)
 
     pairs(p_ref.shape[1], step)
 
 
-def bottom_half(place, own, rim, probe, table, wave_rows, top):
+def bottom_half(place, own, rim, probe, table, wave_rows, wave):
     nm = probe.shape[1]
     return local_call(
         bottom_body,
@@ -227,19 +239,18 @@
         [shape(nm, N, N, dtype=bf16), shape(2, H, N), shape(nm, N, N), shape(H, N)],
         [pltpu.VMEM((PAIR, H, 2 * N), bf16)],
         8,
-    )(place, own, rim, probe, table, wave_rows, top)
-
-
-def low_wave_body(wt, top, bot, wave_ref, sum_ref):
+        {6: 2},
+    )(place, own, rim, probe, table, wave_rows, wave)
+
+
+def low_wave_body(wt, bot, _, wave_ref, sum_ref):
     sum_ref[...] = jnp.zeros_like(sum_ref)
-    pairs(top.shape[0], lambda m0: wave_half(wave_ref, sum_ref, wt, top, bot, m0))
-
-
-def low_wave(wave_rows, top, bot):
-    nm = top.shape[0]
-    return local_call(
-        low_wave_body, "low_wave", [LOCAL] * 3, [shape(nm, N, N), shape(H, N)], [], 5
-    )(wave_rows, top, bot)
+    pairs(bot.shape[0], lambda m0: wave_half(wave_ref, sum_ref, wt, bot, m0))
+
+
+def low_wave(wave_rows, bot, wave):
+    outs = [shape(*wave.shape), shape(H, N)]
+    return local_call(low_wave_body, "low_wave", [LOCAL] * 3, outs, [], 5, {2: 0})(wave_rows, bot, wave)
 
 
 def set_scale(pat, base, s0, s1, scale_s):
@@ -309,10 +320,11 @@
 UNROLL = 8
 LIMIT = 4
 STAGE = pl.CostEstimate(flops=int(5e9), transcendentals=0, bytes_accessed=int(15e6))
-GRADS = [shape(2, 8, 16, N)] * 2
-
-
-def first_block_body(pat, s0, s1, wave_ref, table, bt, top, ptop, pbot, p_ref, half_ref, keep, send, gtop, gbot, scale_s, x_s, back_s):
+GRADS = [shape(2, 8, 16, N), shape(2, 2, 8, 16, N)]
+
+
+def first_block_body(pat, s0, s1, wave_ref, table, bt, top, ptop, pbot, p_ref, half_ref, keep, send, gbot, tops, scale_s, x_s, back_s):
+    gtop = tops.at[0]
     set_scale(pat, H, s0, s1, scale_s)
     gtop[...] = jnp.zeros_like(gtop)
     gbot[...] = jnp.zeros_like(gbot)
@@ -337,34 +349,33 @@
     )(pat, s0, s1, wave, table, back_rows, top, ptop, pbot, probe)
 
 
-def second_block(back_rows, top, bot, ptop, pbot, probe, first, count, grads=None):
+def second_block(back_rows, top, bot, ptop, pbot, probe, first, count, tops, earlier=None):
     nm = top.shape[0]
-    half = [shape(2, 8, 16, N)] * 2
+    given = earlier or []
 
     def body(bt, top, bot, ptop, pbot, p_ref, *refs):
-        if grads is None:
-            keep, send, gtop, gbot, back_s = refs
+        keep, send, gbot, tops, back_s = refs[1 + len(given) :]
+        gtop = tops.at[1]
+        if not given:
             gtop[...] = jnp.zeros_like(gtop)
             gbot[...] = jnp.zeros_like(gbot)
-        else:
-            kin, sin, tin, bin_, keep, send, gtop, gbot, back_s = refs
+        core = lax.axis_index("core")
         loop(
             count,
             lambda m: gradients(
-                lax.axis_index("core"), 1, bt, top, bot, ptop, pbot, p_ref, keep, send, gtop, gbot, back_s, m + first
+                core, 1, bt, top, bot, ptop, pbot, p_ref, keep, send, gtop, gbot, back_s, m + first
             ),
         )
 
-    given = [] if grads is None else grads
     return local_call(
         body,
         "second_block",
-        [LOCAL] * (6 + len(given)),
-        [shape(nm, 16, 16, N)] * 2 + half,
+        [LOCAL] * (7 + len(given)),
+        [shape(nm, 16, 16, N)] * 2 + GRADS,
         [pltpu.VMEM((N, N), f32)],
         6,
-        {6 + i: i for i in range(len(given))},
-    )(back_rows, top, bot, ptop, pbot, probe, *given)
+        {6: 3, **{7 + i: i for i in range(len(given))}},
+    )(back_rows, top, bot, ptop, pbot, probe, tops, *given)
 
 
 SCAN = ("y", "z", "x", "core")
@@ -416,11 +427,12 @@
     def one(i, acc):
         return jnp.maximum(acc, own[at(i, 8), :] + far[at(i, 8), :])
 
-    out[...] = lax.fori_loop(0, H // 8, one, jnp.zeros((8, N), f32))
+    out[...] = lax.fori_loop(0, QUARTER // 8, one, jnp.zeros((8, N), f32))
 
 
 def brightest(own, far):
-    return local_call(brightest_body, "brightest", [LOCAL, LOCAL], [shape(8, N)], [], LIMIT, cost=STAGE)(own, far)[0]
+    outs = [shape(8, N)]
+    return local_call(brightest_body, "brightest", [LOCAL, LOCAL], outs, [], LIMIT, cost=STAGE)(own, far)[0]
 
 
 def core_add_body(keep, recv, own, near, back, far0, far1):
@@ -468,30 +480,34 @@
     )
 
 
-def line_add_body(a, b, c, d, keep, send):
+def line_add_body(most, a, b, c, d, keep, send):
     core = here()[2]
-    for out, side in ((keep, core), (send, 1 - core)):
+    n2 = a.shape[2]
+    for side, out in ((core, keep), (1 - core, send)):
         rows = at(side, 8)
         for block in range(2):
             for j in range(2):
-                out[block, j] = (a[block, j, :, rows] + b[block, j, :, rows]) + (
+                first = (block * 2 + j) * n2
+                out[first : first + n2] = (a[block, j, :, rows] + b[block, j, :, rows]) + (
                     c[block, j, :, rows] + d[block, j, :, rows]
                 )
-
-
-def line_add(arrays):
-    dims = arrays[0].shape
-    outs = [shape(*dims[:3], 8, N)] * 2
-    return local_call(line_add_body, "line_add", [LOCAL] * 4, outs, [], LIMIT, cost=STAGE)(*arrays)
-
-
-def pixel_body(keep, recv, rows, mine, other):
+    send[4 * n2] = most[...]
+
+
+def line_add(most, arrays):
+    n2 = arrays[0].shape[2]
+    outs = [shape(4 * n2, 8, N), shape(4 * n2 + 1, 8, N)]
+    return local_call(line_add_body, "line_add", [LOCAL] * 5, outs, [], LIMIT, cost=STAGE)(most, *arrays)
+
+
+def pixel_body(most, keep, recv, rows, mine, other):
     core, x = here()[2:4]
     scale = 1.0 / math.sqrt(64)
+    nm = rows.shape[1]
 
     def fill(part, ref):
-        mine[part] = ref[x] * scale + rows[part]
-        other[part] = ref[1 - x] * scale
+        mine[part] = ref[pl.ds(x * nm, nm)] * scale + rows[part]
+        other[pl.ds(part * nm, nm)] = ref[pl.ds((1 - x) * nm, nm)] * scale
 
     @pl.when(core == 0)
     def _():
@@ -503,20 +519,21 @@
         fill(0, recv)
         fill(1, keep)
 
-
-def pixel_step(keep, recv, rows):
-    dims = rows.shape
-    return local_call(pixel_body, "pixel_step", [LOCAL] * 3, [shape(*dims)] * 2, [], LIMIT, cost=STAGE)(
-        keep.reshape(dims), recv.reshape(dims), rows
-    )
+    other[2 * nm] = jnp.maximum(most[...], recv[2 * nm])
+
+
+def pixel_step(most, keep, recv, rows):
+    nm = rows.shape[1]
+    outs = [shape(2, nm, 8, N), shape(2 * nm + 1, 8, N)]
+    return local_call(pixel_body, "pixel_step", [LOCAL] * 4, outs, [], LIMIT, cost=STAGE)(most, keep, recv, rows)
 
 
 def mix_body(w_ref, mine, b, c, d, out_ref):
     mode = here()[4]
     nm = mine.shape[1]
     for part in range(2):
-        own = [mine[part, j] + b[part, j] for j in range(nm)]
-        far = [c[part, j] + d[part, j] for j in range(nm)]
+        own = [mine[part, j] + b[part * nm + j] for j in range(nm)]
+        far = [c[part, j] + d[part * nm + j] for j in range(nm)]
         for k in range(nm):
             row = mode * nm + k
             acc = jnp.zeros((8, N), f32)
@@ -531,10 +548,11 @@
     return local_call(mix_body, "mix", [SCALARS] + [LOCAL] * 4, outs, [], LIMIT)(mixing, mine, b, c, d)[0]
 
 
-def object_body(place, before, near_max, far_max, obj, t0, t0f, t1, t1f, b0, b0f, b1, b1f, over, out, new, sems):
+def object_body(place, before, near_max, far_max, obj, t, tf, b0, b0f, b1, b1f, over, out, new, sems):
     shift, col = place[0], pl.multiple_of(place[1] * H, H)
     over_shift, over_col = before[0], pl.multiple_of(before[1] * H, H)
-    largest = jnp.max(jnp.maximum(near_max[...], far_max[...]))
+    last = near_max.shape[0] - 1
+    largest = jnp.max(jnp.maximum(near_max[last], far_max[last]))
     copies = []
     for half in range(2):
         base = half * H
@@ -558,7 +576,7 @@
 
         @pl.when(shift == half)
         def _():
-            add(col, (t0, t0f), (t1, t1f))
+            add(col, (t.at[0], tf.at[0]), (t.at[1], tf.at[1]))
 
         if half == 1:
 
@@ -582,7 +600,7 @@
 def object_update(place, before, near_max, far_max, obj, pieces, over):
     return pl.pallas_call(
         object_body,
-        in_specs=[SCALARS] * 2 + [LOCAL] * 12,
+        in_specs=[SCALARS] * 2 + [LOCAL] * 10,
         out_specs=FAR,
         out_shape=shape(2, N, 4 * H),
         scratch_shapes=[pltpu.VMEM((2, N, 4 * H), f32), pltpu.SemaphoreType.DMA((2,))],
@@ -612,54 +630,54 @@
     before, patch_top = tied(before, patch_top)
     rim = along(rim_rows(before, first_rows), -1)
     half_top, own_light, light_out, rows = top_half(patch_top, probe, minus)
-    rim, half_top, light_out = tied(rim, half_top, light_out)
+    wave_top, wave_bot = first_terms(wave_top_rows, wave_bot_rows, half_top)
+    rim, wave_top, light_out = tied(rim, wave_top, light_out)
     far_light = swapped(light_out, "mode")
     half_bot, patch_bot, wave_top, sum_top = bottom_half(
-        place, own_bot, rim, probe, minus, wave_top_rows, half_top
+        place, own_bot, rim, probe, minus, wave_top_rows, wave_top
     )
     far_top = swapped(sum_top, "mode")
-    wave_bot, sum_bot = low_wave(wave_bot_rows, half_top, half_bot)
+    half_bot, far_light = tied(half_bot, far_light)
+    wave_bot, sum_bot = low_wave(wave_bot_rows, half_bot, wave_bot)
     far_bot = swapped(sum_bot, "mode")
-    wave_top, far_light = tied(wave_top, far_light)
     fixed = fixed_top(patterns, sum_top, far_top, wave_top, plus)
-    low, keep0, send0, top0, bot0 = first_block(
+    low, keep0, send0, bot0, tops = first_block(
         patterns, sum_bot, far_bot, wave_bot, plus, back_rows0, fixed, patch_top, patch_bot, probe
     )
+    most = brightest(own_light, far_light)
     recv0 = swapped(send0, "core")
     bot0_far = swapped(bot0, "mode")
-    half_max = brightest(own_light, far_light)
-    far_max = swapped(half_max, "core")
-    part1 = second_block(back_rows1, fixed, low, patch_top, patch_bot, probe, 0, 3)
+    *part1, tops = second_block(back_rows1, fixed, low, patch_top, patch_bot, probe, 0, 3, tops)
     own0, near0, back0, far0a, far0b = core_add(keep0, recv0)
     ra0, rb0 = turned(far0a, 1, True), turned(far0b, -1, True)
     *part1, near0 = tied(*part1, near0)
-    keep1, send1, top1, bot1 = second_block(back_rows1, fixed, low, patch_top, patch_bot, probe, 3, 3, part1)
+    keep1, send1, bot1, tops = second_block(
+        back_rows1, fixed, low, patch_top, patch_bot, probe, 3, 3, tops, part1
+    )
     recv1 = swapped(send1, "core")
     near0, back0 = relay_add(near0, back0, ra0, rb0)
-    top0_next, bot0_far, _ = tied(top0, bot0_far, near0)
-    top0_far = swapped(top0_next, "mode")
-    bot1_next, top0_far = tied(bot1, top0_far)
-    bot1_far = swapped(bot1_next, "mode")
-    keep1, _, bot0_far = tied(keep1, near0, bot0_far)
+    keep1, _ = tied(keep1, near0)
     own1, near1, back1, far1a, far1b = core_add(keep1, recv1)
     ra1, rb1 = turned(far1a, 1, True), turned(far1b, -1, True)
     plane0 = (own0, turned(near0, 1, True), turned(back0, -1, True))
-    ra1, rb1, top0_far, *plane0 = tied(ra1, rb1, top0_far, *plane0)
+    ra1, rb1, bot0_far, *plane0 = tied(ra1, rb1, bot0_far, *plane0)
+    bot1_next, _ = tied(bot1, bot0_far)
+    bot1_far = swapped(bot1_next, "mode")
     near1, back1 = relay_add(near1, back1, ra1, rb1)
     plane1 = (own1, turned(near1, 1, True), turned(back1, -1, True))
     *plane1, bot1_far = tied(*plane1, bot1_far)
-    top1_next, _ = tied(top1, plane1[1])
-    top1_far = swapped(top1_next, "mode")
+    tops_next, _ = tied(tops, bot1_far)
+    tops_far = swapped(tops_next, "mode")
     over = along(over_sum(bot0, bot0_far, bot1, bot1_far), 1)
     line = plane_add((plane0, plane1))
     line = [line[0]] + [turned(line[r], r, False) for r in (1, 3, 2)]
-    *line, top1_far, far_max = tied(*line, top1_far, far_max)
-    keep, send = line_add(line)
-    mine, other = pixel_step(keep, swapped(send, "core"), rows)
-    mine, other, over = tied(mine, other, over)
-    probe_new = mix(mixing, mine, across(other, 0, 1), across(mine, 1, 0), across(other, 1, 1))
-    pieces = (top0, top0_far, top1, top1_far, bot0, bot0_far, bot1, bot1_far)
-    object_new = object_update(place, before, half_max, far_max, object_field, pieces, over)
+    keep, send = line_add(most, line)
+    recv, over, tops_far = tied(swapped(send, "core"), over, tops_far)
+    mine, other = pixel_step(most, keep, recv, rows)
+    beside = across(other, 0, 1)
+    probe_new = mix(mixing, mine, beside, across(mine, 1, 0), across(other, 1, 1))
+    pieces = (tops, tops_far, bot0, bot0_far, bot1, bot1_far)
+    object_new = object_update(place, before, other, beside, object_field, pieces, over)
     return object_new, probe_new
 
 

time: 184 us -> 187 us (1.016)
  waiting for transfers between devices: 63.5 us -> 82 us
  starting transfers between devices: 63.2 us -> 47.7 us
    ppermute x11 -> x9, starting transfers between devices: 27.4 us -> 13 us  [swapped(): return lax.ppermute(value, axis, [(0, 1), (1, 0)])]
    ppermute x11 -> x9, waiting for transfers between devices: 38.2 us -> 50.4 us  [swapped(): return lax.ppermute(value, axis, [(0, 1), (1, 0)])]
    ppermute x11, waiting for transfers between devices: 12.2 us -> 17.3 us  [turned(): return lax.ppermute(value, RING, pairs)]
    ppermute x3, waiting for transfers between devices: 7.14 us -> 11.9 us  [along(): return lax.ppermute(value, SCAN, [(i, i + steps) for i in range(lo, hi)])]
    ppermute x3, waiting for transfers between devices: 5.9 us -> 2.34 us  [across(): return lax.ppermute(value, ('mode', 'x'), pairs)]
    pallas_call x19 -> x20, Pallas kernels: 46.9 us -> 47.8 us  [call(): pl.pallas_call(body, in_specs=ins, out_specs=[LOCAL] * len(outs), out_sha...]
  transfers between devices with their start and end apart: 28 -> 26, of which waited for: 15 -> 17; matrix products, arithmetic and copies ran while one was open for 0% -> 0% of each run, Pallas kernels for 18% -> 18%
where the time goes in v6:
time: 187 us
  waiting for transfers between devices  82 us (44%)
  Pallas kernels  50.8 us (27%)
  starting transfers between devices  47.7 us (26%)
  local copies, waits for them, and re-layouts  3.81 us (2%)
  between operations  2.17 us (1%)
    ppermute x9, waiting for transfers between devices, swapped(): return lax.ppermute(value, axis, [(0, 1), (1, 0)])  50.4 us
    pallas_call x20, Pallas kernels, call(): pl.pallas_call(body, in_specs=ins, out_specs=[LOCAL] * len(outs), out_sha...  47.8 us
    ppermute x11, starting transfers between devices, turned(): return lax.ppermute(value, RING, pairs)  22.3 us
    ppermute x11, waiting for transfers between devices, turned(): return lax.ppermute(value, RING, pairs)  17.3 us
    ppermute x9, starting transfers between devices, swapped(): return lax.ppermute(value, axis, [(0, 1), (1, 0)])  13 us
    ppermute x3, waiting for transfers between devices, along(): return lax.ppermute(value, SCAN, [(i, i + steps) for i in range(lo, hi)])  11.9 us
    ppermute x3, starting transfers between devices, along(): return lax.ppermute(value, SCAN, [(i, i + steps) for i in range(lo, hi)])  8.76 us
    unnamed x24, local copies, waits for them, and re-layouts  3.81 us
  transfers between devices with their start and end apart: 26, of which 17 were waited for; matrix products, arithmetic and copies ran while one was open for 0% of the time, Pallas kernels for 18%

profile of v6, /device:TPU:1, one launch (start us, length us, event | category | flops | bytes accessed | tf_op | source)
XLA Modules:
  0.0 186.5 jit_solution(1895275487549355203)
XLA Ops:
  2.0 4.8 %collective-permute-start = (s32[2]{0:T(128)S(1)}, s32[2]{0:T(128)S(1)}, u32[]{:S(2)}, u32[]{:S(2)}) collective-permute-start(s32[2]{0:T(128)S(1)} %pad_add_fusion.place), channel_id=1, source_target_pairs={{0,1},{1,2},{2,3},{3,4},{4,5},{5,6},{6,7},{7,8},{8,9},{9,10},{10,1... | collective-permute-start | bytes 32 | tf_op jit(solution)/shard_map/ppermute | solution.py:388
  6.8 2.2 %copy-done.1 = f32[2,512,1024]{2,1,0:T(8,128)S(1)} copy-done((f32[2,512,1024]{2,1,0:T(8,128)S(1)}, f32[2,512,1024]{2,1,0:T(8,128)}, u32[]{:S(2)}) %copy-start.1) | copy-done | bytes 4194328
  9.0 0.8 own_rows.1
  9.8 0.6 rim_rows.1
  10.4 1.9 %collective-permute-start.1 = (f32[2,256,512]{2,1,0:T(8,128)S(1)}, f32[2,256,512]{2,1,0:T(8,128)S(1)}, u32[]{:S(2)}, u32[]{:S(2)}) collective-permute-start(f32[2,256,512]{2,1,0:T(8,128)S(1)} %rim_rows.1), channel_id=1, source_target_pairs={{1,0},{2,1},{3,2},{4,3},{5,4},{6,5},{7,6},{8,7},{9,8},{10,9},{11,1... | collective-permute-start | bytes 3145736 | tf_op jit(solution)/shard_map/ppermute | solution.py:388
  12.4 1.6 copy-done.3
  14.0 5.4 %top_half.1 = (bf16[6,512,512]{2,1,0:T(8,128)(2,1)S(1)}, f32[128,512]{1,0:T(8,128)S(1)}, f32[128,512]{1,0:T(8,128)S(1)}, f32[2,6,8,512]{3,2,1,0:T(8,128)S(1)}) custom-call(f32[2,256,512]{2,1,0:T(8,128)S(1)} %get-tuple-element.81.patch_ref.ptop, bf16[2,6,512,512]{3,2,1,0:T(8,128)(2,1)S(1)} %copy-done, bf16[1024,1024]{1,0:T(8,128)(2,1)S(1)} %copy-done.3), custom_call_target="tpu_custom_call" | custom-call | tf_op jit(solution)/shard_map/top_half/pallas_call | solution.py:58
  19.4 4.3 %first_terms.1 = (f32[6,512,512]{2,1,0:T(8,128)S(1)}, f32[6,512,512]{2,1,0:T(8,128)S(1)}) custom-call(bf16[512,1024]{1,0:T(8,128)(2,1)S(1)} %copy-done.8, bf16[512,1024]{1,0:T(8,128)(2,1)S(1)} %copy-done.7, bf16[6,512,512]{2,1,0:T(8,128)(2,1)S(1)} %get-tuple-element.85.top), custom_call_target="tpu_custom_call" | custom-call | tf_op jit(solution)/shard_map/first_terms/pallas_call | solution.py:58
  23.7 3.1 %collective-permute-done.1.rim = f32[2,256,512]{2,1,0:T(8,128)S(1)} collective-permute-done((f32[2,256,512]{2,1,0:T(8,128)S(1)}, f32[2,256,512]{2,1,0:T(8,128)S(1)}, u32[]{:S(2)}, u32[]{:S(2)}) %collective-permute-start.1) | collective-permute-done | bytes 1048608 | tf_op jit(solution)/shard_map/ppermute | solution.py:388
  26.9 2.2 %collective-permute-start.2 = (f32[128,512]{1,0:T(8,128)S(1)}, f32[128,512]{1,0:T(8,128)S(1)}, u32[]{:S(2)}, u32[]{:S(2)}) collective-permute-start(f32[128,512]{1,0:T(8,128)S(1)} %get-tuple-element.91), channel_id=1, source_target_pairs={{0,64},{64,0},{1,65},{65,1},{2,66},{66,2},{3,67},{67,3},{4,68},{68... | collective-permute-start | bytes 786440 | tf_op jit(solution)/shard_map/ppermute | solution.py:392
  29.0 7.9 %bottom_half.1 = (bf16[6,512,512]{2,1,0:T(8,128)(2,1)S(1)}, f32[2,256,512]{2,1,0:T(8,128)S(1)}, f32[6,512,512]{2,1,0:T(8,128)S(1)}, f32[256,512]{1,0:T(8,128)S(1)}) custom-call(s32[2]{0:T(128)S(1)} %pad_add_fusion.place, f32[2,256,512]{2,1,0:T(8,128)S(1)} %get-tuple-element.83.own, ...), custom_call_target="tpu_custom_call", output_to_operand_aliasing={{2}: (6, {})} | custom-call | tf_op jit(solution)/shard_map/bottom_half/pallas_call | solution.py:58
  36.9 0.9 collective-permute-start.3
  37.8 2.8 %low_wave.1 = (f32[6,512,512]{2,1,0:T(8,128)S(1)}, f32[256,512]{1,0:T(8,128)S(1)}) custom-call(bf16[512,1024]{1,0:T(8,128)(2,1)S(1)} %copy-done.7, bf16[6,512,512]{2,1,0:T(8,128)(2,1)S(1)} %get-tuple-element.95.bot, f32[6,512,512]{2,1,0:T(8,128)S(1)} %get-tuple-element.96._), custom_call_target="tpu_custom_call", output_to_operand_aliasing={{0}: (2, {})} | custom-call | tf_op jit(solution)/shard_map/low_wave/pallas_call | solution.py:58
  40.6 2.2 %collective-permute-start.4 = (f32[256,512]{1,0:T(8,128)S(1)}, f32[256,512]{1,0:T(8,128)S(1)}, u32[]{:S(2)}, u32[]{:S(2)}) collective-permute-start(f32[256,512]{1,0:T(8,128)S(1)} %get-tuple-element.97.s0), channel_id=1, source_target_pairs={{0,64},{64,0},{1,65},{65,1},{2,66},{66,2},{3,67},{67,3},{4,68},{68... | collective-permute-start | bytes 1572872 | tf_op jit(solution)/shard_map/ppermute | solution.py:392
  42.8 9.7 %collective-permute-done.3.s1 = f32[256,512]{1,0:T(8,128)S(1)} collective-permute-done((f32[256,512]{1,0:T(8,128)S(1)}, f32[256,512]{1,0:T(8,128)S(1)}, u32[]{:S(2)}, u32[]{:S(2)}) %collective-permute-start.3) | collective-permute-done | bytes 524320 | tf_op jit(solution)/shard_map/ppermute | solution.py:392
  52.5 4.9 %fixed_top.1.top = bf16[6,512,512]{2,1,0:T(8,128)(2,1)S(1)} custom-call(f32[1,512,512]{2,1,0:T(8,128)S(1)} %copy-done.9, f32[256,512]{1,0:T(8,128)S(1)} %get-tuple-element.93.s0, f32[256,512]{1,0:T(8,128)S(1)} %collective-permute-done.3.s1, f32[6,512,512]{2,1,0:T(8,128)S(1)} %get-tuple-element.94.wave_ref, bf16[1024,1024]{1,0:T(8,128)(2,1)S(1)} %copy-done.5), custom_call_target="tpu_custom_call" | custom-call | tf_op jit(solution)/shard_map/fixed_top/pallas_call | solution.py:58
  57.3 2.5 %collective-permute-done.4.s1 = f32[256,512]{1,0:T(8,128)S(1)} collective-permute-done((f32[256,512]{1,0:T(8,128)S(1)}, f32[256,512]{1,0:T(8,128)S(1)}, u32[]{:S(2)}, u32[]{:S(2)}) %collective-permute-start.4) | collective-permute-done | bytes 524320 | tf_op jit(solution)/shard_map/ppermute | solution.py:392
  59.9 10.8 %first_block.1 = (bf16[6,512,512]{2,1,0:T(8,128)(2,1)S(1)}, f32[6,16,16,512]{3,2,1,0:T(8,128)S(1)}, f32[6,16,16,512]{3,2,1,0:T(8,128)S(1)}, f32[2,8,16,512]{3,2,1,0:T(8,128)S(1)}, f32[2,2,8,16,512]{4,3,2,1,0:T(8,128)S(1)}) custom-call(f32[1,512,512]{2,1,0:T(8,128)S(1)} %copy-done.9, f32[256,512]{1,0:T(8,128)S(1)} %get-tuple-element.97.s0, ...), custom_call_target="tpu_custom_call" | custom-call | tf_op jit(solution)/shard_map/first_block/pallas_call | solution.py:58
  70.7 0.1 collective-permute-start.5
  70.8 3.5 %second_block.2 = (f32[6,16,16,512]{3,2,1,0:T(8,128)S(1)}, f32[6,16,16,512]{3,2,1,0:T(8,128)S(1)}, f32[2,8,16,512]{3,2,1,0:T(8,128)S(1)}, f32[2,2,8,16,512]{4,3,2,1,0:T(8,128)S(1)}) custom-call(bf16[512,1024]{1,0:T(8,128)(2,1)S(1)} %copy-done.6, bf16[6,512,512]{2,1,0:T(8,128)(2,1)S(1)} %fixed_top.1.top, ...), custom_call_target="tpu_custom_call", output_to_operand_aliasing={{3}: (6, {})} | custom-call | tf_op jit(solution)/shard_map/second_block/pallas_call | solution.py:58
  74.4 2.1 %collective-permute-done.5.recv = f32[6,16,16,512]{3,2,1,0:T(8,128)S(1)} collective-permute-done((f32[6,16,16,512]{3,2,1,0:T(8,128)S(1)}, f32[6,16,16,512]{3,2,1,0:T(8,128)S(1)}, u32[]{:S(2)}, u32[]{:S(2)}) %collective-permute-start.5) | collective-permute-done | bytes 3145760 | tf_op jit(solution)/shard_map/ppermute | solution.py:392
  76.5 0.3 core_add.2
  76.8 3.5 %second_block.3 = (f32[6,16,16,512]{3,2,1,0:T(8,128)S(1)}, f32[6,16,16,512]{3,2,1,0:T(8,128)S(1)}, f32[2,8,16,512]{3,2,1,0:T(8,128)S(1)}, f32[2,2,8,16,512]{4,3,2,1,0:T(8,128)S(1)}) custom-call(bf16[512,1024]{1,0:T(8,128)(2,1)S(1)} %copy-done.6, ...), custom_call_target="tpu_custom_call", output_to_operand_aliasing={{3}: (6, {}), {0}: (7, {}), {1}: (8, {}), {2}: (9, {})} | custom-call | tf_op jit(solution)/shard_map/second_block/pallas_call | solution.py:58
  80.3 0.2 collective-permute-start.8
  80.5 5.7 %collective-permute-start.6 = (f32[3,4,16,512]{3,2,1,0:T(8,128)S(1)}, f32[3,4,16,512]{3,2,1,0:T(8,128)S(1)}, u32[]{:S(2)}, u32[]{:S(2)}) collective-permute-start(f32[3,4,16,512]{3,2,1,0:T(8,128)S(1)} %get-tuple-element.115), channel_id=1, source_target_pairs={{0,16},{1,5},{4,20},{5,9},{8,24},{9,13},{12,28},{13,1},{16,32},{17... | collective-permute-start | bytes 1179656 | tf_op jit(solution)/shard_map/ppermute | solution.py:404
  86.2 2.1 %collective-permute-start.7 = (f32[3,4,16,512]{3,2,1,0:T(8,128)S(1)}, f32[3,4,16,512]{3,2,1,0:T(8,128)S(1)}, u32[]{:S(2)}, u32[]{:S(2)}) collective-permute-start(f32[3,4,16,512]{3,2,1,0:T(8,128)S(1)} %get-tuple-element.116), channel_id=1, source_target_pairs={{0,48},{1,13},{4,52},{5,1},{8,56},{9,5},{12,60},{13,9},{16,0},{17,... | collective-permute-start | bytes 1179656 | tf_op jit(solution)/shard_map/ppermute | solution.py:404
  88.3 0.5 collective-permute-start.11
  88.8 4.9 %collective-permute-done.6.ra = f32[3,4,16,512]{3,2,1,0:T(8,128)S(1)} collective-permute-done((f32[3,4,16,512]{3,2,1,0:T(8,128)S(1)}, f32[3,4,16,512]{3,2,1,0:T(8,128)S(1)}, u32[]{:S(2)}, u32[]{:S(2)}) %collective-permute-start.6) | collective-permute-done | bytes 393248 | tf_op jit(solution)/shard_map/ppermute | solution.py:404
  93.7 0.1 relay_add.2
  93.9 1.0 collective-permute-start.12
  94.9 1.8 collective-permute-start.13
  96.7 0.5 core_add.3
  97.3 2.7 %collective-permute-start.10 = (f32[3,4,16,512]{3,2,1,0:T(8,128)S(1)}, f32[3,4,16,512]{3,2,1,0:T(8,128)S(1)}, u32[]{:S(2)}, u32[]{:S(2)}) collective-permute-start(f32[3,4,16,512]{3,2,1,0:T(8,128)S(1)} %get-tuple-element.121), channel_id=1, source_target_pairs={{0,48},{1,13},{4,52},{5,1},{8,56},{9,5},{12,60},{13,9},{16,0},{17,... | collective-permute-start | bytes 1179656 | tf_op jit(solution)/shard_map/ppermute | solution.py:404
  99.9 3.8 %collective-permute-done.11.b0f = f32[2,8,16,512]{3,2,1,0:T(8,128)S(1)} collective-permute-done((f32[2,8,16,512]{3,2,1,0:T(8,128)S(1)}, f32[2,8,16,512]{3,2,1,0:T(8,128)S(1)}, u32[]{:S(2)}, u32[]{:S(2)}) %collective-permute-start.11) | collective-permute-done | bytes 524320 | tf_op jit(solution)/shard_map/ppermute | solution.py:392
  103.7 2.6 %collective-permute-done.12.refs_1_ = f32[2,3,4,16,512]{4,3,2,1,0:T(8,128)S(1)} collective-permute-done((f32[2,3,4,16,512]{4,3,2,1,0:T(8,128)S(1)}, f32[2,3,4,16,512]{4,3,2,1,0:T(8,128)S(1)}, u32[]{:S(2)}, u32[]{:S(2)}) %collective-permute-start.12) | collective-permute-done | bytes 786464 | tf_op jit(solution)/shard_map/ppermute | solution.py:404
  106.3 4.2 %collective-permute-done.9.ra = f32[3,4,16,512]{3,2,1,0:T(8,128)S(1)} collective-permute-done((f32[3,4,16,512]{3,2,1,0:T(8,128)S(1)}, f32[3,4,16,512]{3,2,1,0:T(8,128)S(1)}, u32[]{:S(2)}, u32[]{:S(2)}) %collective-permute-start.9) | collective-permute-done | bytes 393248 | tf_op jit(solution)/shard_map/ppermute | solution.py:404
  110.5 0.1 relay_add.3
  110.7 1.2 collective-permute-start.14
  111.8 1.7 collective-permute-start.15
  113.6 0.5 collective-permute-start.16
  114.1 12.4 %collective-permute-done.16.b1f = f32[2,8,16,512]{3,2,1,0:T(8,128)S(1)} collective-permute-done((f32[2,8,16,512]{3,2,1,0:T(8,128)S(1)}, f32[2,8,16,512]{3,2,1,0:T(8,128)S(1)}, u32[]{:S(2)}, u32[]{:S(2)}) %collective-permute-start.16) | collective-permute-done | bytes 524320 | tf_op jit(solution)/shard_map/ppermute | solution.py:392
  126.5 0.3 plane_add.1
  126.8 2.3 %collective-permute-start.17 = (f32[2,2,3,16,512]{4,3,2,1,0:T(8,128)S(1)}, f32[2,2,3,16,512]{4,3,2,1,0:T(8,128)S(1)}, u32[]{:S(2)}, u32[]{:S(2)}) collective-permute-start(f32[2,2,3,16,512]{4,3,2,1,0:T(8,128)S(1)} %get-tuple-element.142), channel_id=1, source_target_pairs={{0,4},{1,17},{4,8},{5,21},{8,12},{9,25},{12,0},{13,29},{16,20},{17... | collective-permute-start | bytes 1179656 | tf_op jit(solution)/shard_map/ppermute | solution.py:404
  129.1 2.6 %collective-permute-start.18 = (f32[2,2,3,16,512]{4,3,2,1,0:T(8,128)S(1)}, f32[2,2,3,16,512]{4,3,2,1,0:T(8,128)S(1)}, u32[]{:S(2)}, u32[]{:S(2)}) collective-permute-start(f32[2,2,3,16,512]{4,3,2,1,0:T(8,128)S(1)} %get-tuple-element.143), channel_id=1, source_target_pairs={{0,12},{1,49},{4,0},{5,53},{8,4},{9,57},{12,8},{13,61},{16,28},{17... | collective-permute-start | bytes 1179656 | tf_op jit(solution)/shard_map/ppermute | solution.py:404
  131.7 1.1 collective-permute-start.19
  132.8 0.1 over_sum.1
  133.0 2.1 %collective-permute-start.21 = (f32[2,2,8,16,512]{4,3,2,1,0:T(8,128)S(1)}, f32[2,2,8,16,512]{4,3,2,1,0:T(8,128)S(1)}, u32[]{:S(2)}, u32[]{:S(2)}) collective-permute-start(f32[2,2,8,16,512]{4,3,2,1,0:T(8,128)S(1)} %over_sum.1), channel_id=1, source_target_pairs={{0,1},{1,2},{2,3},{3,4},{4,5},{5,6},{6,7},{7,8},{8,9},{9,10},{10,1... | collective-permute-start | bytes 3145736 | tf_op jit(solution)/shard_map/ppermute | solution.py:388
  135.1 1.8 collective-permute-start.22
  136.9 0.1 brightest.1.most
  137.0 0.1 collective-permute-done.17.b
  137.1 3.6 %collective-permute-done.18.c = f32[2,2,3,16,512]{4,3,2,1,0:T(8,128)S(1)} collective-permute-done((f32[2,2,3,16,512]{4,3,2,1,0:T(8,128)S(1)}, f32[2,2,3,16,512]{4,3,2,1,0:T(8,128)S(1)}, u32[]{:S(2)}, u32[]{:S(2)}) %collective-permute-start.18) | collective-permute-done | bytes 393248 | tf_op jit(solution)/shard_map/ppermute | solution.py:404
  140.7 1.8 collective-permute-done.19.d
  142.5 0.1 line_add.1
  142.6 4.6 %collective-permute-start.20 = (f32[13,8,512]{2,1,0:T(8,128)S(1)}, f32[13,8,512]{2,1,0:T(8,128)S(1)}, u32[]{:S(2)}, u32[]{:S(2)}) collective-permute-start(f32[13,8,512]{2,1,0:T(8,128)S(1)} %get-tuple-element.146), channel_id=1, source_target_pairs={{0,1},{1,0},{2,3},{3,2},{4,5},{5,4},{6,7},{7,6},{8,9},{9,8},{10,11... | collective-permute-start | bytes 638984 | tf_op jit(solution)/shard_map/ppermute | solution.py:392
  147.2 1.1 collective-permute-done.20.recv
  148.3 8.8 %collective-permute-done.21.over = f32[2,2,8,16,512]{4,3,2,1,0:T(8,128)S(1)} collective-permute-done((f32[2,2,8,16,512]{4,3,2,1,0:T(8,128)S(1)}, f32[2,2,8,16,512]{4,3,2,1,0:T(8,128)S(1)}, u32[]{:S(2)}, u32[]{:S(2)}) %collective-permute-start.21) | collective-permute-done | bytes 1048608 | tf_op jit(solution)/shard_map/ppermute | solution.py:388
  157.1 18.8 %collective-permute-done.22.tf = f32[2,2,8,16,512]{4,3,2,1,0:T(8,128)S(1)} collective-permute-done((f32[2,2,8,16,512]{4,3,2,1,0:T(8,128)S(1)}, f32[2,2,8,16,512]{4,3,2,1,0:T(8,128)S(1)}, u32[]{:S(2)}, u32[]{:S(2)}) %collective-permute-start.22) | collective-permute-done | bytes 1048608 | tf_op jit(solution)/shard_map/ppermute | solution.py:392
  176.0 0.4 collective-permute-start.23
  176.4 2.1 %collective-permute-start.25 = (f32[13,8,512]{2,1,0:T(8,128)S(1)}, f32[13,8,512]{2,1,0:T(8,128)S(1)}, u32[]{:S(2)}, u32[]{:S(2)}) collective-permute-start(f32[13,8,512]{2,1,0:T(8,128)S(1)} %get-tuple-element.152.near_max), channel_id=1, source_target_pairs={{0,66},{2,64},{64,2},{66,0},{1,67},{3,65},{65,3},{67,1},{4,70},{6,... | collective-permute-start | bytes 638984 | tf_op jit(solution)/shard_map/ppermute | solution.py:409
  178.5 1.1 collective-permute-start.24
  179.6 1.1 collective-permute-done.23.far_max.b
  180.8 3.0 %object_update.1 = f32[2,512,1024]{2,1,0:T(8,128)} custom-call(s32[2]{0:T(128)S(1)} %pad_add_fusion.place, s32[2]{0:T(128)S(1)} %collective-permute-done.place.before, f32[13,8,512]{2,1,0:T(8,128)S(1)} %get-tuple-element.152.near_max, f32[13,8,512]{2,1,0:T(8,128)S(1)} %collective-permute-done.23.far_max.b, f32[2,512,1024]{2,1,0:T(8,128)S(1)} %copy-done.2, ...), custom_call_target="tpu_custom_call" | custom-call | tf_op jit(solution)/shard_map/object_update/pallas_call | solution.py:601
  183.7 1.2 collective-permute-done.24.c
  185.0 1.6 mix.1
  (34 shorter events, 0.3 us)
Async XLA Ops:
  2.0 10.4 %copy-start = (bf16[2,6,512,512]{3,2,1,0:T(8,128)(2,1)S(1)}, bf16[2,6,512,512]{3,2,1,0:T(8,128)(2,1)}, u32[]{:S(2)}) copy-start(bf16[2,6,512,512]{3,2,1,0:T(8,128)(2,1)} %p_ref.9) | copy-start | bytes 18874372
  2.0 7.8 %collective-permute-start = (s32[2]{0:T(128)S(1)}, s32[2]{0:T(128)S(1)}, u32[]{:S(2)}, u32[]{:S(2)}) collective-permute-start(s32[2]{0:T(128)S(1)} %pad_add_fusion.place), channel_id=1, source_target_pairs={{0,1},{1,2},{2,3},{3,4},{4,5},{5,6},{6,7},{7,8},{8,9},{9,10},{10,1... | collective-permute-start | bytes 32 | tf_op jit(solution)/shard_map/ppermute | solution.py:388
  6.8 2.2 %copy-start.1 = (f32[2,512,1024]{2,1,0:T(8,128)S(1)}, f32[2,512,1024]{2,1,0:T(8,128)}, u32[]{:S(2)}) copy-start(f32[2,512,1024]{2,1,0:T(8,128)} %obj.3) | copy-start | bytes 12582916
  10.4 16.4 %collective-permute-start.1 = (f32[2,256,512]{2,1,0:T(8,128)S(1)}, f32[2,256,512]{2,1,0:T(8,128)S(1)}, u32[]{:S(2)}, u32[]{:S(2)}) collective-permute-start(f32[2,256,512]{2,1,0:T(8,128)S(1)} %rim_rows.1), channel_id=1, source_target_pairs={{1,0},{2,1},{3,2},{4,3},{5,4},{6,5},{7,6},{8,7},{9,8},{10,9},{11,1... | collective-permute-start | bytes 3145736 | tf_op jit(solution)/shard_map/ppermute | solution.py:388
  12.4 1.6 copy-start.3
  14.0 5.4 %copy-start.7 = (bf16[512,1024]{1,0:T(8,128)(2,1)S(1)}, bf16[512,1024]{1,0:T(8,128)(2,1)}, u32[]{:S(2)}) copy-start(bf16[512,1024]{1,0:T(8,128)(2,1)} %constant.14.clone.wt1.wt) | copy-start | bytes 3145732
  14.0 5.4 %copy-start.8 = (bf16[512,1024]{1,0:T(8,128)(2,1)S(1)}, bf16[512,1024]{1,0:T(8,128)(2,1)}, u32[]{:S(2)}) copy-start(bf16[512,1024]{1,0:T(8,128)(2,1)} %constant.13.clone.wt0.wt) | copy-start | bytes 3145732
  19.4 9.6 %copy-start.4 = (bf16[1024,1024]{1,0:T(8,128)(2,1)S(1)}, bf16[1024,1024]{1,0:T(8,128)(2,1)}, u32[]{:S(2)}) copy-start(bf16[1024,1024]{1,0:T(8,128)(2,1)} %constant.12.clone.table) | copy-start | bytes 6291460
  26.9 10.9 %collective-permute-start.2 = (f32[128,512]{1,0:T(8,128)S(1)}, f32[128,512]{1,0:T(8,128)S(1)}, u32[]{:S(2)}, u32[]{:S(2)}) collective-permute-start(f32[128,512]{1,0:T(8,128)S(1)} %get-tuple-element.91), channel_id=1, source_target_pairs={{0,64},{64,0},{1,65},{65,1},{2,66},{66,2},{3,67},{67,3},{4,68},{68... | collective-permute-start | bytes 786440 | tf_op jit(solution)/shard_map/ppermute | solution.py:392
  36.9 15.6 %collective-permute-start.3 = (f32[256,512]{1,0:T(8,128)S(1)}, f32[256,512]{1,0:T(8,128)S(1)}, u32[]{:S(2)}, u32[]{:S(2)}) collective-permute-start(f32[256,512]{1,0:T(8,128)S(1)} %get-tuple-element.93.s0), channel_id=1, source_target_pairs={{0,64},{64,0},{1,65},{65,1},{2,66},{66,2},{3,67},{67,3},{4,68},{68... | collective-permute-start | bytes 1572872 | tf_op jit(solution)/shard_map/ppermute | solution.py:392
  37.8 14.7 %copy-start.5 = (bf16[1024,1024]{1,0:T(8,128)(2,1)S(1)}, bf16[1024,1024]{1,0:T(8,128)(2,1)}, u32[]{:S(2)}) copy-start(bf16[1024,1024]{1,0:T(8,128)(2,1)} %constant.15.clone.table) | copy-start | bytes 6291460
  37.8 14.7 %copy-start.9 = (f32[1,512,512]{2,1,0:T(8,128)S(1)}, f32[1,512,512]{2,1,0:T(8,128)}, u32[]{:S(2)}) copy-start(f32[1,512,512]{2,1,0:T(8,128)} %pat.3) | copy-start | bytes 3145732
  40.6 19.3 %collective-permute-start.4 = (f32[256,512]{1,0:T(8,128)S(1)}, f32[256,512]{1,0:T(8,128)S(1)}, u32[]{:S(2)}, u32[]{:S(2)}) collective-permute-start(f32[256,512]{1,0:T(8,128)S(1)} %get-tuple-element.97.s0), channel_id=1, source_target_pairs={{0,64},{64,0},{1,65},{65,1},{2,66},{66,2},{3,67},{67,3},{4,68},{68... | collective-permute-start | bytes 1572872 | tf_op jit(solution)/shard_map/ppermute | solution.py:392
  52.5 7.4 %copy-start.10 = (bf16[512,1024]{1,0:T(8,128)(2,1)S(1)}, bf16[512,1024]{1,0:T(8,128)(2,1)}, u32[]{:S(2)}) copy-start(bf16[512,1024]{1,0:T(8,128)(2,1)} %constant.16.clone.bt) | copy-start | bytes 3145732
  59.9 10.9 %copy-start.6 = (bf16[512,1024]{1,0:T(8,128)(2,1)S(1)}, bf16[512,1024]{1,0:T(8,128)(2,1)}, u32[]{:S(2)}) copy-start(bf16[512,1024]{1,0:T(8,128)(2,1)} %constant.17.clone.bt) | copy-start | bytes 3145732
  70.7 5.7 %collective-permute-start.5 = (f32[6,16,16,512]{3,2,1,0:T(8,128)S(1)}, f32[6,16,16,512]{3,2,1,0:T(8,128)S(1)}, u32[]{:S(2)}, u32[]{:S(2)}) collective-permute-start(f32[6,16,16,512]{3,2,1,0:T(8,128)S(1)} %get-tuple-element.107), channel_id=1, source_target_pairs={{0,1},{1,0},{2,3},{3,2},{4,5},{5,4},{6,7},{7,6},{8,9},{9,8},{10,11... | collective-permute-start | bytes 9437192 | tf_op jit(solution)/shard_map/ppermute | solution.py:392
  80.3 16.5 %collective-permute-start.8 = (f32[6,16,16,512]{3,2,1,0:T(8,128)S(1)}, f32[6,16,16,512]{3,2,1,0:T(8,128)S(1)}, u32[]{:S(2)}, u32[]{:S(2)}) collective-permute-start(f32[6,16,16,512]{3,2,1,0:T(8,128)S(1)} %get-tuple-element.119), channel_id=1, source_target_pairs={{0,1},{1,0},{2,3},{3,2},{4,5},{5,4},{6,7},{7,6},{8,9},{9,8},{10,11... | collective-permute-start | bytes 9437192 | tf_op jit(solution)/shard_map/ppermute | solution.py:392
  80.5 13.3 %collective-permute-start.6 = (f32[3,4,16,512]{3,2,1,0:T(8,128)S(1)}, f32[3,4,16,512]{3,2,1,0:T(8,128)S(1)}, u32[]{:S(2)}, u32[]{:S(2)}) collective-permute-start(f32[3,4,16,512]{3,2,1,0:T(8,128)S(1)} %get-tuple-element.115), channel_id=1, source_target_pairs={{0,16},{1,5},{4,20},{5,9},{8,24},{9,13},{12,28},{13,1},{16,32},{17... | collective-permute-start | bytes 1179656 | tf_op jit(solution)/shard_map/ppermute | solution.py:404
  86.2 7.6 %collective-permute-start.7 = (f32[3,4,16,512]{3,2,1,0:T(8,128)S(1)}, f32[3,4,16,512]{3,2,1,0:T(8,128)S(1)}, u32[]{:S(2)}, u32[]{:S(2)}) collective-permute-start(f32[3,4,16,512]{3,2,1,0:T(8,128)S(1)} %get-tuple-element.116), channel_id=1, source_target_pairs={{0,48},{1,13},{4,52},{5,1},{8,56},{9,5},{12,60},{13,9},{16,0},{17,... | collective-permute-start | bytes 1179656 | tf_op jit(solution)/shard_map/ppermute | solution.py:404
  88.3 15.4 %collective-permute-start.11 = (f32[2,8,16,512]{3,2,1,0:T(8,128)S(1)}, f32[2,8,16,512]{3,2,1,0:T(8,128)S(1)}, u32[]{:S(2)}, u32[]{:S(2)}) collective-permute-start(f32[2,8,16,512]{3,2,1,0:T(8,128)S(1)} %get-tuple-element.122.b0), channel_id=1, source_target_pairs={{0,64},{64,0},{1,65},{65,1},{2,66},{66,2},{3,67},{67,3},{4,68},{68... | collective-permute-start | bytes 1572872 | tf_op jit(solution)/shard_map/ppermute | solution.py:392
  93.9 12.4 %collective-permute-start.12 = (f32[2,3,4,16,512]{4,3,2,1,0:T(8,128)S(1)}, f32[2,3,4,16,512]{4,3,2,1,0:T(8,128)S(1)}, u32[]{:S(2)}, u32[]{:S(2)}) collective-permute-start(f32[2,3,4,16,512]{4,3,2,1,0:T(8,128)S(1)} %get-tuple-element.117), channel_id=1, source_target_pairs={{0,16},{1,5},{4,20},{5,9},{8,24},{9,13},{12,28},{13,1},{16,32},{17... | collective-permute-start | bytes 2359304 | tf_op jit(solution)/shard_map/ppermute | solution.py:404
  94.9 11.4 %collective-permute-start.13 = (f32[2,3,4,16,512]{4,3,2,1,0:T(8,128)S(1)}, f32[2,3,4,16,512]{4,3,2,1,0:T(8,128)S(1)}, u32[]{:S(2)}, u32[]{:S(2)}) collective-permute-start(f32[2,3,4,16,512]{4,3,2,1,0:T(8,128)S(1)} %get-tuple-element.124), channel_id=1, source_target_pairs={{0,48},{1,13},{4,52},{5,1},{8,56},{9,5},{12,60},{13,9},{16,0},{17,... | collective-permute-start | bytes 2359304 | tf_op jit(solution)/shard_map/ppermute | solution.py:404
  97.2 13.4 %collective-permute-start.9 = (f32[3,4,16,512]{3,2,1,0:T(8,128)S(1)}, f32[3,4,16,512]{3,2,1,0:T(8,128)S(1)}, u32[]{:S(2)}, u32[]{:S(2)}) collective-permute-start(f32[3,4,16,512]{3,2,1,0:T(8,128)S(1)} %get-tuple-element.120), channel_id=1, source_target_pairs={{0,16},{1,5},{4,20},{5,9},{8,24},{9,13},{12,28},{13,1},{16,32},{17... | collective-permute-start | bytes 1179656 | tf_op jit(solution)/shard_map/ppermute | solution.py:404
  97.3 13.3 %collective-permute-start.10 = (f32[3,4,16,512]{3,2,1,0:T(8,128)S(1)}, f32[3,4,16,512]{3,2,1,0:T(8,128)S(1)}, u32[]{:S(2)}, u32[]{:S(2)}) collective-permute-start(f32[3,4,16,512]{3,2,1,0:T(8,128)S(1)} %get-tuple-element.121), channel_id=1, source_target_pairs={{0,48},{1,13},{4,52},{5,1},{8,56},{9,5},{12,60},{13,9},{16,0},{17,... | collective-permute-start | bytes 1179656 | tf_op jit(solution)/shard_map/ppermute | solution.py:404
  110.7 15.8 %collective-permute-start.14 = (f32[2,3,4,16,512]{4,3,2,1,0:T(8,128)S(1)}, f32[2,3,4,16,512]{4,3,2,1,0:T(8,128)S(1)}, u32[]{:S(2)}, u32[]{:S(2)}) collective-permute-start(f32[2,3,4,16,512]{4,3,2,1,0:T(8,128)S(1)} %get-tuple-element.133), channel_id=1, source_target_pairs={{0,16},{1,5},{4,20},{5,9},{8,24},{9,13},{12,28},{13,1},{16,32},{17... | collective-permute-start | bytes 2359304 | tf_op jit(solution)/shard_map/ppermute | solution.py:404
  111.8 14.6 %collective-permute-start.15 = (f32[2,3,4,16,512]{4,3,2,1,0:T(8,128)S(1)}, f32[2,3,4,16,512]{4,3,2,1,0:T(8,128)S(1)}, u32[]{:S(2)}, u32[]{:S(2)}) collective-permute-start(f32[2,3,4,16,512]{4,3,2,1,0:T(8,128)S(1)} %get-tuple-element.134), channel_id=1, source_target_pairs={{0,48},{1,13},{4,52},{5,1},{8,56},{9,5},{12,60},{13,9},{16,0},{17,... | collective-permute-start | bytes 2359304 | tf_op jit(solution)/shard_map/ppermute | solution.py:404
  113.6 12.9 %collective-permute-start.16 = (f32[2,8,16,512]{3,2,1,0:T(8,128)S(1)}, f32[2,8,16,512]{3,2,1,0:T(8,128)S(1)}, u32[]{:S(2)}, u32[]{:S(2)}) collective-permute-start(f32[2,8,16,512]{3,2,1,0:T(8,128)S(1)} %get-tuple-element.137.b1), channel_id=1, source_target_pairs={{0,64},{64,0},{1,65},{65,1},{2,66},{66,2},{3,67},{67,3},{4,68},{68... | collective-permute-start | bytes 1572872 | tf_op jit(solution)/shard_map/ppermute | solution.py:392
  126.8 10.3 %collective-permute-start.17 = (f32[2,2,3,16,512]{4,3,2,1,0:T(8,128)S(1)}, f32[2,2,3,16,512]{4,3,2,1,0:T(8,128)S(1)}, u32[]{:S(2)}, u32[]{:S(2)}) collective-permute-start(f32[2,2,3,16,512]{4,3,2,1,0:T(8,128)S(1)} %get-tuple-element.142), channel_id=1, source_target_pairs={{0,4},{1,17},{4,8},{5,21},{8,12},{9,25},{12,0},{13,29},{16,20},{17... | collective-permute-start | bytes 1179656 | tf_op jit(solution)/shard_map/ppermute | solution.py:404
  129.1 11.5 %collective-permute-start.18 = (f32[2,2,3,16,512]{4,3,2,1,0:T(8,128)S(1)}, f32[2,2,3,16,512]{4,3,2,1,0:T(8,128)S(1)}, u32[]{:S(2)}, u32[]{:S(2)}) collective-permute-start(f32[2,2,3,16,512]{4,3,2,1,0:T(8,128)S(1)} %get-tuple-element.143), channel_id=1, source_target_pairs={{0,12},{1,49},{4,0},{5,53},{8,4},{9,57},{12,8},{13,61},{16,28},{17... | collective-permute-start | bytes 1179656 | tf_op jit(solution)/shard_map/ppermute | solution.py:404
  131.7 10.8 %collective-permute-start.19 = (f32[2,2,3,16,512]{4,3,2,1,0:T(8,128)S(1)}, f32[2,2,3,16,512]{4,3,2,1,0:T(8,128)S(1)}, u32[]{:S(2)}, u32[]{:S(2)}) collective-permute-start(f32[2,2,3,16,512]{4,3,2,1,0:T(8,128)S(1)} %get-tuple-element.144), channel_id=1, source_target_pairs={{0,8},{1,33},{4,12},{5,37},{8,0},{9,41},{12,4},{13,45},{16,24},{17... | collective-permute-start | bytes 1179656 | tf_op jit(solution)/shard_map/ppermute | solution.py:404
  133.0 24.1 %collective-permute-start.21 = (f32[2,2,8,16,512]{4,3,2,1,0:T(8,128)S(1)}, f32[2,2,8,16,512]{4,3,2,1,0:T(8,128)S(1)}, u32[]{:S(2)}, u32[]{:S(2)}) collective-permute-start(f32[2,2,8,16,512]{4,3,2,1,0:T(8,128)S(1)} %over_sum.1), channel_id=1, source_target_pairs={{0,1},{1,2},{2,3},{3,4},{4,5},{5,6},{6,7},{7,8},{8,9},{9,10},{10,1... | collective-permute-start | bytes 3145736 | tf_op jit(solution)/shard_map/ppermute | solution.py:388
  135.1 40.9 %collective-permute-start.22 = (f32[2,2,8,16,512]{4,3,2,1,0:T(8,128)S(1)}, f32[2,2,8,16,512]{4,3,2,1,0:T(8,128)S(1)}, u32[]{:S(2)}, u32[]{:S(2)}) collective-permute-start(f32[2,2,8,16,512]{4,3,2,1,0:T(8,128)S(1)} %get-tuple-element.149.t), channel_id=1, source_target_pairs={{0,64},{64,0},{1,65},{65,1},{2,66},{66,2},{3,67},{67,3},{4,68},{68... | collective-permute-start | bytes 3145736 | tf_op jit(solution)/shard_map/ppermute | solution.py:392
  142.6 5.7 %collective-permute-start.20 = (f32[13,8,512]{2,1,0:T(8,128)S(1)}, f32[13,8,512]{2,1,0:T(8,128)S(1)}, u32[]{:S(2)}, u32[]{:S(2)}) collective-permute-start(f32[13,8,512]{2,1,0:T(8,128)S(1)} %get-tuple-element.146), channel_id=1, source_target_pairs={{0,1},{1,0},{2,3},{3,2},{4,5},{5,4},{6,7},{7,6},{8,9},{9,8},{10,11... | collective-permute-start | bytes 638984 | tf_op jit(solution)/shard_map/ppermute | solution.py:392
  175.9 4.8 %copy-start.2 = (f32[2,512,1024]{2,1,0:T(8,128)S(1)}, f32[2,512,1024]{2,1,0:T(8,128)}, u32[]{:S(2)}) copy-start(f32[2,512,1024]{2,1,0:T(8,128)} %obj.3) | copy-start | bytes 12582916
  176.0 4.8 %collective-permute-start.23 = (f32[13,8,512]{2,1,0:T(8,128)S(1)}, f32[13,8,512]{2,1,0:T(8,128)S(1)}, u32[]{:S(2)}, u32[]{:S(2)}) collective-permute-start(f32[13,8,512]{2,1,0:T(8,128)S(1)} %get-tuple-element.152.near_max), channel_id=1, source_target_pairs={{0,2},{2,0},{64,66},{66,64},{1,3},{3,1},{65,67},{67,65},{4,6},{6,4... | collective-permute-start | bytes 638984 | tf_op jit(solution)/shard_map/ppermute | solution.py:409
  176.4 8.5 %collective-permute-start.25 = (f32[13,8,512]{2,1,0:T(8,128)S(1)}, f32[13,8,512]{2,1,0:T(8,128)S(1)}, u32[]{:S(2)}, u32[]{:S(2)}) collective-permute-start(f32[13,8,512]{2,1,0:T(8,128)S(1)} %get-tuple-element.152.near_max), channel_id=1, source_target_pairs={{0,66},{2,64},{64,2},{66,0},{1,67},{3,65},{65,3},{67,1},{4,70},{6,... | collective-permute-start | bytes 638984 | tf_op jit(solution)/shard_map/ppermute | solution.py:409
  178.5 6.4 %copy-start.11 = (s32[12,12]{1,0:T(8,128)S(1)}, s32[12,12]{1,0:T(8,128)}, u32[]{:S(2)}) copy-start(s32[12,12]{1,0:T(8,128)} %w_ref.1) | copy-start | bytes 1732
  178.5 6.4 %collective-permute-start.24 = (f32[2,6,8,512]{3,2,1,0:T(8,128)S(1)}, f32[2,6,8,512]{3,2,1,0:T(8,128)S(1)}, u32[]{:S(2)}, u32[]{:S(2)}) collective-permute-start(f32[2,6,8,512]{3,2,1,0:T(8,128)S(1)} %get-tuple-element.155.mine), channel_id=1, source_target_pairs={{0,64},{2,66},{64,0},{66,2},{1,65},{3,67},{65,1},{67,3},{4,68},{6,... | collective-permute-start | bytes 589832 | tf_op jit(solution)/shard_map/ppermute | solution.py:409

commit v7 on v6

--- a/solution.py
+++ b/solution.py
@@ -320,11 +320,11 @@
 UNROLL = 8
 LIMIT = 4
 STAGE = pl.CostEstimate(flops=int(5e9), transcendentals=0, bytes_accessed=int(15e6))
-GRADS = [shape(2, 8, 16, N), shape(2, 2, 8, 16, N)]
-
-
-def first_block_body(pat, s0, s1, wave_ref, table, bt, top, ptop, pbot, p_ref, half_ref, keep, send, gbot, tops, scale_s, x_s, back_s):
-    gtop = tops.at[0]
+GRADS = [shape(2, 2, 8, 16, N)] * 2
+
+
+def first_block_body(pat, s0, s1, wave_ref, table, bt, top, ptop, pbot, p_ref, half_ref, keep, send, bots, tops, scale_s, x_s, back_s):
+    gtop, gbot = tops.at[0], bots.at[0]
     set_scale(pat, H, s0, s1, scale_s)
     gtop[...] = jnp.zeros_like(gtop)
     gbot[...] = jnp.zeros_like(gbot)
@@ -349,13 +349,13 @@
     )(pat, s0, s1, wave, table, back_rows, top, ptop, pbot, probe)
 
 
-def second_block(back_rows, top, bot, ptop, pbot, probe, first, count, tops, earlier=None):
+def second_block(back_rows, top, bot, ptop, pbot, probe, first, count, bots, tops, earlier=None):
     nm = top.shape[0]
     given = earlier or []
 
     def body(bt, top, bot, ptop, pbot, p_ref, *refs):
-        keep, send, gbot, tops, back_s = refs[1 + len(given) :]
-        gtop = tops.at[1]
+        keep, send, bots, tops, back_s = refs[2 + len(given) :]
+        gtop, gbot = tops.at[1], bots.at[1]
         if not given:
             gtop[...] = jnp.zeros_like(gtop)
             gbot[...] = jnp.zeros_like(gbot)
@@ -370,12 +370,12 @@
     return local_call(
         body,
         "second_block",
-        [LOCAL] * (7 + len(given)),
+        [LOCAL] * (8 + len(given)),
         [shape(nm, 16, 16, N)] * 2 + GRADS,
         [pltpu.VMEM((N, N), f32)],
         6,
-        {6: 3, **{7 + i: i for i in range(len(given))}},
-    )(back_rows, top, bot, ptop, pbot, probe, tops, *given)
+        {6: 2, 7: 3, **{8 + i: i for i in range(len(given))}},
+    )(back_rows, top, bot, ptop, pbot, probe, bots, tops, *given)
 
 
 SCAN = ("y", "z", "x", "core")
@@ -548,7 +548,7 @@
     return local_call(mix_body, "mix", [SCALARS] + [LOCAL] * 4, outs, [], LIMIT)(mixing, mine, b, c, d)[0]
 
 
-def object_body(place, before, near_max, far_max, obj, t, tf, b0, b0f, b1, b1f, over, out, new, sems):
+def object_body(place, before, near_max, far_max, obj, t, tf, b, bf, over, out, new, sems):
     shift, col = place[0], pl.multiple_of(place[1] * H, H)
     over_shift, over_col = before[0], pl.multiple_of(before[1] * H, H)
     last = near_max.shape[0] - 1
@@ -582,7 +582,7 @@
 
             @pl.when(shift == 0)
             def _():
-                add(col, (b0, b0f), (b1, b1f))
+                add(col, (b.at[0], bf.at[0]), (b.at[1], bf.at[1]))
 
         else:
 
@@ -600,7 +600,7 @@
 def object_update(place, before, near_max, far_max, obj, pieces, over):
     return pl.pallas_call(
         object_body,
-        in_specs=[SCALARS] * 2 + [LOCAL] * 10,
+        in_specs=[SCALARS] * 2 + [LOCAL] * 8,
         out_specs=FAR,
         out_shape=shape(2, N, 4 * H),
         scratch_shapes=[pltpu.VMEM((2, N, 4 * H), f32), pltpu.SemaphoreType.DMA((2,))],
@@ -609,13 +609,13 @@
     )(place, before, near_max, far_max, obj, *pieces, over)
 
 
-def over_body(b0, b0f, b1, b1f, out):
-    out[0] = b0[...] + b0f[...]
-    out[1] = b1[...] + b1f[...]
-
-
-def over_sum(b0, b0f, b1, b1f):
-    return local_call(over_body, "over_sum", [LOCAL] * 4, [shape(2, 2, 8, 16, N)], [], LIMIT, cost=STAGE)(b0, b0f, b1, b1f)[0]
+def over_body(g, gf, out):
+    out[...] = g[...] + gf[...]
+
+
+def over_sum(grads, far):
+    outs = [shape(2, 2, 8, 16, N)]
+    return local_call(over_body, "over_sum", [LOCAL] * 2, outs, [], LIMIT, cost=STAGE)(grads, far)[0]
 
 
 def tied(*values):
@@ -641,34 +641,30 @@
     wave_bot, sum_bot = low_wave(wave_bot_rows, half_bot, wave_bot)
     far_bot = swapped(sum_bot, "mode")
     fixed = fixed_top(patterns, sum_top, far_top, wave_top, plus)
-    low, keep0, send0, bot0, tops = first_block(
+    low, keep0, send0, bots, tops = first_block(
         patterns, sum_bot, far_bot, wave_bot, plus, back_rows0, fixed, patch_top, patch_bot, probe
     )
     most = brightest(own_light, far_light)
     recv0 = swapped(send0, "core")
-    bot0_far = swapped(bot0, "mode")
-    *part1, tops = second_block(back_rows1, fixed, low, patch_top, patch_bot, probe, 0, 3, tops)
+    *part1, bots, tops = second_block(back_rows1, fixed, low, patch_top, patch_bot, probe, 0, 3, bots, tops)
     own0, near0, back0, far0a, far0b = core_add(keep0, recv0)
     ra0, rb0 = turned(far0a, 1, True), turned(far0b, -1, True)
     *part1, near0 = tied(*part1, near0)
-    keep1, send1, bot1, tops = second_block(
-        back_rows1, fixed, low, patch_top, patch_bot, probe, 3, 3, tops, part1
+    keep1, send1, bots, tops = second_block(
+        back_rows1, fixed, low, patch_top, patch_bot, probe, 3, 3, bots, tops, part1
     )
+    bots_far = swapped(bots, "mode")
     recv1 = swapped(send1, "core")
     near0, back0 = relay_add(near0, back0, ra0, rb0)
     keep1, _ = tied(keep1, near0)
     own1, near1, back1, far1a, far1b = core_add(keep1, recv1)
     ra1, rb1 = turned(far1a, 1, True), turned(far1b, -1, True)
     plane0 = (own0, turned(near0, 1, True), turned(back0, -1, True))
-    ra1, rb1, bot0_far, *plane0 = tied(ra1, rb1, bot0_far, *plane0)
-    bot1_next, _ = tied(bot1, bot0_far)
-    bot1_far = swapped(bot1_next, "mode")
+    ra1, rb1, bots_far, *plane0 = tied(ra1, rb1, bots_far, *plane0)
     near1, back1 = relay_add(near1, back1, ra1, rb1)
     plane1 = (own1, turned(near1, 1, True), turned(back1, -1, True))
-    *plane1, bot1_far = tied(*plane1, bot1_far)
-    tops_next, _ = tied(tops, bot1_far)
-    tops_far = swapped(tops_next, "mode")
-    over = along(over_sum(bot0, bot0_far, bot1, bot1_far), 1)
+    tops_far = swapped(tops, "mode")
+    over = along(over_sum(bots, bots_far), 1)
     line = plane_add((plane0, plane1))
     line = [line[0]] + [turned(line[r], r, False) for r in (1, 3, 2)]
     keep, send = line_add(most, line)
@@ -676,8 +672,7 @@
     mine, other = pixel_step(most, keep, recv, rows)
     beside = across(other, 0, 1)
     probe_new = mix(mixing, mine, beside, across(mine, 1, 0), across(other, 1, 1))
-    pieces = (tops, tops_far, bot0, bot0_far, bot1, bot1_far)
-    object_new = object_update(place, before, other, beside, object_field, pieces, over)
+    object_new = object_update(place, before, other, beside, object_field, (tops, tops_far, bots, bots_far), over)
     return object_new, probe_new
 
 

time: 187 us -> 170 us (0.909)
  waiting for transfers between devices: 82 us -> 58.9 us
  starting transfers between devices: 47.7 us -> 53.2 us
    ppermute x9 -> x8, waiting for transfers between devices: 50.4 us -> 30.6 us  [swapped(): return lax.ppermute(value, axis, [(0, 1), (1, 0)])]
    ppermute x3, waiting for transfers between devices: 11.9 us -> 3.1 us  [along(): return lax.ppermute(value, SCAN, [(i, i + steps) for i in range(lo, hi)])]
    ppermute x9 -> x8, starting transfers between devices: 13 us -> 20.5 us  [swapped(): return lax.ppermute(value, axis, [(0, 1), (1, 0)])]
    ppermute x3, waiting for transfers between devices: 2.34 us -> 5.55 us  [across(): return lax.ppermute(value, ('mode', 'x'), pairs)]
    ppermute x11, starting transfers between devices: 22.3 us -> 19.3 us  [turned(): return lax.ppermute(value, RING, pairs)]
    ppermute x11, waiting for transfers between devices: 17.3 us -> 19.6 us  [turned(): return lax.ppermute(value, RING, pairs)]
  transfers between devices with their start and end apart: 26 -> 25, of which waited for: 17 -> 13; matrix products, arithmetic and copies ran while one was open for 0% -> 0% of each run, Pallas kernels for 18% -> 20%
where the time goes in v7:
time: 170 us; the launch traced here: 169 us
  waiting for transfers between devices  58.9 us (35%)
  starting transfers between devices  53.2 us (31%)
  Pallas kernels  50.7 us (30%)
  local copies, waits for them, and re-layouts  3.81 us (2%)
  between operations  2.21 us (1%)
    pallas_call x20, Pallas kernels, call(): pl.pallas_call(body, in_specs=ins, out_specs=[LOCAL] * len(outs), out_sha...  47.5 us
    ppermute x8, waiting for transfers between devices, swapped(): return lax.ppermute(value, axis, [(0, 1), (1, 0)])  30.6 us
    ppermute x8, starting transfers between devices, swapped(): return lax.ppermute(value, axis, [(0, 1), (1, 0)])  20.5 us
    ppermute x11, waiting for transfers between devices, turned(): return lax.ppermute(value, RING, pairs)  19.6 us
    ppermute x11, starting transfers between devices, turned(): return lax.ppermute(value, RING, pairs)  19.3 us
    ppermute x3, starting transfers between devices, along(): return lax.ppermute(value, SCAN, [(i, i + steps) for i in range(lo, hi)])  10.1 us
    ppermute x3, waiting for transfers between devices, across(): return lax.ppermute(value, ('mode', 'x'), pairs)  5.55 us
    unnamed x24, local copies, waits for them, and re-layouts  3.81 us
  transfers between devices with their start and end apart: 25, of which 13 were waited for; matrix products, arithmetic and copies ran while one was open for 0% of the time, Pallas kernels for 20%

profile of v7, /device:TPU:1, one launch (start us, length us, event | category | flops | bytes accessed | tf_op | source)
XLA Modules:
  0.0 168.9 jit_solution(11367863623407663901)
XLA Ops:
  1.9 0.1 pad_add_fusion.place
  2.0 4.8 %collective-permute-start = (s32[2]{0:T(128)S(1)}, s32[2]{0:T(128)S(1)}, u32[]{:S(2)}, u32[]{:S(2)}) collective-permute-start(s32[2]{0:T(128)S(1)} %pad_add_fusion.place), channel_id=1, source_target_pairs={{0,1},{1,2},{2,3},{3,4},{4,5},{5,6},{6,7},{7,8},{8,9},{9,10},{10,1... | collective-permute-start | bytes 32 | tf_op jit(solution)/shard_map/ppermute | solution.py:388
  6.8 0.0 copy-start.1
  6.8 2.2 %copy-done.1 = f32[2,512,1024]{2,1,0:T(8,128)S(1)} copy-done((f32[2,512,1024]{2,1,0:T(8,128)S(1)}, f32[2,512,1024]{2,1,0:T(8,128)}, u32[]{:S(2)}) %copy-start.1) | copy-done | bytes 4194328
  9.0 0.8 own_rows.1
  9.8 0.6 rim_rows.1
  10.4 1.9 %collective-permute-start.1 = (f32[2,256,512]{2,1,0:T(8,128)S(1)}, f32[2,256,512]{2,1,0:T(8,128)S(1)}, u32[]{:S(2)}, u32[]{:S(2)}) collective-permute-start(f32[2,256,512]{2,1,0:T(8,128)S(1)} %rim_rows.1), channel_id=1, source_target_pairs={{1,0},{2,1},{3,2},{4,3},{5,4},{6,5},{7,6},{8,7},{9,8},{10,9},{11,1... | collective-permute-start | bytes 3145736 | tf_op jit(solution)/shard_map/ppermute | solution.py:388
  12.4 0.0 copy-start.3
  12.4 1.6 copy-done.3
  14.0 5.4 %top_half.1 = (bf16[6,512,512]{2,1,0:T(8,128)(2,1)S(1)}, f32[128,512]{1,0:T(8,128)S(1)}, f32[128,512]{1,0:T(8,128)S(1)}, f32[2,6,8,512]{3,2,1,0:T(8,128)S(1)}) custom-call(f32[2,256,512]{2,1,0:T(8,128)S(1)} %get-tuple-element.74.patch_ref.ptop, bf16[2,6,512,512]{3,2,1,0:T(8,128)(2,1)S(1)} %copy-done, bf16[1024,1024]{1,0:T(8,128)(2,1)S(1)} %copy-done.3), custom_call_target="tpu_custom_call" | custom-call | tf_op jit(solution)/shard_map/top_half/pallas_call | solution.py:58
  19.4 0.0 copy-start.4
  19.4 4.3 %first_terms.1 = (f32[6,512,512]{2,1,0:T(8,128)S(1)}, f32[6,512,512]{2,1,0:T(8,128)S(1)}) custom-call(bf16[512,1024]{1,0:T(8,128)(2,1)S(1)} %copy-done.8, bf16[512,1024]{1,0:T(8,128)(2,1)S(1)} %copy-done.7, bf16[6,512,512]{2,1,0:T(8,128)(2,1)S(1)} %get-tuple-element.78.top), custom_call_target="tpu_custom_call" | custom-call | tf_op jit(solution)/shard_map/first_terms/pallas_call | solution.py:58
  23.8 3.1 %collective-permute-done.1.rim = f32[2,256,512]{2,1,0:T(8,128)S(1)} collective-permute-done((f32[2,256,512]{2,1,0:T(8,128)S(1)}, f32[2,256,512]{2,1,0:T(8,128)S(1)}, u32[]{:S(2)}, u32[]{:S(2)}) %collective-permute-start.1) | collective-permute-done | bytes 1048608 | tf_op jit(solution)/shard_map/ppermute | solution.py:388
  26.9 2.2 %collective-permute-start.2 = (f32[128,512]{1,0:T(8,128)S(1)}, f32[128,512]{1,0:T(8,128)S(1)}, u32[]{:S(2)}, u32[]{:S(2)}) collective-permute-start(f32[128,512]{1,0:T(8,128)S(1)} %get-tuple-element.84), channel_id=1, source_target_pairs={{0,64},{64,0},{1,65},{65,1},{2,66},{66,2},{3,67},{67,3},{4,68},{68... | collective-permute-start | bytes 786440 | tf_op jit(solution)/shard_map/ppermute | solution.py:392
  29.0 7.9 %bottom_half.1 = (bf16[6,512,512]{2,1,0:T(8,128)(2,1)S(1)}, f32[2,256,512]{2,1,0:T(8,128)S(1)}, f32[6,512,512]{2,1,0:T(8,128)S(1)}, f32[256,512]{1,0:T(8,128)S(1)}) custom-call(s32[2]{0:T(128)S(1)} %pad_add_fusion.place, f32[2,256,512]{2,1,0:T(8,128)S(1)} %get-tuple-element.76.own, ...), custom_call_target="tpu_custom_call", output_to_operand_aliasing={{2}: (6, {})} | custom-call | tf_op jit(solution)/shard_map/bottom_half/pallas_call | solution.py:58
  36.9 0.9 collective-permute-start.3
  37.8 2.7 %low_wave.1 = (f32[6,512,512]{2,1,0:T(8,128)S(1)}, f32[256,512]{1,0:T(8,128)S(1)}) custom-call(bf16[512,1024]{1,0:T(8,128)(2,1)S(1)} %copy-done.7, bf16[6,512,512]{2,1,0:T(8,128)(2,1)S(1)} %get-tuple-element.88.bot, f32[6,512,512]{2,1,0:T(8,128)S(1)} %get-tuple-element.89._), custom_call_target="tpu_custom_call", output_to_operand_aliasing={{0}: (2, {})} | custom-call | tf_op jit(solution)/shard_map/low_wave/pallas_call | solution.py:58
  40.5 2.2 %collective-permute-start.4 = (f32[256,512]{1,0:T(8,128)S(1)}, f32[256,512]{1,0:T(8,128)S(1)}, u32[]{:S(2)}, u32[]{:S(2)}) collective-permute-start(f32[256,512]{1,0:T(8,128)S(1)} %get-tuple-element.90.s0), channel_id=1, source_target_pairs={{0,64},{64,0},{1,65},{65,1},{2,66},{66,2},{3,67},{67,3},{4,68},{68... | collective-permute-start | bytes 1572872 | tf_op jit(solution)/shard_map/ppermute | solution.py:392
  42.8 9.7 %collective-permute-done.3.s1 = f32[256,512]{1,0:T(8,128)S(1)} collective-permute-done((f32[256,512]{1,0:T(8,128)S(1)}, f32[256,512]{1,0:T(8,128)S(1)}, u32[]{:S(2)}, u32[]{:S(2)}) %collective-permute-start.3) | collective-permute-done | bytes 524320 | tf_op jit(solution)/shard_map/ppermute | solution.py:392
  52.5 4.9 %fixed_top.1.top = bf16[6,512,512]{2,1,0:T(8,128)(2,1)S(1)} custom-call(f32[1,512,512]{2,1,0:T(8,128)S(1)} %copy-done.9, f32[256,512]{1,0:T(8,128)S(1)} %get-tuple-element.86.s0, f32[256,512]{1,0:T(8,128)S(1)} %collective-permute-done.3.s1, f32[6,512,512]{2,1,0:T(8,128)S(1)} %get-tuple-element.87.wave_ref, bf16[1024,1024]{1,0:T(8,128)(2,1)S(1)} %copy-done.5), custom_call_target="tpu_custom_call" | custom-call | tf_op jit(solution)/shard_map/fixed_top/pallas_call | solution.py:58
  57.4 2.6 %collective-permute-done.4.s1 = f32[256,512]{1,0:T(8,128)S(1)} collective-permute-done((f32[256,512]{1,0:T(8,128)S(1)}, f32[256,512]{1,0:T(8,128)S(1)}, u32[]{:S(2)}, u32[]{:S(2)}) %collective-permute-start.4) | collective-permute-done | bytes 524320 | tf_op jit(solution)/shard_map/ppermute | solution.py:392
  60.0 10.8 %first_block.1 = (bf16[6,512,512]{2,1,0:T(8,128)(2,1)S(1)}, f32[6,16,16,512]{3,2,1,0:T(8,128)S(1)}, f32[6,16,16,512]{3,2,1,0:T(8,128)S(1)}, f32[2,2,8,16,512]{4,3,2,1,0:T(8,128)S(1)}, f32[2,2,8,16,512]{4,3,2,1,0:T(8,128)S(1)}) custom-call(f32[1,512,512]{2,1,0:T(8,128)S(1)} %copy-done.9, f32[256,512]{1,0:T(8,128)S(1)} %get-tuple-element.90.s0, ...), custom_call_target="tpu_custom_call" | custom-call | tf_op jit(solution)/shard_map/first_block/pallas_call | solution.py:58
  70.8 0.1 collective-permute-start.5
  70.9 3.4 %second_block.2 = (f32[6,16,16,512]{3,2,1,0:T(8,128)S(1)}, f32[6,16,16,512]{3,2,1,0:T(8,128)S(1)}, f32[2,2,8,16,512]{4,3,2,1,0:T(8,128)S(1)}, f32[2,2,8,16,512]{4,3,2,1,0:T(8,128)S(1)}) custom-call(bf16[512,1024]{1,0:T(8,128)(2,1)S(1)} %copy-done.6, bf16[6,512,512]{2,1,0:T(8,128)(2,1)S(1)} %fixed_top.1.top, ...), custom_call_target="tpu_custom_call", output_to_operand_aliasing={{2}: (6, {}), {3}: (7, {})} | custom-call | tf_op jit(solution)/shard_map/second_block/pallas_call | solution.py:58
  74.4 2.2 %collective-permute-done.5.recv = f32[6,16,16,512]{3,2,1,0:T(8,128)S(1)} collective-permute-done((f32[6,16,16,512]{3,2,1,0:T(8,128)S(1)}, f32[6,16,16,512]{3,2,1,0:T(8,128)S(1)}, u32[]{:S(2)}, u32[]{:S(2)}) %collective-permute-start.5) | collective-permute-done | bytes 3145760 | tf_op jit(solution)/shard_map/ppermute | solution.py:392
  76.6 0.3 core_add.2
  76.9 3.4 %second_block.3 = (f32[6,16,16,512]{3,2,1,0:T(8,128)S(1)}, f32[6,16,16,512]{3,2,1,0:T(8,128)S(1)}, f32[2,2,8,16,512]{4,3,2,1,0:T(8,128)S(1)}, f32[2,2,8,16,512]{4,3,2,1,0:T(8,128)S(1)}) custom-call(bf16[512,1024]{1,0:T(8,128)(2,1)S(1)} %copy-done.6, ...), custom_call_target="tpu_custom_call", output_to_operand_aliasing={{2}: (6, {}), {3}: (7, {}), {0}: (8, {}), {1}: (9, {})} | custom-call | tf_op jit(solution)/shard_map/second_block/pallas_call | solution.py:58
  80.3 0.2 collective-permute-start.8
  80.5 5.7 %collective-permute-start.6 = (f32[3,4,16,512]{3,2,1,0:T(8,128)S(1)}, f32[3,4,16,512]{3,2,1,0:T(8,128)S(1)}, u32[]{:S(2)}, u32[]{:S(2)}) collective-permute-start(f32[3,4,16,512]{3,2,1,0:T(8,128)S(1)} %get-tuple-element.108), channel_id=1, source_target_pairs={{0,16},{1,5},{4,20},{5,9},{8,24},{9,13},{12,28},{13,1},{16,32},{17... | collective-permute-start | bytes 1179656 | tf_op jit(solution)/shard_map/ppermute | solution.py:404
  86.1 2.1 %collective-permute-start.7 = (f32[3,4,16,512]{3,2,1,0:T(8,128)S(1)}, f32[3,4,16,512]{3,2,1,0:T(8,128)S(1)}, u32[]{:S(2)}, u32[]{:S(2)}) collective-permute-start(f32[3,4,16,512]{3,2,1,0:T(8,128)S(1)} %get-tuple-element.109), channel_id=1, source_target_pairs={{0,48},{1,13},{4,52},{5,1},{8,56},{9,5},{12,60},{13,9},{16,0},{17,... | collective-permute-start | bytes 1179656 | tf_op jit(solution)/shard_map/ppermute | solution.py:404
  88.2 0.5 collective-permute-start.11
  88.8 4.9 %collective-permute-done.6.ra = f32[3,4,16,512]{3,2,1,0:T(8,128)S(1)} collective-permute-done((f32[3,4,16,512]{3,2,1,0:T(8,128)S(1)}, f32[3,4,16,512]{3,2,1,0:T(8,128)S(1)}, u32[]{:S(2)}, u32[]{:S(2)}) %collective-permute-start.6) | collective-permute-done | bytes 393248 | tf_op jit(solution)/shard_map/ppermute | solution.py:404
  93.7 0.1 relay_add.2
  93.8 1.0 collective-permute-start.12
  94.9 1.8 %collective-permute-start.13 = (f32[2,3,4,16,512]{4,3,2,1,0:T(8,128)S(1)}, f32[2,3,4,16,512]{4,3,2,1,0:T(8,128)S(1)}, u32[]{:S(2)}, u32[]{:S(2)}) collective-permute-start(f32[2,3,4,16,512]{4,3,2,1,0:T(8,128)S(1)} %get-tuple-element.117), channel_id=1, source_target_pairs={{0,48},{1,13},{4,52},{5,1},{8,56},{9,5},{12,60},{13,9},{16,0},{17,... | collective-permute-start | bytes 2359304 | tf_op jit(solution)/shard_map/ppermute | solution.py:404
  96.7 0.4 core_add.3
  97.1 0.1 collective-permute-start.9
  97.2 2.7 %collective-permute-start.10 = (f32[3,4,16,512]{3,2,1,0:T(8,128)S(1)}, f32[3,4,16,512]{3,2,1,0:T(8,128)S(1)}, u32[]{:S(2)}, u32[]{:S(2)}) collective-permute-start(f32[3,4,16,512]{3,2,1,0:T(8,128)S(1)} %get-tuple-element.114), channel_id=1, source_target_pairs={{0,48},{1,13},{4,52},{5,1},{8,56},{9,5},{12,60},{13,9},{16,0},{17,... | collective-permute-start | bytes 1179656 | tf_op jit(solution)/shard_map/ppermute | solution.py:404
  99.8 15.0 %collective-permute-done.11.gf.bf = f32[2,2,8,16,512]{4,3,2,1,0:T(8,128)S(1)} collective-permute-done((f32[2,2,8,16,512]{4,3,2,1,0:T(8,128)S(1)}, f32[2,2,8,16,512]{4,3,2,1,0:T(8,128)S(1)}, u32[]{:S(2)}, u32[]{:S(2)}) %collective-permute-start.11) | collective-permute-done | bytes 1048608 | tf_op jit(solution)/shard_map/ppermute | solution.py:392
  114.9 0.1 relay_add.3
  115.0 0.1 collective-permute-start.14
  115.1 2.7 %collective-permute-start.15 = (f32[2,3,4,16,512]{4,3,2,1,0:T(8,128)S(1)}, f32[2,3,4,16,512]{4,3,2,1,0:T(8,128)S(1)}, u32[]{:S(2)}, u32[]{:S(2)}) collective-permute-start(f32[2,3,4,16,512]{4,3,2,1,0:T(8,128)S(1)} %get-tuple-element.127), channel_id=1, source_target_pairs={{0,48},{1,13},{4,52},{5,1},{8,56},{9,5},{12,60},{13,9},{16,0},{17,... | collective-permute-start | bytes 2359304 | tf_op jit(solution)/shard_map/ppermute | solution.py:404
  117.8 0.5 collective-permute-start.21
  118.3 0.1 over_sum.1
  118.4 3.4 %collective-permute-start.20 = (f32[2,2,8,16,512]{4,3,2,1,0:T(8,128)S(1)}, f32[2,2,8,16,512]{4,3,2,1,0:T(8,128)S(1)}, u32[]{:S(2)}, u32[]{:S(2)}) collective-permute-start(f32[2,2,8,16,512]{4,3,2,1,0:T(8,128)S(1)} %over_sum.1), channel_id=1, source_target_pairs={{0,1},{1,2},{2,3},{3,4},{4,5},{5,6},{6,7},{7,8},{8,9},{9,10},{10,1... | collective-permute-start | bytes 3145736 | tf_op jit(solution)/shard_map/ppermute | solution.py:388
  121.9 5.6 %collective-permute-done.14.refs_4_ = f32[2,3,4,16,512]{4,3,2,1,0:T(8,128)S(1)} collective-permute-done((f32[2,3,4,16,512]{4,3,2,1,0:T(8,128)S(1)}, f32[2,3,4,16,512]{4,3,2,1,0:T(8,128)S(1)}, u32[]{:S(2)}, u32[]{:S(2)}) %collective-permute-start.14) | collective-permute-done | bytes 786464 | tf_op jit(solution)/shard_map/ppermute | solution.py:404
  127.4 0.3 plane_add.1
  127.7 0.1 collective-permute-start.16
  127.9 2.6 %collective-permute-start.17 = (f32[2,2,3,16,512]{4,3,2,1,0:T(8,128)S(1)}, f32[2,2,3,16,512]{4,3,2,1,0:T(8,128)S(1)}, u32[]{:S(2)}, u32[]{:S(2)}) collective-permute-start(f32[2,2,3,16,512]{4,3,2,1,0:T(8,128)S(1)} %get-tuple-element.130), channel_id=1, source_target_pairs={{0,12},{1,49},{4,0},{5,53},{8,4},{9,57},{12,8},{13,61},{16,28},{17... | collective-permute-start | bytes 1179656 | tf_op jit(solution)/shard_map/ppermute | solution.py:404
  130.5 0.5 collective-permute-start.18
  130.9 0.1 brightest.1.most
  131.0 4.9 %collective-permute-done.16.b = f32[2,2,3,16,512]{4,3,2,1,0:T(8,128)S(1)} collective-permute-done((f32[2,2,3,16,512]{4,3,2,1,0:T(8,128)S(1)}, f32[2,2,3,16,512]{4,3,2,1,0:T(8,128)S(1)}, u32[]{:S(2)}, u32[]{:S(2)}) %collective-permute-start.16) | collective-permute-done | bytes 393248 | tf_op jit(solution)/shard_map/ppermute | solution.py:404
  135.9 3.5 %collective-permute-done.17.c = f32[2,2,3,16,512]{4,3,2,1,0:T(8,128)S(1)} collective-permute-done((f32[2,2,3,16,512]{4,3,2,1,0:T(8,128)S(1)}, f32[2,2,3,16,512]{4,3,2,1,0:T(8,128)S(1)}, u32[]{:S(2)}, u32[]{:S(2)}) %collective-permute-start.17) | collective-permute-done | bytes 393248 | tf_op jit(solution)/shard_map/ppermute | solution.py:404
  139.4 0.7 collective-permute-done.18.d
  140.2 0.1 line_add.1
  140.3 13.8 %collective-permute-start.19 = (f32[13,8,512]{2,1,0:T(8,128)S(1)}, f32[13,8,512]{2,1,0:T(8,128)S(1)}, u32[]{:S(2)}, u32[]{:S(2)}) collective-permute-start(f32[13,8,512]{2,1,0:T(8,128)S(1)} %get-tuple-element.133), channel_id=1, source_target_pairs={{0,1},{1,0},{2,3},{3,2},{4,5},{5,4},{6,7},{7,6},{8,9},{9,8},{10,11... | collective-permute-start | bytes 638984 | tf_op jit(solution)/shard_map/ppermute | solution.py:392
  154.1 1.1 collective-permute-done.19.recv
  155.2 0.1 collective-permute-start.22
  155.3 0.8 collective-permute-start.24
  156.1 2.5 %collective-permute-start.23 = (f32[2,6,8,512]{3,2,1,0:T(8,128)S(1)}, f32[2,6,8,512]{3,2,1,0:T(8,128)S(1)}, u32[]{:S(2)}, u32[]{:S(2)}) collective-permute-start(f32[2,6,8,512]{3,2,1,0:T(8,128)S(1)} %get-tuple-element.141.mine), channel_id=1, source_target_pairs={{0,64},{2,66},{64,0},{66,2},{1,65},{3,67},{65,1},{67,3},{4,68},{6,... | collective-permute-start | bytes 589832 | tf_op jit(solution)/shard_map/ppermute | solution.py:409
  158.6 3.2 %collective-permute-done.22.far_max.b = f32[13,8,512]{2,1,0:T(8,128)S(1)} collective-permute-done((f32[13,8,512]{2,1,0:T(8,128)S(1)}, f32[13,8,512]{2,1,0:T(8,128)S(1)}, u32[]{:S(2)}, u32[]{:S(2)}) %collective-permute-start.22) | collective-permute-done | bytes 213024 | tf_op jit(solution)/shard_map/ppermute | solution.py:409
  161.8 3.1 %object_update.1 = f32[2,512,1024]{2,1,0:T(8,128)} custom-call(s32[2]{0:T(128)S(1)} %pad_add_fusion.place, s32[2]{0:T(128)S(1)} %collective-permute-done.place.before, f32[13,8,512]{2,1,0:T(8,128)S(1)} %get-tuple-element.138.near_max, f32[13,8,512]{2,1,0:T(8,128)S(1)} %collective-permute-done.22.far_max.b, f32[2,512,1024]{2,1,0:T(8,128)S(1)} %copy-done.2, ...), custom_call_target="tpu_custom_call" | custom-call | tf_op jit(solution)/shard_map/object_update/pallas_call | solution.py:601
  164.9 2.3 %collective-permute-done.24.d = f32[13,8,512]{2,1,0:T(8,128)S(1)} collective-permute-done((f32[13,8,512]{2,1,0:T(8,128)S(1)}, f32[13,8,512]{2,1,0:T(8,128)S(1)}, u32[]{:S(2)}, u32[]{:S(2)}) %collective-permute-start.24) | collective-permute-done | bytes 213024 | tf_op jit(solution)/shard_map/ppermute | solution.py:409
  167.3 1.6 mix.1
  (32 shorter events, 0.1 us)
Async XLA Ops:
  2.0 10.4 %copy-start = (bf16[2,6,512,512]{3,2,1,0:T(8,128)(2,1)S(1)}, bf16[2,6,512,512]{3,2,1,0:T(8,128)(2,1)}, u32[]{:S(2)}) copy-start(bf16[2,6,512,512]{3,2,1,0:T(8,128)(2,1)} %p_ref.9) | copy-start | bytes 18874372
  2.0 7.8 %collective-permute-start = (s32[2]{0:T(128)S(1)}, s32[2]{0:T(128)S(1)}, u32[]{:S(2)}, u32[]{:S(2)}) collective-permute-start(s32[2]{0:T(128)S(1)} %pad_add_fusion.place), channel_id=1, source_target_pairs={{0,1},{1,2},{2,3},{3,4},{4,5},{5,6},{6,7},{7,8},{8,9},{9,10},{10,1... | collective-permute-start | bytes 32 | tf_op jit(solution)/shard_map/ppermute | solution.py:388
  6.8 2.2 %copy-start.1 = (f32[2,512,1024]{2,1,0:T(8,128)S(1)}, f32[2,512,1024]{2,1,0:T(8,128)}, u32[]{:S(2)}) copy-start(f32[2,512,1024]{2,1,0:T(8,128)} %obj.3) | copy-start | bytes 12582916
  10.4 16.4 %collective-permute-start.1 = (f32[2,256,512]{2,1,0:T(8,128)S(1)}, f32[2,256,512]{2,1,0:T(8,128)S(1)}, u32[]{:S(2)}, u32[]{:S(2)}) collective-permute-start(f32[2,256,512]{2,1,0:T(8,128)S(1)} %rim_rows.1), channel_id=1, source_target_pairs={{1,0},{2,1},{3,2},{4,3},{5,4},{6,5},{7,6},{8,7},{9,8},{10,9},{11,1... | collective-permute-start | bytes 3145736 | tf_op jit(solution)/shard_map/ppermute | solution.py:388
  12.4 1.6 copy-start.3
  14.0 5.4 %copy-start.7 = (bf16[512,1024]{1,0:T(8,128)(2,1)S(1)}, bf16[512,1024]{1,0:T(8,128)(2,1)}, u32[]{:S(2)}) copy-start(bf16[512,1024]{1,0:T(8,128)(2,1)} %constant.14.clone.wt1.wt) | copy-start | bytes 3145732
  14.0 5.4 %copy-start.8 = (bf16[512,1024]{1,0:T(8,128)(2,1)S(1)}, bf16[512,1024]{1,0:T(8,128)(2,1)}, u32[]{:S(2)}) copy-start(bf16[512,1024]{1,0:T(8,128)(2,1)} %constant.13.clone.wt0.wt) | copy-start | bytes 3145732
  19.4 9.6 %copy-start.4 = (bf16[1024,1024]{1,0:T(8,128)(2,1)S(1)}, bf16[1024,1024]{1,0:T(8,128)(2,1)}, u32[]{:S(2)}) copy-start(bf16[1024,1024]{1,0:T(8,128)(2,1)} %constant.12.clone.table) | copy-start | bytes 6291460
  26.9 11.0 %collective-permute-start.2 = (f32[128,512]{1,0:T(8,128)S(1)}, f32[128,512]{1,0:T(8,128)S(1)}, u32[]{:S(2)}, u32[]{:S(2)}) collective-permute-start(f32[128,512]{1,0:T(8,128)S(1)} %get-tuple-element.84), channel_id=1, source_target_pairs={{0,64},{64,0},{1,65},{65,1},{2,66},{66,2},{3,67},{67,3},{4,68},{68... | collective-permute-start | bytes 786440 | tf_op jit(solution)/shard_map/ppermute | solution.py:392
  36.9 15.6 %collective-permute-start.3 = (f32[256,512]{1,0:T(8,128)S(1)}, f32[256,512]{1,0:T(8,128)S(1)}, u32[]{:S(2)}, u32[]{:S(2)}) collective-permute-start(f32[256,512]{1,0:T(8,128)S(1)} %get-tuple-element.86.s0), channel_id=1, source_target_pairs={{0,64},{64,0},{1,65},{65,1},{2,66},{66,2},{3,67},{67,3},{4,68},{68... | collective-permute-start | bytes 1572872 | tf_op jit(solution)/shard_map/ppermute | solution.py:392
  37.8 14.7 %copy-start.5 = (bf16[1024,1024]{1,0:T(8,128)(2,1)S(1)}, bf16[1024,1024]{1,0:T(8,128)(2,1)}, u32[]{:S(2)}) copy-start(bf16[1024,1024]{1,0:T(8,128)(2,1)} %constant.15.clone.table) | copy-start | bytes 6291460
  37.8 14.7 %copy-start.9 = (f32[1,512,512]{2,1,0:T(8,128)S(1)}, f32[1,512,512]{2,1,0:T(8,128)}, u32[]{:S(2)}) copy-start(f32[1,512,512]{2,1,0:T(8,128)} %pat.3) | copy-start | bytes 3145732
  40.5 19.4 %collective-permute-start.4 = (f32[256,512]{1,0:T(8,128)S(1)}, f32[256,512]{1,0:T(8,128)S(1)}, u32[]{:S(2)}, u32[]{:S(2)}) collective-permute-start(f32[256,512]{1,0:T(8,128)S(1)} %get-tuple-element.90.s0), channel_id=1, source_target_pairs={{0,64},{64,0},{1,65},{65,1},{2,66},{66,2},{3,67},{67,3},{4,68},{68... | collective-permute-start | bytes 1572872 | tf_op jit(solution)/shard_map/ppermute | solution.py:392
  52.5 7.4 %copy-start.10 = (bf16[512,1024]{1,0:T(8,128)(2,1)S(1)}, bf16[512,1024]{1,0:T(8,128)(2,1)}, u32[]{:S(2)}) copy-start(bf16[512,1024]{1,0:T(8,128)(2,1)} %constant.16.clone.bt) | copy-start | bytes 3145732
  60.0 10.9 %copy-start.6 = (bf16[512,1024]{1,0:T(8,128)(2,1)S(1)}, bf16[512,1024]{1,0:T(8,128)(2,1)}, u32[]{:S(2)}) copy-start(bf16[512,1024]{1,0:T(8,128)(2,1)} %constant.17.clone.bt) | copy-start | bytes 3145732
  70.8 5.7 %collective-permute-start.5 = (f32[6,16,16,512]{3,2,1,0:T(8,128)S(1)}, f32[6,16,16,512]{3,2,1,0:T(8,128)S(1)}, u32[]{:S(2)}, u32[]{:S(2)}) collective-permute-start(f32[6,16,16,512]{3,2,1,0:T(8,128)S(1)} %get-tuple-element.101), channel_id=1, source_target_pairs={{0,1},{1,0},{2,3},{3,2},{4,5},{5,4},{6,7},{7,6},{8,9},{9,8},{10,11... | collective-permute-start | bytes 9437192 | tf_op jit(solution)/shard_map/ppermute | solution.py:392
  80.3 16.4 %collective-permute-start.8 = (f32[6,16,16,512]{3,2,1,0:T(8,128)S(1)}, f32[6,16,16,512]{3,2,1,0:T(8,128)S(1)}, u32[]{:S(2)}, u32[]{:S(2)}) collective-permute-start(f32[6,16,16,512]{3,2,1,0:T(8,128)S(1)} %get-tuple-element.112), channel_id=1, source_target_pairs={{0,1},{1,0},{2,3},{3,2},{4,5},{5,4},{6,7},{7,6},{8,9},{9,8},{10,11... | collective-permute-start | bytes 9437192 | tf_op jit(solution)/shard_map/ppermute | solution.py:392
  80.5 13.2 %collective-permute-start.6 = (f32[3,4,16,512]{3,2,1,0:T(8,128)S(1)}, f32[3,4,16,512]{3,2,1,0:T(8,128)S(1)}, u32[]{:S(2)}, u32[]{:S(2)}) collective-permute-start(f32[3,4,16,512]{3,2,1,0:T(8,128)S(1)} %get-tuple-element.108), channel_id=1, source_target_pairs={{0,16},{1,5},{4,20},{5,9},{8,24},{9,13},{12,28},{13,1},{16,32},{17... | collective-permute-start | bytes 1179656 | tf_op jit(solution)/shard_map/ppermute | solution.py:404
  86.1 7.6 %collective-permute-start.7 = (f32[3,4,16,512]{3,2,1,0:T(8,128)S(1)}, f32[3,4,16,512]{3,2,1,0:T(8,128)S(1)}, u32[]{:S(2)}, u32[]{:S(2)}) collective-permute-start(f32[3,4,16,512]{3,2,1,0:T(8,128)S(1)} %get-tuple-element.109), channel_id=1, source_target_pairs={{0,48},{1,13},{4,52},{5,1},{8,56},{9,5},{12,60},{13,9},{16,0},{17,... | collective-permute-start | bytes 1179656 | tf_op jit(solution)/shard_map/ppermute | solution.py:404
  88.2 26.6 %collective-permute-start.11 = (f32[2,2,8,16,512]{4,3,2,1,0:T(8,128)S(1)}, f32[2,2,8,16,512]{4,3,2,1,0:T(8,128)S(1)}, u32[]{:S(2)}, u32[]{:S(2)}) collective-permute-start(f32[2,2,8,16,512]{4,3,2,1,0:T(8,128)S(1)} %get-tuple-element.115.g.b), channel_id=1, source_target_pairs={{0,64},{64,0},{1,65},{65,1},{2,66},{66,2},{3,67},{67,3},{4,68},{68... | collective-permute-start | bytes 3145736 | tf_op jit(solution)/shard_map/ppermute | solution.py:392
  93.8 21.0 %collective-permute-start.12 = (f32[2,3,4,16,512]{4,3,2,1,0:T(8,128)S(1)}, f32[2,3,4,16,512]{4,3,2,1,0:T(8,128)S(1)}, u32[]{:S(2)}, u32[]{:S(2)}) collective-permute-start(f32[2,3,4,16,512]{4,3,2,1,0:T(8,128)S(1)} %get-tuple-element.110), channel_id=1, source_target_pairs={{0,16},{1,5},{4,20},{5,9},{8,24},{9,13},{12,28},{13,1},{16,32},{17... | collective-permute-start | bytes 2359304 | tf_op jit(solution)/shard_map/ppermute | solution.py:404
  94.9 20.0 %collective-permute-start.13 = (f32[2,3,4,16,512]{4,3,2,1,0:T(8,128)S(1)}, f32[2,3,4,16,512]{4,3,2,1,0:T(8,128)S(1)}, u32[]{:S(2)}, u32[]{:S(2)}) collective-permute-start(f32[2,3,4,16,512]{4,3,2,1,0:T(8,128)S(1)} %get-tuple-element.117), channel_id=1, source_target_pairs={{0,48},{1,13},{4,52},{5,1},{8,56},{9,5},{12,60},{13,9},{16,0},{17,... | collective-permute-start | bytes 2359304 | tf_op jit(solution)/shard_map/ppermute | solution.py:404
  97.1 17.8 %collective-permute-start.9 = (f32[3,4,16,512]{3,2,1,0:T(8,128)S(1)}, f32[3,4,16,512]{3,2,1,0:T(8,128)S(1)}, u32[]{:S(2)}, u32[]{:S(2)}) collective-permute-start(f32[3,4,16,512]{3,2,1,0:T(8,128)S(1)} %get-tuple-element.113), channel_id=1, source_target_pairs={{0,16},{1,5},{4,20},{5,9},{8,24},{9,13},{12,28},{13,1},{16,32},{17... | collective-permute-start | bytes 1179656 | tf_op jit(solution)/shard_map/ppermute | solution.py:404
  97.2 17.7 %collective-permute-start.10 = (f32[3,4,16,512]{3,2,1,0:T(8,128)S(1)}, f32[3,4,16,512]{3,2,1,0:T(8,128)S(1)}, u32[]{:S(2)}, u32[]{:S(2)}) collective-permute-start(f32[3,4,16,512]{3,2,1,0:T(8,128)S(1)} %get-tuple-element.114), channel_id=1, source_target_pairs={{0,48},{1,13},{4,52},{5,1},{8,56},{9,5},{12,60},{13,9},{16,0},{17,... | collective-permute-start | bytes 1179656 | tf_op jit(solution)/shard_map/ppermute | solution.py:404
  115.0 12.4 %collective-permute-start.14 = (f32[2,3,4,16,512]{4,3,2,1,0:T(8,128)S(1)}, f32[2,3,4,16,512]{4,3,2,1,0:T(8,128)S(1)}, u32[]{:S(2)}, u32[]{:S(2)}) collective-permute-start(f32[2,3,4,16,512]{4,3,2,1,0:T(8,128)S(1)} %get-tuple-element.126), channel_id=1, source_target_pairs={{0,16},{1,5},{4,20},{5,9},{8,24},{9,13},{12,28},{13,1},{16,32},{17... | collective-permute-start | bytes 2359304 | tf_op jit(solution)/shard_map/ppermute | solution.py:404
  115.1 12.3 %collective-permute-start.15 = (f32[2,3,4,16,512]{4,3,2,1,0:T(8,128)S(1)}, f32[2,3,4,16,512]{4,3,2,1,0:T(8,128)S(1)}, u32[]{:S(2)}, u32[]{:S(2)}) collective-permute-start(f32[2,3,4,16,512]{4,3,2,1,0:T(8,128)S(1)} %get-tuple-element.127), channel_id=1, source_target_pairs={{0,48},{1,13},{4,52},{5,1},{8,56},{9,5},{12,60},{13,9},{16,0},{17,... | collective-permute-start | bytes 2359304 | tf_op jit(solution)/shard_map/ppermute | solution.py:404
  117.8 36.3 %collective-permute-start.21 = (f32[2,2,8,16,512]{4,3,2,1,0:T(8,128)S(1)}, f32[2,2,8,16,512]{4,3,2,1,0:T(8,128)S(1)}, u32[]{:S(2)}, u32[]{:S(2)}) collective-permute-start(f32[2,2,8,16,512]{4,3,2,1,0:T(8,128)S(1)} %get-tuple-element.135.t), channel_id=1, source_target_pairs={{0,64},{64,0},{1,65},{65,1},{2,66},{66,2},{3,67},{67,3},{4,68},{68... | collective-permute-start | bytes 3145736 | tf_op jit(solution)/shard_map/ppermute | solution.py:392
  118.4 35.6 %collective-permute-start.20 = (f32[2,2,8,16,512]{4,3,2,1,0:T(8,128)S(1)}, f32[2,2,8,16,512]{4,3,2,1,0:T(8,128)S(1)}, u32[]{:S(2)}, u32[]{:S(2)}) collective-permute-start(f32[2,2,8,16,512]{4,3,2,1,0:T(8,128)S(1)} %over_sum.1), channel_id=1, source_target_pairs={{0,1},{1,2},{2,3},{3,4},{4,5},{5,6},{6,7},{7,8},{8,9},{9,10},{10,1... | collective-permute-start | bytes 3145736 | tf_op jit(solution)/shard_map/ppermute | solution.py:388
  127.7 8.2 %collective-permute-start.16 = (f32[2,2,3,16,512]{4,3,2,1,0:T(8,128)S(1)}, f32[2,2,3,16,512]{4,3,2,1,0:T(8,128)S(1)}, u32[]{:S(2)}, u32[]{:S(2)}) collective-permute-start(f32[2,2,3,16,512]{4,3,2,1,0:T(8,128)S(1)} %get-tuple-element.129), channel_id=1, source_target_pairs={{0,4},{1,17},{4,8},{5,21},{8,12},{9,25},{12,0},{13,29},{16,20},{17... | collective-permute-start | bytes 1179656 | tf_op jit(solution)/shard_map/ppermute | solution.py:404
  127.9 11.6 %collective-permute-start.17 = (f32[2,2,3,16,512]{4,3,2,1,0:T(8,128)S(1)}, f32[2,2,3,16,512]{4,3,2,1,0:T(8,128)S(1)}, u32[]{:S(2)}, u32[]{:S(2)}) collective-permute-start(f32[2,2,3,16,512]{4,3,2,1,0:T(8,128)S(1)} %get-tuple-element.130), channel_id=1, source_target_pairs={{0,12},{1,49},{4,0},{5,53},{8,4},{9,57},{12,8},{13,61},{16,28},{17... | collective-permute-start | bytes 1179656 | tf_op jit(solution)/shard_map/ppermute | solution.py:404
  130.5 9.7 %collective-permute-start.18 = (f32[2,2,3,16,512]{4,3,2,1,0:T(8,128)S(1)}, f32[2,2,3,16,512]{4,3,2,1,0:T(8,128)S(1)}, u32[]{:S(2)}, u32[]{:S(2)}) collective-permute-start(f32[2,2,3,16,512]{4,3,2,1,0:T(8,128)S(1)} %get-tuple-element.131), channel_id=1, source_target_pairs={{0,8},{1,33},{4,12},{5,37},{8,0},{9,41},{12,4},{13,45},{16,24},{17... | collective-permute-start | bytes 1179656 | tf_op jit(solution)/shard_map/ppermute | solution.py:404
  140.3 14.9 %collective-permute-start.19 = (f32[13,8,512]{2,1,0:T(8,128)S(1)}, f32[13,8,512]{2,1,0:T(8,128)S(1)}, u32[]{:S(2)}, u32[]{:S(2)}) collective-permute-start(f32[13,8,512]{2,1,0:T(8,128)S(1)} %get-tuple-element.133), channel_id=1, source_target_pairs={{0,1},{1,0},{2,3},{3,2},{4,5},{5,4},{6,7},{7,6},{8,9},{9,8},{10,11... | collective-permute-start | bytes 638984 | tf_op jit(solution)/shard_map/ppermute | solution.py:392
  155.2 6.6 %copy-start.2 = (f32[2,512,1024]{2,1,0:T(8,128)S(1)}, f32[2,512,1024]{2,1,0:T(8,128)}, u32[]{:S(2)}) copy-start(f32[2,512,1024]{2,1,0:T(8,128)} %obj.3) | copy-start | bytes 12582916
  155.2 6.5 %collective-permute-start.22 = (f32[13,8,512]{2,1,0:T(8,128)S(1)}, f32[13,8,512]{2,1,0:T(8,128)S(1)}, u32[]{:S(2)}, u32[]{:S(2)}) collective-permute-start(f32[13,8,512]{2,1,0:T(8,128)S(1)} %get-tuple-element.138.near_max), channel_id=1, source_target_pairs={{0,2},{2,0},{64,66},{66,64},{1,3},{3,1},{65,67},{67,65},{4,6},{6,4... | collective-permute-start | bytes 638984 | tf_op jit(solution)/shard_map/ppermute | solution.py:409
  155.3 12.0 %collective-permute-start.24 = (f32[13,8,512]{2,1,0:T(8,128)S(1)}, f32[13,8,512]{2,1,0:T(8,128)S(1)}, u32[]{:S(2)}, u32[]{:S(2)}) collective-permute-start(f32[13,8,512]{2,1,0:T(8,128)S(1)} %get-tuple-element.138.near_max), channel_id=1, source_target_pairs={{0,66},{2,64},{64,2},{66,0},{1,67},{3,65},{65,3},{67,1},{4,70},{6,... | collective-permute-start | bytes 638984 | tf_op jit(solution)/shard_map/ppermute | solution.py:409
  156.1 11.2 %copy-start.11 = (s32[12,12]{1,0:T(8,128)S(1)}, s32[12,12]{1,0:T(8,128)}, u32[]{:S(2)}) copy-start(s32[12,12]{1,0:T(8,128)} %w_ref.1) | copy-start | bytes 1732
  156.1 8.8 %collective-permute-start.23 = (f32[2,6,8,512]{3,2,1,0:T(8,128)S(1)}, f32[2,6,8,512]{3,2,1,0:T(8,128)S(1)}, u32[]{:S(2)}, u32[]{:S(2)}) collective-permute-start(f32[2,6,8,512]{3,2,1,0:T(8,128)S(1)} %get-tuple-element.141.mine), channel_id=1, source_target_pairs={{0,64},{2,66},{64,0},{66,2},{1,65},{3,67},{65,1},{67,3},{4,68},{6,... | collective-permute-start | bytes 589832 | tf_op jit(solution)/shard_map/ppermute | solution.py:409

commit v8 on v7

--- a/solution.py
+++ b/solution.py
@@ -668,9 +668,10 @@
     line = plane_add((plane0, plane1))
     line = [line[0]] + [turned(line[r], r, False) for r in (1, 3, 2)]
     keep, send = line_add(most, line)
-    recv, over, tops_far = tied(swapped(send, "core"), over, tops_far)
+    recv = swapped(send, "core")
     mine, other = pixel_step(most, keep, recv, rows)
     beside = across(other, 0, 1)
+    beside, over, tops_far = tied(beside, over, tops_far)
     probe_new = mix(mixing, mine, beside, across(mine, 1, 0), across(other, 1, 1))
     object_new = object_update(place, before, other, beside, object_field, (tops, tops_far, bots, bots_far), over)
     return object_new, probe_new

time: 170 us -> 169 us (level)
  transfers between devices with their start and end apart: 25 -> 25, of which waited for: 13 -> 14; matrix products, arithmetic and copies ran while one was open for 0% -> 0% of each run, Pallas kernels for 20% -> 20%
where the time goes in v8:
time: 169 us
  waiting for transfers between devices  58.8 us (35%)
  starting transfers between devices  53.4 us (32%)
  Pallas kernels  50.6 us (30%)
  local copies, waits for them, and re-layouts  3.81 us (2%)
  between operations  2.2 us (1%)
    pallas_call x20, Pallas kernels, call(): pl.pallas_call(body, in_specs=ins, out_specs=[LOCAL] * len(outs), out_sha...  47.6 us
    ppermute x8, waiting for transfers between devices, swapped(): return lax.ppermute(value, axis, [(0, 1), (1, 0)])  30.6 us
    ppermute x8, starting transfers between devices, swapped(): return lax.ppermute(value, axis, [(0, 1), (1, 0)])  20.6 us
    ppermute x11, waiting for transfers between devices, turned(): return lax.ppermute(value, RING, pairs)  19.4 us
    ppermute x11, starting transfers between devices, turned(): return lax.ppermute(value, RING, pairs)  19.3 us
    ppermute x3, starting transfers between devices, along(): return lax.ppermute(value, SCAN, [(i, i + steps) for i in range(lo, hi)])  10.3 us
    ppermute x3, waiting for transfers between devices, across(): return lax.ppermute(value, ('mode', 'x'), pairs)  5.68 us
    unnamed x24, local copies, waits for them, and re-layouts  3.81 us
  transfers between devices with their start and end apart: 25, of which 14 were waited for; matrix products, arithmetic and copies ran while one was open for 0% of the time, Pallas kernels for 20%

profile of v8, /device:TPU:1, one launch (start us, length us, event | category | flops | bytes accessed | tf_op | source)
XLA Modules:
  0.0 168.9 jit_solution(6649707201487625522)
XLA Ops:
  1.9 0.1 pad_add_fusion.place
  2.0 4.8 %collective-permute-start = (s32[2]{0:T(128)S(1)}, s32[2]{0:T(128)S(1)}, u32[]{:S(2)}, u32[]{:S(2)}) collective-permute-start(s32[2]{0:T(128)S(1)} %pad_add_fusion.place), channel_id=1, source_target_pairs={{0,1},{1,2},{2,3},{3,4},{4,5},{5,6},{6,7},{7,8},{8,9},{9,10},{10,1... | collective-permute-start | bytes 32 | tf_op jit(solution)/shard_map/ppermute | solution.py:388
  6.8 2.2 %copy-done.1 = f32[2,512,1024]{2,1,0:T(8,128)S(1)} copy-done((f32[2,512,1024]{2,1,0:T(8,128)S(1)}, f32[2,512,1024]{2,1,0:T(8,128)}, u32[]{:S(2)}) %copy-start.1) | copy-done | bytes 4194328
  9.0 0.8 own_rows.1
  9.8 0.6 rim_rows.1
  10.4 1.9 %collective-permute-start.1 = (f32[2,256,512]{2,1,0:T(8,128)S(1)}, f32[2,256,512]{2,1,0:T(8,128)S(1)}, u32[]{:S(2)}, u32[]{:S(2)}) collective-permute-start(f32[2,256,512]{2,1,0:T(8,128)S(1)} %rim_rows.1), channel_id=1, source_target_pairs={{1,0},{2,1},{3,2},{4,3},{5,4},{6,5},{7,6},{8,7},{9,8},{10,9},{11,1... | collective-permute-start | bytes 3145736 | tf_op jit(solution)/shard_map/ppermute | solution.py:388
  12.4 0.0 copy-start.3
  12.4 1.6 copy-done.3
  14.0 5.4 %top_half.1 = (bf16[6,512,512]{2,1,0:T(8,128)(2,1)S(1)}, f32[128,512]{1,0:T(8,128)S(1)}, f32[128,512]{1,0:T(8,128)S(1)}, f32[2,6,8,512]{3,2,1,0:T(8,128)S(1)}) custom-call(f32[2,256,512]{2,1,0:T(8,128)S(1)} %get-tuple-element.74.patch_ref.ptop, bf16[2,6,512,512]{3,2,1,0:T(8,128)(2,1)S(1)} %copy-done, bf16[1024,1024]{1,0:T(8,128)(2,1)S(1)} %copy-done.3), custom_call_target="tpu_custom_call" | custom-call | tf_op jit(solution)/shard_map/top_half/pallas_call | solution.py:58
  19.4 0.0 copy-start.4
  19.4 4.3 %first_terms.1 = (f32[6,512,512]{2,1,0:T(8,128)S(1)}, f32[6,512,512]{2,1,0:T(8,128)S(1)}) custom-call(bf16[512,1024]{1,0:T(8,128)(2,1)S(1)} %copy-done.8, bf16[512,1024]{1,0:T(8,128)(2,1)S(1)} %copy-done.7, bf16[6,512,512]{2,1,0:T(8,128)(2,1)S(1)} %get-tuple-element.78.top), custom_call_target="tpu_custom_call" | custom-call | tf_op jit(solution)/shard_map/first_terms/pallas_call | solution.py:58
  23.8 3.1 %collective-permute-done.1.rim = f32[2,256,512]{2,1,0:T(8,128)S(1)} collective-permute-done((f32[2,256,512]{2,1,0:T(8,128)S(1)}, f32[2,256,512]{2,1,0:T(8,128)S(1)}, u32[]{:S(2)}, u32[]{:S(2)}) %collective-permute-start.1) | collective-permute-done | bytes 1048608 | tf_op jit(solution)/shard_map/ppermute | solution.py:388
  26.9 2.2 %collective-permute-start.2 = (f32[128,512]{1,0:T(8,128)S(1)}, f32[128,512]{1,0:T(8,128)S(1)}, u32[]{:S(2)}, u32[]{:S(2)}) collective-permute-start(f32[128,512]{1,0:T(8,128)S(1)} %get-tuple-element.84), channel_id=1, source_target_pairs={{0,64},{64,0},{1,65},{65,1},{2,66},{66,2},{3,67},{67,3},{4,68},{68... | collective-permute-start | bytes 786440 | tf_op jit(solution)/shard_map/ppermute | solution.py:392
  29.0 7.9 %bottom_half.1 = (bf16[6,512,512]{2,1,0:T(8,128)(2,1)S(1)}, f32[2,256,512]{2,1,0:T(8,128)S(1)}, f32[6,512,512]{2,1,0:T(8,128)S(1)}, f32[256,512]{1,0:T(8,128)S(1)}) custom-call(s32[2]{0:T(128)S(1)} %pad_add_fusion.place, f32[2,256,512]{2,1,0:T(8,128)S(1)} %get-tuple-element.76.own, ...), custom_call_target="tpu_custom_call", output_to_operand_aliasing={{2}: (6, {})} | custom-call | tf_op jit(solution)/shard_map/bottom_half/pallas_call | solution.py:58
  36.9 0.9 collective-permute-start.3
  37.8 2.7 %low_wave.1 = (f32[6,512,512]{2,1,0:T(8,128)S(1)}, f32[256,512]{1,0:T(8,128)S(1)}) custom-call(bf16[512,1024]{1,0:T(8,128)(2,1)S(1)} %copy-done.7, bf16[6,512,512]{2,1,0:T(8,128)(2,1)S(1)} %get-tuple-element.88.bot, f32[6,512,512]{2,1,0:T(8,128)S(1)} %get-tuple-element.89._), custom_call_target="tpu_custom_call", output_to_operand_aliasing={{0}: (2, {})} | custom-call | tf_op jit(solution)/shard_map/low_wave/pallas_call | solution.py:58
  40.5 2.2 %collective-permute-start.4 = (f32[256,512]{1,0:T(8,128)S(1)}, f32[256,512]{1,0:T(8,128)S(1)}, u32[]{:S(2)}, u32[]{:S(2)}) collective-permute-start(f32[256,512]{1,0:T(8,128)S(1)} %get-tuple-element.90.s0), channel_id=1, source_target_pairs={{0,64},{64,0},{1,65},{65,1},{2,66},{66,2},{3,67},{67,3},{4,68},{68... | collective-permute-start | bytes 1572872 | tf_op jit(solution)/shard_map/ppermute | solution.py:392
  42.8 9.7 %collective-permute-done.3.s1 = f32[256,512]{1,0:T(8,128)S(1)} collective-permute-done((f32[256,512]{1,0:T(8,128)S(1)}, f32[256,512]{1,0:T(8,128)S(1)}, u32[]{:S(2)}, u32[]{:S(2)}) %collective-permute-start.3) | collective-permute-done | bytes 524320 | tf_op jit(solution)/shard_map/ppermute | solution.py:392
  52.5 4.9 %fixed_top.1.top = bf16[6,512,512]{2,1,0:T(8,128)(2,1)S(1)} custom-call(f32[1,512,512]{2,1,0:T(8,128)S(1)} %copy-done.9, f32[256,512]{1,0:T(8,128)S(1)} %get-tuple-element.86.s0, f32[256,512]{1,0:T(8,128)S(1)} %collective-permute-done.3.s1, f32[6,512,512]{2,1,0:T(8,128)S(1)} %get-tuple-element.87.wave_ref, bf16[1024,1024]{1,0:T(8,128)(2,1)S(1)} %copy-done.5), custom_call_target="tpu_custom_call" | custom-call | tf_op jit(solution)/shard_map/fixed_top/pallas_call | solution.py:58
  57.4 2.6 %collective-permute-done.4.s1 = f32[256,512]{1,0:T(8,128)S(1)} collective-permute-done((f32[256,512]{1,0:T(8,128)S(1)}, f32[256,512]{1,0:T(8,128)S(1)}, u32[]{:S(2)}, u32[]{:S(2)}) %collective-permute-start.4) | collective-permute-done | bytes 524320 | tf_op jit(solution)/shard_map/ppermute | solution.py:392
  60.0 10.8 %first_block.1 = (bf16[6,512,512]{2,1,0:T(8,128)(2,1)S(1)}, f32[6,16,16,512]{3,2,1,0:T(8,128)S(1)}, f32[6,16,16,512]{3,2,1,0:T(8,128)S(1)}, f32[2,2,8,16,512]{4,3,2,1,0:T(8,128)S(1)}, f32[2,2,8,16,512]{4,3,2,1,0:T(8,128)S(1)}) custom-call(f32[1,512,512]{2,1,0:T(8,128)S(1)} %copy-done.9, f32[256,512]{1,0:T(8,128)S(1)} %get-tuple-element.90.s0, ...), custom_call_target="tpu_custom_call" | custom-call | tf_op jit(solution)/shard_map/first_block/pallas_call | solution.py:58
  70.8 0.1 collective-permute-start.5
  70.9 3.4 %second_block.2 = (f32[6,16,16,512]{3,2,1,0:T(8,128)S(1)}, f32[6,16,16,512]{3,2,1,0:T(8,128)S(1)}, f32[2,2,8,16,512]{4,3,2,1,0:T(8,128)S(1)}, f32[2,2,8,16,512]{4,3,2,1,0:T(8,128)S(1)}) custom-call(bf16[512,1024]{1,0:T(8,128)(2,1)S(1)} %copy-done.6, bf16[6,512,512]{2,1,0:T(8,128)(2,1)S(1)} %fixed_top.1.top, ...), custom_call_target="tpu_custom_call", output_to_operand_aliasing={{2}: (6, {}), {3}: (7, {})} | custom-call | tf_op jit(solution)/shard_map/second_block/pallas_call | solution.py:58
  74.4 2.2 %collective-permute-done.5.recv = f32[6,16,16,512]{3,2,1,0:T(8,128)S(1)} collective-permute-done((f32[6,16,16,512]{3,2,1,0:T(8,128)S(1)}, f32[6,16,16,512]{3,2,1,0:T(8,128)S(1)}, u32[]{:S(2)}, u32[]{:S(2)}) %collective-permute-start.5) | collective-permute-done | bytes 3145760 | tf_op jit(solution)/shard_map/ppermute | solution.py:392
  76.6 0.3 core_add.2
  76.9 3.4 %second_block.3 = (f32[6,16,16,512]{3,2,1,0:T(8,128)S(1)}, f32[6,16,16,512]{3,2,1,0:T(8,128)S(1)}, f32[2,2,8,16,512]{4,3,2,1,0:T(8,128)S(1)}, f32[2,2,8,16,512]{4,3,2,1,0:T(8,128)S(1)}) custom-call(bf16[512,1024]{1,0:T(8,128)(2,1)S(1)} %copy-done.6, ...), custom_call_target="tpu_custom_call", output_to_operand_aliasing={{2}: (6, {}), {3}: (7, {}), {0}: (8, {}), {1}: (9, {})} | custom-call | tf_op jit(solution)/shard_map/second_block/pallas_call | solution.py:58
  80.3 0.2 collective-permute-start.8
  80.5 5.7 %collective-permute-start.6 = (f32[3,4,16,512]{3,2,1,0:T(8,128)S(1)}, f32[3,4,16,512]{3,2,1,0:T(8,128)S(1)}, u32[]{:S(2)}, u32[]{:S(2)}) collective-permute-start(f32[3,4,16,512]{3,2,1,0:T(8,128)S(1)} %get-tuple-element.108), channel_id=1, source_target_pairs={{0,16},{1,5},{4,20},{5,9},{8,24},{9,13},{12,28},{13,1},{16,32},{17... | collective-permute-start | bytes 1179656 | tf_op jit(solution)/shard_map/ppermute | solution.py:404
  86.1 2.1 %collective-permute-start.7 = (f32[3,4,16,512]{3,2,1,0:T(8,128)S(1)}, f32[3,4,16,512]{3,2,1,0:T(8,128)S(1)}, u32[]{:S(2)}, u32[]{:S(2)}) collective-permute-start(f32[3,4,16,512]{3,2,1,0:T(8,128)S(1)} %get-tuple-element.109), channel_id=1, source_target_pairs={{0,48},{1,13},{4,52},{5,1},{8,56},{9,5},{12,60},{13,9},{16,0},{17,... | collective-permute-start | bytes 1179656 | tf_op jit(solution)/shard_map/ppermute | solution.py:404
  88.2 0.5 collective-permute-start.11
  88.8 4.9 %collective-permute-done.6.ra = f32[3,4,16,512]{3,2,1,0:T(8,128)S(1)} collective-permute-done((f32[3,4,16,512]{3,2,1,0:T(8,128)S(1)}, f32[3,4,16,512]{3,2,1,0:T(8,128)S(1)}, u32[]{:S(2)}, u32[]{:S(2)}) %collective-permute-start.6) | collective-permute-done | bytes 393248 | tf_op jit(solution)/shard_map/ppermute | solution.py:404
  93.7 0.1 relay_add.2
  93.8 1.0 collective-permute-start.12
  94.9 1.8 %collective-permute-start.13 = (f32[2,3,4,16,512]{4,3,2,1,0:T(8,128)S(1)}, f32[2,3,4,16,512]{4,3,2,1,0:T(8,128)S(1)}, u32[]{:S(2)}, u32[]{:S(2)}) collective-permute-start(f32[2,3,4,16,512]{4,3,2,1,0:T(8,128)S(1)} %get-tuple-element.117), channel_id=1, source_target_pairs={{0,48},{1,13},{4,52},{5,1},{8,56},{9,5},{12,60},{13,9},{16,0},{17,... | collective-permute-start | bytes 2359304 | tf_op jit(solution)/shard_map/ppermute | solution.py:404
  96.7 0.4 core_add.3
  97.1 0.1 collective-permute-start.9
  97.2 2.7 %collective-permute-start.10 = (f32[3,4,16,512]{3,2,1,0:T(8,128)S(1)}, f32[3,4,16,512]{3,2,1,0:T(8,128)S(1)}, u32[]{:S(2)}, u32[]{:S(2)}) collective-permute-start(f32[3,4,16,512]{3,2,1,0:T(8,128)S(1)} %get-tuple-element.114), channel_id=1, source_target_pairs={{0,48},{1,13},{4,52},{5,1},{8,56},{9,5},{12,60},{13,9},{16,0},{17,... | collective-permute-start | bytes 1179656 | tf_op jit(solution)/shard_map/ppermute | solution.py:404
  99.8 15.0 %collective-permute-done.11.gf.bf = f32[2,2,8,16,512]{4,3,2,1,0:T(8,128)S(1)} collective-permute-done((f32[2,2,8,16,512]{4,3,2,1,0:T(8,128)S(1)}, f32[2,2,8,16,512]{4,3,2,1,0:T(8,128)S(1)}, u32[]{:S(2)}, u32[]{:S(2)}) %collective-permute-start.11) | collective-permute-done | bytes 1048608 | tf_op jit(solution)/shard_map/ppermute | solution.py:392
  114.9 0.1 relay_add.3
  115.0 0.1 collective-permute-start.14
  115.1 2.7 %collective-permute-start.15 = (f32[2,3,4,16,512]{4,3,2,1,0:T(8,128)S(1)}, f32[2,3,4,16,512]{4,3,2,1,0:T(8,128)S(1)}, u32[]{:S(2)}, u32[]{:S(2)}) collective-permute-start(f32[2,3,4,16,512]{4,3,2,1,0:T(8,128)S(1)} %get-tuple-element.127), channel_id=1, source_target_pairs={{0,48},{1,13},{4,52},{5,1},{8,56},{9,5},{12,60},{13,9},{16,0},{17,... | collective-permute-start | bytes 2359304 | tf_op jit(solution)/shard_map/ppermute | solution.py:404
  117.8 0.1 brightest.1.most
  117.9 0.6 collective-permute-start.22
  118.5 9.0 %collective-permute-done.14.refs_4_ = f32[2,3,4,16,512]{4,3,2,1,0:T(8,128)S(1)} collective-permute-done((f32[2,3,4,16,512]{4,3,2,1,0:T(8,128)S(1)}, f32[2,3,4,16,512]{4,3,2,1,0:T(8,128)S(1)}, u32[]{:S(2)}, u32[]{:S(2)}) %collective-permute-start.14) | collective-permute-done | bytes 786464 | tf_op jit(solution)/shard_map/ppermute | solution.py:404
  127.4 0.3 plane_add.1
  127.8 0.1 collective-permute-start.16
  127.9 2.6 %collective-permute-start.17 = (f32[2,2,3,16,512]{4,3,2,1,0:T(8,128)S(1)}, f32[2,2,3,16,512]{4,3,2,1,0:T(8,128)S(1)}, u32[]{:S(2)}, u32[]{:S(2)}) collective-permute-start(f32[2,2,3,16,512]{4,3,2,1,0:T(8,128)S(1)} %get-tuple-element.130), channel_id=1, source_target_pairs={{0,12},{1,49},{4,0},{5,53},{8,4},{9,57},{12,8},{13,61},{16,28},{17... | collective-permute-start | bytes 1179656 | tf_op jit(solution)/shard_map/ppermute | solution.py:404
  130.5 0.5 collective-permute-start.18
  131.0 0.1 over_sum.1
  131.1 3.6 %collective-permute-start.21 = (f32[2,2,8,16,512]{4,3,2,1,0:T(8,128)S(1)}, f32[2,2,8,16,512]{4,3,2,1,0:T(8,128)S(1)}, u32[]{:S(2)}, u32[]{:S(2)}) collective-permute-start(f32[2,2,8,16,512]{4,3,2,1,0:T(8,128)S(1)} %over_sum.1), channel_id=1, source_target_pairs={{0,1},{1,2},{2,3},{3,4},{4,5},{5,6},{6,7},{7,8},{8,9},{9,10},{10,1... | collective-permute-start | bytes 3145736 | tf_op jit(solution)/shard_map/ppermute | solution.py:388
  134.7 1.2 collective-permute-done.16.b
  136.0 3.5 %collective-permute-done.17.c = f32[2,2,3,16,512]{4,3,2,1,0:T(8,128)S(1)} collective-permute-done((f32[2,2,3,16,512]{4,3,2,1,0:T(8,128)S(1)}, f32[2,2,3,16,512]{4,3,2,1,0:T(8,128)S(1)}, u32[]{:S(2)}, u32[]{:S(2)}) %collective-permute-start.17) | collective-permute-done | bytes 393248 | tf_op jit(solution)/shard_map/ppermute | solution.py:404
  139.5 0.7 collective-permute-done.18.d
  140.2 0.1 line_add.1
  140.3 13.8 %collective-permute-start.19 = (f32[13,8,512]{2,1,0:T(8,128)S(1)}, f32[13,8,512]{2,1,0:T(8,128)S(1)}, u32[]{:S(2)}, u32[]{:S(2)}) collective-permute-start(f32[13,8,512]{2,1,0:T(8,128)S(1)} %get-tuple-element.133), channel_id=1, source_target_pairs={{0,1},{1,0},{2,3},{3,2},{4,5},{5,4},{6,7},{7,6},{8,9},{9,8},{10,11... | collective-permute-start | bytes 638984 | tf_op jit(solution)/shard_map/ppermute | solution.py:392
  154.1 1.1 collective-permute-done.19.recv
  155.3 0.1 collective-permute-start.20
  155.4 0.8 collective-permute-start.24
  156.1 2.5 %collective-permute-start.23 = (f32[2,6,8,512]{3,2,1,0:T(8,128)S(1)}, f32[2,6,8,512]{3,2,1,0:T(8,128)S(1)}, u32[]{:S(2)}, u32[]{:S(2)}) collective-permute-start(f32[2,6,8,512]{3,2,1,0:T(8,128)S(1)} %get-tuple-element.141.mine), channel_id=1, source_target_pairs={{0,64},{2,66},{64,0},{66,2},{1,65},{3,67},{65,1},{67,3},{4,68},{6,... | collective-permute-start | bytes 589832 | tf_op jit(solution)/shard_map/ppermute | solution.py:409
  158.6 3.2 %collective-permute-done.20.far_max.b = f32[13,8,512]{2,1,0:T(8,128)S(1)} collective-permute-done((f32[13,8,512]{2,1,0:T(8,128)S(1)}, f32[13,8,512]{2,1,0:T(8,128)S(1)}, u32[]{:S(2)}, u32[]{:S(2)}) %collective-permute-start.20) | collective-permute-done | bytes 213024 | tf_op jit(solution)/shard_map/ppermute | solution.py:409
  161.8 3.0 %object_update.1 = f32[2,512,1024]{2,1,0:T(8,128)} custom-call(s32[2]{0:T(128)S(1)} %pad_add_fusion.place, s32[2]{0:T(128)S(1)} %collective-permute-done.place.before, f32[13,8,512]{2,1,0:T(8,128)S(1)} %get-tuple-element.135.near_max, f32[13,8,512]{2,1,0:T(8,128)S(1)} %collective-permute-done.20.far_max.b, f32[2,512,1024]{2,1,0:T(8,128)S(1)} %copy-done.2, ...), custom_call_target="tpu_custom_call" | custom-call | tf_op jit(solution)/shard_map/object_update/pallas_call | solution.py:601
  164.8 0.6 collective-permute-done.23.c
  165.4 1.9 %collective-permute-done.24.d = f32[13,8,512]{2,1,0:T(8,128)S(1)} collective-permute-done((f32[13,8,512]{2,1,0:T(8,128)S(1)}, f32[13,8,512]{2,1,0:T(8,128)S(1)}, u32[]{:S(2)}, u32[]{:S(2)}) %collective-permute-start.24) | collective-permute-done | bytes 213024 | tf_op jit(solution)/shard_map/ppermute | solution.py:409
  167.3 1.6 mix.1
  (32 shorter events, 0.1 us)
Async XLA Ops:
  2.0 10.4 %copy-start = (bf16[2,6,512,512]{3,2,1,0:T(8,128)(2,1)S(1)}, bf16[2,6,512,512]{3,2,1,0:T(8,128)(2,1)}, u32[]{:S(2)}) copy-start(bf16[2,6,512,512]{3,2,1,0:T(8,128)(2,1)} %p_ref.9) | copy-start | bytes 18874372
  2.0 7.8 %collective-permute-start = (s32[2]{0:T(128)S(1)}, s32[2]{0:T(128)S(1)}, u32[]{:S(2)}, u32[]{:S(2)}) collective-permute-start(s32[2]{0:T(128)S(1)} %pad_add_fusion.place), channel_id=1, source_target_pairs={{0,1},{1,2},{2,3},{3,4},{4,5},{5,6},{6,7},{7,8},{8,9},{9,10},{10,1... | collective-permute-start | bytes 32 | tf_op jit(solution)/shard_map/ppermute | solution.py:388
  6.8 2.2 %copy-start.1 = (f32[2,512,1024]{2,1,0:T(8,128)S(1)}, f32[2,512,1024]{2,1,0:T(8,128)}, u32[]{:S(2)}) copy-start(f32[2,512,1024]{2,1,0:T(8,128)} %obj.3) | copy-start | bytes 12582916
  10.4 16.4 %collective-permute-start.1 = (f32[2,256,512]{2,1,0:T(8,128)S(1)}, f32[2,256,512]{2,1,0:T(8,128)S(1)}, u32[]{:S(2)}, u32[]{:S(2)}) collective-permute-start(f32[2,256,512]{2,1,0:T(8,128)S(1)} %rim_rows.1), channel_id=1, source_target_pairs={{1,0},{2,1},{3,2},{4,3},{5,4},{6,5},{7,6},{8,7},{9,8},{10,9},{11,1... | collective-permute-start | bytes 3145736 | tf_op jit(solution)/shard_map/ppermute | solution.py:388
  12.4 1.6 copy-start.3
  14.0 5.4 %copy-start.7 = (bf16[512,1024]{1,0:T(8,128)(2,1)S(1)}, bf16[512,1024]{1,0:T(8,128)(2,1)}, u32[]{:S(2)}) copy-start(bf16[512,1024]{1,0:T(8,128)(2,1)} %constant.14.clone.wt1.wt) | copy-start | bytes 3145732
  14.0 5.4 %copy-start.8 = (bf16[512,1024]{1,0:T(8,128)(2,1)S(1)}, bf16[512,1024]{1,0:T(8,128)(2,1)}, u32[]{:S(2)}) copy-start(bf16[512,1024]{1,0:T(8,128)(2,1)} %constant.13.clone.wt0.wt) | copy-start | bytes 3145732
  19.4 9.6 %copy-start.4 = (bf16[1024,1024]{1,0:T(8,128)(2,1)S(1)}, bf16[1024,1024]{1,0:T(8,128)(2,1)}, u32[]{:S(2)}) copy-start(bf16[1024,1024]{1,0:T(8,128)(2,1)} %constant.12.clone.table) | copy-start | bytes 6291460
  26.9 11.0 %collective-permute-start.2 = (f32[128,512]{1,0:T(8,128)S(1)}, f32[128,512]{1,0:T(8,128)S(1)}, u32[]{:S(2)}, u32[]{:S(2)}) collective-permute-start(f32[128,512]{1,0:T(8,128)S(1)} %get-tuple-element.84), channel_id=1, source_target_pairs={{0,64},{64,0},{1,65},{65,1},{2,66},{66,2},{3,67},{67,3},{4,68},{68... | collective-permute-start | bytes 786440 | tf_op jit(solution)/shard_map/ppermute | solution.py:392
  36.9 15.6 %collective-permute-start.3 = (f32[256,512]{1,0:T(8,128)S(1)}, f32[256,512]{1,0:T(8,128)S(1)}, u32[]{:S(2)}, u32[]{:S(2)}) collective-permute-start(f32[256,512]{1,0:T(8,128)S(1)} %get-tuple-element.86.s0), channel_id=1, source_target_pairs={{0,64},{64,0},{1,65},{65,1},{2,66},{66,2},{3,67},{67,3},{4,68},{68... | collective-permute-start | bytes 1572872 | tf_op jit(solution)/shard_map/ppermute | solution.py:392
  37.8 14.7 %copy-start.5 = (bf16[1024,1024]{1,0:T(8,128)(2,1)S(1)}, bf16[1024,1024]{1,0:T(8,128)(2,1)}, u32[]{:S(2)}) copy-start(bf16[1024,1024]{1,0:T(8,128)(2,1)} %constant.15.clone.table) | copy-start | bytes 6291460
  37.8 14.7 %copy-start.9 = (f32[1,512,512]{2,1,0:T(8,128)S(1)}, f32[1,512,512]{2,1,0:T(8,128)}, u32[]{:S(2)}) copy-start(f32[1,512,512]{2,1,0:T(8,128)} %pat.3) | copy-start | bytes 3145732
  40.5 19.4 %collective-permute-start.4 = (f32[256,512]{1,0:T(8,128)S(1)}, f32[256,512]{1,0:T(8,128)S(1)}, u32[]{:S(2)}, u32[]{:S(2)}) collective-permute-start(f32[256,512]{1,0:T(8,128)S(1)} %get-tuple-element.90.s0), channel_id=1, source_target_pairs={{0,64},{64,0},{1,65},{65,1},{2,66},{66,2},{3,67},{67,3},{4,68},{68... | collective-permute-start | bytes 1572872 | tf_op jit(solution)/shard_map/ppermute | solution.py:392
  52.5 7.4 %copy-start.10 = (bf16[512,1024]{1,0:T(8,128)(2,1)S(1)}, bf16[512,1024]{1,0:T(8,128)(2,1)}, u32[]{:S(2)}) copy-start(bf16[512,1024]{1,0:T(8,128)(2,1)} %constant.16.clone.bt) | copy-start | bytes 3145732
  60.0 10.9 %copy-start.6 = (bf16[512,1024]{1,0:T(8,128)(2,1)S(1)}, bf16[512,1024]{1,0:T(8,128)(2,1)}, u32[]{:S(2)}) copy-start(bf16[512,1024]{1,0:T(8,128)(2,1)} %constant.17.clone.bt) | copy-start | bytes 3145732
  70.8 5.7 %collective-permute-start.5 = (f32[6,16,16,512]{3,2,1,0:T(8,128)S(1)}, f32[6,16,16,512]{3,2,1,0:T(8,128)S(1)}, u32[]{:S(2)}, u32[]{:S(2)}) collective-permute-start(f32[6,16,16,512]{3,2,1,0:T(8,128)S(1)} %get-tuple-element.101), channel_id=1, source_target_pairs={{0,1},{1,0},{2,3},{3,2},{4,5},{5,4},{6,7},{7,6},{8,9},{9,8},{10,11... | collective-permute-start | bytes 9437192 | tf_op jit(solution)/shard_map/ppermute | solution.py:392
  80.3 16.4 %collective-permute-start.8 = (f32[6,16,16,512]{3,2,1,0:T(8,128)S(1)}, f32[6,16,16,512]{3,2,1,0:T(8,128)S(1)}, u32[]{:S(2)}, u32[]{:S(2)}) collective-permute-start(f32[6,16,16,512]{3,2,1,0:T(8,128)S(1)} %get-tuple-element.112), channel_id=1, source_target_pairs={{0,1},{1,0},{2,3},{3,2},{4,5},{5,4},{6,7},{7,6},{8,9},{9,8},{10,11... | collective-permute-start | bytes 9437192 | tf_op jit(solution)/shard_map/ppermute | solution.py:392
  80.5 13.2 %collective-permute-start.6 = (f32[3,4,16,512]{3,2,1,0:T(8,128)S(1)}, f32[3,4,16,512]{3,2,1,0:T(8,128)S(1)}, u32[]{:S(2)}, u32[]{:S(2)}) collective-permute-start(f32[3,4,16,512]{3,2,1,0:T(8,128)S(1)} %get-tuple-element.108), channel_id=1, source_target_pairs={{0,16},{1,5},{4,20},{5,9},{8,24},{9,13},{12,28},{13,1},{16,32},{17... | collective-permute-start | bytes 1179656 | tf_op jit(solution)/shard_map/ppermute | solution.py:404
  86.1 7.6 %collective-permute-start.7 = (f32[3,4,16,512]{3,2,1,0:T(8,128)S(1)}, f32[3,4,16,512]{3,2,1,0:T(8,128)S(1)}, u32[]{:S(2)}, u32[]{:S(2)}) collective-permute-start(f32[3,4,16,512]{3,2,1,0:T(8,128)S(1)} %get-tuple-element.109), channel_id=1, source_target_pairs={{0,48},{1,13},{4,52},{5,1},{8,56},{9,5},{12,60},{13,9},{16,0},{17,... | collective-permute-start | bytes 1179656 | tf_op jit(solution)/shard_map/ppermute | solution.py:404
  88.2 26.6 %collective-permute-start.11 = (f32[2,2,8,16,512]{4,3,2,1,0:T(8,128)S(1)}, f32[2,2,8,16,512]{4,3,2,1,0:T(8,128)S(1)}, u32[]{:S(2)}, u32[]{:S(2)}) collective-permute-start(f32[2,2,8,16,512]{4,3,2,1,0:T(8,128)S(1)} %get-tuple-element.115.g.b), channel_id=1, source_target_pairs={{0,64},{64,0},{1,65},{65,1},{2,66},{66,2},{3,67},{67,3},{4,68},{68... | collective-permute-start | bytes 3145736 | tf_op jit(solution)/shard_map/ppermute | solution.py:392
  93.8 21.0 %collective-permute-start.12 = (f32[2,3,4,16,512]{4,3,2,1,0:T(8,128)S(1)}, f32[2,3,4,16,512]{4,3,2,1,0:T(8,128)S(1)}, u32[]{:S(2)}, u32[]{:S(2)}) collective-permute-start(f32[2,3,4,16,512]{4,3,2,1,0:T(8,128)S(1)} %get-tuple-element.110), channel_id=1, source_target_pairs={{0,16},{1,5},{4,20},{5,9},{8,24},{9,13},{12,28},{13,1},{16,32},{17... | collective-permute-start | bytes 2359304 | tf_op jit(solution)/shard_map/ppermute | solution.py:404
  94.9 20.0 %collective-permute-start.13 = (f32[2,3,4,16,512]{4,3,2,1,0:T(8,128)S(1)}, f32[2,3,4,16,512]{4,3,2,1,0:T(8,128)S(1)}, u32[]{:S(2)}, u32[]{:S(2)}) collective-permute-start(f32[2,3,4,16,512]{4,3,2,1,0:T(8,128)S(1)} %get-tuple-element.117), channel_id=1, source_target_pairs={{0,48},{1,13},{4,52},{5,1},{8,56},{9,5},{12,60},{13,9},{16,0},{17,... | collective-permute-start | bytes 2359304 | tf_op jit(solution)/shard_map/ppermute | solution.py:404
  97.1 17.8 %collective-permute-start.9 = (f32[3,4,16,512]{3,2,1,0:T(8,128)S(1)}, f32[3,4,16,512]{3,2,1,0:T(8,128)S(1)}, u32[]{:S(2)}, u32[]{:S(2)}) collective-permute-start(f32[3,4,16,512]{3,2,1,0:T(8,128)S(1)} %get-tuple-element.113), channel_id=1, source_target_pairs={{0,16},{1,5},{4,20},{5,9},{8,24},{9,13},{12,28},{13,1},{16,32},{17... | collective-permute-start | bytes 1179656 | tf_op jit(solution)/shard_map/ppermute | solution.py:404
  97.2 17.7 %collective-permute-start.10 = (f32[3,4,16,512]{3,2,1,0:T(8,128)S(1)}, f32[3,4,16,512]{3,2,1,0:T(8,128)S(1)}, u32[]{:S(2)}, u32[]{:S(2)}) collective-permute-start(f32[3,4,16,512]{3,2,1,0:T(8,128)S(1)} %get-tuple-element.114), channel_id=1, source_target_pairs={{0,48},{1,13},{4,52},{5,1},{8,56},{9,5},{12,60},{13,9},{16,0},{17,... | collective-permute-start | bytes 1179656 | tf_op jit(solution)/shard_map/ppermute | solution.py:404
  115.0 12.4 %collective-permute-start.14 = (f32[2,3,4,16,512]{4,3,2,1,0:T(8,128)S(1)}, f32[2,3,4,16,512]{4,3,2,1,0:T(8,128)S(1)}, u32[]{:S(2)}, u32[]{:S(2)}) collective-permute-start(f32[2,3,4,16,512]{4,3,2,1,0:T(8,128)S(1)} %get-tuple-element.126), channel_id=1, source_target_pairs={{0,16},{1,5},{4,20},{5,9},{8,24},{9,13},{12,28},{13,1},{16,32},{17... | collective-permute-start | bytes 2359304 | tf_op jit(solution)/shard_map/ppermute | solution.py:404
  115.1 12.3 %collective-permute-start.15 = (f32[2,3,4,16,512]{4,3,2,1,0:T(8,128)S(1)}, f32[2,3,4,16,512]{4,3,2,1,0:T(8,128)S(1)}, u32[]{:S(2)}, u32[]{:S(2)}) collective-permute-start(f32[2,3,4,16,512]{4,3,2,1,0:T(8,128)S(1)} %get-tuple-element.127), channel_id=1, source_target_pairs={{0,48},{1,13},{4,52},{5,1},{8,56},{9,5},{12,60},{13,9},{16,0},{17,... | collective-permute-start | bytes 2359304 | tf_op jit(solution)/shard_map/ppermute | solution.py:404
  117.9 40.7 %collective-permute-start.22 = (f32[2,2,8,16,512]{4,3,2,1,0:T(8,128)S(1)}, f32[2,2,8,16,512]{4,3,2,1,0:T(8,128)S(1)}, u32[]{:S(2)}, u32[]{:S(2)}) collective-permute-start(f32[2,2,8,16,512]{4,3,2,1,0:T(8,128)S(1)} %get-tuple-element.137.t), channel_id=1, source_target_pairs={{0,64},{64,0},{1,65},{65,1},{2,66},{66,2},{3,67},{67,3},{4,68},{68... | collective-permute-start | bytes 3145736 | tf_op jit(solution)/shard_map/ppermute | solution.py:392
  127.8 8.2 %collective-permute-start.16 = (f32[2,2,3,16,512]{4,3,2,1,0:T(8,128)S(1)}, f32[2,2,3,16,512]{4,3,2,1,0:T(8,128)S(1)}, u32[]{:S(2)}, u32[]{:S(2)}) collective-permute-start(f32[2,2,3,16,512]{4,3,2,1,0:T(8,128)S(1)} %get-tuple-element.129), channel_id=1, source_target_pairs={{0,4},{1,17},{4,8},{5,21},{8,12},{9,25},{12,0},{13,29},{16,20},{17... | collective-permute-start | bytes 1179656 | tf_op jit(solution)/shard_map/ppermute | solution.py:404
  127.9 11.6 %collective-permute-start.17 = (f32[2,2,3,16,512]{4,3,2,1,0:T(8,128)S(1)}, f32[2,2,3,16,512]{4,3,2,1,0:T(8,128)S(1)}, u32[]{:S(2)}, u32[]{:S(2)}) collective-permute-start(f32[2,2,3,16,512]{4,3,2,1,0:T(8,128)S(1)} %get-tuple-element.130), channel_id=1, source_target_pairs={{0,12},{1,49},{4,0},{5,53},{8,4},{9,57},{12,8},{13,61},{16,28},{17... | collective-permute-start | bytes 1179656 | tf_op jit(solution)/shard_map/ppermute | solution.py:404
  130.5 9.7 %collective-permute-start.18 = (f32[2,2,3,16,512]{4,3,2,1,0:T(8,128)S(1)}, f32[2,2,3,16,512]{4,3,2,1,0:T(8,128)S(1)}, u32[]{:S(2)}, u32[]{:S(2)}) collective-permute-start(f32[2,2,3,16,512]{4,3,2,1,0:T(8,128)S(1)} %get-tuple-element.131), channel_id=1, source_target_pairs={{0,8},{1,33},{4,12},{5,37},{8,0},{9,41},{12,4},{13,45},{16,24},{17... | collective-permute-start | bytes 1179656 | tf_op jit(solution)/shard_map/ppermute | solution.py:404
  131.1 27.5 %collective-permute-start.21 = (f32[2,2,8,16,512]{4,3,2,1,0:T(8,128)S(1)}, f32[2,2,8,16,512]{4,3,2,1,0:T(8,128)S(1)}, u32[]{:S(2)}, u32[]{:S(2)}) collective-permute-start(f32[2,2,8,16,512]{4,3,2,1,0:T(8,128)S(1)} %over_sum.1), channel_id=1, source_target_pairs={{0,1},{1,2},{2,3},{3,4},{4,5},{5,6},{6,7},{7,8},{8,9},{9,10},{10,1... | collective-permute-start | bytes 3145736 | tf_op jit(solution)/shard_map/ppermute | solution.py:388
  140.3 14.9 %collective-permute-start.19 = (f32[13,8,512]{2,1,0:T(8,128)S(1)}, f32[13,8,512]{2,1,0:T(8,128)S(1)}, u32[]{:S(2)}, u32[]{:S(2)}) collective-permute-start(f32[13,8,512]{2,1,0:T(8,128)S(1)} %get-tuple-element.133), channel_id=1, source_target_pairs={{0,1},{1,0},{2,3},{3,2},{4,5},{5,4},{6,7},{7,6},{8,9},{9,8},{10,11... | collective-permute-start | bytes 638984 | tf_op jit(solution)/shard_map/ppermute | solution.py:392
  155.2 6.6 %copy-start.2 = (f32[2,512,1024]{2,1,0:T(8,128)S(1)}, f32[2,512,1024]{2,1,0:T(8,128)}, u32[]{:S(2)}) copy-start(f32[2,512,1024]{2,1,0:T(8,128)} %obj.3) | copy-start | bytes 12582916
  155.3 6.5 %collective-permute-start.20 = (f32[13,8,512]{2,1,0:T(8,128)S(1)}, f32[13,8,512]{2,1,0:T(8,128)S(1)}, u32[]{:S(2)}, u32[]{:S(2)}) collective-permute-start(f32[13,8,512]{2,1,0:T(8,128)S(1)} %get-tuple-element.135.near_max), channel_id=1, source_target_pairs={{0,2},{2,0},{64,66},{66,64},{1,3},{3,1},{65,67},{67,65},{4,6},{6,4... | collective-permute-start | bytes 638984 | tf_op jit(solution)/shard_map/ppermute | solution.py:409
  155.4 12.0 %collective-permute-start.24 = (f32[13,8,512]{2,1,0:T(8,128)S(1)}, f32[13,8,512]{2,1,0:T(8,128)S(1)}, u32[]{:S(2)}, u32[]{:S(2)}) collective-permute-start(f32[13,8,512]{2,1,0:T(8,128)S(1)} %get-tuple-element.135.near_max), channel_id=1, source_target_pairs={{0,66},{2,64},{64,2},{66,0},{1,67},{3,65},{65,3},{67,1},{4,70},{6,... | collective-permute-start | bytes 638984 | tf_op jit(solution)/shard_map/ppermute | solution.py:409
  156.1 11.2 %copy-start.11 = (s32[12,12]{1,0:T(8,128)S(1)}, s32[12,12]{1,0:T(8,128)}, u32[]{:S(2)}) copy-start(s32[12,12]{1,0:T(8,128)} %w_ref.1) | copy-start | bytes 1732
  156.1 9.3 %collective-permute-start.23 = (f32[2,6,8,512]{3,2,1,0:T(8,128)S(1)}, f32[2,6,8,512]{3,2,1,0:T(8,128)S(1)}, u32[]{:S(2)}, u32[]{:S(2)}) collective-permute-start(f32[2,6,8,512]{3,2,1,0:T(8,128)S(1)} %get-tuple-element.141.mine), channel_id=1, source_target_pairs={{0,64},{2,66},{64,0},{66,2},{1,65},{3,67},{65,1},{67,3},{4,68},{6,... | collective-permute-start | bytes 589832 | tf_op jit(solution)/shard_map/ppermute | solution.py:409

commit v9 on v8

--- a/solution.py
+++ b/solution.py
@@ -664,10 +664,12 @@
     near1, back1 = relay_add(near1, back1, ra1, rb1)
     plane1 = (own1, turned(near1, 1, True), turned(back1, -1, True))
     tops_far = swapped(tops, "mode")
-    over = along(over_sum(bots, bots_far), 1)
+    over_out = over_sum(bots, bots_far)
     line = plane_add((plane0, plane1))
     line = [line[0]] + [turned(line[r], r, False) for r in (1, 3, 2)]
     keep, send = line_add(most, line)
+    over_out, _ = tied(over_out, keep)
+    over = along(over_out, 1)
     recv = swapped(send, "core")
     mine, other = pixel_step(most, keep, recv, rows)
     beside = across(other, 0, 1)

time: 169 us -> 171 us (1.012)
  waiting for transfers between devices: 58.8 us -> 73.1 us
  starting transfers between devices: 53.4 us -> 40.6 us
    ppermute x8, starting transfers between devices: 20.6 us -> 6.81 us  [swapped(): return lax.ppermute(value, axis, [(0, 1), (1, 0)])]
    ppermute x3, waiting for transfers between devices: 5.68 us -> 15.3 us  [across(): return lax.ppermute(value, ('mode', 'x'), pairs)]
    ppermute x11, waiting for transfers between devices: 19.4 us -> 23 us  [turned(): return lax.ppermute(value, RING, pairs)]
  transfers between devices with their start and end apart: 25 -> 25, of which waited for: 14 -> 12; matrix products, arithmetic and copies ran while one was open for 0% -> 0% of each run, Pallas kernels for 20% -> 20%
where the time goes in v9:
time: 171 us
  waiting for transfers between devices  73.1 us (43%)
  Pallas kernels  50.8 us (30%)
  starting transfers between devices  40.6 us (24%)
  local copies, waits for them, and re-layouts  3.81 us (2%)
  between operations  2.22 us (1%)
    pallas_call x20, Pallas kernels, call(): pl.pallas_call(body, in_specs=ins, out_specs=[LOCAL] * len(outs), out_sha...  47.6 us
    ppermute x8, waiting for transfers between devices, swapped(): return lax.ppermute(value, axis, [(0, 1), (1, 0)])  31.7 us
    ppermute x11, waiting for transfers between devices, turned(): return lax.ppermute(value, RING, pairs)  23 us
    ppermute x11, starting transfers between devices, turned(): return lax.ppermute(value, RING, pairs)  19.3 us
    ppermute x3, waiting for transfers between devices, across(): return lax.ppermute(value, ('mode', 'x'), pairs)  15.3 us
    ppermute x3, starting transfers between devices, along(): return lax.ppermute(value, SCAN, [(i, i + steps) for i in range(lo, hi)])  10.6 us
    ppermute x8, starting transfers between devices, swapped(): return lax.ppermute(value, axis, [(0, 1), (1, 0)])  6.81 us
    ppermute x3, starting transfers between devices, across(): return lax.ppermute(value, ('mode', 'x'), pairs)  3.89 us
  transfers between devices with their start and end apart: 25, of which 12 were waited for; matrix products, arithmetic and copies ran while one was open for 0% of the time, Pallas kernels for 20%

profile of v9, /device:TPU:1, one launch (start us, length us, event | category | flops | bytes accessed | tf_op | source)
XLA Modules:
  0.0 170.6 jit_solution(16854472101678464416)
XLA Ops:
  1.9 0.1 pad_add_fusion.place
  2.0 4.8 %collective-permute-start = (s32[2]{0:T(128)S(1)}, s32[2]{0:T(128)S(1)}, u32[]{:S(2)}, u32[]{:S(2)}) collective-permute-start(s32[2]{0:T(128)S(1)} %pad_add_fusion.place), channel_id=1, source_target_pairs={{0,1},{1,2},{2,3},{3,4},{4,5},{5,6},{6,7},{7,8},{8,9},{9,10},{10,1... | collective-permute-start | bytes 32 | tf_op jit(solution)/shard_map/ppermute | solution.py:388
  6.8 0.0 copy-start.1
  6.8 2.2 %copy-done.1 = f32[2,512,1024]{2,1,0:T(8,128)S(1)} copy-done((f32[2,512,1024]{2,1,0:T(8,128)S(1)}, f32[2,512,1024]{2,1,0:T(8,128)}, u32[]{:S(2)}) %copy-start.1) | copy-done | bytes 4194328
  9.0 0.8 own_rows.1
  9.8 0.6 rim_rows.1
  10.4 1.9 %collective-permute-start.1 = (f32[2,256,512]{2,1,0:T(8,128)S(1)}, f32[2,256,512]{2,1,0:T(8,128)S(1)}, u32[]{:S(2)}, u32[]{:S(2)}) collective-permute-start(f32[2,256,512]{2,1,0:T(8,128)S(1)} %rim_rows.1), channel_id=1, source_target_pairs={{1,0},{2,1},{3,2},{4,3},{5,4},{6,5},{7,6},{8,7},{9,8},{10,9},{11,1... | collective-permute-start | bytes 3145736 | tf_op jit(solution)/shard_map/ppermute | solution.py:388
  12.4 0.0 copy-start.3
  12.4 1.6 copy-done.3
  14.0 5.4 %top_half.1 = (bf16[6,512,512]{2,1,0:T(8,128)(2,1)S(1)}, f32[128,512]{1,0:T(8,128)S(1)}, f32[128,512]{1,0:T(8,128)S(1)}, f32[2,6,8,512]{3,2,1,0:T(8,128)S(1)}) custom-call(f32[2,256,512]{2,1,0:T(8,128)S(1)} %get-tuple-element.75.patch_ref.ptop, bf16[2,6,512,512]{3,2,1,0:T(8,128)(2,1)S(1)} %copy-done, bf16[1024,1024]{1,0:T(8,128)(2,1)S(1)} %copy-done.3), custom_call_target="tpu_custom_call" | custom-call | tf_op jit(solution)/shard_map/top_half/pallas_call | solution.py:58
  19.4 0.0 copy-start.4
  19.4 4.3 %first_terms.1 = (f32[6,512,512]{2,1,0:T(8,128)S(1)}, f32[6,512,512]{2,1,0:T(8,128)S(1)}) custom-call(bf16[512,1024]{1,0:T(8,128)(2,1)S(1)} %copy-done.8, bf16[512,1024]{1,0:T(8,128)(2,1)S(1)} %copy-done.7, bf16[6,512,512]{2,1,0:T(8,128)(2,1)S(1)} %get-tuple-element.79.top), custom_call_target="tpu_custom_call" | custom-call | tf_op jit(solution)/shard_map/first_terms/pallas_call | solution.py:58
  23.8 3.1 %collective-permute-done.1.rim = f32[2,256,512]{2,1,0:T(8,128)S(1)} collective-permute-done((f32[2,256,512]{2,1,0:T(8,128)S(1)}, f32[2,256,512]{2,1,0:T(8,128)S(1)}, u32[]{:S(2)}, u32[]{:S(2)}) %collective-permute-start.1) | collective-permute-done | bytes 1048608 | tf_op jit(solution)/shard_map/ppermute | solution.py:388
  26.9 2.2 %collective-permute-start.2 = (f32[128,512]{1,0:T(8,128)S(1)}, f32[128,512]{1,0:T(8,128)S(1)}, u32[]{:S(2)}, u32[]{:S(2)}) collective-permute-start(f32[128,512]{1,0:T(8,128)S(1)} %get-tuple-element.85), channel_id=1, source_target_pairs={{0,64},{64,0},{1,65},{65,1},{2,66},{66,2},{3,67},{67,3},{4,68},{68... | collective-permute-start | bytes 786440 | tf_op jit(solution)/shard_map/ppermute | solution.py:392
  29.0 7.9 %bottom_half.1 = (bf16[6,512,512]{2,1,0:T(8,128)(2,1)S(1)}, f32[2,256,512]{2,1,0:T(8,128)S(1)}, f32[6,512,512]{2,1,0:T(8,128)S(1)}, f32[256,512]{1,0:T(8,128)S(1)}) custom-call(s32[2]{0:T(128)S(1)} %pad_add_fusion.place, f32[2,256,512]{2,1,0:T(8,128)S(1)} %get-tuple-element.77.own, ...), custom_call_target="tpu_custom_call", output_to_operand_aliasing={{2}: (6, {})} | custom-call | tf_op jit(solution)/shard_map/bottom_half/pallas_call | solution.py:58
  36.9 0.9 collective-permute-start.3
  37.8 2.7 %low_wave.1 = (f32[6,512,512]{2,1,0:T(8,128)S(1)}, f32[256,512]{1,0:T(8,128)S(1)}) custom-call(bf16[512,1024]{1,0:T(8,128)(2,1)S(1)} %copy-done.7, bf16[6,512,512]{2,1,0:T(8,128)(2,1)S(1)} %get-tuple-element.89.bot, f32[6,512,512]{2,1,0:T(8,128)S(1)} %get-tuple-element.90._), custom_call_target="tpu_custom_call", output_to_operand_aliasing={{0}: (2, {})} | custom-call | tf_op jit(solution)/shard_map/low_wave/pallas_call | solution.py:58
  40.5 2.2 %collective-permute-start.4 = (f32[256,512]{1,0:T(8,128)S(1)}, f32[256,512]{1,0:T(8,128)S(1)}, u32[]{:S(2)}, u32[]{:S(2)}) collective-permute-start(f32[256,512]{1,0:T(8,128)S(1)} %get-tuple-element.91.s0), channel_id=1, source_target_pairs={{0,64},{64,0},{1,65},{65,1},{2,66},{66,2},{3,67},{67,3},{4,68},{68... | collective-permute-start | bytes 1572872 | tf_op jit(solution)/shard_map/ppermute | solution.py:392
  42.8 9.7 %collective-permute-done.3.s1 = f32[256,512]{1,0:T(8,128)S(1)} collective-permute-done((f32[256,512]{1,0:T(8,128)S(1)}, f32[256,512]{1,0:T(8,128)S(1)}, u32[]{:S(2)}, u32[]{:S(2)}) %collective-permute-start.3) | collective-permute-done | bytes 524320 | tf_op jit(solution)/shard_map/ppermute | solution.py:392
  52.5 4.9 %fixed_top.1.top = bf16[6,512,512]{2,1,0:T(8,128)(2,1)S(1)} custom-call(f32[1,512,512]{2,1,0:T(8,128)S(1)} %copy-done.9, f32[256,512]{1,0:T(8,128)S(1)} %get-tuple-element.87.s0, f32[256,512]{1,0:T(8,128)S(1)} %collective-permute-done.3.s1, f32[6,512,512]{2,1,0:T(8,128)S(1)} %get-tuple-element.88.wave_ref, bf16[1024,1024]{1,0:T(8,128)(2,1)S(1)} %copy-done.5), custom_call_target="tpu_custom_call" | custom-call | tf_op jit(solution)/shard_map/fixed_top/pallas_call | solution.py:58
  57.4 2.6 %collective-permute-done.4.s1 = f32[256,512]{1,0:T(8,128)S(1)} collective-permute-done((f32[256,512]{1,0:T(8,128)S(1)}, f32[256,512]{1,0:T(8,128)S(1)}, u32[]{:S(2)}, u32[]{:S(2)}) %collective-permute-start.4) | collective-permute-done | bytes 524320 | tf_op jit(solution)/shard_map/ppermute | solution.py:392
  60.0 10.8 %first_block.1 = (bf16[6,512,512]{2,1,0:T(8,128)(2,1)S(1)}, f32[6,16,16,512]{3,2,1,0:T(8,128)S(1)}, f32[6,16,16,512]{3,2,1,0:T(8,128)S(1)}, f32[2,2,8,16,512]{4,3,2,1,0:T(8,128)S(1)}, f32[2,2,8,16,512]{4,3,2,1,0:T(8,128)S(1)}) custom-call(f32[1,512,512]{2,1,0:T(8,128)S(1)} %copy-done.9, f32[256,512]{1,0:T(8,128)S(1)} %get-tuple-element.91.s0, ...), custom_call_target="tpu_custom_call" | custom-call | tf_op jit(solution)/shard_map/first_block/pallas_call | solution.py:58
  70.8 0.1 collective-permute-start.5
  70.9 3.4 %second_block.2 = (f32[6,16,16,512]{3,2,1,0:T(8,128)S(1)}, f32[6,16,16,512]{3,2,1,0:T(8,128)S(1)}, f32[2,2,8,16,512]{4,3,2,1,0:T(8,128)S(1)}, f32[2,2,8,16,512]{4,3,2,1,0:T(8,128)S(1)}) custom-call(bf16[512,1024]{1,0:T(8,128)(2,1)S(1)} %copy-done.6, bf16[6,512,512]{2,1,0:T(8,128)(2,1)S(1)} %fixed_top.1.top, ...), custom_call_target="tpu_custom_call", output_to_operand_aliasing={{2}: (6, {}), {3}: (7, {})} | custom-call | tf_op jit(solution)/shard_map/second_block/pallas_call | solution.py:58
  74.4 2.2 %collective-permute-done.5.recv = f32[6,16,16,512]{3,2,1,0:T(8,128)S(1)} collective-permute-done((f32[6,16,16,512]{3,2,1,0:T(8,128)S(1)}, f32[6,16,16,512]{3,2,1,0:T(8,128)S(1)}, u32[]{:S(2)}, u32[]{:S(2)}) %collective-permute-start.5) | collective-permute-done | bytes 3145760 | tf_op jit(solution)/shard_map/ppermute | solution.py:392
  76.6 0.3 core_add.2
  76.9 3.4 %second_block.3 = (f32[6,16,16,512]{3,2,1,0:T(8,128)S(1)}, f32[6,16,16,512]{3,2,1,0:T(8,128)S(1)}, f32[2,2,8,16,512]{4,3,2,1,0:T(8,128)S(1)}, f32[2,2,8,16,512]{4,3,2,1,0:T(8,128)S(1)}) custom-call(bf16[512,1024]{1,0:T(8,128)(2,1)S(1)} %copy-done.6, ...), custom_call_target="tpu_custom_call", output_to_operand_aliasing={{2}: (6, {}), {3}: (7, {}), {0}: (8, {}), {1}: (9, {})} | custom-call | tf_op jit(solution)/shard_map/second_block/pallas_call | solution.py:58
  80.3 0.2 collective-permute-start.8
  80.5 5.7 %collective-permute-start.6 = (f32[3,4,16,512]{3,2,1,0:T(8,128)S(1)}, f32[3,4,16,512]{3,2,1,0:T(8,128)S(1)}, u32[]{:S(2)}, u32[]{:S(2)}) collective-permute-start(f32[3,4,16,512]{3,2,1,0:T(8,128)S(1)} %get-tuple-element.109), channel_id=1, source_target_pairs={{0,16},{1,5},{4,20},{5,9},{8,24},{9,13},{12,28},{13,1},{16,32},{17... | collective-permute-start | bytes 1179656 | tf_op jit(solution)/shard_map/ppermute | solution.py:404
  86.1 2.1 %collective-permute-start.7 = (f32[3,4,16,512]{3,2,1,0:T(8,128)S(1)}, f32[3,4,16,512]{3,2,1,0:T(8,128)S(1)}, u32[]{:S(2)}, u32[]{:S(2)}) collective-permute-start(f32[3,4,16,512]{3,2,1,0:T(8,128)S(1)} %get-tuple-element.110), channel_id=1, source_target_pairs={{0,48},{1,13},{4,52},{5,1},{8,56},{9,5},{12,60},{13,9},{16,0},{17,... | collective-permute-start | bytes 1179656 | tf_op jit(solution)/shard_map/ppermute | solution.py:404
  88.2 0.5 collective-permute-start.11
  88.8 4.9 %collective-permute-done.6.ra = f32[3,4,16,512]{3,2,1,0:T(8,128)S(1)} collective-permute-done((f32[3,4,16,512]{3,2,1,0:T(8,128)S(1)}, f32[3,4,16,512]{3,2,1,0:T(8,128)S(1)}, u32[]{:S(2)}, u32[]{:S(2)}) %collective-permute-start.6) | collective-permute-done | bytes 393248 | tf_op jit(solution)/shard_map/ppermute | solution.py:404
  93.7 0.1 relay_add.2
  93.8 1.0 collective-permute-start.12
  94.9 1.8 %collective-permute-start.13 = (f32[2,3,4,16,512]{4,3,2,1,0:T(8,128)S(1)}, f32[2,3,4,16,512]{4,3,2,1,0:T(8,128)S(1)}, u32[]{:S(2)}, u32[]{:S(2)}) collective-permute-start(f32[2,3,4,16,512]{4,3,2,1,0:T(8,128)S(1)} %get-tuple-element.118), channel_id=1, source_target_pairs={{0,48},{1,13},{4,52},{5,1},{8,56},{9,5},{12,60},{13,9},{16,0},{17,... | collective-permute-start | bytes 2359304 | tf_op jit(solution)/shard_map/ppermute | solution.py:404
  96.7 0.0 collective-permute-done.8.recv
  96.7 0.4 core_add.3
  97.1 0.1 collective-permute-start.9
  97.2 2.7 %collective-permute-start.10 = (f32[3,4,16,512]{3,2,1,0:T(8,128)S(1)}, f32[3,4,16,512]{3,2,1,0:T(8,128)S(1)}, u32[]{:S(2)}, u32[]{:S(2)}) collective-permute-start(f32[3,4,16,512]{3,2,1,0:T(8,128)S(1)} %get-tuple-element.115), channel_id=1, source_target_pairs={{0,48},{1,13},{4,52},{5,1},{8,56},{9,5},{12,60},{13,9},{16,0},{17,... | collective-permute-start | bytes 1179656 | tf_op jit(solution)/shard_map/ppermute | solution.py:404
  99.8 15.0 %collective-permute-done.11.gf.bf = f32[2,2,8,16,512]{4,3,2,1,0:T(8,128)S(1)} collective-permute-done((f32[2,2,8,16,512]{4,3,2,1,0:T(8,128)S(1)}, f32[2,2,8,16,512]{4,3,2,1,0:T(8,128)S(1)}, u32[]{:S(2)}, u32[]{:S(2)}) %collective-permute-start.11) | collective-permute-done | bytes 1048608 | tf_op jit(solution)/shard_map/ppermute | solution.py:392
  114.9 0.0 collective-permute-done.13.refs_2_
  114.9 0.1 relay_add.3
  115.0 0.1 collective-permute-start.14
  115.1 2.7 %collective-permute-start.15 = (f32[2,3,4,16,512]{4,3,2,1,0:T(8,128)S(1)}, f32[2,3,4,16,512]{4,3,2,1,0:T(8,128)S(1)}, u32[]{:S(2)}, u32[]{:S(2)}) collective-permute-start(f32[2,3,4,16,512]{4,3,2,1,0:T(8,128)S(1)} %get-tuple-element.128), channel_id=1, source_target_pairs={{0,48},{1,13},{4,52},{5,1},{8,56},{9,5},{12,60},{13,9},{16,0},{17,... | collective-permute-start | bytes 2359304 | tf_op jit(solution)/shard_map/ppermute | solution.py:404
  117.8 0.1 brightest.1.most
  117.9 0.6 collective-permute-start.22
  118.5 9.0 %collective-permute-done.14.refs_4_ = f32[2,3,4,16,512]{4,3,2,1,0:T(8,128)S(1)} collective-permute-done((f32[2,3,4,16,512]{4,3,2,1,0:T(8,128)S(1)}, f32[2,3,4,16,512]{4,3,2,1,0:T(8,128)S(1)}, u32[]{:S(2)}, u32[]{:S(2)}) %collective-permute-start.14) | collective-permute-done | bytes 786464 | tf_op jit(solution)/shard_map/ppermute | solution.py:404
  127.4 0.3 plane_add.1
  127.8 0.1 collective-permute-start.16
  127.9 2.6 %collective-permute-start.17 = (f32[2,2,3,16,512]{4,3,2,1,0:T(8,128)S(1)}, f32[2,2,3,16,512]{4,3,2,1,0:T(8,128)S(1)}, u32[]{:S(2)}, u32[]{:S(2)}) collective-permute-start(f32[2,2,3,16,512]{4,3,2,1,0:T(8,128)S(1)} %get-tuple-element.131), channel_id=1, source_target_pairs={{0,12},{1,49},{4,0},{5,53},{8,4},{9,57},{12,8},{13,61},{16,28},{17... | collective-permute-start | bytes 1179656 | tf_op jit(solution)/shard_map/ppermute | solution.py:404
  130.5 0.5 collective-permute-start.18
  131.0 0.1 over_sum.1
  131.1 4.8 %collective-permute-done.16.b = f32[2,2,3,16,512]{4,3,2,1,0:T(8,128)S(1)} collective-permute-done((f32[2,2,3,16,512]{4,3,2,1,0:T(8,128)S(1)}, f32[2,2,3,16,512]{4,3,2,1,0:T(8,128)S(1)}, u32[]{:S(2)}, u32[]{:S(2)}) %collective-permute-start.16) | collective-permute-done | bytes 393248 | tf_op jit(solution)/shard_map/ppermute | solution.py:404
  136.0 3.5 %collective-permute-done.17.c = f32[2,2,3,16,512]{4,3,2,1,0:T(8,128)S(1)} collective-permute-done((f32[2,2,3,16,512]{4,3,2,1,0:T(8,128)S(1)}, f32[2,2,3,16,512]{4,3,2,1,0:T(8,128)S(1)}, u32[]{:S(2)}, u32[]{:S(2)}) %collective-permute-start.17) | collective-permute-done | bytes 393248 | tf_op jit(solution)/shard_map/ppermute | solution.py:404
  139.5 0.7 collective-permute-done.18.d
  140.2 0.1 line_add.1
  140.3 4.0 %collective-permute-start.21 = (f32[2,2,8,16,512]{4,3,2,1,0:T(8,128)S(1)}, f32[2,2,8,16,512]{4,3,2,1,0:T(8,128)S(1)}, u32[]{:S(2)}, u32[]{:S(2)}) collective-permute-start(f32[2,2,8,16,512]{4,3,2,1,0:T(8,128)S(1)} %over_sum.1), channel_id=1, source_target_pairs={{0,1},{1,2},{2,3},{3,4},{4,5},{5,6},{6,7},{7,8},{8,9},{9,10},{10,1... | collective-permute-start | bytes 3145736 | tf_op jit(solution)/shard_map/ppermute | solution.py:388
  144.3 0.1 collective-permute-start.19
  144.4 2.2 %collective-permute-done.19.recv = f32[13,8,512]{2,1,0:T(8,128)S(1)} collective-permute-done((f32[13,8,512]{2,1,0:T(8,128)S(1)}, f32[13,8,512]{2,1,0:T(8,128)S(1)}, u32[]{:S(2)}, u32[]{:S(2)}) %collective-permute-start.19) | collective-permute-done | bytes 213024 | tf_op jit(solution)/shard_map/ppermute | solution.py:392
  146.6 2.0 %collective-permute-start.20 = (f32[13,8,512]{2,1,0:T(8,128)S(1)}, f32[13,8,512]{2,1,0:T(8,128)S(1)}, u32[]{:S(2)}, u32[]{:S(2)}) collective-permute-start(f32[13,8,512]{2,1,0:T(8,128)S(1)} %get-tuple-element.136.near_max), channel_id=1, source_target_pairs={{0,2},{2,0},{64,66},{66,64},{1,3},{3,1},{65,67},{67,65},{4,6},{6,4... | collective-permute-start | bytes 638984 | tf_op jit(solution)/shard_map/ppermute | solution.py:409
  148.6 1.9 %collective-permute-start.23 = (f32[2,6,8,512]{3,2,1,0:T(8,128)S(1)}, f32[2,6,8,512]{3,2,1,0:T(8,128)S(1)}, u32[]{:S(2)}, u32[]{:S(2)}) collective-permute-start(f32[2,6,8,512]{3,2,1,0:T(8,128)S(1)} %get-tuple-element.143.mine), channel_id=1, source_target_pairs={{0,64},{2,66},{64,0},{66,2},{1,65},{3,67},{65,1},{67,3},{4,68},{6,... | collective-permute-start | bytes 589832 | tf_op jit(solution)/shard_map/ppermute | solution.py:409
  150.5 15.3 %collective-permute-done.20.far_max.b = f32[13,8,512]{2,1,0:T(8,128)S(1)} collective-permute-done((f32[13,8,512]{2,1,0:T(8,128)S(1)}, f32[13,8,512]{2,1,0:T(8,128)S(1)}, u32[]{:S(2)}, u32[]{:S(2)}) %collective-permute-start.20) | collective-permute-done | bytes 213024 | tf_op jit(solution)/shard_map/ppermute | solution.py:409
  165.8 3.2 %object_update.1 = f32[2,512,1024]{2,1,0:T(8,128)} custom-call(s32[2]{0:T(128)S(1)} %pad_add_fusion.place, s32[2]{0:T(128)S(1)} %collective-permute-done.place.before, f32[13,8,512]{2,1,0:T(8,128)S(1)} %get-tuple-element.136.near_max, f32[13,8,512]{2,1,0:T(8,128)S(1)} %collective-permute-done.20.far_max.b, f32[2,512,1024]{2,1,0:T(8,128)S(1)} %copy-done.2, ...), custom_call_target="tpu_custom_call" | custom-call | tf_op jit(solution)/shard_map/object_update/pallas_call | solution.py:601
  169.0 1.6 mix.1
  (32 shorter events, 0.1 us)
Async XLA Ops:
  2.0 10.4 %copy-start = (bf16[2,6,512,512]{3,2,1,0:T(8,128)(2,1)S(1)}, bf16[2,6,512,512]{3,2,1,0:T(8,128)(2,1)}, u32[]{:S(2)}) copy-start(bf16[2,6,512,512]{3,2,1,0:T(8,128)(2,1)} %p_ref.9) | copy-start | bytes 18874372
  2.0 7.8 %collective-permute-start = (s32[2]{0:T(128)S(1)}, s32[2]{0:T(128)S(1)}, u32[]{:S(2)}, u32[]{:S(2)}) collective-permute-start(s32[2]{0:T(128)S(1)} %pad_add_fusion.place), channel_id=1, source_target_pairs={{0,1},{1,2},{2,3},{3,4},{4,5},{5,6},{6,7},{7,8},{8,9},{9,10},{10,1... | collective-permute-start | bytes 32 | tf_op jit(solution)/shard_map/ppermute | solution.py:388
  6.8 2.2 %copy-start.1 = (f32[2,512,1024]{2,1,0:T(8,128)S(1)}, f32[2,512,1024]{2,1,0:T(8,128)}, u32[]{:S(2)}) copy-start(f32[2,512,1024]{2,1,0:T(8,128)} %obj.3) | copy-start | bytes 12582916
  10.4 16.4 %collective-permute-start.1 = (f32[2,256,512]{2,1,0:T(8,128)S(1)}, f32[2,256,512]{2,1,0:T(8,128)S(1)}, u32[]{:S(2)}, u32[]{:S(2)}) collective-permute-start(f32[2,256,512]{2,1,0:T(8,128)S(1)} %rim_rows.1), channel_id=1, source_target_pairs={{1,0},{2,1},{3,2},{4,3},{5,4},{6,5},{7,6},{8,7},{9,8},{10,9},{11,1... | collective-permute-start | bytes 3145736 | tf_op jit(solution)/shard_map/ppermute | solution.py:388
  12.4 1.6 copy-start.3
  14.0 5.4 %copy-start.7 = (bf16[512,1024]{1,0:T(8,128)(2,1)S(1)}, bf16[512,1024]{1,0:T(8,128)(2,1)}, u32[]{:S(2)}) copy-start(bf16[512,1024]{1,0:T(8,128)(2,1)} %constant.14.clone.wt1.wt) | copy-start | bytes 3145732
  14.0 5.4 %copy-start.8 = (bf16[512,1024]{1,0:T(8,128)(2,1)S(1)}, bf16[512,1024]{1,0:T(8,128)(2,1)}, u32[]{:S(2)}) copy-start(bf16[512,1024]{1,0:T(8,128)(2,1)} %constant.13.clone.wt0.wt) | copy-start | bytes 3145732
  19.4 9.6 %copy-start.4 = (bf16[1024,1024]{1,0:T(8,128)(2,1)S(1)}, bf16[1024,1024]{1,0:T(8,128)(2,1)}, u32[]{:S(2)}) copy-start(bf16[1024,1024]{1,0:T(8,128)(2,1)} %constant.12.clone.table) | copy-start | bytes 6291460
  26.9 11.0 %collective-permute-start.2 = (f32[128,512]{1,0:T(8,128)S(1)}, f32[128,512]{1,0:T(8,128)S(1)}, u32[]{:S(2)}, u32[]{:S(2)}) collective-permute-start(f32[128,512]{1,0:T(8,128)S(1)} %get-tuple-element.85), channel_id=1, source_target_pairs={{0,64},{64,0},{1,65},{65,1},{2,66},{66,2},{3,67},{67,3},{4,68},{68... | collective-permute-start | bytes 786440 | tf_op jit(solution)/shard_map/ppermute | solution.py:392
  36.9 15.6 %collective-permute-start.3 = (f32[256,512]{1,0:T(8,128)S(1)}, f32[256,512]{1,0:T(8,128)S(1)}, u32[]{:S(2)}, u32[]{:S(2)}) collective-permute-start(f32[256,512]{1,0:T(8,128)S(1)} %get-tuple-element.87.s0), channel_id=1, source_target_pairs={{0,64},{64,0},{1,65},{65,1},{2,66},{66,2},{3,67},{67,3},{4,68},{68... | collective-permute-start | bytes 1572872 | tf_op jit(solution)/shard_map/ppermute | solution.py:392
  37.8 14.7 %copy-start.5 = (bf16[1024,1024]{1,0:T(8,128)(2,1)S(1)}, bf16[1024,1024]{1,0:T(8,128)(2,1)}, u32[]{:S(2)}) copy-start(bf16[1024,1024]{1,0:T(8,128)(2,1)} %constant.15.clone.table) | copy-start | bytes 6291460
  37.8 14.7 %copy-start.9 = (f32[1,512,512]{2,1,0:T(8,128)S(1)}, f32[1,512,512]{2,1,0:T(8,128)}, u32[]{:S(2)}) copy-start(f32[1,512,512]{2,1,0:T(8,128)} %pat.3) | copy-start | bytes 3145732
  40.5 19.4 %collective-permute-start.4 = (f32[256,512]{1,0:T(8,128)S(1)}, f32[256,512]{1,0:T(8,128)S(1)}, u32[]{:S(2)}, u32[]{:S(2)}) collective-permute-start(f32[256,512]{1,0:T(8,128)S(1)} %get-tuple-element.91.s0), channel_id=1, source_target_pairs={{0,64},{64,0},{1,65},{65,1},{2,66},{66,2},{3,67},{67,3},{4,68},{68... | collective-permute-start | bytes 1572872 | tf_op jit(solution)/shard_map/ppermute | solution.py:392
  52.5 7.4 %copy-start.10 = (bf16[512,1024]{1,0:T(8,128)(2,1)S(1)}, bf16[512,1024]{1,0:T(8,128)(2,1)}, u32[]{:S(2)}) copy-start(bf16[512,1024]{1,0:T(8,128)(2,1)} %constant.16.clone.bt) | copy-start | bytes 3145732
  60.0 10.9 %copy-start.6 = (bf16[512,1024]{1,0:T(8,128)(2,1)S(1)}, bf16[512,1024]{1,0:T(8,128)(2,1)}, u32[]{:S(2)}) copy-start(bf16[512,1024]{1,0:T(8,128)(2,1)} %constant.17.clone.bt) | copy-start | bytes 3145732
  70.8 5.7 %collective-permute-start.5 = (f32[6,16,16,512]{3,2,1,0:T(8,128)S(1)}, f32[6,16,16,512]{3,2,1,0:T(8,128)S(1)}, u32[]{:S(2)}, u32[]{:S(2)}) collective-permute-start(f32[6,16,16,512]{3,2,1,0:T(8,128)S(1)} %get-tuple-element.102), channel_id=1, source_target_pairs={{0,1},{1,0},{2,3},{3,2},{4,5},{5,4},{6,7},{7,6},{8,9},{9,8},{10,11... | collective-permute-start | bytes 9437192 | tf_op jit(solution)/shard_map/ppermute | solution.py:392
  80.3 16.4 %collective-permute-start.8 = (f32[6,16,16,512]{3,2,1,0:T(8,128)S(1)}, f32[6,16,16,512]{3,2,1,0:T(8,128)S(1)}, u32[]{:S(2)}, u32[]{:S(2)}) collective-permute-start(f32[6,16,16,512]{3,2,1,0:T(8,128)S(1)} %get-tuple-element.113), channel_id=1, source_target_pairs={{0,1},{1,0},{2,3},{3,2},{4,5},{5,4},{6,7},{7,6},{8,9},{9,8},{10,11... | collective-permute-start | bytes 9437192 | tf_op jit(solution)/shard_map/ppermute | solution.py:392
  80.5 13.2 %collective-permute-start.6 = (f32[3,4,16,512]{3,2,1,0:T(8,128)S(1)}, f32[3,4,16,512]{3,2,1,0:T(8,128)S(1)}, u32[]{:S(2)}, u32[]{:S(2)}) collective-permute-start(f32[3,4,16,512]{3,2,1,0:T(8,128)S(1)} %get-tuple-element.109), channel_id=1, source_target_pairs={{0,16},{1,5},{4,20},{5,9},{8,24},{9,13},{12,28},{13,1},{16,32},{17... | collective-permute-start | bytes 1179656 | tf_op jit(solution)/shard_map/ppermute | solution.py:404
  86.1 7.6 %collective-permute-start.7 = (f32[3,4,16,512]{3,2,1,0:T(8,128)S(1)}, f32[3,4,16,512]{3,2,1,0:T(8,128)S(1)}, u32[]{:S(2)}, u32[]{:S(2)}) collective-permute-start(f32[3,4,16,512]{3,2,1,0:T(8,128)S(1)} %get-tuple-element.110), channel_id=1, source_target_pairs={{0,48},{1,13},{4,52},{5,1},{8,56},{9,5},{12,60},{13,9},{16,0},{17,... | collective-permute-start | bytes 1179656 | tf_op jit(solution)/shard_map/ppermute | solution.py:404
  88.2 26.6 %collective-permute-start.11 = (f32[2,2,8,16,512]{4,3,2,1,0:T(8,128)S(1)}, f32[2,2,8,16,512]{4,3,2,1,0:T(8,128)S(1)}, u32[]{:S(2)}, u32[]{:S(2)}) collective-permute-start(f32[2,2,8,16,512]{4,3,2,1,0:T(8,128)S(1)} %get-tuple-element.116.g.b), channel_id=1, source_target_pairs={{0,64},{64,0},{1,65},{65,1},{2,66},{66,2},{3,67},{67,3},{4,68},{68... | collective-permute-start | bytes 3145736 | tf_op jit(solution)/shard_map/ppermute | solution.py:392
  93.8 21.0 %collective-permute-start.12 = (f32[2,3,4,16,512]{4,3,2,1,0:T(8,128)S(1)}, f32[2,3,4,16,512]{4,3,2,1,0:T(8,128)S(1)}, u32[]{:S(2)}, u32[]{:S(2)}) collective-permute-start(f32[2,3,4,16,512]{4,3,2,1,0:T(8,128)S(1)} %get-tuple-element.111), channel_id=1, source_target_pairs={{0,16},{1,5},{4,20},{5,9},{8,24},{9,13},{12,28},{13,1},{16,32},{17... | collective-permute-start | bytes 2359304 | tf_op jit(solution)/shard_map/ppermute | solution.py:404
  94.9 20.0 %collective-permute-start.13 = (f32[2,3,4,16,512]{4,3,2,1,0:T(8,128)S(1)}, f32[2,3,4,16,512]{4,3,2,1,0:T(8,128)S(1)}, u32[]{:S(2)}, u32[]{:S(2)}) collective-permute-start(f32[2,3,4,16,512]{4,3,2,1,0:T(8,128)S(1)} %get-tuple-element.118), channel_id=1, source_target_pairs={{0,48},{1,13},{4,52},{5,1},{8,56},{9,5},{12,60},{13,9},{16,0},{17,... | collective-permute-start | bytes 2359304 | tf_op jit(solution)/shard_map/ppermute | solution.py:404
  97.1 17.8 %collective-permute-start.9 = (f32[3,4,16,512]{3,2,1,0:T(8,128)S(1)}, f32[3,4,16,512]{3,2,1,0:T(8,128)S(1)}, u32[]{:S(2)}, u32[]{:S(2)}) collective-permute-start(f32[3,4,16,512]{3,2,1,0:T(8,128)S(1)} %get-tuple-element.114), channel_id=1, source_target_pairs={{0,16},{1,5},{4,20},{5,9},{8,24},{9,13},{12,28},{13,1},{16,32},{17... | collective-permute-start | bytes 1179656 | tf_op jit(solution)/shard_map/ppermute | solution.py:404
  97.2 17.7 %collective-permute-start.10 = (f32[3,4,16,512]{3,2,1,0:T(8,128)S(1)}, f32[3,4,16,512]{3,2,1,0:T(8,128)S(1)}, u32[]{:S(2)}, u32[]{:S(2)}) collective-permute-start(f32[3,4,16,512]{3,2,1,0:T(8,128)S(1)} %get-tuple-element.115), channel_id=1, source_target_pairs={{0,48},{1,13},{4,52},{5,1},{8,56},{9,5},{12,60},{13,9},{16,0},{17,... | collective-permute-start | bytes 1179656 | tf_op jit(solution)/shard_map/ppermute | solution.py:404
  115.0 12.4 %collective-permute-start.14 = (f32[2,3,4,16,512]{4,3,2,1,0:T(8,128)S(1)}, f32[2,3,4,16,512]{4,3,2,1,0:T(8,128)S(1)}, u32[]{:S(2)}, u32[]{:S(2)}) collective-permute-start(f32[2,3,4,16,512]{4,3,2,1,0:T(8,128)S(1)} %get-tuple-element.127), channel_id=1, source_target_pairs={{0,16},{1,5},{4,20},{5,9},{8,24},{9,13},{12,28},{13,1},{16,32},{17... | collective-permute-start | bytes 2359304 | tf_op jit(solution)/shard_map/ppermute | solution.py:404
  115.1 12.3 %collective-permute-start.15 = (f32[2,3,4,16,512]{4,3,2,1,0:T(8,128)S(1)}, f32[2,3,4,16,512]{4,3,2,1,0:T(8,128)S(1)}, u32[]{:S(2)}, u32[]{:S(2)}) collective-permute-start(f32[2,3,4,16,512]{4,3,2,1,0:T(8,128)S(1)} %get-tuple-element.128), channel_id=1, source_target_pairs={{0,48},{1,13},{4,52},{5,1},{8,56},{9,5},{12,60},{13,9},{16,0},{17,... | collective-permute-start | bytes 2359304 | tf_op jit(solution)/shard_map/ppermute | solution.py:404
  117.9 32.6 %collective-permute-start.22 = (f32[2,2,8,16,512]{4,3,2,1,0:T(8,128)S(1)}, f32[2,2,8,16,512]{4,3,2,1,0:T(8,128)S(1)}, u32[]{:S(2)}, u32[]{:S(2)}) collective-permute-start(f32[2,2,8,16,512]{4,3,2,1,0:T(8,128)S(1)} %get-tuple-element.139.t), channel_id=1, source_target_pairs={{0,64},{64,0},{1,65},{65,1},{2,66},{66,2},{3,67},{67,3},{4,68},{68... | collective-permute-start | bytes 3145736 | tf_op jit(solution)/shard_map/ppermute | solution.py:392
  127.8 8.2 %collective-permute-start.16 = (f32[2,2,3,16,512]{4,3,2,1,0:T(8,128)S(1)}, f32[2,2,3,16,512]{4,3,2,1,0:T(8,128)S(1)}, u32[]{:S(2)}, u32[]{:S(2)}) collective-permute-start(f32[2,2,3,16,512]{4,3,2,1,0:T(8,128)S(1)} %get-tuple-element.130), channel_id=1, source_target_pairs={{0,4},{1,17},{4,8},{5,21},{8,12},{9,25},{12,0},{13,29},{16,20},{17... | collective-permute-start | bytes 1179656 | tf_op jit(solution)/shard_map/ppermute | solution.py:404
  127.9 11.6 %collective-permute-start.17 = (f32[2,2,3,16,512]{4,3,2,1,0:T(8,128)S(1)}, f32[2,2,3,16,512]{4,3,2,1,0:T(8,128)S(1)}, u32[]{:S(2)}, u32[]{:S(2)}) collective-permute-start(f32[2,2,3,16,512]{4,3,2,1,0:T(8,128)S(1)} %get-tuple-element.131), channel_id=1, source_target_pairs={{0,12},{1,49},{4,0},{5,53},{8,4},{9,57},{12,8},{13,61},{16,28},{17... | collective-permute-start | bytes 1179656 | tf_op jit(solution)/shard_map/ppermute | solution.py:404
  130.5 9.7 %collective-permute-start.18 = (f32[2,2,3,16,512]{4,3,2,1,0:T(8,128)S(1)}, f32[2,2,3,16,512]{4,3,2,1,0:T(8,128)S(1)}, u32[]{:S(2)}, u32[]{:S(2)}) collective-permute-start(f32[2,2,3,16,512]{4,3,2,1,0:T(8,128)S(1)} %get-tuple-element.132), channel_id=1, source_target_pairs={{0,8},{1,33},{4,12},{5,37},{8,0},{9,41},{12,4},{13,45},{16,24},{17... | collective-permute-start | bytes 1179656 | tf_op jit(solution)/shard_map/ppermute | solution.py:404
  140.3 25.5 %collective-permute-start.21 = (f32[2,2,8,16,512]{4,3,2,1,0:T(8,128)S(1)}, f32[2,2,8,16,512]{4,3,2,1,0:T(8,128)S(1)}, u32[]{:S(2)}, u32[]{:S(2)}) collective-permute-start(f32[2,2,8,16,512]{4,3,2,1,0:T(8,128)S(1)} %over_sum.1), channel_id=1, source_target_pairs={{0,1},{1,2},{2,3},{3,4},{4,5},{5,6},{6,7},{7,8},{8,9},{9,10},{10,1... | collective-permute-start | bytes 3145736 | tf_op jit(solution)/shard_map/ppermute | solution.py:388
  144.3 2.3 %collective-permute-start.19 = (f32[13,8,512]{2,1,0:T(8,128)S(1)}, f32[13,8,512]{2,1,0:T(8,128)S(1)}, u32[]{:S(2)}, u32[]{:S(2)}) collective-permute-start(f32[13,8,512]{2,1,0:T(8,128)S(1)} %get-tuple-element.134), channel_id=1, source_target_pairs={{0,1},{1,0},{2,3},{3,2},{4,5},{5,4},{6,7},{7,6},{8,9},{9,8},{10,11... | collective-permute-start | bytes 638984 | tf_op jit(solution)/shard_map/ppermute | solution.py:392
  146.6 19.2 %copy-start.2 = (f32[2,512,1024]{2,1,0:T(8,128)S(1)}, f32[2,512,1024]{2,1,0:T(8,128)}, u32[]{:S(2)}) copy-start(f32[2,512,1024]{2,1,0:T(8,128)} %obj.3) | copy-start | bytes 12582916
  146.6 19.2 %collective-permute-start.20 = (f32[13,8,512]{2,1,0:T(8,128)S(1)}, f32[13,8,512]{2,1,0:T(8,128)S(1)}, u32[]{:S(2)}, u32[]{:S(2)}) collective-permute-start(f32[13,8,512]{2,1,0:T(8,128)S(1)} %get-tuple-element.136.near_max), channel_id=1, source_target_pairs={{0,2},{2,0},{64,66},{66,64},{1,3},{3,1},{65,67},{67,65},{4,6},{6,4... | collective-permute-start | bytes 638984 | tf_op jit(solution)/shard_map/ppermute | solution.py:409
  148.6 20.3 %collective-permute-start.24 = (f32[13,8,512]{2,1,0:T(8,128)S(1)}, f32[13,8,512]{2,1,0:T(8,128)S(1)}, u32[]{:S(2)}, u32[]{:S(2)}) collective-permute-start(f32[13,8,512]{2,1,0:T(8,128)S(1)} %get-tuple-element.136.near_max), channel_id=1, source_target_pairs={{0,66},{2,64},{64,2},{66,0},{1,67},{3,65},{65,3},{67,1},{4,70},{6,... | collective-permute-start | bytes 638984 | tf_op jit(solution)/shard_map/ppermute | solution.py:409
  148.6 20.3 %copy-start.11 = (s32[12,12]{1,0:T(8,128)S(1)}, s32[12,12]{1,0:T(8,128)}, u32[]{:S(2)}) copy-start(s32[12,12]{1,0:T(8,128)} %w_ref.1) | copy-start | bytes 1732
  148.6 20.3 %collective-permute-start.23 = (f32[2,6,8,512]{3,2,1,0:T(8,128)S(1)}, f32[2,6,8,512]{3,2,1,0:T(8,128)S(1)}, u32[]{:S(2)}, u32[]{:S(2)}) collective-permute-start(f32[2,6,8,512]{3,2,1,0:T(8,128)S(1)} %get-tuple-element.143.mine), channel_id=1, source_target_pairs={{0,64},{2,66},{64,0},{66,2},{1,65},{3,67},{65,1},{67,3},{4,68},{6,... | collective-permute-start | bytes 589832 | tf_op jit(solution)/shard_map/ppermute | solution.py:409

commit v10 on v8

--- a/solution.py
+++ b/solution.py
@@ -663,15 +663,17 @@
     ra1, rb1, bots_far, *plane0 = tied(ra1, rb1, bots_far, *plane0)
     near1, back1 = relay_add(near1, back1, ra1, rb1)
     plane1 = (own1, turned(near1, 1, True), turned(back1, -1, True))
-    tops_far = swapped(tops, "mode")
     over = along(over_sum(bots, bots_far), 1)
+    *plane1, over = tied(*plane1, over)
+    tops_next, _ = tied(tops, over)
+    tops_far = swapped(tops_next, "mode")
     line = plane_add((plane0, plane1))
     line = [line[0]] + [turned(line[r], r, False) for r in (1, 3, 2)]
     keep, send = line_add(most, line)
     recv = swapped(send, "core")
     mine, other = pixel_step(most, keep, recv, rows)
     beside = across(other, 0, 1)
-    beside, over, tops_far = tied(beside, over, tops_far)
+    beside, tops_far = tied(beside, tops_far)
     probe_new = mix(mixing, mine, beside, across(mine, 1, 0), across(other, 1, 1))
     object_new = object_update(place, before, other, beside, object_field, (tops, tops_far, bots, bots_far), over)
     return object_new, probe_new

time: 169 us -> 181 us (1.071)
  waiting for transfers between devices: 58.8 us -> 83.5 us
  starting transfers between devices: 53.4 us -> 39.8 us
    ppermute x11, waiting for transfers between devices: 19.4 us -> 33.1 us  [turned(): return lax.ppermute(value, RING, pairs)]
    ppermute x8, starting transfers between devices: 20.6 us -> 8.83 us  [swapped(): return lax.ppermute(value, axis, [(0, 1), (1, 0)])]
    ppermute x3, waiting for transfers between devices: 5.68 us -> 16.3 us  [across(): return lax.ppermute(value, ('mode', 'x'), pairs)]
  transfers between devices with their start and end apart: 25 -> 25, of which waited for: 14 -> 13; matrix products, arithmetic and copies ran while one was open for 0% -> 0% of each run, Pallas kernels for 20% -> 19%
where the time goes in v10:
time: 181 us; the launch traced here: 180 us
  waiting for transfers between devices  83.5 us (46%)
  Pallas kernels  50.6 us (28%)
  starting transfers between devices  39.8 us (22%)
  local copies, waits for them, and re-layouts  3.81 us (2%)
  between operations  2.21 us (1%)
    pallas_call x20, Pallas kernels, call(): pl.pallas_call(body, in_specs=ins, out_specs=[LOCAL] * len(outs), out_sha...  47.6 us
    ppermute x11, waiting for transfers between devices, turned(): return lax.ppermute(value, RING, pairs)  33.1 us
    ppermute x8, waiting for transfers between devices, swapped(): return lax.ppermute(value, axis, [(0, 1), (1, 0)])  31 us
    ppermute x11, starting transfers between devices, turned(): return lax.ppermute(value, RING, pairs)  19 us
    ppermute x3, waiting for transfers between devices, across(): return lax.ppermute(value, ('mode', 'x'), pairs)  16.3 us
    ppermute x8, starting transfers between devices, swapped(): return lax.ppermute(value, axis, [(0, 1), (1, 0)])  8.83 us
    ppermute x3, starting transfers between devices, along(): return lax.ppermute(value, SCAN, [(i, i + steps) for i in range(lo, hi)])  8.68 us
    unnamed x24, local copies, waits for them, and re-layouts  3.81 us
  transfers between devices with their start and end apart: 25, of which 13 were waited for; matrix products, arithmetic and copies ran while one was open for 0% of the time, Pallas kernels for 19%

profile of v10, /device:TPU:1, one launch (start us, length us, event | category | flops | bytes accessed | tf_op | source)
XLA Modules:
  0.0 180.0 jit_solution(6954557845116380981)
XLA Ops:
  1.9 0.1 pad_add_fusion.place
  2.0 4.8 %collective-permute-start = (s32[2]{0:T(128)S(1)}, s32[2]{0:T(128)S(1)}, u32[]{:S(2)}, u32[]{:S(2)}) collective-permute-start(s32[2]{0:T(128)S(1)} %pad_add_fusion.place), channel_id=1, source_target_pairs={{0,1},{1,2},{2,3},{3,4},{4,5},{5,6},{6,7},{7,8},{8,9},{9,10},{10,1... | collective-permute-start | bytes 32 | tf_op jit(solution)/shard_map/ppermute | solution.py:388
  6.8 0.0 copy-start.1
  6.8 2.2 %copy-done.1 = f32[2,512,1024]{2,1,0:T(8,128)S(1)} copy-done((f32[2,512,1024]{2,1,0:T(8,128)S(1)}, f32[2,512,1024]{2,1,0:T(8,128)}, u32[]{:S(2)}) %copy-start.1) | copy-done | bytes 4194328
  9.0 0.8 own_rows.1
  9.8 0.6 rim_rows.1
  10.4 1.9 %collective-permute-start.1 = (f32[2,256,512]{2,1,0:T(8,128)S(1)}, f32[2,256,512]{2,1,0:T(8,128)S(1)}, u32[]{:S(2)}, u32[]{:S(2)}) collective-permute-start(f32[2,256,512]{2,1,0:T(8,128)S(1)} %rim_rows.1), channel_id=1, source_target_pairs={{1,0},{2,1},{3,2},{4,3},{5,4},{6,5},{7,6},{8,7},{9,8},{10,9},{11,1... | collective-permute-start | bytes 3145736 | tf_op jit(solution)/shard_map/ppermute | solution.py:388
  12.4 0.0 copy-start.3
  12.4 1.6 copy-done.3
  14.0 5.4 %top_half.1 = (bf16[6,512,512]{2,1,0:T(8,128)(2,1)S(1)}, f32[128,512]{1,0:T(8,128)S(1)}, f32[128,512]{1,0:T(8,128)S(1)}, f32[2,6,8,512]{3,2,1,0:T(8,128)S(1)}) custom-call(f32[2,256,512]{2,1,0:T(8,128)S(1)} %get-tuple-element.78.patch_ref.ptop, bf16[2,6,512,512]{3,2,1,0:T(8,128)(2,1)S(1)} %copy-done, bf16[1024,1024]{1,0:T(8,128)(2,1)S(1)} %copy-done.3), custom_call_target="tpu_custom_call" | custom-call | tf_op jit(solution)/shard_map/top_half/pallas_call | solution.py:58
  19.4 0.0 copy-start.4
  19.4 4.3 %first_terms.1 = (f32[6,512,512]{2,1,0:T(8,128)S(1)}, f32[6,512,512]{2,1,0:T(8,128)S(1)}) custom-call(bf16[512,1024]{1,0:T(8,128)(2,1)S(1)} %copy-done.8, bf16[512,1024]{1,0:T(8,128)(2,1)S(1)} %copy-done.7, bf16[6,512,512]{2,1,0:T(8,128)(2,1)S(1)} %get-tuple-element.82.top), custom_call_target="tpu_custom_call" | custom-call | tf_op jit(solution)/shard_map/first_terms/pallas_call | solution.py:58
  23.8 3.1 %collective-permute-done.1.rim = f32[2,256,512]{2,1,0:T(8,128)S(1)} collective-permute-done((f32[2,256,512]{2,1,0:T(8,128)S(1)}, f32[2,256,512]{2,1,0:T(8,128)S(1)}, u32[]{:S(2)}, u32[]{:S(2)}) %collective-permute-start.1) | collective-permute-done | bytes 1048608 | tf_op jit(solution)/shard_map/ppermute | solution.py:388
  26.9 2.2 %collective-permute-start.2 = (f32[128,512]{1,0:T(8,128)S(1)}, f32[128,512]{1,0:T(8,128)S(1)}, u32[]{:S(2)}, u32[]{:S(2)}) collective-permute-start(f32[128,512]{1,0:T(8,128)S(1)} %get-tuple-element.88), channel_id=1, source_target_pairs={{0,64},{64,0},{1,65},{65,1},{2,66},{66,2},{3,67},{67,3},{4,68},{68... | collective-permute-start | bytes 786440 | tf_op jit(solution)/shard_map/ppermute | solution.py:392
  29.0 7.9 %bottom_half.1 = (bf16[6,512,512]{2,1,0:T(8,128)(2,1)S(1)}, f32[2,256,512]{2,1,0:T(8,128)S(1)}, f32[6,512,512]{2,1,0:T(8,128)S(1)}, f32[256,512]{1,0:T(8,128)S(1)}) custom-call(s32[2]{0:T(128)S(1)} %pad_add_fusion.place, f32[2,256,512]{2,1,0:T(8,128)S(1)} %get-tuple-element.80.own, ...), custom_call_target="tpu_custom_call", output_to_operand_aliasing={{2}: (6, {})} | custom-call | tf_op jit(solution)/shard_map/bottom_half/pallas_call | solution.py:58
  36.9 0.9 collective-permute-start.3
  37.8 2.7 %low_wave.1 = (f32[6,512,512]{2,1,0:T(8,128)S(1)}, f32[256,512]{1,0:T(8,128)S(1)}) custom-call(bf16[512,1024]{1,0:T(8,128)(2,1)S(1)} %copy-done.7, bf16[6,512,512]{2,1,0:T(8,128)(2,1)S(1)} %get-tuple-element.92.bot, f32[6,512,512]{2,1,0:T(8,128)S(1)} %get-tuple-element.93._), custom_call_target="tpu_custom_call", output_to_operand_aliasing={{0}: (2, {})} | custom-call | tf_op jit(solution)/shard_map/low_wave/pallas_call | solution.py:58
  40.5 2.2 %collective-permute-start.4 = (f32[256,512]{1,0:T(8,128)S(1)}, f32[256,512]{1,0:T(8,128)S(1)}, u32[]{:S(2)}, u32[]{:S(2)}) collective-permute-start(f32[256,512]{1,0:T(8,128)S(1)} %get-tuple-element.94.s0), channel_id=1, source_target_pairs={{0,64},{64,0},{1,65},{65,1},{2,66},{66,2},{3,67},{67,3},{4,68},{68... | collective-permute-start | bytes 1572872 | tf_op jit(solution)/shard_map/ppermute | solution.py:392
  42.8 9.7 %collective-permute-done.3.s1 = f32[256,512]{1,0:T(8,128)S(1)} collective-permute-done((f32[256,512]{1,0:T(8,128)S(1)}, f32[256,512]{1,0:T(8,128)S(1)}, u32[]{:S(2)}, u32[]{:S(2)}) %collective-permute-start.3) | collective-permute-done | bytes 524320 | tf_op jit(solution)/shard_map/ppermute | solution.py:392
  52.5 4.9 %fixed_top.1.top = bf16[6,512,512]{2,1,0:T(8,128)(2,1)S(1)} custom-call(f32[1,512,512]{2,1,0:T(8,128)S(1)} %copy-done.9, f32[256,512]{1,0:T(8,128)S(1)} %get-tuple-element.90.s0, f32[256,512]{1,0:T(8,128)S(1)} %collective-permute-done.3.s1, f32[6,512,512]{2,1,0:T(8,128)S(1)} %get-tuple-element.91.wave_ref, bf16[1024,1024]{1,0:T(8,128)(2,1)S(1)} %copy-done.5), custom_call_target="tpu_custom_call" | custom-call | tf_op jit(solution)/shard_map/fixed_top/pallas_call | solution.py:58
  57.4 2.6 %collective-permute-done.4.s1 = f32[256,512]{1,0:T(8,128)S(1)} collective-permute-done((f32[256,512]{1,0:T(8,128)S(1)}, f32[256,512]{1,0:T(8,128)S(1)}, u32[]{:S(2)}, u32[]{:S(2)}) %collective-permute-start.4) | collective-permute-done | bytes 524320 | tf_op jit(solution)/shard_map/ppermute | solution.py:392
  60.0 10.8 %first_block.1 = (bf16[6,512,512]{2,1,0:T(8,128)(2,1)S(1)}, f32[6,16,16,512]{3,2,1,0:T(8,128)S(1)}, f32[6,16,16,512]{3,2,1,0:T(8,128)S(1)}, f32[2,2,8,16,512]{4,3,2,1,0:T(8,128)S(1)}, f32[2,2,8,16,512]{4,3,2,1,0:T(8,128)S(1)}) custom-call(f32[1,512,512]{2,1,0:T(8,128)S(1)} %copy-done.9, f32[256,512]{1,0:T(8,128)S(1)} %get-tuple-element.94.s0, ...), custom_call_target="tpu_custom_call" | custom-call | tf_op jit(solution)/shard_map/first_block/pallas_call | solution.py:58
  70.8 0.1 collective-permute-start.5
  70.9 3.4 %second_block.2 = (f32[6,16,16,512]{3,2,1,0:T(8,128)S(1)}, f32[6,16,16,512]{3,2,1,0:T(8,128)S(1)}, f32[2,2,8,16,512]{4,3,2,1,0:T(8,128)S(1)}, f32[2,2,8,16,512]{4,3,2,1,0:T(8,128)S(1)}) custom-call(bf16[512,1024]{1,0:T(8,128)(2,1)S(1)} %copy-done.6, bf16[6,512,512]{2,1,0:T(8,128)(2,1)S(1)} %fixed_top.1.top, ...), custom_call_target="tpu_custom_call", output_to_operand_aliasing={{2}: (6, {}), {3}: (7, {})} | custom-call | tf_op jit(solution)/shard_map/second_block/pallas_call | solution.py:58
  74.4 2.2 %collective-permute-done.5.recv = f32[6,16,16,512]{3,2,1,0:T(8,128)S(1)} collective-permute-done((f32[6,16,16,512]{3,2,1,0:T(8,128)S(1)}, f32[6,16,16,512]{3,2,1,0:T(8,128)S(1)}, u32[]{:S(2)}, u32[]{:S(2)}) %collective-permute-start.5) | collective-permute-done | bytes 3145760 | tf_op jit(solution)/shard_map/ppermute | solution.py:392
  76.6 0.3 core_add.2
  76.9 3.4 %second_block.3 = (f32[6,16,16,512]{3,2,1,0:T(8,128)S(1)}, f32[6,16,16,512]{3,2,1,0:T(8,128)S(1)}, f32[2,2,8,16,512]{4,3,2,1,0:T(8,128)S(1)}, f32[2,2,8,16,512]{4,3,2,1,0:T(8,128)S(1)}) custom-call(bf16[512,1024]{1,0:T(8,128)(2,1)S(1)} %copy-done.6, ...), custom_call_target="tpu_custom_call", output_to_operand_aliasing={{2}: (6, {}), {3}: (7, {}), {0}: (8, {}), {1}: (9, {})} | custom-call | tf_op jit(solution)/shard_map/second_block/pallas_call | solution.py:58
  80.3 0.2 collective-permute-start.8
  80.5 5.7 %collective-permute-start.6 = (f32[3,4,16,512]{3,2,1,0:T(8,128)S(1)}, f32[3,4,16,512]{3,2,1,0:T(8,128)S(1)}, u32[]{:S(2)}, u32[]{:S(2)}) collective-permute-start(f32[3,4,16,512]{3,2,1,0:T(8,128)S(1)} %get-tuple-element.112), channel_id=1, source_target_pairs={{0,16},{1,5},{4,20},{5,9},{8,24},{9,13},{12,28},{13,1},{16,32},{17... | collective-permute-start | bytes 1179656 | tf_op jit(solution)/shard_map/ppermute | solution.py:404
  86.1 2.1 %collective-permute-start.7 = (f32[3,4,16,512]{3,2,1,0:T(8,128)S(1)}, f32[3,4,16,512]{3,2,1,0:T(8,128)S(1)}, u32[]{:S(2)}, u32[]{:S(2)}) collective-permute-start(f32[3,4,16,512]{3,2,1,0:T(8,128)S(1)} %get-tuple-element.113), channel_id=1, source_target_pairs={{0,48},{1,13},{4,52},{5,1},{8,56},{9,5},{12,60},{13,9},{16,0},{17,... | collective-permute-start | bytes 1179656 | tf_op jit(solution)/shard_map/ppermute | solution.py:404
  88.2 0.5 collective-permute-start.11
  88.8 4.9 %collective-permute-done.6.ra = f32[3,4,16,512]{3,2,1,0:T(8,128)S(1)} collective-permute-done((f32[3,4,16,512]{3,2,1,0:T(8,128)S(1)}, f32[3,4,16,512]{3,2,1,0:T(8,128)S(1)}, u32[]{:S(2)}, u32[]{:S(2)}) %collective-permute-start.6) | collective-permute-done | bytes 393248 | tf_op jit(solution)/shard_map/ppermute | solution.py:404
  93.7 0.1 relay_add.2
  93.8 1.0 collective-permute-start.12
  94.9 1.8 collective-permute-start.13
  96.7 0.4 core_add.3
  97.1 0.1 collective-permute-start.9
  97.2 2.7 %collective-permute-start.10 = (f32[3,4,16,512]{3,2,1,0:T(8,128)S(1)}, f32[3,4,16,512]{3,2,1,0:T(8,128)S(1)}, u32[]{:S(2)}, u32[]{:S(2)}) collective-permute-start(f32[3,4,16,512]{3,2,1,0:T(8,128)S(1)} %get-tuple-element.118), channel_id=1, source_target_pairs={{0,48},{1,13},{4,52},{5,1},{8,56},{9,5},{12,60},{13,9},{16,0},{17,... | collective-permute-start | bytes 1179656 | tf_op jit(solution)/shard_map/ppermute | solution.py:404
  99.8 15.0 %collective-permute-done.11.gf.bf = f32[2,2,8,16,512]{4,3,2,1,0:T(8,128)S(1)} collective-permute-done((f32[2,2,8,16,512]{4,3,2,1,0:T(8,128)S(1)}, f32[2,2,8,16,512]{4,3,2,1,0:T(8,128)S(1)}, u32[]{:S(2)}, u32[]{:S(2)}) %collective-permute-start.11) | collective-permute-done | bytes 1048608 | tf_op jit(solution)/shard_map/ppermute | solution.py:392
  114.9 0.1 over_sum.1
  115.0 2.0 %collective-permute-start.16 = (f32[2,2,8,16,512]{4,3,2,1,0:T(8,128)S(1)}, f32[2,2,8,16,512]{4,3,2,1,0:T(8,128)S(1)}, u32[]{:S(2)}, u32[]{:S(2)}) collective-permute-start(f32[2,2,8,16,512]{4,3,2,1,0:T(8,128)S(1)} %over_sum.1), channel_id=1, source_target_pairs={{0,1},{1,2},{2,3},{3,4},{4,5},{5,6},{6,7},{7,8},{8,9},{9,10},{10,1... | collective-permute-start | bytes 3145736 | tf_op jit(solution)/shard_map/ppermute | solution.py:388
  117.0 0.1 relay_add.3
  117.2 0.1 collective-permute-start.14
  117.3 2.7 %collective-permute-start.15 = (f32[2,3,4,16,512]{4,3,2,1,0:T(8,128)S(1)}, f32[2,3,4,16,512]{4,3,2,1,0:T(8,128)S(1)}, u32[]{:S(2)}, u32[]{:S(2)}) collective-permute-start(f32[2,3,4,16,512]{4,3,2,1,0:T(8,128)S(1)} %get-tuple-element.131), channel_id=1, source_target_pairs={{0,48},{1,13},{4,52},{5,1},{8,56},{9,5},{12,60},{13,9},{16,0},{17,... | collective-permute-start | bytes 2359304 | tf_op jit(solution)/shard_map/ppermute | solution.py:404
  119.9 21.4 %collective-permute-done.14.refs_4_ = f32[2,3,4,16,512]{4,3,2,1,0:T(8,128)S(1)} collective-permute-done((f32[2,3,4,16,512]{4,3,2,1,0:T(8,128)S(1)}, f32[2,3,4,16,512]{4,3,2,1,0:T(8,128)S(1)}, u32[]{:S(2)}, u32[]{:S(2)}) %collective-permute-start.14) | collective-permute-done | bytes 786464 | tf_op jit(solution)/shard_map/ppermute | solution.py:404
  141.3 0.3 plane_add.1
  141.6 0.1 collective-permute-start.17
  141.7 2.7 %collective-permute-start.18 = (f32[2,2,3,16,512]{4,3,2,1,0:T(8,128)S(1)}, f32[2,2,3,16,512]{4,3,2,1,0:T(8,128)S(1)}, u32[]{:S(2)}, u32[]{:S(2)}) collective-permute-start(f32[2,2,3,16,512]{4,3,2,1,0:T(8,128)S(1)} %get-tuple-element.138), channel_id=1, source_target_pairs={{0,12},{1,49},{4,0},{5,53},{8,4},{9,57},{12,8},{13,61},{16,28},{17... | collective-permute-start | bytes 1179656 | tf_op jit(solution)/shard_map/ppermute | solution.py:404
  144.4 0.2 collective-permute-start.19
  144.5 0.1 brightest.1.most
  144.6 2.6 %collective-permute-start.22 = (f32[2,2,8,16,512]{4,3,2,1,0:T(8,128)S(1)}, f32[2,2,8,16,512]{4,3,2,1,0:T(8,128)S(1)}, u32[]{:S(2)}, u32[]{:S(2)}) collective-permute-start(f32[2,2,8,16,512]{4,3,2,1,0:T(8,128)S(1)} %get-tuple-element.146.t), channel_id=1, source_target_pairs={{0,64},{64,0},{1,65},{65,1},{2,66},{66,2},{3,67},{67,3},{4,68},{68... | collective-permute-start | bytes 3145736 | tf_op jit(solution)/shard_map/ppermute | solution.py:392
  147.3 2.5 %collective-permute-done.17.b = f32[2,2,3,16,512]{4,3,2,1,0:T(8,128)S(1)} collective-permute-done((f32[2,2,3,16,512]{4,3,2,1,0:T(8,128)S(1)}, f32[2,2,3,16,512]{4,3,2,1,0:T(8,128)S(1)}, u32[]{:S(2)}, u32[]{:S(2)}) %collective-permute-start.17) | collective-permute-done | bytes 393248 | tf_op jit(solution)/shard_map/ppermute | solution.py:404
  149.8 3.5 %collective-permute-done.18.c = f32[2,2,3,16,512]{4,3,2,1,0:T(8,128)S(1)} collective-permute-done((f32[2,2,3,16,512]{4,3,2,1,0:T(8,128)S(1)}, f32[2,2,3,16,512]{4,3,2,1,0:T(8,128)S(1)}, u32[]{:S(2)}, u32[]{:S(2)}) %collective-permute-start.18) | collective-permute-done | bytes 393248 | tf_op jit(solution)/shard_map/ppermute | solution.py:404
  153.3 0.7 collective-permute-done.19.d
  154.0 0.1 line_add.1
  154.1 0.1 collective-permute-start.20
  154.2 1.5 collective-permute-done.20.recv
  155.7 0.1 collective-permute-start.21
  155.8 2.2 %collective-permute-start.24 = (f32[13,8,512]{2,1,0:T(8,128)S(1)}, f32[13,8,512]{2,1,0:T(8,128)S(1)}, u32[]{:S(2)}, u32[]{:S(2)}) collective-permute-start(f32[13,8,512]{2,1,0:T(8,128)S(1)} %get-tuple-element.143.near_max), channel_id=1, source_target_pairs={{0,66},{2,64},{64,2},{66,0},{1,67},{3,65},{65,3},{67,1},{4,70},{6,... | collective-permute-start | bytes 638984 | tf_op jit(solution)/shard_map/ppermute | solution.py:409
  158.1 1.0 collective-permute-start.23
  159.1 14.3 %collective-permute-done.21.far_max.b = f32[13,8,512]{2,1,0:T(8,128)S(1)} collective-permute-done((f32[13,8,512]{2,1,0:T(8,128)S(1)}, f32[13,8,512]{2,1,0:T(8,128)S(1)}, u32[]{:S(2)}, u32[]{:S(2)}) %collective-permute-start.21) | collective-permute-done | bytes 213024 | tf_op jit(solution)/shard_map/ppermute | solution.py:409
  173.4 3.0 %object_update.1 = f32[2,512,1024]{2,1,0:T(8,128)} custom-call(s32[2]{0:T(128)S(1)} %pad_add_fusion.place, s32[2]{0:T(128)S(1)} %collective-permute-done.place.before, f32[13,8,512]{2,1,0:T(8,128)S(1)} %get-tuple-element.143.near_max, f32[13,8,512]{2,1,0:T(8,128)S(1)} %collective-permute-done.21.far_max.b, f32[2,512,1024]{2,1,0:T(8,128)S(1)} %copy-done.2, ...), custom_call_target="tpu_custom_call" | custom-call | tf_op jit(solution)/shard_map/object_update/pallas_call | solution.py:601
  176.4 2.0 %collective-permute-done.23.c = f32[2,6,8,512]{3,2,1,0:T(8,128)S(1)} collective-permute-done((f32[2,6,8,512]{3,2,1,0:T(8,128)S(1)}, f32[2,6,8,512]{3,2,1,0:T(8,128)S(1)}, u32[]{:S(2)}, u32[]{:S(2)}) %collective-permute-start.23) | collective-permute-done | bytes 196640 | tf_op jit(solution)/shard_map/ppermute | solution.py:409
  178.4 1.6 mix.1
  (32 shorter events, 0.1 us)
Async XLA Ops:
  2.0 10.4 %copy-start = (bf16[2,6,512,512]{3,2,1,0:T(8,128)(2,1)S(1)}, bf16[2,6,512,512]{3,2,1,0:T(8,128)(2,1)}, u32[]{:S(2)}) copy-start(bf16[2,6,512,512]{3,2,1,0:T(8,128)(2,1)} %p_ref.9) | copy-start | bytes 18874372
  2.0 7.8 %collective-permute-start = (s32[2]{0:T(128)S(1)}, s32[2]{0:T(128)S(1)}, u32[]{:S(2)}, u32[]{:S(2)}) collective-permute-start(s32[2]{0:T(128)S(1)} %pad_add_fusion.place), channel_id=1, source_target_pairs={{0,1},{1,2},{2,3},{3,4},{4,5},{5,6},{6,7},{7,8},{8,9},{9,10},{10,1... | collective-permute-start | bytes 32 | tf_op jit(solution)/shard_map/ppermute | solution.py:388
  6.8 2.2 %copy-start.1 = (f32[2,512,1024]{2,1,0:T(8,128)S(1)}, f32[2,512,1024]{2,1,0:T(8,128)}, u32[]{:S(2)}) copy-start(f32[2,512,1024]{2,1,0:T(8,128)} %obj.3) | copy-start | bytes 12582916
  10.4 16.4 %collective-permute-start.1 = (f32[2,256,512]{2,1,0:T(8,128)S(1)}, f32[2,256,512]{2,1,0:T(8,128)S(1)}, u32[]{:S(2)}, u32[]{:S(2)}) collective-permute-start(f32[2,256,512]{2,1,0:T(8,128)S(1)} %rim_rows.1), channel_id=1, source_target_pairs={{1,0},{2,1},{3,2},{4,3},{5,4},{6,5},{7,6},{8,7},{9,8},{10,9},{11,1... | collective-permute-start | bytes 3145736 | tf_op jit(solution)/shard_map/ppermute | solution.py:388
  12.4 1.6 copy-start.3
  14.0 5.4 %copy-start.7 = (bf16[512,1024]{1,0:T(8,128)(2,1)S(1)}, bf16[512,1024]{1,0:T(8,128)(2,1)}, u32[]{:S(2)}) copy-start(bf16[512,1024]{1,0:T(8,128)(2,1)} %constant.14.clone.wt1.wt) | copy-start | bytes 3145732
  14.0 5.4 %copy-start.8 = (bf16[512,1024]{1,0:T(8,128)(2,1)S(1)}, bf16[512,1024]{1,0:T(8,128)(2,1)}, u32[]{:S(2)}) copy-start(bf16[512,1024]{1,0:T(8,128)(2,1)} %constant.13.clone.wt0.wt) | copy-start | bytes 3145732
  19.4 9.6 %copy-start.4 = (bf16[1024,1024]{1,0:T(8,128)(2,1)S(1)}, bf16[1024,1024]{1,0:T(8,128)(2,1)}, u32[]{:S(2)}) copy-start(bf16[1024,1024]{1,0:T(8,128)(2,1)} %constant.12.clone.table) | copy-start | bytes 6291460
  26.9 11.0 %collective-permute-start.2 = (f32[128,512]{1,0:T(8,128)S(1)}, f32[128,512]{1,0:T(8,128)S(1)}, u32[]{:S(2)}, u32[]{:S(2)}) collective-permute-start(f32[128,512]{1,0:T(8,128)S(1)} %get-tuple-element.88), channel_id=1, source_target_pairs={{0,64},{64,0},{1,65},{65,1},{2,66},{66,2},{3,67},{67,3},{4,68},{68... | collective-permute-start | bytes 786440 | tf_op jit(solution)/shard_map/ppermute | solution.py:392
  36.9 15.6 %collective-permute-start.3 = (f32[256,512]{1,0:T(8,128)S(1)}, f32[256,512]{1,0:T(8,128)S(1)}, u32[]{:S(2)}, u32[]{:S(2)}) collective-permute-start(f32[256,512]{1,0:T(8,128)S(1)} %get-tuple-element.90.s0), channel_id=1, source_target_pairs={{0,64},{64,0},{1,65},{65,1},{2,66},{66,2},{3,67},{67,3},{4,68},{68... | collective-permute-start | bytes 1572872 | tf_op jit(solution)/shard_map/ppermute | solution.py:392
  37.8 14.7 %copy-start.5 = (bf16[1024,1024]{1,0:T(8,128)(2,1)S(1)}, bf16[1024,1024]{1,0:T(8,128)(2,1)}, u32[]{:S(2)}) copy-start(bf16[1024,1024]{1,0:T(8,128)(2,1)} %constant.15.clone.table) | copy-start | bytes 6291460
  37.8 14.7 %copy-start.9 = (f32[1,512,512]{2,1,0:T(8,128)S(1)}, f32[1,512,512]{2,1,0:T(8,128)}, u32[]{:S(2)}) copy-start(f32[1,512,512]{2,1,0:T(8,128)} %pat.3) | copy-start | bytes 3145732
  40.5 19.4 %collective-permute-start.4 = (f32[256,512]{1,0:T(8,128)S(1)}, f32[256,512]{1,0:T(8,128)S(1)}, u32[]{:S(2)}, u32[]{:S(2)}) collective-permute-start(f32[256,512]{1,0:T(8,128)S(1)} %get-tuple-element.94.s0), channel_id=1, source_target_pairs={{0,64},{64,0},{1,65},{65,1},{2,66},{66,2},{3,67},{67,3},{4,68},{68... | collective-permute-start | bytes 1572872 | tf_op jit(solution)/shard_map/ppermute | solution.py:392
  52.5 7.4 %copy-start.10 = (bf16[512,1024]{1,0:T(8,128)(2,1)S(1)}, bf16[512,1024]{1,0:T(8,128)(2,1)}, u32[]{:S(2)}) copy-start(bf16[512,1024]{1,0:T(8,128)(2,1)} %constant.16.clone.bt) | copy-start | bytes 3145732
  60.0 10.9 %copy-start.6 = (bf16[512,1024]{1,0:T(8,128)(2,1)S(1)}, bf16[512,1024]{1,0:T(8,128)(2,1)}, u32[]{:S(2)}) copy-start(bf16[512,1024]{1,0:T(8,128)(2,1)} %constant.17.clone.bt) | copy-start | bytes 3145732
  70.8 5.7 %collective-permute-start.5 = (f32[6,16,16,512]{3,2,1,0:T(8,128)S(1)}, f32[6,16,16,512]{3,2,1,0:T(8,128)S(1)}, u32[]{:S(2)}, u32[]{:S(2)}) collective-permute-start(f32[6,16,16,512]{3,2,1,0:T(8,128)S(1)} %get-tuple-element.105), channel_id=1, source_target_pairs={{0,1},{1,0},{2,3},{3,2},{4,5},{5,4},{6,7},{7,6},{8,9},{9,8},{10,11... | collective-permute-start | bytes 9437192 | tf_op jit(solution)/shard_map/ppermute | solution.py:392
  80.3 16.4 %collective-permute-start.8 = (f32[6,16,16,512]{3,2,1,0:T(8,128)S(1)}, f32[6,16,16,512]{3,2,1,0:T(8,128)S(1)}, u32[]{:S(2)}, u32[]{:S(2)}) collective-permute-start(f32[6,16,16,512]{3,2,1,0:T(8,128)S(1)} %get-tuple-element.116), channel_id=1, source_target_pairs={{0,1},{1,0},{2,3},{3,2},{4,5},{5,4},{6,7},{7,6},{8,9},{9,8},{10,11... | collective-permute-start | bytes 9437192 | tf_op jit(solution)/shard_map/ppermute | solution.py:392
  80.5 13.2 %collective-permute-start.6 = (f32[3,4,16,512]{3,2,1,0:T(8,128)S(1)}, f32[3,4,16,512]{3,2,1,0:T(8,128)S(1)}, u32[]{:S(2)}, u32[]{:S(2)}) collective-permute-start(f32[3,4,16,512]{3,2,1,0:T(8,128)S(1)} %get-tuple-element.112), channel_id=1, source_target_pairs={{0,16},{1,5},{4,20},{5,9},{8,24},{9,13},{12,28},{13,1},{16,32},{17... | collective-permute-start | bytes 1179656 | tf_op jit(solution)/shard_map/ppermute | solution.py:404
  86.1 7.6 %collective-permute-start.7 = (f32[3,4,16,512]{3,2,1,0:T(8,128)S(1)}, f32[3,4,16,512]{3,2,1,0:T(8,128)S(1)}, u32[]{:S(2)}, u32[]{:S(2)}) collective-permute-start(f32[3,4,16,512]{3,2,1,0:T(8,128)S(1)} %get-tuple-element.113), channel_id=1, source_target_pairs={{0,48},{1,13},{4,52},{5,1},{8,56},{9,5},{12,60},{13,9},{16,0},{17,... | collective-permute-start | bytes 1179656 | tf_op jit(solution)/shard_map/ppermute | solution.py:404
  88.2 26.6 %collective-permute-start.11 = (f32[2,2,8,16,512]{4,3,2,1,0:T(8,128)S(1)}, f32[2,2,8,16,512]{4,3,2,1,0:T(8,128)S(1)}, u32[]{:S(2)}, u32[]{:S(2)}) collective-permute-start(f32[2,2,8,16,512]{4,3,2,1,0:T(8,128)S(1)} %get-tuple-element.119.g.b), channel_id=1, source_target_pairs={{0,64},{64,0},{1,65},{65,1},{2,66},{66,2},{3,67},{67,3},{4,68},{68... | collective-permute-start | bytes 3145736 | tf_op jit(solution)/shard_map/ppermute | solution.py:392
  93.8 21.0 %collective-permute-start.12 = (f32[2,3,4,16,512]{4,3,2,1,0:T(8,128)S(1)}, f32[2,3,4,16,512]{4,3,2,1,0:T(8,128)S(1)}, u32[]{:S(2)}, u32[]{:S(2)}) collective-permute-start(f32[2,3,4,16,512]{4,3,2,1,0:T(8,128)S(1)} %get-tuple-element.114), channel_id=1, source_target_pairs={{0,16},{1,5},{4,20},{5,9},{8,24},{9,13},{12,28},{13,1},{16,32},{17... | collective-permute-start | bytes 2359304 | tf_op jit(solution)/shard_map/ppermute | solution.py:404
  94.9 20.0 %collective-permute-start.13 = (f32[2,3,4,16,512]{4,3,2,1,0:T(8,128)S(1)}, f32[2,3,4,16,512]{4,3,2,1,0:T(8,128)S(1)}, u32[]{:S(2)}, u32[]{:S(2)}) collective-permute-start(f32[2,3,4,16,512]{4,3,2,1,0:T(8,128)S(1)} %get-tuple-element.121), channel_id=1, source_target_pairs={{0,48},{1,13},{4,52},{5,1},{8,56},{9,5},{12,60},{13,9},{16,0},{17,... | collective-permute-start | bytes 2359304 | tf_op jit(solution)/shard_map/ppermute | solution.py:404
  97.1 17.8 %collective-permute-start.9 = (f32[3,4,16,512]{3,2,1,0:T(8,128)S(1)}, f32[3,4,16,512]{3,2,1,0:T(8,128)S(1)}, u32[]{:S(2)}, u32[]{:S(2)}) collective-permute-start(f32[3,4,16,512]{3,2,1,0:T(8,128)S(1)} %get-tuple-element.117), channel_id=1, source_target_pairs={{0,16},{1,5},{4,20},{5,9},{8,24},{9,13},{12,28},{13,1},{16,32},{17... | collective-permute-start | bytes 1179656 | tf_op jit(solution)/shard_map/ppermute | solution.py:404
  97.2 17.7 %collective-permute-start.10 = (f32[3,4,16,512]{3,2,1,0:T(8,128)S(1)}, f32[3,4,16,512]{3,2,1,0:T(8,128)S(1)}, u32[]{:S(2)}, u32[]{:S(2)}) collective-permute-start(f32[3,4,16,512]{3,2,1,0:T(8,128)S(1)} %get-tuple-element.118), channel_id=1, source_target_pairs={{0,48},{1,13},{4,52},{5,1},{8,56},{9,5},{12,60},{13,9},{16,0},{17,... | collective-permute-start | bytes 1179656 | tf_op jit(solution)/shard_map/ppermute | solution.py:404
  115.0 26.3 %collective-permute-start.16 = (f32[2,2,8,16,512]{4,3,2,1,0:T(8,128)S(1)}, f32[2,2,8,16,512]{4,3,2,1,0:T(8,128)S(1)}, u32[]{:S(2)}, u32[]{:S(2)}) collective-permute-start(f32[2,2,8,16,512]{4,3,2,1,0:T(8,128)S(1)} %over_sum.1), channel_id=1, source_target_pairs={{0,1},{1,2},{2,3},{3,4},{4,5},{5,6},{6,7},{7,8},{8,9},{9,10},{10,1... | collective-permute-start | bytes 3145736 | tf_op jit(solution)/shard_map/ppermute | solution.py:388
  117.2 24.1 %collective-permute-start.14 = (f32[2,3,4,16,512]{4,3,2,1,0:T(8,128)S(1)}, f32[2,3,4,16,512]{4,3,2,1,0:T(8,128)S(1)}, u32[]{:S(2)}, u32[]{:S(2)}) collective-permute-start(f32[2,3,4,16,512]{4,3,2,1,0:T(8,128)S(1)} %get-tuple-element.130), channel_id=1, source_target_pairs={{0,16},{1,5},{4,20},{5,9},{8,24},{9,13},{12,28},{13,1},{16,32},{17... | collective-permute-start | bytes 2359304 | tf_op jit(solution)/shard_map/ppermute | solution.py:404
  117.3 24.0 %collective-permute-start.15 = (f32[2,3,4,16,512]{4,3,2,1,0:T(8,128)S(1)}, f32[2,3,4,16,512]{4,3,2,1,0:T(8,128)S(1)}, u32[]{:S(2)}, u32[]{:S(2)}) collective-permute-start(f32[2,3,4,16,512]{4,3,2,1,0:T(8,128)S(1)} %get-tuple-element.131), channel_id=1, source_target_pairs={{0,48},{1,13},{4,52},{5,1},{8,56},{9,5},{12,60},{13,9},{16,0},{17,... | collective-permute-start | bytes 2359304 | tf_op jit(solution)/shard_map/ppermute | solution.py:404
  141.6 8.2 %collective-permute-start.17 = (f32[2,2,3,16,512]{4,3,2,1,0:T(8,128)S(1)}, f32[2,2,3,16,512]{4,3,2,1,0:T(8,128)S(1)}, u32[]{:S(2)}, u32[]{:S(2)}) collective-permute-start(f32[2,2,3,16,512]{4,3,2,1,0:T(8,128)S(1)} %get-tuple-element.137), channel_id=1, source_target_pairs={{0,4},{1,17},{4,8},{5,21},{8,12},{9,25},{12,0},{13,29},{16,20},{17... | collective-permute-start | bytes 1179656 | tf_op jit(solution)/shard_map/ppermute | solution.py:404
  141.7 11.6 %collective-permute-start.18 = (f32[2,2,3,16,512]{4,3,2,1,0:T(8,128)S(1)}, f32[2,2,3,16,512]{4,3,2,1,0:T(8,128)S(1)}, u32[]{:S(2)}, u32[]{:S(2)}) collective-permute-start(f32[2,2,3,16,512]{4,3,2,1,0:T(8,128)S(1)} %get-tuple-element.138), channel_id=1, source_target_pairs={{0,12},{1,49},{4,0},{5,53},{8,4},{9,57},{12,8},{13,61},{16,28},{17... | collective-permute-start | bytes 1179656 | tf_op jit(solution)/shard_map/ppermute | solution.py:404
  144.4 9.7 %collective-permute-start.19 = (f32[2,2,3,16,512]{4,3,2,1,0:T(8,128)S(1)}, f32[2,2,3,16,512]{4,3,2,1,0:T(8,128)S(1)}, u32[]{:S(2)}, u32[]{:S(2)}) collective-permute-start(f32[2,2,3,16,512]{4,3,2,1,0:T(8,128)S(1)} %get-tuple-element.139), channel_id=1, source_target_pairs={{0,8},{1,33},{4,12},{5,37},{8,0},{9,41},{12,4},{13,45},{16,24},{17... | collective-permute-start | bytes 1179656 | tf_op jit(solution)/shard_map/ppermute | solution.py:404
  144.6 28.8 %collective-permute-start.22 = (f32[2,2,8,16,512]{4,3,2,1,0:T(8,128)S(1)}, f32[2,2,8,16,512]{4,3,2,1,0:T(8,128)S(1)}, u32[]{:S(2)}, u32[]{:S(2)}) collective-permute-start(f32[2,2,8,16,512]{4,3,2,1,0:T(8,128)S(1)} %get-tuple-element.146.t), channel_id=1, source_target_pairs={{0,64},{64,0},{1,65},{65,1},{2,66},{66,2},{3,67},{67,3},{4,68},{68... | collective-permute-start | bytes 3145736 | tf_op jit(solution)/shard_map/ppermute | solution.py:392
  154.1 1.5 collective-permute-start.20
  155.7 17.7 %copy-start.2 = (f32[2,512,1024]{2,1,0:T(8,128)S(1)}, f32[2,512,1024]{2,1,0:T(8,128)}, u32[]{:S(2)}) copy-start(f32[2,512,1024]{2,1,0:T(8,128)} %obj.3) | copy-start | bytes 12582916
  155.7 17.6 %collective-permute-start.21 = (f32[13,8,512]{2,1,0:T(8,128)S(1)}, f32[13,8,512]{2,1,0:T(8,128)S(1)}, u32[]{:S(2)}, u32[]{:S(2)}) collective-permute-start(f32[13,8,512]{2,1,0:T(8,128)S(1)} %get-tuple-element.143.near_max), channel_id=1, source_target_pairs={{0,2},{2,0},{64,66},{66,64},{1,3},{3,1},{65,67},{67,65},{4,6},{6,4... | collective-permute-start | bytes 638984 | tf_op jit(solution)/shard_map/ppermute | solution.py:409
  155.8 22.6 %collective-permute-start.24 = (f32[13,8,512]{2,1,0:T(8,128)S(1)}, f32[13,8,512]{2,1,0:T(8,128)S(1)}, u32[]{:S(2)}, u32[]{:S(2)}) collective-permute-start(f32[13,8,512]{2,1,0:T(8,128)S(1)} %get-tuple-element.143.near_max), channel_id=1, source_target_pairs={{0,66},{2,64},{64,2},{66,0},{1,67},{3,65},{65,3},{67,1},{4,70},{6,... | collective-permute-start | bytes 638984 | tf_op jit(solution)/shard_map/ppermute | solution.py:409
  158.1 20.4 %copy-start.11 = (s32[12,12]{1,0:T(8,128)S(1)}, s32[12,12]{1,0:T(8,128)}, u32[]{:S(2)}) copy-start(s32[12,12]{1,0:T(8,128)} %w_ref.1) | copy-start | bytes 1732
  158.1 20.3 %collective-permute-start.23 = (f32[2,6,8,512]{3,2,1,0:T(8,128)S(1)}, f32[2,6,8,512]{3,2,1,0:T(8,128)S(1)}, u32[]{:S(2)}, u32[]{:S(2)}) collective-permute-start(f32[2,6,8,512]{3,2,1,0:T(8,128)S(1)} %get-tuple-element.149.mine), channel_id=1, source_target_pairs={{0,64},{2,66},{64,0},{66,2},{1,65},{3,67},{65,1},{67,3},{4,68},{6,... | collective-permute-start | bytes 589832 | tf_op jit(solution)/shard_map/ppermute | solution.py:409
